TPU v7x, 128 devices: a whole 4x4x4 slice. The times are simulated.
128 devices in a mesh: dp: 8 (over x, core), seq: 16 (over z, y).
Axes of the slice: x: 4, y: 4, z: 4, core: 2. Of those that a mesh axis runs over, the one named last changes fastest.
Arguments:
- queries: bfloat16 [8, 2048, 4096], P('dp', 'seq'), may hold values from -24 to 24
- keys: bfloat16 [8, 2048, 1024], P('dp', 'seq'), may hold values from -6 to 6
- values: bfloat16 [8, 2048, 1024], P('dp', 'seq'), may hold values from -48 to 48
- stem_kv: bfloat16 [8, 2, 4096, 1024], P('dp', None, 'seq'), may hold values from -48 to 48
- seg_ids: int32 [8, 2048], P('dp'), may hold values from 0 to 15, never falling along the last dimension, each value on 1 to 512 neighbouring positions
- seg_parent: int32 [8, 16], P('dp'), may hold values from 0 to 14, as said below
- stem_owner: int32 [8], replicated, may hold values from 0 to 7
Outputs:
- attended: bfloat16 [8, 2048, 4096], P('dp', 'seq')
Inputs may be any that keep to these rules, and one draw needn't show every extreme that they name: seg_parent[g, 0] = 0 and seg_parent[g, s] < s for s >= 1, so each pack's segments form a tree rooted at segment 0. Pack g attends to the stem stored by group stem_owner[g].
All inputs are finite; a program needn't handle non-finite values.
Results may differ from a plain program's by a relative error of at most 0.0088.
Values may be sent and summed in bfloat16 or wider, within the bound.
No kernel may reach another device: no remote copies, remote signals or barrier semaphores. Data moves between devices by JAX's collectives and lax.ppermute only.
A program may use at most 64 MiB of HBM per device.

v0:
```python
import math

import jax
import jax.numpy as jnp
import numpy as np
from jax import lax
from jax.sharding import PartitionSpec as P

H = 32
KVH = 8
HD = 128
STEM = 4096
SEGS = 16


def as_sent(value):

    def short(part):
        return part.astype(jnp.bfloat16) if part.dtype == jnp.float32 else part

    return jax.tree.map(short, value)


def rotary_table():
    halves = np.arange(0, HD, 2) / HD
    inverse = 1.0 / 500000.0**halves
    wavelen = 2.0 * np.pi / inverse
    smooth = (8192.0 / wavelen - 1.0) / 3.0
    blended = (1.0 - smooth) * inverse / 8.0 + smooth * inverse
    scaled = np.where(wavelen < 2048.0, inverse, np.where(wavelen > 8192.0, inverse / 8.0, blended))
    return jnp.asarray(scaled, dtype=jnp.float32)


def rotate(head_block, places):
    rotary = rotary_table()
    angles = places[:, None] * rotary[None, :]
    cosine = jnp.concatenate([jnp.cos(angles), jnp.cos(angles)], axis=1)[:, None, :]
    sine_full = jnp.concatenate([jnp.sin(angles), jnp.sin(angles)], axis=1)[:, None, :]
    widened = head_block.astype(jnp.float32)
    rolled = jnp.concatenate([-widened[..., HD // 2 :], widened[..., : HD // 2]], axis=-1)
    return (widened * cosine + rolled * sine_full).astype(jnp.bfloat16)


def ancestry(parents):
    seg_count = parents.shape[0]
    indices = jnp.arange(seg_count, dtype=jnp.int32)
    linked = (
        (indices[:, None] == indices[None, :]) | (parents[:, None] == indices[None, :])
    ).astype(jnp.float32)
    for sweep in range(max(1, (seg_count - 1).bit_length())):
        linked = (
            jnp.dot(
                linked, linked, precision=lax.Precision.HIGHEST, preferred_element_type=jnp.float32
            )
            > 0.5
        ).astype(jnp.float32)
    return linked


def token_places(seg_row, linked):
    seg_count = linked.shape[0]
    onehot = (seg_row[:, None] == jnp.arange(seg_count, dtype=jnp.int32)[None, :]).astype(
        jnp.float32
    )
    lengths = jnp.sum(onehot, axis=0)
    starts = jnp.cumsum(lengths) - lengths
    before = jnp.sum(linked * lengths[None, :], axis=1) - lengths
    token_ids = jnp.arange(seg_row.shape[0], dtype=jnp.int32).astype(jnp.float32)
    return (
        STEM
        + token_ids
        - jnp.sum(onehot * starts[None, :], axis=1)
        + jnp.sum(onehot * before[None, :], axis=1)
    )


def shards(queries, keys, values, stem_kv, seg_ids, seg_parent, stem_owner):
    tok_count = queries.shape[1]
    seq_count = lax.axis_size("seq")
    pack_len = tok_count * seq_count
    group_size = H // KVH
    local_heads = H // seq_count
    repeat = max(1, seq_count // KVH)
    kv_local = max(KVH, seq_count) // seq_count
    seg_row = seg_ids[0]
    linked = ancestry(seg_parent[0])
    places = token_places(seg_row, linked)
    own_places = lax.dynamic_slice_in_dim(places, lax.axis_index("seq") * tok_count, tok_count)
    q_rot = rotate(queries[0].reshape(tok_count, H, HD), own_places).reshape(tok_count, H * HD)
    k_rot = rotate(keys[0].reshape(tok_count, KVH, HD), own_places)
    k_wide = jnp.repeat(k_rot, repeat, axis=1).reshape(tok_count, repeat * KVH * HD)
    v_wide = jnp.repeat(values[0].reshape(tok_count, KVH, HD), repeat, axis=1).reshape(
        tok_count, repeat * KVH * HD
    )
    q_heads, k_heads, v_heads = (
        lax.all_to_all(q_rot, "seq", split_axis=1, concat_axis=0, tiled=True),
        lax.all_to_all(k_wide, "seq", split_axis=1, concat_axis=0, tiled=True),
        lax.all_to_all(v_wide, "seq", split_axis=1, concat_axis=0, tiled=True),
    )
    owner_group = lax.dynamic_index_in_dim(stem_owner, lax.axis_index("dp"), 0, keepdims=False)
    empty_block = jnp.zeros(stem_kv.shape[1:], jnp.bfloat16)
    incoming = lax.all_gather(stem_kv, "dp", axis=0, tiled=True)
    inside = (owner_group >= 0) & (owner_group < incoming.shape[0])
    chosen = lax.dynamic_index_in_dim(
        incoming, jnp.clip(owner_group, 0, incoming.shape[0] - 1), 0, keepdims=False
    )
    owned = jnp.where(inside, chosen, empty_block)
    stem_rows = owned.shape[1]
    stem_wide = jnp.repeat(owned.reshape(2, stem_rows, KVH, HD), repeat, axis=2).reshape(
        2, stem_rows, repeat * KVH * HD
    )
    stem_heads = lax.all_to_all(stem_wide, "seq", split_axis=2, concat_axis=1, tiled=True)
    stem_len = stem_heads.shape[1]
    key_sets = jnp.concatenate(
        [stem_heads[0].reshape(stem_len, kv_local, HD), k_heads.reshape(pack_len, kv_local, HD)],
        axis=0,
    )
    value_sets = jnp.concatenate(
        [stem_heads[1].reshape(stem_len, kv_local, HD), v_heads.reshape(pack_len, kv_local, HD)],
        axis=0,
    )
    onehot = (seg_row[:, None] == jnp.arange(SEGS, dtype=jnp.int32)[None, :]).astype(jnp.float32)
    reach_rows = jnp.dot(
        onehot, linked, precision=lax.Precision.HIGHEST, preferred_element_type=jnp.float32
    )
    qblock = math.gcd(512, pack_len)
    score_scale = HD ** (-0.5)
    token_ids = jnp.arange(pack_len, dtype=jnp.int32)

    def block_out(block_index):
        row_start = block_index * qblock
        reach_block = lax.dynamic_slice_in_dim(reach_rows, row_start, qblock)
        reach_mask = (
            jnp.dot(
                reach_block,
                onehot.T,
                precision=lax.Precision.HIGHEST,
                preferred_element_type=jnp.float32,
            )
            > 0.5
        )
        row_ids = row_start + jnp.arange(qblock, dtype=jnp.int32)
        visible = jnp.concatenate(
            [
                jnp.ones((qblock, stem_len), dtype=jnp.bool_),
                reach_mask & (token_ids[None, :] <= row_ids[:, None]),
            ],
            axis=1,
        )
        pieces = []
        for head_index in range(local_heads):
            kv_head = head_index // group_size
            query_rows = lax.dynamic_slice(q_heads, (row_start, head_index * HD), (qblock, HD))
            scores = (
                jnp.einsum(
                    "qd,kd->qk",
                    query_rows,
                    key_sets[:, kv_head],
                    preferred_element_type=jnp.float32,
                )
                * score_scale
            )
            masked = jnp.where(visible, scores, -jnp.inf)
            row_max = jnp.max(masked, axis=1, keepdims=True)
            exp_scores = jnp.exp(masked - row_max)
            totals = jnp.sum(exp_scores, axis=1, keepdims=True)
            mixed_sum = jnp.dot(
                exp_scores.astype(jnp.bfloat16),
                value_sets[:, kv_head],
                preferred_element_type=jnp.float32,
            )
            pieces.append((mixed_sum / totals).astype(jnp.bfloat16))
        return jnp.concatenate(pieces, axis=1)

    blocks = lax.map(block_out, jnp.arange(pack_len // qblock, dtype=jnp.int32))
    attended_heads = blocks.reshape(pack_len, local_heads * HD)
    back = lax.all_to_all(
        as_sent(attended_heads), "seq", split_axis=0, concat_axis=1, tiled=True
    ).astype(attended_heads.dtype)
    return back.reshape(1, tok_count, H * HD)


def solution(mesh):
    placed = (
        P("dp", "seq", None),
        P("dp", "seq", None),
        P("dp", "seq", None),
        P("dp", None, "seq", None),
        P("dp", None),
        P("dp", None),
        P(),
    )
    return jax.shard_map(
        shards, mesh=mesh, in_specs=placed, out_specs=P("dp", "seq", None), check_vma=False
    )
```

profile of v0, /device:TPU:1, one launch (start us, length us, event | category | flops | bytes accessed | tf_op | source)
XLA Modules:
  0.0 251.2 jit_solution(1753289735646659849)
XLA Ops:
  12.9 8.6 %all-to-all-start = ((bf16[128,16,256]{0,2,1:T(8,128)(2,1)}), bf16[128,16,256]{0,2,1:T(8,128)(2,1)S(1)}, u32[]{:S(2)}, u32[]{:S(2)}) async-start(bf16[128,16,256]{0,2,1:T(8,128)(2,1)} %fusion.47), calls=%async_computation | async-start | bytes 2097152 | tf_op jit(solution)/shard_map/all_to_all | solution.py:96
  23.8 38.6 %all-gather.2.cloned.1.call-done = bf16[8,2,256,1024]{3,2,1,0:T(8,128)(2,1)} async-done(((bf16[1,2,256,1024]{3,2,1,0:T(8,128)(2,1)}), bf16[8,2,256,1024]{3,2,1,0:T(8,128)(2,1)}) %all-gather.2.cloned.1.call-update) | async-done | bytes 8388624 | tf_op jit(solution)/shard_map/all_gather | solution.py:102
  64.7 3.0 %broadcast_in_dim.19 = bf16[2,256,8,2,128]{1,0,4,3,2:T(2,128)(2,1)} broadcast(bf16[2,256,8,128]{1,0,3,2:T(2,128)(2,1)S(1)} %bitcast.98), dimensions={0,1,2,4} | broadcast | bytes 3145728 | tf_op jit(solution)/shard_map/broadcast_in_dim | solution.py:109
  67.7 6.7 %all-to-all-start.1 = ((bf16[2,256,2048]{1,0,2:T(2,128)(2,1)}), bf16[2,256,2048]{1,0,2:T(2,128)(2,1)S(1)}, u32[]{:S(2)}, u32[]{:S(2)}) async-start(bf16[2,256,2048]{1,0,2:T(2,128)(2,1)} %bitcast.93), calls=%async_computation.1 | async-start | bytes 4194304 | tf_op jit(solution)/shard_map/all_to_all | solution.py:112
  77.7 29.3 %all-to-all-done.1 = bf16[2,256,2048]{1,0,2:T(2,128)(2,1)S(1)} async-done(((bf16[2,256,2048]{1,0,2:T(2,128)(2,1)}), bf16[2,256,2048]{1,0,2:T(2,128)(2,1)S(1)}, u32[]{:S(2)}, u32[]{:S(2)}) %all-to-all-start.1) | async-done | bytes 2097184 | tf_op jit(solution)/shard_map/all_to_all | solution.py:112
  108.9 4.2 %all-to-all-start.2 = ((bf16[128,16,128]{2,0,1:T(8,128)(2,1)}), bf16[128,16,128]{2,0,1:T(8,128)(2,1)}, u32[]{:S(2)}, u32[]{:S(2)}) async-start(bf16[128,16,128]{2,0,1:T(8,128)(2,1)} %bitcast.102), calls=%async_computation.2 | async-start | bytes 1048576 | tf_op jit(solution)/shard_map/all_to_all | solution.py:97
  118.3 5.1 %all-to-all-done.2 = bf16[128,16,128]{2,0,1:T(8,128)(2,1)} async-done(((bf16[128,16,128]{2,0,1:T(8,128)(2,1)}), bf16[128,16,128]{2,0,1:T(8,128)(2,1)}, u32[]{:S(2)}, u32[]{:S(2)}) %all-to-all-start.2) | async-done | bytes 524320 | tf_op jit(solution)/shard_map/all_to_all | solution.py:97
  124.3 3.6 %all-to-all-start.3 = ((bf16[128,16,128]{2,0,1:T(8,128)(2,1)}), bf16[128,16,128]{2,0,1:T(8,128)(2,1)S(1)}, u32[]{:S(2)}, u32[]{:S(2)}) async-start(bf16[128,16,128]{2,0,1:T(8,128)(2,1)} %bitcast.21), calls=%async_computation.3 | async-start | bytes 1048576 | tf_op jit(solution)/shard_map/all_to_all | solution.py:98
  127.8 2.3 pad_maximum_fusion
  130.2 7.1 %all-to-all-done.3 = bf16[128,16,128]{2,0,1:T(8,128)(2,1)S(1)} async-done(((bf16[128,16,128]{2,0,1:T(8,128)(2,1)}), bf16[128,16,128]{2,0,1:T(8,128)(2,1)S(1)}, u32[]{:S(2)}, u32[]{:S(2)}) %all-to-all-start.3) | async-done | bytes 524320 | tf_op jit(solution)/shard_map/all_to_all | solution.py:98
  137.4 87.5 %while.11 = (s32[]{:T(128)}, bf16[4,512,256]{2,1,0:T(8,128)(2,1)}, s32[4]{0:T(128)S(1)}, f32[2048,16]{0,1:T(8,128)S(1)}, bf16[2048,256]{1,0:T(8,128)(2,1)}, /*in...) while((s32[]{:T(128)}, bf16[4,512,256]{2,1,0:T(8,128)(2,1)}, ...), condition=%wide.region_10.11_spmd.clone, body=%wide.region_5.10_spmd.clone.sunk | while | flops 3470588416 | bytes 93389528 | solution.py:175
  138.7 5.0 %fusion.86 = pred[512,2048]{1,0:T(32,128)(4,1)S(1)} fusion(s32[512]{0:T(512)S(1)} %iota_add_fusion.2, s32[2048]{0:T(1024)S(1)} %get-tuple-element.197, f32[2048,16]{0,1:T(8,128)S(1)} %get-tuple-element.193, s32[]{:T(128)S(6)} %select_n.46), kind=kOutput, calls=%fused_computation.15.clone.1 | convolution fusion | flops 204537856 | bytes 1091588 | tf_op jit(solution)/shard_map/while/body/eval_jaxpr/dot_general | solution.py:134
  143.8 3.1 %fusion.90 = (f32[512]{0:T(512)S(1)}, f32[512,6144]{1,0:T(8,128)S(1)}) fusion(bf16[6144,1,128]{2,0,1:T(8,128)(2,1)S(1)} %copy-done, bf16[2048,256]{1,0:T(8,128)(2,1)} %get-tuple-element.194, s32[]{:T(128)S(6)} %select_n.46, pred[512,2048]{1,0:T(32,128)(4,1)S(1)} %fusion.86), kind=kOutput, calls=%fused_computation.73.clone.1 | convolution fusion | flops 814743040 | bytes 15337476 | tf_op jit(solution)/shard_map/while/body/eval_jaxpr/qd,kd->qk/dot_general | solution.py:155
  148.8 2.4 fusion.92
  151.1 3.1 %fusion.87 = (f32[512]{0:T(512)S(1)}, f32[512,6144]{1,0:T(8,128)S(1)}) fusion(bf16[6144,1,128]{2,0,1:T(8,128)(2,1)S(1)} %copy-done, bf16[2048,256]{1,0:T(8,128)(2,1)} %get-tuple-element.194, s32[]{:T(128)S(6)} %select_n.46, pred[512,2048]{1,0:T(32,128)(4,1)S(1)} %fusion.86), kind=kOutput, calls=%fused_computation.72.clone.1 | convolution fusion | flops 814743040 | bytes 15337476 | tf_op jit(solution)/shard_map/while/body/eval_jaxpr/qd,kd->qk/dot_general | solution.py:155
  156.1 2.4 fusion.89
  160.6 5.0 %fusion.86 = pred[512,2048]{1,0:T(32,128)(4,1)S(1)} fusion(s32[512]{0:T(512)S(1)} %iota_add_fusion.2, s32[2048]{0:T(1024)S(1)} %get-tuple-element.197, f32[2048,16]{0,1:T(8,128)S(1)} %get-tuple-element.193, s32[]{:T(128)S(6)} %select_n.46), kind=kOutput, calls=%fused_computation.15.clone.1 | convolution fusion | flops 204537856 | bytes 1091588 | tf_op jit(solution)/shard_map/while/body/eval_jaxpr/dot_general | solution.py:134
  165.6 3.1 %fusion.90 = (f32[512]{0:T(512)S(1)}, f32[512,6144]{1,0:T(8,128)S(1)}) fusion(bf16[6144,1,128]{2,0,1:T(8,128)(2,1)S(1)} %copy-done, bf16[2048,256]{1,0:T(8,128)(2,1)} %get-tuple-element.194, s32[]{:T(128)S(6)} %select_n.46, pred[512,2048]{1,0:T(32,128)(4,1)S(1)} %fusion.86), kind=kOutput, calls=%fused_computation.73.clone.1 | convolution fusion | flops 814743040 | bytes 15337476 | tf_op jit(solution)/shard_map/while/body/eval_jaxpr/qd,kd->qk/dot_general | solution.py:155
  170.6 2.4 fusion.92
  172.9 3.1 %fusion.87 = (f32[512]{0:T(512)S(1)}, f32[512,6144]{1,0:T(8,128)S(1)}) fusion(bf16[6144,1,128]{2,0,1:T(8,128)(2,1)S(1)} %copy-done, bf16[2048,256]{1,0:T(8,128)(2,1)} %get-tuple-element.194, s32[]{:T(128)S(6)} %select_n.46, pred[512,2048]{1,0:T(32,128)(4,1)S(1)} %fusion.86), kind=kOutput, calls=%fused_computation.72.clone.1 | convolution fusion | flops 814743040 | bytes 15337476 | tf_op jit(solution)/shard_map/while/body/eval_jaxpr/qd,kd->qk/dot_general | solution.py:155
  178.0 2.4 fusion.89
  182.4 5.0 %fusion.86 = pred[512,2048]{1,0:T(32,128)(4,1)S(1)} fusion(s32[512]{0:T(512)S(1)} %iota_add_fusion.2, s32[2048]{0:T(1024)S(1)} %get-tuple-element.197, f32[2048,16]{0,1:T(8,128)S(1)} %get-tuple-element.193, s32[]{:T(128)S(6)} %select_n.46), kind=kOutput, calls=%fused_computation.15.clone.1 | convolution fusion | flops 204537856 | bytes 1091588 | tf_op jit(solution)/shard_map/while/body/eval_jaxpr/dot_general | solution.py:134
  187.4 3.1 %fusion.90 = (f32[512]{0:T(512)S(1)}, f32[512,6144]{1,0:T(8,128)S(1)}) fusion(bf16[6144,1,128]{2,0,1:T(8,128)(2,1)S(1)} %copy-done, bf16[2048,256]{1,0:T(8,128)(2,1)} %get-tuple-element.194, s32[]{:T(128)S(6)} %select_n.46, pred[512,2048]{1,0:T(32,128)(4,1)S(1)} %fusion.86), kind=kOutput, calls=%fused_computation.73.clone.1 | convolution fusion | flops 814743040 | bytes 15337476 | tf_op jit(solution)/shard_map/while/body/eval_jaxpr/qd,kd->qk/dot_general | solution.py:155
  192.4 2.4 fusion.92
  194.8 3.1 %fusion.87 = (f32[512]{0:T(512)S(1)}, f32[512,6144]{1,0:T(8,128)S(1)}) fusion(bf16[6144,1,128]{2,0,1:T(8,128)(2,1)S(1)} %copy-done, bf16[2048,256]{1,0:T(8,128)(2,1)} %get-tuple-element.194, s32[]{:T(128)S(6)} %select_n.46, pred[512,2048]{1,0:T(32,128)(4,1)S(1)} %fusion.86), kind=kOutput, calls=%fused_computation.72.clone.1 | convolution fusion | flops 814743040 | bytes 15337476 | tf_op jit(solution)/shard_map/while/body/eval_jaxpr/qd,kd->qk/dot_general | solution.py:155
  199.8 2.4 fusion.89
  204.2 5.0 %fusion.86 = pred[512,2048]{1,0:T(32,128)(4,1)S(1)} fusion(s32[512]{0:T(512)S(1)} %iota_add_fusion.2, s32[2048]{0:T(1024)S(1)} %get-tuple-element.197, f32[2048,16]{0,1:T(8,128)S(1)} %get-tuple-element.193, s32[]{:T(128)S(6)} %select_n.46), kind=kOutput, calls=%fused_computation.15.clone.1 | convolution fusion | flops 204537856 | bytes 1091588 | tf_op jit(solution)/shard_map/while/body/eval_jaxpr/dot_general | solution.py:134
  209.2 3.1 %fusion.90 = (f32[512]{0:T(512)S(1)}, f32[512,6144]{1,0:T(8,128)S(1)}) fusion(bf16[6144,1,128]{2,0,1:T(8,128)(2,1)S(1)} %copy-done, bf16[2048,256]{1,0:T(8,128)(2,1)} %get-tuple-element.194, s32[]{:T(128)S(6)} %select_n.46, pred[512,2048]{1,0:T(32,128)(4,1)S(1)} %fusion.86), kind=kOutput, calls=%fused_computation.73.clone.1 | convolution fusion | flops 814743040 | bytes 15337476 | tf_op jit(solution)/shard_map/while/body/eval_jaxpr/qd,kd->qk/dot_general | solution.py:155
  214.2 2.4 fusion.92
  216.6 3.1 %fusion.87 = (f32[512]{0:T(512)S(1)}, f32[512,6144]{1,0:T(8,128)S(1)}) fusion(bf16[6144,1,128]{2,0,1:T(8,128)(2,1)S(1)} %copy-done, bf16[2048,256]{1,0:T(8,128)(2,1)} %get-tuple-element.194, s32[]{:T(128)S(6)} %select_n.46, pred[512,2048]{1,0:T(32,128)(4,1)S(1)} %fusion.86), kind=kOutput, calls=%fused_computation.72.clone.1 | convolution fusion | flops 814743040 | bytes 15337476 | tf_op jit(solution)/shard_map/while/body/eval_jaxpr/qd,kd->qk/dot_general | solution.py:155
  221.6 2.4 fusion.89
  224.8 17.5 %all_to_all.79 = bf16[16,128,256]{2,1,0:T(8,128)(2,1)S(1)} all-to-all(bf16[16,128,256]{2,1,0:T(8,128)(2,1)} %bitcast.105), channel_id=1, replica_groups=mesh['dp'=8,'seq'=16] {'seq'}, dimensions={0} | all-to-all | bytes 2097152 | tf_op jit(solution)/shard_map/all_to_all | solution.py:177
  (98 shorter events, 43.3 us)
Async XLA Ops:
  6.5 4.2 %copy-start.6 = (f32[64]{0:T(128)S(1)}, f32[64]{0:T(128)}, u32[]{:S(2)}) copy-start(f32[64]{0:T(128)} %constant.76.clone) | copy-start | bytes 772
  6.5 4.0 %copy-start.5 = (s32[1,2048]{1,0:T(1,128)S(1)}, s32[1,2048]{1,0:T(1,128)}, u32[]{:S(2)}) copy-start(s32[1,2048]{1,0:T(1,128)} %param.15) | copy-start | bytes 24580
  6.5 3.3 %copy-start.7 = (s32[1,16]{1,0:T(1,128)S(1)}, s32[1,16]{1,0:T(1,128)}, u32[]{:S(2)}) copy-start(s32[1,16]{1,0:T(1,128)} %param.16) | copy-start | bytes 196
  6.5 55.9 %all-gather.2.cloned.1.call-start = ((), (), s32[]{:S(2)}) async-start(), calls=%async_computation.5 | async-start | bytes 9437184 | tf_op jit(solution)/shard_map/all_gather | solution.py:102
  11.5 10.0 %copy-start.8 = (s32[8]{0:T(128)S(1)}, s32[8]{0:T(128)}, u32[]{:S(2)}) copy-start(s32[8]{0:T(128)} %param.17) | copy-start | bytes 100
  12.9 51.8 %all-to-all-start = ((bf16[128,16,256]{0,2,1:T(8,128)(2,1)}), bf16[128,16,256]{0,2,1:T(8,128)(2,1)S(1)}, u32[]{:S(2)}, u32[]{:S(2)}) async-start(bf16[128,16,256]{0,2,1:T(8,128)(2,1)} %fusion.47), calls=%async_computation | async-start | bytes 2097152 | tf_op jit(solution)/shard_map/all_to_all | solution.py:96
  64.7 11.1 %copy-start.1 = (bf16[1,128,1024]{2,1,0:T(8,128)(2,1)S(1)}, bf16[1,128,1024]{2,1,0:T(8,128)(2,1)}, u32[]{:S(2)}) copy-start(bf16[1,128,1024]{2,1,0:T(8,128)(2,1)} %param.12) | copy-start | bytes 786436
  67.7 39.4 %all-to-all-start.1 = ((bf16[2,256,2048]{1,0,2:T(2,128)(2,1)}), bf16[2,256,2048]{1,0,2:T(2,128)(2,1)S(1)}, u32[]{:S(2)}, u32[]{:S(2)}) async-start(bf16[2,256,2048]{1,0,2:T(2,128)(2,1)} %bitcast.93), calls=%async_computation.1 | async-start | bytes 4194304 | tf_op jit(solution)/shard_map/all_to_all | solution.py:112
  75.1 1.1 copy-start.2
  75.8 0.8 copy-start.3
  75.8 1.8 copy-start.4
  108.9 14.5 %all-to-all-start.2 = ((bf16[128,16,128]{2,0,1:T(8,128)(2,1)}), bf16[128,16,128]{2,0,1:T(8,128)(2,1)}, u32[]{:S(2)}, u32[]{:S(2)}) async-start(bf16[128,16,128]{2,0,1:T(8,128)(2,1)} %bitcast.102), calls=%async_computation.2 | async-start | bytes 1048576 | tf_op jit(solution)/shard_map/all_to_all | solution.py:97
  124.3 13.0 %all-to-all-start.3 = ((bf16[128,16,128]{2,0,1:T(8,128)(2,1)}), bf16[128,16,128]{2,0,1:T(8,128)(2,1)S(1)}, u32[]{:S(2)}, u32[]{:S(2)}) async-start(bf16[128,16,128]{2,0,1:T(8,128)(2,1)} %bitcast.21), calls=%async_computation.3 | async-start | bytes 1048576 | tf_op jit(solution)/shard_map/all_to_all | solution.py:98
  138.7 5.0 %copy-start = (bf16[6144,1,128]{2,0,1:T(8,128)(2,1)S(1)}, bf16[6144,1,128]{2,0,1:T(8,128)(2,1)}, u32[]{:S(2)}) copy-start(bf16[6144,1,128]{2,0,1:T(8,128)(2,1)} %get-tuple-element.195) | copy-start | bytes 4718596 | tf_op jit(solution)/shard_map/while
  160.5 5.0 %copy-start = (bf16[6144,1,128]{2,0,1:T(8,128)(2,1)S(1)}, bf16[6144,1,128]{2,0,1:T(8,128)(2,1)}, u32[]{:S(2)}) copy-start(bf16[6144,1,128]{2,0,1:T(8,128)(2,1)} %get-tuple-element.195) | copy-start | bytes 4718596 | tf_op jit(solution)/shard_map/while
  182.4 5.0 %copy-start = (bf16[6144,1,128]{2,0,1:T(8,128)(2,1)S(1)}, bf16[6144,1,128]{2,0,1:T(8,128)(2,1)}, u32[]{:S(2)}) copy-start(bf16[6144,1,128]{2,0,1:T(8,128)(2,1)} %get-tuple-element.195) | copy-start | bytes 4718596 | tf_op jit(solution)/shard_map/while
  204.2 5.0 %copy-start = (bf16[6144,1,128]{2,0,1:T(8,128)(2,1)S(1)}, bf16[6144,1,128]{2,0,1:T(8,128)(2,1)}, u32[]{:S(2)}) copy-start(bf16[6144,1,128]{2,0,1:T(8,128)(2,1)} %get-tuple-element.195) | copy-start | bytes 4718596 | tf_op jit(solution)/shard_map/while
Sparse Core Ops, SparseCore 0:
  9.1 53.3 all-gather.1
where the time goes:
time: 255 us; the launch traced here: 251 us
  waiting for transfers between devices  80.8 us (32%)
  matrix products  64.6 us (25%)
  local copies, waits for them, and re-layouts  24.6 us (10%)
  starting transfers between devices  23.1 us (9%)
  other arithmetic  22.4 us (9%)
  blocking collectives  17.5 us (7%)
  between operations  15.4 us (6%)
  loops' own time  2.79 us (1%)
    all_gather x1, waiting for transfers between devices, shards(): incoming = lax.all_gather(stem_kv, 'dp', axis=0, tiled=True)  38.6 us
    all_to_all x1, waiting for transfers between devices, shards(): lax.all_to_all(stem_wide, 'seq', split_axis=2, concat_axis=1, tiled=True)  29.3 us
    dot_general x8, matrix products, block_out(): jnp.einsum('qd,kd->qk', query_rows, key_sets[:, kv_head], preferred_eleme...  24.9 us
    dot_general x4, matrix products, block_out(): jnp.dot(reach_block, onehot.T, precision=lax.Precision.HIGHEST, preferred...  20 us
    dot_general x8, matrix products, block_out(): jnp.dot(exp_scores.astype(jnp.bfloat16), value_sets[:, kv_head], preferre...  18.8 us
    all_to_all x1, blocking collectives, shards(): lax.all_to_all(as_sent(attended_heads), 'seq', split_axis=0, concat_axis=...  17.5 us
    reduce_sum x8, other arithmetic, block_out(): totals = jnp.sum(exp_scores, axis=1, keepdims=True)  15.1 us
    all_to_all x1, starting transfers between devices, shards(): lax.all_to_all(q_rot, 'seq', split_axis=1, concat_axis=0, tiled=True)  8.6 us
  transfers between devices with their start and end apart: 5, of which 4 were waited for; matrix products, arithmetic and copies ran while one was open for 7% of the time, Pallas kernels for 0%

commit v1 on v0

--- a/solution.py
+++ b/solution.py
@@ -1,9 +1,12 @@
+import functools
 import math
 
 import jax
 import jax.numpy as jnp
 import numpy as np
 from jax import lax
+from jax.experimental import pallas as pl
+from jax.experimental.pallas import tpu as pltpu
 from jax.sharding import PartitionSpec as P
 
 H = 32
@@ -72,6 +75,117 @@
         - jnp.sum(onehot * starts[None, :], axis=1)
         + jnp.sum(onehot * before[None, :], axis=1)
     )
+
+
+BARRED = -1e30
+BQ = 512
+SCALE=HD**-0.5*math.log2(math.e)
+SHIFT=60.0/SCALE
+TINY=2.0**-60
+NT=(((1,),(1,)),((),()))
+
+def attn_kernel(vis_ref, q_ref, qb_ref, kb_ref, ks_ref, vs_ref, kp_ref, vp_ref, o_ref, qa, ka, va, kap, vap, acc, kmax, *, BQ, CK, stem, pack):
+    qi=pl.program_id(0)
+    R=2*BQ
+    lane=lax.broadcasted_iota(jnp.int32,(1,128),1)
+    @pl.when(qi==0)
+    def _():
+        def sq(x):
+            x=x.astype(jnp.float32); return jnp.max(jnp.sum(x*x,axis=1,keepdims=True),axis=0,keepdims=True)
+        ka[:, :128]=ks_ref[...]
+        ka[:, 128:]=jnp.broadcast_to(jnp.where(lane==16,-1.0,0.0).astype(jnp.bfloat16),(stem,128))
+        va[:, :128]=vs_ref[...]
+        va[:, 128:]=jnp.ones((stem,128),jnp.bfloat16)
+        kap[:, :128]=kp_ref[...]
+        kap[:, 128:]=kb_ref[...]
+        vap[:, :128]=vp_ref[...]
+        vap[:, 128:]=jnp.ones((pack,128),jnp.bfloat16)
+        m=jnp.zeros((1,1),jnp.float32)
+        for c in range(stem//512):
+            m=jnp.maximum(m,sq(ks_ref[pl.ds(c*512,512),:]))
+        for c in range(pack//512):
+            m=jnp.maximum(m,sq(kp_ref[pl.ds(c*512,512),:]))
+        kmax[...]=jnp.broadcast_to(jnp.sqrt(m),(8,128))
+    qf=jnp.concatenate([q_ref[:, :128],q_ref[:,128:]],axis=0)
+    qa[:, :128]=qf
+    qb=qb_ref[...]
+    qb2=jnp.concatenate([qb,qb],axis=0)
+    q32=qf.astype(jnp.float32)
+    bound=jnp.sqrt(jnp.sum(q32*q32,axis=1,keepdims=True))*kmax[0:1,0:1]*1.02-SHIFT
+
+    def set_m(m):
+        qa[:,128:]=jnp.where(lane==16,m,qb2.astype(jnp.float32)).astype(jnp.bfloat16)
+
+    def scores(kref,start,size):
+        return lax.dot_general(qa[...],kref[pl.ds(start,size),:],NT,preferred_element_type=jnp.float32)
+
+    def run():
+        n=stem//CK
+        a=None
+        s=scores(ka,0,CK)
+        for c in range(n):
+            s_next=scores(ka,(c+1)*CK,CK) if c+1<n else None
+            p=jnp.exp2(s*SCALE).astype(jnp.bfloat16)
+            d=jnp.dot(p,va[pl.ds(c*CK,CK),:],preferred_element_type=jnp.float32)
+            a=d if a is None else a+d
+            s=s_next
+        st=pl.multiple_of(qi*BQ,BQ)
+        s=scores(kap,st,BQ)
+        r=lax.broadcasted_iota(jnp.int32,(R,BQ),0)
+        r=jnp.where(r>=BQ,r-BQ,r)
+        col=lax.broadcasted_iota(jnp.int32,(R,BQ),1)
+        p=jnp.where(col<=r,jnp.exp2(s*SCALE),0.0).astype(jnp.bfloat16)
+        a=a+jnp.dot(p,vap[pl.ds(st,BQ),:],preferred_element_type=jnp.float32)
+        acc[...]=a
+        def body(kj,_):
+            @pl.when(vis_ref[qi,kj]>0)
+            def _():
+                st=pl.multiple_of(kj*BQ,BQ)
+                p=jnp.exp2(scores(kap,st,BQ)*SCALE).astype(jnp.bfloat16)
+                acc[...]+=jnp.dot(p,vap[pl.ds(st,BQ),:],preferred_element_type=jnp.float32)
+            return 0
+        lax.fori_loop(0,qi,body,0)
+
+    def finish():
+        a=acc[...]
+        o=(a[:, :128]/a[:,128:129]).astype(jnp.bfloat16)
+        o_ref[:, :128]=o[:BQ]
+        o_ref[:, 128:]=o[BQ:]
+    set_m(bound)
+    run()
+    finish()
+    low=jnp.min(acc[:,128:])
+    @pl.when(low<TINY)
+    def _():
+        set_m(jnp.zeros((R,1),jnp.float32))
+        def smax(c,m):
+            return jnp.maximum(m,jnp.max(scores(ka,pl.multiple_of(c*512,512),512),axis=1,keepdims=True))
+        m=lax.fori_loop(0,stem//512,smax,jnp.full((R,1),-1e30,jnp.float32))
+        def pmax(kj,m):
+            s=scores(kap,pl.multiple_of(kj*BQ,BQ),BQ)
+            r=lax.broadcasted_iota(jnp.int32,(R,BQ),0)
+            r=jnp.where(r>=BQ,r-BQ,r)+qi*BQ
+            col=lax.broadcasted_iota(jnp.int32,(R,BQ),1)+kj*BQ
+            return jnp.maximum(m,jnp.max(jnp.where(col<=r,s,-1e30),axis=1,keepdims=True))
+        m=lax.fori_loop(0,qi+1,pmax,m)
+        set_m(m)
+        run()
+        finish()
+
+def attention(vis,q,qb,kb,ks,vs,kp,vp,*,BQ=256,CK=512):
+    stem=ks.shape[0]; pack=q.shape[0]
+    full=lambda n:pl.BlockSpec((n,128),lambda i,v:(0,0),pipeline_mode=pl.Buffered(1))
+    return pl.pallas_call(
+        functools.partial(attn_kernel,BQ=BQ,CK=CK,stem=stem,pack=pack),
+        out_shape=jax.ShapeDtypeStruct((pack,256),jnp.bfloat16),
+        grid_spec=pltpu.PrefetchScalarGridSpec(num_scalar_prefetch=1,grid=(pack//BQ,),
+            in_specs=[pl.BlockSpec((BQ,256),lambda i,v:(i,0)),pl.BlockSpec((BQ,128),lambda i,v:(i,0)),full(pack),full(stem),full(stem),full(pack),full(pack)],
+            out_specs=pl.BlockSpec((BQ,256),lambda i,v:(i,0)),
+            scratch_shapes=[pltpu.VMEM((2*BQ,256),jnp.bfloat16),pltpu.VMEM((stem,256),jnp.bfloat16),pltpu.VMEM((stem,256),jnp.bfloat16),
+                pltpu.VMEM((pack,256),jnp.bfloat16),pltpu.VMEM((pack,256),jnp.bfloat16),pltpu.VMEM((2*BQ,256),jnp.float32),pltpu.VMEM((8,128),jnp.float32)]),
+        compiler_params=pltpu.CompilerParams(vmem_limit_bytes=56*1024*1024),
+        name="attn",
+    )(vis,q,qb,kb,ks,vs,kp,vp)
 
 
 def shards(queries, keys, values, stem_kv, seg_ids, seg_parent, stem_owner):
@@ -110,73 +224,16 @@
         2, stem_rows, repeat * KVH * HD
     )
     stem_heads = lax.all_to_all(stem_wide, "seq", split_axis=2, concat_axis=1, tiled=True)
-    stem_len = stem_heads.shape[1]
-    key_sets = jnp.concatenate(
-        [stem_heads[0].reshape(stem_len, kv_local, HD), k_heads.reshape(pack_len, kv_local, HD)],
-        axis=0,
-    )
-    value_sets = jnp.concatenate(
-        [stem_heads[1].reshape(stem_len, kv_local, HD), v_heads.reshape(pack_len, kv_local, HD)],
-        axis=0,
-    )
-    onehot = (seg_row[:, None] == jnp.arange(SEGS, dtype=jnp.int32)[None, :]).astype(jnp.float32)
-    reach_rows = jnp.dot(
-        onehot, linked, precision=lax.Precision.HIGHEST, preferred_element_type=jnp.float32
-    )
-    qblock = math.gcd(512, pack_len)
-    score_scale = HD ** (-0.5)
-    token_ids = jnp.arange(pack_len, dtype=jnp.int32)
-
-    def block_out(block_index):
-        row_start = block_index * qblock
-        reach_block = lax.dynamic_slice_in_dim(reach_rows, row_start, qblock)
-        reach_mask = (
-            jnp.dot(
-                reach_block,
-                onehot.T,
-                precision=lax.Precision.HIGHEST,
-                preferred_element_type=jnp.float32,
-            )
-            > 0.5
-        )
-        row_ids = row_start + jnp.arange(qblock, dtype=jnp.int32)
-        visible = jnp.concatenate(
-            [
-                jnp.ones((qblock, stem_len), dtype=jnp.bool_),
-                reach_mask & (token_ids[None, :] <= row_ids[:, None]),
-            ],
-            axis=1,
-        )
-        pieces = []
-        for head_index in range(local_heads):
-            kv_head = head_index // group_size
-            query_rows = lax.dynamic_slice(q_heads, (row_start, head_index * HD), (qblock, HD))
-            scores = (
-                jnp.einsum(
-                    "qd,kd->qk",
-                    query_rows,
-                    key_sets[:, kv_head],
-                    preferred_element_type=jnp.float32,
-                )
-                * score_scale
-            )
-            masked = jnp.where(visible, scores, -jnp.inf)
-            row_max = jnp.max(masked, axis=1, keepdims=True)
-            exp_scores = jnp.exp(masked - row_max)
-            totals = jnp.sum(exp_scores, axis=1, keepdims=True)
-            mixed_sum = jnp.dot(
-                exp_scores.astype(jnp.bfloat16),
-                value_sets[:, kv_head],
-                preferred_element_type=jnp.float32,
-            )
-            pieces.append((mixed_sum / totals).astype(jnp.bfloat16))
-        return jnp.concatenate(pieces, axis=1)
-
-    blocks = lax.map(block_out, jnp.arange(pack_len // qblock, dtype=jnp.int32))
-    attended_heads = blocks.reshape(pack_len, local_heads * HD)
-    back = lax.all_to_all(
-        as_sent(attended_heads), "seq", split_axis=0, concat_axis=1, tiled=True
-    ).astype(attended_heads.dtype)
+    onehot = (seg_row[:, None] == jnp.arange(128, dtype=jnp.int32)[None, :]).astype(jnp.float32)
+    barred = jnp.pad(BARRED * (1.0 - linked), ((0, 112), (0, 112)))
+    q_bias = jnp.dot(onehot, barred, precision=lax.Precision.HIGHEST).astype(jnp.bfloat16)
+    k_bias = jnp.where(jnp.arange(128)[None, :] == SEGS, -1.0, onehot).astype(jnp.bfloat16)
+    present = onehot.reshape(pack_len // BQ, BQ, 128).max(axis=1)[:, :SEGS]
+    seen = (present @ linked @ present.T > 0.5).astype(jnp.int32)
+    attended_heads = attention(
+        seen, q_heads, q_bias, k_bias, stem_heads[0], stem_heads[1], k_heads, v_heads, BQ=BQ, CK=256
+    )
+    back = lax.all_to_all(attended_heads, "seq", split_axis=0, concat_axis=1, tiled=True)
     return back.reshape(1, tok_count, H * HD)
 
 

time: 255 us -> 188 us (0.74)
  matrix products: 64.6 us -> 3.73 us
  Pallas kernels: 0 us -> 35.4 us
  waiting for transfers between devices: 80.8 us -> 63.2 us
  other arithmetic: 22.4 us -> 9.27 us
  local copies, waits for them, and re-layouts: 24.6 us -> 16.2 us
  loops' own time: 2.79 us -> 0 us
    dot_general x21 -> x2, matrix products: 63.9 us -> 2.32 us  [the longest x1 1.52 us: shards(): jnp.dot(onehot, barred, precision=lax.Precision.HIGHEST)]
    pallas_call x0 -> x1, Pallas kernels: none -> 35.4 us  [attention(): pl.pallas_call(functools.partial(attn_kernel, BQ=BQ, CK=CK, stem=stem, pa...]
    all_gather x1, waiting for transfers between devices: 38.6 us -> 22 us  [shards(): incoming = lax.all_gather(stem_kv, 'dp', axis=0, tiled=True)]
    reduce_sum x8 -> x0, other arithmetic: 15.1 us -> none  [block_out(): totals = jnp.sum(exp_scores, axis=1, keepdims=True)]
    all_to_all x1, starting transfers between devices: 8.6 us -> 3.66 us  [shards(): lax.all_to_all(q_rot, 'seq', split_axis=1, concat_axis=0, tiled=True)]
    all_to_all x1, starting transfers between devices: 4.24 us -> 8.6 us  [shards(): lax.all_to_all(k_wide, 'seq', split_axis=1, concat_axis=0, tiled=True)]
    dynamic_update_slice x8 -> x0, local copies, waits for them, and re-layouts: 3.43 us -> none  [shards(): blocks = lax.map(block_out, jnp.arange(pack_len // qblock, dtype=jnp.int32))]
    another operation x1 -> x0, loops' own time: 2.79 us -> none  [shards(): blocks = lax.map(block_out, jnp.arange(pack_len // qblock, dtype=jnp.int32))]
  transfers between devices with their start and end apart: 5 -> 5, of which waited for: 4 -> 4; matrix products, arithmetic and copies ran while one was open for 7% -> 12% of each run, Pallas kernels for 0% -> 0%
where the time goes in v1:
time: 188 us; the launch traced here: 186 us
  waiting for transfers between devices  63.2 us (34%)
  Pallas kernels  35.4 us (19%)
  starting transfers between devices  23.3 us (12%)
  blocking collectives  19.2 us (10%)
  local copies, waits for them, and re-layouts  16.2 us (9%)
  between operations  15.6 us (8%)
  other arithmetic  9.27 us (5%)
  matrix products  3.73 us (2%)
    pallas_call x1, Pallas kernels, attention(): pl.pallas_call(functools.partial(attn_kernel, BQ=BQ, CK=CK, stem=stem, pa...  35.4 us
    all_to_all x1, waiting for transfers between devices, shards(): lax.all_to_all(stem_wide, 'seq', split_axis=2, concat_axis=1, tiled=True)  28.3 us
    all_gather x1, waiting for transfers between devices, shards(): incoming = lax.all_gather(stem_kv, 'dp', axis=0, tiled=True)  22 us
    all_to_all x1, blocking collectives, shards(): lax.all_to_all(attended_heads, 'seq', split_axis=0, concat_axis=1, tiled=...  19.2 us
    all_to_all x1, starting transfers between devices, shards(): lax.all_to_all(k_wide, 'seq', split_axis=1, concat_axis=0, tiled=True)  8.6 us
    all_to_all x1, waiting for transfers between devices, shards(): lax.all_to_all(k_wide, 'seq', split_axis=1, concat_axis=0, tiled=True)  7.07 us
    all_to_all x1, starting transfers between devices, shards(): lax.all_to_all(stem_wide, 'seq', split_axis=2, concat_axis=1, tiled=True)  6.83 us
    all_to_all x1, waiting for transfers between devices, shards(): lax.all_to_all(v_wide, 'seq', split_axis=1, concat_axis=0, tiled=True)  5.09 us
  transfers between devices with their start and end apart: 5, of which 4 were waited for; matrix products, arithmetic and copies ran while one was open for 12% of the time, Pallas kernels for 0%

profile of v1, /device:TPU:1, one launch (start us, length us, event | category | flops | bytes accessed | tf_op | source)
XLA Modules:
  0.0 185.9 jit_solution(17475254940490719155)
XLA Ops:
  6.5 0.7 all-gather.2.cloned.1.call-update
  7.3 0.8 convert_reduce_fusion.1
  8.3 0.9 convolution_compare_fusion.3
  9.8 0.8 select_reduce_fusion.1
  10.7 0.8 multiply_cosine_fusion
  11.7 1.0 convert_bitcast_fusion
  13.3 0.9 broadcast_in_dim.20
  14.3 8.6 %all-to-all-start.2 = ((bf16[128,16,128]{2,0,1:T(8,128)(2,1)}), bf16[128,16,128]{2,0,1:T(8,128)(2,1)S(1)}, u32[]{:S(2)}, u32[]{:S(2)}) async-start(bf16[128,16,128]{2,0,1:T(8,128)(2,1)} %bitcast.18), calls=%async_computation.2 | async-start | bytes 1048576 | tf_op jit(solution)/shard_map/all_to_all | solution.py:211
  22.9 1.5 copy.42
  25.0 1.3 fusion
  26.3 7.1 %all-to-all-done.2 = bf16[128,16,128]{2,0,1:T(8,128)(2,1)S(1)} async-done(((bf16[128,16,128]{2,0,1:T(8,128)(2,1)}), bf16[128,16,128]{2,0,1:T(8,128)(2,1)S(1)}, u32[]{:S(2)}, u32[]{:S(2)}) %all-to-all-start.2) | async-done | bytes 524320 | tf_op jit(solution)/shard_map/all_to_all | solution.py:211
  33.4 0.8 copy-done
  34.2 3.7 %all-to-all-start = ((bf16[128,16,256]{0,2,1:T(8,128)(2,1)}), bf16[128,16,256]{0,2,1:T(8,128)(2,1)S(1)}, u32[]{:S(2)}, u32[]{:S(2)}) async-start(bf16[128,16,256]{0,2,1:T(8,128)(2,1)} %fusion), calls=%async_computation | async-start | bytes 2097152 | tf_op jit(solution)/shard_map/all_to_all | solution.py:210
  40.4 22.0 %all-gather.2.cloned.1.call-done = bf16[8,2,256,1024]{3,2,1,0:T(8,128)(2,1)} async-done(((bf16[1,2,256,1024]{3,2,1,0:T(8,128)(2,1)}), bf16[8,2,256,1024]{3,2,1,0:T(8,128)(2,1)}) %all-gather.2.cloned.1.call-update) | async-done | bytes 8388624 | tf_op jit(solution)/shard_map/all_gather | solution.py:216
  62.4 1.3 dynamic-slice_select_fusion
  63.7 0.9 copy.56
  64.7 3.0 %broadcast_in_dim.19 = bf16[2,256,8,2,128]{1,0,4,3,2:T(2,128)(2,1)} broadcast(bf16[2,256,8,128]{1,0,3,2:T(2,128)(2,1)S(1)} %bitcast.58), dimensions={0,1,2,4} | broadcast | bytes 3145728 | tf_op jit(solution)/shard_map/broadcast_in_dim | solution.py:223
  67.6 6.8 %all-to-all-start.1 = ((bf16[2,256,2048]{1,0,2:T(2,128)(2,1)}), bf16[2,256,2048]{1,0,2:T(2,128)(2,1)S(1)}, u32[]{:S(2)}, u32[]{:S(2)}) async-start(bf16[2,256,2048]{1,0,2:T(2,128)(2,1)} %bitcast.55), calls=%async_computation.1 | async-start | bytes 4194304 | tf_op jit(solution)/shard_map/all_to_all | solution.py:226
  75.0 0.7 reduce.4
  76.2 1.5 convolution_convert_fusion.qb_ref
  77.7 1.1 select_convert_fusion.kb_ref
  78.8 28.3 %all-to-all-done.1 = bf16[2,256,2048]{1,0,2:T(2,128)(2,1)S(1)} async-done(((bf16[2,256,2048]{1,0,2:T(2,128)(2,1)}), bf16[2,256,2048]{1,0,2:T(2,128)(2,1)S(1)}, u32[]{:S(2)}, u32[]{:S(2)}) %all-to-all-start.1) | async-done | bytes 2097184 | tf_op jit(solution)/shard_map/all_to_all | solution.py:226
  107.1 0.9 broadcast_in_dim.21
  108.0 4.2 %all-to-all-start.3 = ((bf16[128,16,128]{2,0,1:T(8,128)(2,1)}), bf16[128,16,128]{2,0,1:T(8,128)(2,1)}, u32[]{:S(2)}, u32[]{:S(2)}) async-start(bf16[128,16,128]{2,0,1:T(8,128)(2,1)} %bitcast.66), calls=%async_computation.3 | async-start | bytes 1048576 | tf_op jit(solution)/shard_map/all_to_all | solution.py:212
  112.3 0.8 fusion.7.vis_ref
  113.1 1.3 copy.45
  114.8 1.3 copy.48
  116.1 1.3 copy.49
  117.5 5.1 %all-to-all-done.3 = bf16[128,16,128]{2,0,1:T(8,128)(2,1)} async-done(((bf16[128,16,128]{2,0,1:T(8,128)(2,1)}), bf16[128,16,128]{2,0,1:T(8,128)(2,1)}, u32[]{:S(2)}, u32[]{:S(2)}) %all-to-all-start.3) | async-done | bytes 524320 | tf_op jit(solution)/shard_map/all_to_all | solution.py:212
  122.5 35.4 %attn.1 = bf16[2048,256]{1,0:T(8,128)(2,1)} custom-call(s32[4,4]{1,0:T(4,128)} %fusion.7.vis_ref, bf16[2048,256]{1,0:T(8,128)(2,1)} %bitcast.61, bf16[2048,128]{1,0:T(8,128)(2,1)} %convolution_convert_fusion.qb_ref, bf16[2048,128]{1,0:T(8,128)(2,1)} %select_convert_fusion.kb_ref, bf16[4096,128]{1,0:T(8,128)(2,1)} %bitcast.62, bf16[4096,128]{1,0:T(8,128)(2,1)} %bitcast.63, ...), custom_call_target="tpu_custom_call" | custom-call | tf_op jit(solution)/shard_map/attn/pallas_call | solution.py:178
  157.9 19.2 %all_to_all.85 = bf16[16,128,256]{2,1,0:T(8,128)(2,1)S(1)} all-to-all(bf16[16,128,256]{2,1,0:T(8,128)(2,1)} %bitcast.64), channel_id=1, replica_groups=mesh['dp'=8,'seq'=16] {'seq'}, dimensions={0} | all-to-all | bytes 2097152 | tf_op jit(solution)/shard_map/all_to_all | solution.py:236
  177.7 1.3 reshape.112
  (37 shorter events, 4.7 us)
Async XLA Ops:
  6.5 55.9 %all-gather.2.cloned.1.call-start = ((), (), s32[]{:S(2)}) async-start(), calls=%async_computation.5 | async-start | bytes 9437184 | tf_op jit(solution)/shard_map/all_gather | solution.py:216
  14.3 19.1 %all-to-all-start.2 = ((bf16[128,16,128]{2,0,1:T(8,128)(2,1)}), bf16[128,16,128]{2,0,1:T(8,128)(2,1)S(1)}, u32[]{:S(2)}, u32[]{:S(2)}) async-start(bf16[128,16,128]{2,0,1:T(8,128)(2,1)} %bitcast.18), calls=%async_computation.2 | async-start | bytes 1048576 | tf_op jit(solution)/shard_map/all_to_all | solution.py:211
  26.3 11.6 %copy-start.3 = (s32[8]{0:T(128)S(1)}, s32[8]{0:T(128)}, u32[]{:S(2)}) copy-start(s32[8]{0:T(128)} %param.15) | copy-start | bytes 100
  33.4 0.8 copy-start
  34.2 30.4 %all-to-all-start = ((bf16[128,16,256]{0,2,1:T(8,128)(2,1)}), bf16[128,16,256]{0,2,1:T(8,128)(2,1)S(1)}, u32[]{:S(2)}, u32[]{:S(2)}) async-start(bf16[128,16,256]{0,2,1:T(8,128)(2,1)} %fusion), calls=%async_computation | async-start | bytes 2097152 | tf_op jit(solution)/shard_map/all_to_all | solution.py:210
  67.6 7.4 %copy-start.2 = (s32[1,2048]{1,0:T(1,128)S(1)}, s32[1,2048]{1,0:T(1,128)}, u32[]{:S(2)}) copy-start(s32[1,2048]{1,0:T(1,128)} %param.13) | copy-start | bytes 24580
  67.6 8.0 %copy-start.1 = (bf16[1,128,1024]{2,1,0:T(8,128)(2,1)S(1)}, bf16[1,128,1024]{2,1,0:T(8,128)(2,1)}, u32[]{:S(2)}) copy-start(bf16[1,128,1024]{2,1,0:T(8,128)(2,1)} %param.11) | copy-start | bytes 786436
  67.6 39.5 %all-to-all-start.1 = ((bf16[2,256,2048]{1,0,2:T(2,128)(2,1)}), bf16[2,256,2048]{1,0,2:T(2,128)(2,1)S(1)}, u32[]{:S(2)}, u32[]{:S(2)}) async-start(bf16[2,256,2048]{1,0,2:T(2,128)(2,1)} %bitcast.55), calls=%async_computation.1 | async-start | bytes 4194304 | tf_op jit(solution)/shard_map/all_to_all | solution.py:226
  108.0 14.5 %all-to-all-start.3 = ((bf16[128,16,128]{2,0,1:T(8,128)(2,1)}), bf16[128,16,128]{2,0,1:T(8,128)(2,1)}, u32[]{:S(2)}, u32[]{:S(2)}) async-start(bf16[128,16,128]{2,0,1:T(8,128)(2,1)} %bitcast.66), calls=%async_computation.3 | async-start | bytes 1048576 | tf_op jit(solution)/shard_map/all_to_all | solution.py:212
Sparse Core Ops, SparseCore 0:
  9.1 53.3 all-gather.1

commit v2 on v0

v2 whole, which is shorter than its diff:
```python
import functools
import math

import jax
import jax.numpy as jnp
import numpy as np
from jax import lax
from jax.experimental import pallas as pl
from jax.experimental.pallas import tpu as pltpu
from jax.sharding import Mesh
from jax.sharding import PartitionSpec as P

H = 32
KVH = 8
HD = 128
STEM = 4096
SEGS = 16
BARRED = -1e30
BQ = 512
CK = 256
SCALE = HD**-0.5 * math.log2(math.e)
SHIFT = 70.0 / SCALE
TINY = 2.0**-16
FLIP = [(0, 1), (1, 0)]
NEAR = [(0, 1), (1, 0), (2, 3), (3, 2)]
FAR = [(0, 3), (3, 0), (1, 2), (2, 1)]
SEQ = ("z", "y")
NT = (((1,), (1,)), ((), ()))
ROOM = 56 * 1024 * 1024


def rotary_table():
    halves = np.arange(0, HD, 2) / HD
    inverse = 1.0 / 500000.0**halves
    wavelen = 2.0 * np.pi / inverse
    smooth = (8192.0 / wavelen - 1.0) / 3.0
    blended = (1.0 - smooth) * inverse / 8.0 + smooth * inverse
    scaled = np.where(wavelen < 2048.0, inverse, np.where(wavelen > 8192.0, inverse / 8.0, blended))
    return jnp.asarray(scaled, dtype=jnp.float32)


def ancestry(parents):
    seg_count = parents.shape[0]
    indices = jnp.arange(seg_count, dtype=jnp.int32)
    linked = (
        (indices[:, None] == indices[None, :]) | (parents[:, None] == indices[None, :])
    ).astype(jnp.float32)
    for sweep in range(max(1, (seg_count - 1).bit_length())):
        linked = (
            jnp.dot(
                linked, linked, precision=lax.Precision.HIGHEST, preferred_element_type=jnp.float32
            )
            > 0.5
        ).astype(jnp.float32)
    return linked


def token_places(seg_row, linked):
    seg_count = linked.shape[0]
    onehot = (seg_row[:, None] == jnp.arange(seg_count, dtype=jnp.int32)[None, :]).astype(
        jnp.float32
    )
    lengths = jnp.sum(onehot, axis=0)
    starts = jnp.cumsum(lengths) - lengths
    before = jnp.sum(linked * lengths[None, :], axis=1) - lengths
    token_ids = jnp.arange(seg_row.shape[0], dtype=jnp.int32).astype(jnp.float32)
    return (
        STEM
        + token_ids
        - jnp.sum(onehot * starts[None, :], axis=1)
        + jnp.sum(onehot * before[None, :], axis=1)
    )


def turn_kernel(q_ref, k_ref, v_ref, cos_ref, sin_ref, o_ref):
    cosine = cos_ref[...]
    sine = sin_ref[...]

    def turned(part):
        wide = part.astype(jnp.float32)
        return (wide * cosine + pltpu.roll(wide, HD // 2, 1) * sine).astype(jnp.bfloat16)

    for head in range(4):
        at = head % 2 * HD
        o_ref[head // 2, 0, :, at : at + HD] = turned(q_ref[:, head * HD : head * HD + HD])
    o_ref[0, 0, :, 2 * HD :] = turned(k_ref[...])
    o_ref[1, 0, :, 2 * HD :] = v_ref[...]


def turn(q, k, v, cosine, sine):
    tok = q.shape[0]
    return pl.pallas_call(
        turn_kernel,
        out_shape=jax.ShapeDtypeStruct((2, KVH, tok, 3 * HD), jnp.bfloat16),
        grid=(KVH,),
        in_specs=[
            pl.BlockSpec((tok, 4 * HD), lambda e: (0, e)),
            pl.BlockSpec((tok, HD), lambda e: (0, e)),
            pl.BlockSpec((tok, HD), lambda e: (0, e)),
            pl.BlockSpec((tok, HD), lambda e: (0, 0)),
            pl.BlockSpec((tok, HD), lambda e: (0, 0)),
        ],
        out_specs=pl.BlockSpec((2, 1, tok, 3 * HD), lambda e: (0, e, 0, 0)),
        name="turn",
    )(q, k, v, cosine, sine)


def relay_kernel(plan, a_own, b_own, a_got, b_got, a_out, b_out):
    item = pl.program_id(0)
    a_out[...] = jnp.where(plan[2, item] > 0, a_own[...], a_got[...])
    b_out[...] = jnp.where(plan[3, item] > 0, b_own[...], b_got[...])


def relay(plan, items, a_got, b_got):
    rows, width = a_got.shape[1:]
    block = (1, rows, width)
    return pl.pallas_call(
        relay_kernel,
        out_shape=[jax.ShapeDtypeStruct((2, rows, width), jnp.bfloat16)] * 2,
        grid_spec=pltpu.PrefetchScalarGridSpec(
            num_scalar_prefetch=1,
            grid=(2,),
            in_specs=[
                pl.BlockSpec(block, lambda i, plan: (plan[0, i], 0, 0)),
                pl.BlockSpec(block, lambda i, plan: (plan[1, i], 1, 0)),
                pl.BlockSpec(block, lambda i, plan: (plan[0, i], 0, 0)),
                pl.BlockSpec(block, lambda i, plan: (plan[1, i], 0, 0)),
            ],
            out_specs=[pl.BlockSpec(block, lambda i, plan: (i, 0, 0))] * 2,
        ),
        name="relay",
    )(plan, items, items, a_got, b_got)


def settle_kernel(plan, own, a_one, b_one, a_two, b_two, out):
    pack = pl.program_id(0)
    half = a_one.shape[1]
    mine = plan[1, pack] == 0
    a = jnp.where(mine, own[0, :half], jnp.where(plan[1, pack] == 1, a_one[0], a_two[0]))
    b = jnp.where(mine, own[0, half:], jnp.where(plan[1, pack] == 2, b_one[0], b_two[0]))
    for e in range(out.shape[1]):
        out[0, e, :half] = a[:, e * HD : e * HD + HD]
        out[0, e, half:] = b[:, e * HD : e * HD + HD]


def settle(plan, items, a_one, b_one, a_two, b_two):
    rows, width = a_one.shape[1:]
    part = width // 2
    block = (1, rows, part)
    return pl.pallas_call(
        settle_kernel,
        out_shape=jax.ShapeDtypeStruct((2, KVH, 2 * rows, HD), jnp.bfloat16),
        grid_spec=pltpu.PrefetchScalarGridSpec(
            num_scalar_prefetch=1,
            grid=(2, 2),
            in_specs=[
                pl.BlockSpec((1, 2 * rows, part), lambda i, j, plan: (plan[0, i], 0, j)),
                pl.BlockSpec(block, lambda i, j, plan: (plan[0, i], 0, j)),
                pl.BlockSpec(block, lambda i, j, plan: (plan[0, i], 0, j)),
                pl.BlockSpec(block, lambda i, j, plan: (i, 0, j)),
                pl.BlockSpec(block, lambda i, j, plan: (i, 0, j)),
            ],
            out_specs=pl.BlockSpec(
                (1, KVH // 2, 2 * rows, HD), lambda i, j, plan: (i, j, 0, 0)
            ),
        ),
        name="settle",
    )(plan, items, a_one, b_one, a_two, b_two)


def longest(ref, rows):
    most = jnp.zeros((1, 1), jnp.float32)
    for at in range(0, rows, 512):
        wide = ref[at : at + 512, :HD].astype(jnp.float32)
        norms = jnp.sum(wide * wide, axis=1, keepdims=True)
        most = jnp.maximum(most, jnp.max(norms, axis=0, keepdims=True))
    return jnp.broadcast_to(jnp.sqrt(most), (8, HD))


def stacked(q_ref):
    return jnp.concatenate([q_ref[:, :HD], q_ref[:, HD : 2 * HD]], axis=0)


def ceiling(rows, top):
    wide = rows.astype(jnp.float32)
    return jnp.sqrt(jnp.sum(wide * wide, axis=1, keepdims=True)) * top * 1.02 - SHIFT


def score(qa, ref, start, size):
    return lax.dot_general(
        qa[...], ref[pl.ds(start, size), :], NT, preferred_element_type=jnp.float32
    )


def fill(core, mine_ref, other_ref, k_side, ka, va):
    mine = mine_ref[...]
    other = other_ref[...]
    first = core == 0
    ka[:, :HD] = jnp.where(first, mine, other)
    va[:, :HD] = jnp.where(first, other, mine)
    ka[:, HD:] = k_side
    va[:, HD:] = jnp.ones_like(k_side)


def pack_kernel(
    core, seen, q_ref, mine_ref, other_ref, qb_ref, kb_ref, o_ref, qa, ka, va, top, acc
):
    qi = pl.program_id(0)
    rows = 2 * BQ
    lane = lax.broadcasted_iota(jnp.int32, (1, HD), 1)

    @pl.when(qi == 0)
    def _():
        fill(core[0], mine_ref, other_ref, kb_ref[...], ka, va)
        top[...] = longest(ka, ka.shape[0])

    q_rows = stacked(q_ref)
    qa[:, :HD] = q_rows
    side = jnp.concatenate([qb_ref[...], qb_ref[...]], axis=0).astype(jnp.float32)
    row = lax.broadcasted_iota(jnp.int32, (rows, BQ), 0)
    ahead = lax.broadcasted_iota(jnp.int32, (rows, BQ), 1) > jnp.where(row >= BQ, row - BQ, row)
    here = pl.multiple_of(qi * BQ, BQ)

    def run(shift):
        qa[:, HD:] = jnp.where(lane == SEGS, shift, side).astype(jnp.bfloat16)
        weights = jnp.where(ahead, 0.0, jnp.exp2(score(qa, ka, here, BQ) * SCALE))
        acc[...] = jnp.dot(
            weights.astype(jnp.bfloat16), va[pl.ds(here, BQ), :], preferred_element_type=jnp.float32
        )

        def body(kj, carry):
            @pl.when(seen[qi, kj] > 0)
            def _():
                at = pl.multiple_of(kj * CK, CK)
                part = jnp.exp2(score(qa, ka, at, CK) * SCALE).astype(jnp.bfloat16)
                acc[...] += jnp.dot(
                    part, va[pl.ds(at, CK), :], preferred_element_type=jnp.float32
                )

            return carry

        lax.fori_loop(0, qi * (BQ // CK), body, 0)
        kept = qa[:, HD:].astype(jnp.float32)
        shift_kept = jnp.sum(jnp.where(lane == SEGS, kept, 0.0), axis=1, keepdims=True)
        o_ref[:, :HD] = acc[:, :HD]
        o_ref[:, HD:] = jnp.where(lane == 1, shift_kept, acc[:, HD:])

    run(ceiling(q_rows, top[0:1, 0:1]))

    @pl.when(jnp.min(acc[:, HD:]) < TINY)
    def _():
        qa[:, HD:] = side.astype(jnp.bfloat16)
        most = jnp.max(
            jnp.where(ahead, BARRED, score(qa, ka, here, BQ)), axis=1, keepdims=True
        )

        def body(kj, most):
            part = score(qa, ka, pl.multiple_of(kj * BQ, BQ), BQ)
            return jnp.maximum(most, jnp.max(part, axis=1, keepdims=True))

        run(lax.fori_loop(0, qi, body, most))


def pack_part(core, seen, arrived, other, q_side, k_side):
    pack = arrived.shape[0]
    once = dict(pipeline_mode=pl.Buffered(1))
    return pl.pallas_call(
        pack_kernel,
        out_shape=jax.ShapeDtypeStruct((2 * pack, 2 * HD), jnp.float32),
        grid_spec=pltpu.PrefetchScalarGridSpec(
            num_scalar_prefetch=2,
            grid=(pack // BQ,),
            in_specs=[
                pl.BlockSpec((BQ, 2 * HD), lambda i, *_: (i, 0)),
                pl.BlockSpec((pack, HD), lambda i, *_: (0, 2), **once),
                pl.BlockSpec((pack, HD), lambda i, *_: (0, 0), **once),
                pl.BlockSpec((BQ, HD), lambda i, *_: (i, 0)),
                pl.BlockSpec((pack, HD), lambda i, *_: (0, 0), **once),
            ],
            out_specs=pl.BlockSpec((2 * BQ, 2 * HD), lambda i, *_: (i, 0)),
            scratch_shapes=[
                pltpu.VMEM((2 * BQ, 2 * HD), jnp.bfloat16),
                pltpu.VMEM((pack, 2 * HD), jnp.bfloat16),
                pltpu.VMEM((pack, 2 * HD), jnp.bfloat16),
                pltpu.VMEM((8, HD), jnp.float32),
                pltpu.VMEM((2 * BQ, 2 * HD), jnp.float32),
            ],
        ),
        compiler_params=pltpu.CompilerParams(vmem_limit_bytes=ROOM),
        cost_estimate=pl.CostEstimate(
            flops=8 * pack * pack * HD, bytes_accessed=8 << 20, transcendentals=pack * pack
        ),
        name="pack_part",
    )(core, seen, arrived, arrived, other, q_side, k_side)


def stem_kernel(core, q_ref, mine_ref, other_ref, part_ref, o_ref, qa, ka, va, top, acc):
    stem = ka.shape[0]
    lane = lax.broadcasted_iota(jnp.int32, (1, HD), 1)

    @pl.when(pl.program_id(0) == 0)
    def _():
        side = jnp.broadcast_to(jnp.where(lane == SEGS, -1.0, 0.0).astype(jnp.bfloat16), (stem, HD))
        fill(core[0], mine_ref, other_ref, side, ka, va)
        top[...] = longest(ka, stem)

    q_rows = stacked(q_ref)
    qa[:, :HD] = q_rows

    def run(shift):
        qa[:, HD:] = jnp.where(lane == SEGS, shift, 0.0).astype(jnp.bfloat16)
        total = None
        held = score(qa, ka, 0, CK)
        for at in range(0, stem, CK):
            ahead = score(qa, ka, at + CK, CK) if at + CK < stem else None
            weights = jnp.exp2(held * SCALE).astype(jnp.bfloat16)
            part = jnp.dot(weights, va[at : at + CK, :], preferred_element_type=jnp.float32)
            total = part if total is None else total + part
            held = ahead
        acc[...] = total

    def finish():
        kept = qa[:, HD:].astype(jnp.float32)
        shift = jnp.sum(jnp.where(lane == SEGS, kept, 0.0), axis=1, keepdims=True)
        before = part_ref[:, HD + 1 : HD + 2]
        most = jnp.maximum(shift, before)
        new = jnp.exp2((shift - most) * SCALE)
        old = jnp.exp2((before - most) * SCALE)
        total = acc[:, HD : HD + 1] * new + part_ref[:, HD : HD + 1] * old
        mixed = ((acc[:, :HD] * new + part_ref[:, :HD] * old) / total).astype(jnp.bfloat16)
        o_ref[:, :HD] = mixed[:BQ]
        o_ref[:, HD:] = mixed[BQ:]

    run(ceiling(q_rows, top[0:1, 0:1]))
    finish()

    @pl.when(jnp.min(acc[:, HD:]) < TINY)
    def _():
        qa[:, HD:] = jnp.zeros_like(q_rows)

        def body(step, most):
            part = score(qa, ka, pl.multiple_of(step * BQ, BQ), BQ)
            return jnp.maximum(most, jnp.max(part, axis=1, keepdims=True))

        low = jnp.full((2 * BQ, 1), BARRED, jnp.float32)
        run(lax.fori_loop(0, stem // BQ, body, low))
        finish()


def stem_part(core, arrived, mine, other, before):
    pack = arrived.shape[0]
    stem = mine.shape[0]
    once = dict(pipeline_mode=pl.Buffered(1))
    return pl.pallas_call(
        stem_kernel,
        out_shape=jax.ShapeDtypeStruct((pack, 2 * HD), jnp.bfloat16),
        grid_spec=pltpu.PrefetchScalarGridSpec(
            num_scalar_prefetch=1,
            grid=(pack // BQ,),
            in_specs=[
                pl.BlockSpec((BQ, 2 * HD), lambda i, *_: (i, 0)),
                pl.BlockSpec((stem, HD), lambda i, *_: (0, 0), **once),
                pl.BlockSpec((stem, HD), lambda i, *_: (0, 0), **once),
                pl.BlockSpec((2 * BQ, 2 * HD), lambda i, *_: (i, 0)),
            ],
            out_specs=pl.BlockSpec((BQ, 2 * HD), lambda i, *_: (i, 0)),
            scratch_shapes=[
                pltpu.VMEM((2 * BQ, 2 * HD), jnp.bfloat16),
                pltpu.VMEM((stem, 2 * HD), jnp.bfloat16),
                pltpu.VMEM((stem, 2 * HD), jnp.bfloat16),
                pltpu.VMEM((8, HD), jnp.float32),
                pltpu.VMEM((2 * BQ, 2 * HD), jnp.float32),
            ],
        ),
        compiler_params=pltpu.CompilerParams(vmem_limit_bytes=ROOM),
        cost_estimate=pl.CostEstimate(
            flops=8 * pack * stem * HD, bytes_accessed=8 << 20, transcendentals=2 * pack * stem
        ),
        name="stem_part",
    )(core, arrived, mine, other, before)


def gather_kernel(core, mine_ref, other_ref, o_ref):
    first = core[0] == 0
    for e in range(mine_ref.shape[1]):
        mine = mine_ref[0, e]
        other = other_ref[e]
        at = 4 * HD * e
        o_ref[:, at : at + 2 * HD] = jnp.where(first, mine, other)
        o_ref[:, at + 2 * HD : at + 4 * HD] = jnp.where(first, other, mine)


def gather(core, mine, other):
    tok = mine.shape[2]
    heads = KVH // 2
    return pl.pallas_call(
        gather_kernel,
        out_shape=jax.ShapeDtypeStruct((tok, H * HD), jnp.bfloat16),
        grid_spec=pltpu.PrefetchScalarGridSpec(
            num_scalar_prefetch=1,
            grid=(2,),
            in_specs=[
                pl.BlockSpec((1, heads, tok, 2 * HD), lambda i, core: (core[0], i, 0, 0)),
                pl.BlockSpec((heads, tok, 2 * HD), lambda i, core: (i, 0, 0)),
            ],
            out_specs=pl.BlockSpec((tok, H * HD // 2), lambda i, core: (0, i)),
        ),
        name="gather",
    )(core, mine, other)


def shards(queries, keys, values, stem_kv, seg_ids, seg_parent, stem_owner):
    tok = queries.shape[1]
    x = lax.axis_index("x")
    core = lax.axis_index("core")
    spot = lax.axis_index(SEQ)
    pack_len = tok * 16
    core_row = core[None].astype(jnp.int32)

    items = lax.all_to_all(stem_kv[0], "core", split_axis=0, concat_axis=0, tiled=True)
    half = items.shape[1] // 2
    near, far = x ^ 1, 3 - x
    a_one = lax.ppermute(items[:, :half], "x", NEAR)
    b_one = lax.ppermute(items[:, half:], "x", FAR)
    follow = stem_owner.reshape(4, 2)
    for_far, for_near, for_us = follow[far], follow[near], follow[x]
    plan = jnp.stack(
        [for_far % 2, for_near % 2, (for_far // 2 == x) * 1, (for_near // 2 == x) * 1]
    ).astype(jnp.int32)
    a_send, b_send = relay(plan, items, a_one, b_one)
    a_two = lax.ppermute(a_send, "x", FAR)
    b_two = lax.ppermute(b_send, "x", NEAR)
    chip = for_us // 2
    source = jnp.where(chip == x, 0, jnp.where(chip == near, 1, jnp.where(chip == far, 2, 3)))
    stems = settle(
        jnp.stack([for_us % 2, source]).astype(jnp.int32), items, a_one, b_one, a_two, b_two
    ).reshape(16, 2 * half, HD)

    linked = ancestry(seg_parent[0])
    places = token_places(seg_ids[0], linked)
    own_places = lax.dynamic_slice_in_dim(places, spot * tok, tok)
    angles = own_places[:, None] * rotary_table()[None, :]
    cosine, sine = jnp.cos(angles), jnp.sin(angles)
    sent = turn(
        queries[0],
        keys[0],
        values[0],
        jnp.concatenate([cosine, cosine], axis=1),
        jnp.concatenate([-sine, sine], axis=1),
    )
    crossed = lax.all_to_all(sent, "core", split_axis=0, concat_axis=0, tiled=True)
    arrived = lax.all_to_all(
        crossed.reshape(16, tok, 3 * HD), SEQ, split_axis=0, concat_axis=0, tiled=True
    ).reshape(pack_len, 3 * HD)
    pair = lax.ppermute(arrived[:, 2 * HD :], "core", FLIP)

    rows = jnp.concatenate([seg_ids[0], seg_parent[0]])
    rows = jnp.where(spot // KVH == core, rows, lax.ppermute(rows, "core", FLIP))
    seg_row, reach = rows[:pack_len], ancestry(rows[pack_len:])
    onehot = (seg_row[:, None] == jnp.arange(HD, dtype=jnp.int32)[None, :]).astype(jnp.float32)
    barred = jnp.pad(BARRED * (1.0 - reach), ((0, HD - SEGS), (0, HD - SEGS)))
    q_side = jnp.dot(onehot, barred, precision=lax.Precision.HIGHEST).astype(jnp.bfloat16)
    k_side = jnp.where(jnp.arange(HD)[None, :] == SEGS, -1.0, onehot).astype(jnp.bfloat16)
    q_has = onehot.reshape(pack_len // BQ, BQ, HD).max(axis=1)[:, :SEGS]
    k_has = onehot.reshape(pack_len // CK, CK, HD).max(axis=1)[:, :SEGS]
    seen = (q_has @ reach @ k_has.T > 0.5).astype(jnp.int32)

    before = pack_part(core_row, seen, arrived, pair, q_side, k_side)
    mine = lax.all_to_all(stems, SEQ, split_axis=0, concat_axis=0, tiled=True).reshape(STEM, HD)
    other = lax.ppermute(mine, "core", FLIP)
    mixed = stem_part(core_row, arrived, mine, other, before)

    back = lax.all_to_all(
        mixed.reshape(16, tok, 2 * HD), SEQ, split_axis=0, concat_axis=0, tiled=True
    ).reshape(2, KVH, tok, 2 * HD)
    away = lax.dynamic_index_in_dim(back, 1 - core, 0, keepdims=False)
    return gather(core_row, back, lax.ppermute(away, "core", FLIP))[None]


def solution(mesh):
    grid = Mesh(mesh.devices.reshape(4, 2, 4, 4), ("x", "core", "z", "y"))
    dp, seq = ("x", "core"), SEQ
    placed = (
        P(dp, seq, None),
        P(dp, seq, None),
        P(dp, seq, None),
        P(dp, None, seq, None),
        P(dp, None),
        P(dp, None),
        P(),
    )
    return jax.shard_map(
        shards, mesh=grid, in_specs=placed, out_specs=P(dp, seq, None), check_vma=False
    )
```

time: 255 us -> 170 us (0.67); the launches traced: 251 us -> 169 us
  matrix products: 64.6 us -> 4.34 us
  Pallas kernels: 0 us -> 57.8 us
  waiting for transfers between devices: 80.8 us -> 48.7 us
  local copies, waits for them, and re-layouts: 24.6 us -> 5.07 us
  other arithmetic: 22.4 us -> 6.64 us
  between operations: 15.4 us -> 0.18 us
  starting transfers between devices: 23.1 us -> 32.8 us
  blocking collectives: 17.5 us -> 13.6 us
  loops' own time: 2.79 us -> 0 us
    dot_general x21 -> x2, matrix products: 63.9 us -> 2.36 us  [the longest x1 1.54 us: shards(): jnp.dot(onehot, barred, precision=lax.Precision.HIGHEST)]
    pallas_call x0 -> x6, Pallas kernels: none -> 57.8 us  [the longest x1 25.6 us: stem_part(): pl.pallas_call(stem_kernel, out_shape=jax.ShapeDtypeStruct((pack, 2 * HD)...]
    all_gather x1 -> x0, waiting for transfers between devices: 38.6 us -> none  [shards(): incoming = lax.all_gather(stem_kv, 'dp', axis=0, tiled=True)]
    ppermute x0 -> x8, waiting for transfers between devices: none -> 21.7 us  [the longest x1 10.6 us: shards(): a_two = lax.ppermute(a_send, 'x', FAR)]
    ppermute x0 -> x8, starting transfers between devices: none -> 15.2 us  [the longest x1 4.65 us: shards(): other = lax.ppermute(mine, 'core', FLIP)]
    reduce_sum x8 -> x0, other arithmetic: 15.1 us -> none  [block_out(): totals = jnp.sum(exp_scores, axis=1, keepdims=True)]
    all_to_all x4 -> x3, waiting for transfers between devices: 41.4 us -> 27 us  [the longest x1 18.8 us: shards(): lax.all_to_all(mixed.reshape(16, tok, 2 * HD), SEQ, split_axis=0, concat_...]
    broadcast_in_dim x3 -> x0, local copies, waits for them, and re-layouts: 5.71 us -> none  [the longest x1 2.96 us: shards(): jnp.repeat(owned.reshape(2, stem_rows, KVH, HD), repeat, axis=2)]
  transfers between devices with their start and end apart: 5 -> 11, of which waited for: 4 -> 7; matrix products, arithmetic and copies ran while one was open for 7% -> 4% of each run, Pallas kernels for 0% -> 14%
where the time goes in v2:
time: 170 us; the launch traced here: 169 us
  Pallas kernels  57.8 us (34%)
  waiting for transfers between devices  48.7 us (29%)
  starting transfers between devices  32.8 us (19%)
  blocking collectives  13.6 us (8%)
  other arithmetic  6.64 us (4%)
  local copies, waits for them, and re-layouts  5.07 us (3%)
  matrix products  4.34 us (3%)
    pallas_call x1, Pallas kernels, stem_part(): pl.pallas_call(stem_kernel, out_shape=jax.ShapeDtypeStruct((pack, 2 * HD)...  25.6 us
    all_to_all x1, waiting for transfers between devices, shards(): lax.all_to_all(mixed.reshape(16, tok, 2 * HD), SEQ, split_axis=0, concat_...  18.8 us
    pallas_call x1, Pallas kernels, pack_part(): pl.pallas_call(pack_kernel, out_shape=jax.ShapeDtypeStruct((2 * pack, 2 *...  16.8 us
    ppermute x1, waiting for transfers between devices, shards(): a_two = lax.ppermute(a_send, 'x', FAR)  10.6 us
    all_to_all x1, blocking collectives, shards(): lax.all_to_all(sent, 'core', split_axis=0, concat_axis=0, tiled=True)  9.02 us
    all_to_all x1, waiting for transfers between devices, shards(): lax.all_to_all(stems, SEQ, split_axis=0, concat_axis=0, tiled=True)  8.19 us
    all_to_all x1, starting transfers between devices, shards(): lax.all_to_all(crossed.reshape(16, tok, 3 * HD), SEQ, split_axis=0, conca...  7.85 us
    ppermute x1, waiting for transfers between devices, shards(): a_one = lax.ppermute(items[:, :half], 'x', NEAR)  7.4 us
  transfers between devices with their start and end apart: 11, of which 7 were waited for; matrix products, arithmetic and copies ran while one was open for 4% of the time, Pallas kernels for 14%

profile of v2, /device:TPU:1, one launch (start us, length us, event | category | flops | bytes accessed | tf_op | source)
XLA Modules:
  0.0 169.1 jit_solution(1038253161629352755)
XLA Ops:
  0.0 0.9 convolution_compare_fusion.7
  1.2 0.8 convert_reduce_fusion.2
  3.4 1.0 fusion.13
  5.1 5.8 %turn.1 = bf16[2,8,128,384]{3,2,1,0:T(8,128)(2,1)} custom-call(bf16[128,4096]{1,0:T(8,128)(2,1)} %bitcast.37, bf16[128,1024]{1,0:T(8,128)(2,1)} %bitcast.42, bf16[128,1024]{1,0:T(8,128)(2,1)} %bitcast.43, f32[128,128]{1,0:T(8,128)} %get-tuple-element.30.cos_ref, f32[128,128]{1,0:T(8,128)} %get-tuple-element.31.sin_ref), custom_call_target="tpu_custom_call" | custom-call | tf_op jit(solution)/shard_map/turn/pallas_call | solution.py:92
  11.0 9.0 %all_to_all.25 = bf16[2,8,128,384]{3,2,1,0:T(8,128)(2,1)} all-to-all(bf16[2,8,128,384]{3,2,1,0:T(8,128)(2,1)} %turn.1), channel_id=1, replica_groups=mesh['x'=4,'core'=2,'z'=4,'y'=4] {'core'}, dimensions={0} | all-to-all | bytes 3145728 | tf_op jit(solution)/shard_map/all_to_all | solution.py:451
  20.0 4.6 %all_to_all.26.a_own.b_own.own = bf16[2,256,1024]{2,1,0:T(8,128)(2,1)S(1)} all-to-all(bf16[2,256,1024]{2,1,0:T(8,128)(2,1)S(1)} %bitcast.38), channel_id=1, replica_groups=mesh['x'=4,'core'=2,'z'=4,'y'=4] {'core'}, dimensions={0} | all-to-all | bytes 2097152 | tf_op jit(solution)/shard_map/all_to_all | solution.py:420
  24.5 7.9 %all-to-all-start.1 = ((bf16[16,128,384]{2,1,0:T(8,128)(2,1)}), bf16[16,128,384]{2,1,0:T(8,128)(2,1)S(1)}, u32[]{:S(2)}, u32[]{:S(2)}) async-start(bf16[16,128,384]{2,1,0:T(8,128)(2,1)} %bitcast.7), calls=%async_computation.1 | async-start | bytes 3145728 | tf_op jit(solution)/shard_map/all_to_all | solution.py:452
  32.5 0.9 fusion.25
  33.4 1.2 collective-permute-start
  34.6 1.8 %collective-permute-start.1 = (bf16[2,128,1024]{2,1,0:T(8,128)(2,1)S(1)}, bf16[2,128,1024]{2,1,0:T(8,128)(2,1)S(1)}, u32[]{:S(2)}, u32[]{:S(2)}) collective-permute-start(bf16[2,128,1024]{2,1,0:T(8,128)(2,1)S(1)} %get-tuple-element.15), channel_id=1, source_target_pairs={{0,96},{96,0},{32,64},{64,32},{1,97},{97,1},{33,65},{65,33},{2,98}... | collective-permute-start | bytes 1572872 | tf_op jit(solution)/shard_map/ppermute | solution.py:424
  36.4 1.3 collective-permute-start.5
  39.0 7.4 %collective-permute-done.a_got.a_one = bf16[2,128,1024]{2,1,0:T(8,128)(2,1)S(1)} collective-permute-done((bf16[2,128,1024]{2,1,0:T(8,128)(2,1)}, bf16[2,128,1024]{2,1,0:T(8,128)(2,1)S(1)}, u32[]{:S(2)}, u32[]{:S(2)}) %collective-permute-start) | collective-permute-done | bytes 524320 | tf_op jit(solution)/shard_map/ppermute | solution.py:423
  46.4 1.9 %collective-permute-done.1.b_got.b_one = bf16[2,128,1024]{2,1,0:T(8,128)(2,1)S(1)} collective-permute-done((bf16[2,128,1024]{2,1,0:T(8,128)(2,1)S(1)}, bf16[2,128,1024]{2,1,0:T(8,128)(2,1)S(1)}, u32[]{:S(2)}, u32[]{:S(2)}) %collective-permute-start.1) | collective-permute-done | bytes 524320 | tf_op jit(solution)/shard_map/ppermute | solution.py:424
  49.1 2.9 %relay.1 = (bf16[2,128,1024]{2,1,0:T(8,128)(2,1)}, bf16[2,128,1024]{2,1,0:T(8,128)(2,1)}) custom-call(s32[4,2]{1,0:T(4,128)} %pad_add_fusion.1.plan, bf16[2,256,1024]{2,1,0:T(8,128)(2,1)} %copy-done, bf16[2,256,1024]{2,1,0:T(8,128)(2,1)} %copy-done, bf16[2,128,1024]{2,1,0:T(8,128)(2,1)} %copy-done.3, bf16[2,128,1024]{2,1,0:T(8,128)(2,1)} %copy-done.4), custom_call_target="tpu_custom_call" | custom-call | tf_op jit(solution)/shard_map/relay/pallas_call | solution.py:117
  52.0 1.8 %collective-permute-start.2 = (bf16[2,128,1024]{2,1,0:T(8,128)(2,1)}, bf16[2,128,1024]{2,1,0:T(8,128)(2,1)S(1)}, u32[]{:S(2)}, u32[]{:S(2)}) collective-permute-start(bf16[2,128,1024]{2,1,0:T(8,128)(2,1)} %get-tuple-element.7), channel_id=1, source_target_pairs={{0,96},{96,0},{32,64},{64,32},{1,97},{97,1},{33,65},{65,33},{2,98}... | collective-permute-start | bytes 1572872 | tf_op jit(solution)/shard_map/ppermute | solution.py:431
  54.4 10.6 %collective-permute-done.2.a_two = bf16[2,128,1024]{2,1,0:T(8,128)(2,1)S(1)} collective-permute-done((bf16[2,128,1024]{2,1,0:T(8,128)(2,1)}, bf16[2,128,1024]{2,1,0:T(8,128)(2,1)S(1)}, u32[]{:S(2)}, u32[]{:S(2)}) %collective-permute-start.2) | collective-permute-done | bytes 524320 | tf_op jit(solution)/shard_map/ppermute | solution.py:431
  66.6 4.5 %settle.1 = bf16[2,8,256,128]{3,2,1,0:T(8,128)(2,1)} custom-call(s32[2,2]{1,0:T(2,128)} %pad_add_fusion.2.plan, bf16[2,256,1024]{2,1,0:T(8,128)(2,1)} %copy-done, bf16[2,128,1024]{2,1,0:T(8,128)(2,1)} %copy-done.3, bf16[2,128,1024]{2,1,0:T(8,128)(2,1)} %copy-done.4, bf16[2,128,1024]{2,1,0:T(8,128)(2,1)} %copy-done.7, bf16[2,128,1024]{2,1,0:T(8,128)(2,1)} %copy-done.8), custom_call_target="tpu_custom_call" | custom-call | tf_op jit(solution)/shard_map/settle/pallas_call | solution.py:150
  71.2 6.1 %all-to-all-start.3 = ((bf16[16,256,128]{2,1,0:T(8,128)(2,1)}), bf16[16,256,128]{2,1,0:T(8,128)(2,1)S(1)}, u32[]{:S(2)}, u32[]{:S(2)}) async-start(bf16[16,256,128]{2,1,0:T(8,128)(2,1)} %bitcast.32), calls=%async_computation.3 | async-start | bytes 2097152 | tf_op jit(solution)/shard_map/all_to_all | solution.py:469
  78.0 1.5 convolution_convert_fusion.qb_ref
  79.6 3.4 %collective-permute-start.6 = (bf16[2048,128]{1,0:T(8,128)(2,1)S(1)}, bf16[2048,128]{1,0:T(8,128)(2,1)}, u32[]{:S(2)}, u32[]{:S(2)}) collective-permute-start(bf16[2048,128]{1,0:T(8,128)(2,1)S(1)} %slice.32), channel_id=1, source_target_pairs={{0,16},{16,0},{1,17},{17,1},{2,18},{18,2},{3,19},{19,3},{4,20},{20... | collective-permute-start | bytes 1572872 | tf_op jit(solution)/shard_map/ppermute | solution.py:455
  83.0 8.2 %all-to-all-done.3 = bf16[16,256,128]{2,1,0:T(8,128)(2,1)S(1)} async-done(((bf16[16,256,128]{2,1,0:T(8,128)(2,1)}), bf16[16,256,128]{2,1,0:T(8,128)(2,1)S(1)}, u32[]{:S(2)}, u32[]{:S(2)}) %all-to-all-start.3) | async-done | bytes 1048608 | tf_op jit(solution)/shard_map/all_to_all | solution.py:469
  91.2 4.7 %collective-permute-start.4 = (bf16[4096,128]{1,0:T(8,128)(2,1)S(1)}, bf16[4096,128]{1,0:T(8,128)(2,1)S(1)}, u32[]{:S(2)}, u32[]{:S(2)}) collective-permute-start(bf16[4096,128]{1,0:T(8,128)(2,1)S(1)} %bitcast.39), channel_id=1, source_target_pairs={{0,16},{16,0},{1,17},{17,1},{2,18},{18,2},{3,19},{19,3},{4,20},{20... | collective-permute-start | bytes 3145736 | tf_op jit(solution)/shard_map/ppermute | solution.py:470
  96.6 1.1 select_convert_fusion.kb_ref
  97.8 16.8 %pack_part.1.part_ref = f32[4096,256]{1,0:T(8,128)} custom-call(s32[1]{0:T(128)} %bitcast.core, s32[4,8]{1,0:T(4,128)} %fusion.8.seen, bf16[2048,384]{1,0:T(8,128)(2,1)} %bitcast.34, bf16[2048,384]{1,0:T(8,128)(2,1)} %bitcast.35, bf16[2048,128]{1,0:T(8,128)(2,1)} %collective-permute-done.6.other_ref, bf16[2048,128]{1,0:T(8,128)(2,1)} %convolution_convert_fusion.qb_ref, ...), custom_call_target="tpu_custom_call" | custom-call | flops 4294967296 | bytes 8388608 | tf_op jit(solution)/shard_map/pack_part/pallas_call | solution.py:267
  114.6 1.0 copy-done.13
  115.6 25.6 %stem_part.1 = bf16[2048,256]{1,0:T(8,128)(2,1)} custom-call(s32[1]{0:T(128)} %bitcast.core, bf16[2048,384]{1,0:T(8,128)(2,1)} %bitcast.36, bf16[4096,128]{1,0:T(8,128)(2,1)} %bitcast.40, bf16[4096,128]{1,0:T(8,128)(2,1)} %copy-done.13, f32[4096,256]{1,0:T(8,128)} %pack_part.1.part_ref), custom_call_target="tpu_custom_call" | custom-call | flops 8589934592 | bytes 8388608 | tf_op jit(solution)/shard_map/stem_part/pallas_call | solution.py:354
  141.2 3.7 %all-to-all-start.4 = ((bf16[16,128,256]{2,1,0:T(8,128)(2,1)}), bf16[16,128,256]{2,1,0:T(8,128)(2,1)S(1)}, u32[]{:S(2)}, u32[]{:S(2)}) async-start(bf16[16,128,256]{2,1,0:T(8,128)(2,1)} %bitcast.41), calls=%async_computation.4 | async-start | bytes 2097152 | tf_op jit(solution)/shard_map/all_to_all | solution.py:473
  144.9 18.8 %all-to-all-done.4 = bf16[16,128,256]{2,1,0:T(8,128)(2,1)S(1)} async-done(((bf16[16,128,256]{2,1,0:T(8,128)(2,1)}), bf16[16,128,256]{2,1,0:T(8,128)(2,1)S(1)}, u32[]{:S(2)}, u32[]{:S(2)}) %all-to-all-start.4) | async-done | bytes 1048608 | tf_op jit(solution)/shard_map/all_to_all | solution.py:473
  163.7 1.0 collective-permute-start.7
  164.7 1.5 collective-permute-done.7.other_ref
  166.2 0.8 copy-done.9
  167.0 2.0 %gather.1 = bf16[128,4096]{1,0:T(8,128)(2,1)} custom-call(s32[1]{0:T(128)} %bitcast.core, bf16[2,8,128,256]{3,2,1,0:T(8,128)(2,1)} %bitcast.31, bf16[8,128,256]{2,1,0:T(8,128)(2,1)} %copy-done.9), custom_call_target="tpu_custom_call" | custom-call | tf_op jit(solution)/shard_map/gather/pallas_call | solution.py:396
  (63 shorter events, 8.3 us)
Async XLA Ops:
  11.0 9.0 %copy-start.5 = (bf16[1,2,256,1024]{3,2,1,0:T(8,128)(2,1)S(1)}, bf16[1,2,256,1024]{3,2,1,0:T(8,128)(2,1)}, u32[]{:S(2)}) copy-start(bf16[1,2,256,1024]{3,2,1,0:T(8,128)(2,1)} %param.11) | copy-start | bytes 3145732
  24.5 7.9 %copy-start = (bf16[2,256,1024]{2,1,0:T(8,128)(2,1)}, bf16[2,256,1024]{2,1,0:T(8,128)(2,1)S(1)}, u32[]{:S(2)}) copy-start(bf16[2,256,1024]{2,1,0:T(8,128)(2,1)S(1)} %all_to_all.26.a_own.b_own.own) | copy-start | bytes 3145732
  24.5 46.6 %all-to-all-start.1 = ((bf16[16,128,384]{2,1,0:T(8,128)(2,1)}), bf16[16,128,384]{2,1,0:T(8,128)(2,1)S(1)}, u32[]{:S(2)}, u32[]{:S(2)}) async-start(bf16[16,128,384]{2,1,0:T(8,128)(2,1)} %bitcast.7), calls=%async_computation.1 | async-start | bytes 3145728 | tf_op jit(solution)/shard_map/all_to_all | solution.py:452
  32.4 4.0 %copy-start.10 = (s32[1,2048]{1,0:T(1,128)S(1)}, s32[1,2048]{1,0:T(1,128)}, u32[]{:S(2)}) copy-start(s32[1,2048]{1,0:T(1,128)} %param.12) | copy-start | bytes 24580
  32.4 4.0 %copy-start.11 = (s32[1,16]{1,0:T(1,128)S(1)}, s32[1,16]{1,0:T(1,128)}, u32[]{:S(2)}) copy-start(s32[1,16]{1,0:T(1,128)} %param.13) | copy-start | bytes 196
  32.4 5.3 %copy-start.12 = (s32[8]{0:T(128)S(1)}, s32[8]{0:T(128)}, u32[]{:S(2)}) copy-start(s32[8]{0:T(128)} %param.14) | copy-start | bytes 100
  33.4 13.0 %collective-permute-start = (bf16[2,128,1024]{2,1,0:T(8,128)(2,1)}, bf16[2,128,1024]{2,1,0:T(8,128)(2,1)S(1)}, u32[]{:S(2)}, u32[]{:S(2)}) collective-permute-start(bf16[2,128,1024]{2,1,0:T(8,128)(2,1)} %get-tuple-element.16), channel_id=1, source_target_pairs={{0,32},{32,0},{64,96},{96,64},{1,33},{33,1},{65,97},{97,65},{2,34}... | collective-permute-start | bytes 1572872 | tf_op jit(solution)/shard_map/ppermute | solution.py:423
  34.6 13.7 %collective-permute-start.1 = (bf16[2,128,1024]{2,1,0:T(8,128)(2,1)S(1)}, bf16[2,128,1024]{2,1,0:T(8,128)(2,1)S(1)}, u32[]{:S(2)}, u32[]{:S(2)}) collective-permute-start(bf16[2,128,1024]{2,1,0:T(8,128)(2,1)S(1)} %get-tuple-element.15), channel_id=1, source_target_pairs={{0,96},{96,0},{32,64},{64,32},{1,97},{97,1},{33,65},{65,33},{2,98}... | collective-permute-start | bytes 1572872 | tf_op jit(solution)/shard_map/ppermute | solution.py:424
  36.4 17.5 %collective-permute-start.5 = (s32[2064]{0:T(1024)S(1)}, s32[2064]{0:T(1024)S(1)}, u32[]{:S(2)}, u32[]{:S(2)}) collective-permute-start(s32[2064]{0:T(1024)S(1)} %pad_add_fusion), channel_id=1, source_target_pairs={{0,16},{16,0},{1,17},{17,1},{2,18},{18,2},{3,19},{19,3},{4,20},{20... | collective-permute-start | bytes 24776 | tf_op jit(solution)/shard_map/ppermute | solution.py:458
  46.4 1.9 %copy-start.3 = (bf16[2,128,1024]{2,1,0:T(8,128)(2,1)}, bf16[2,128,1024]{2,1,0:T(8,128)(2,1)S(1)}, u32[]{:S(2)}) copy-start(bf16[2,128,1024]{2,1,0:T(8,128)(2,1)S(1)} %collective-permute-done.a_got.a_one) | copy-start | bytes 1572868
  48.3 0.8 copy-start.4
  52.0 13.0 %collective-permute-start.2 = (bf16[2,128,1024]{2,1,0:T(8,128)(2,1)}, bf16[2,128,1024]{2,1,0:T(8,128)(2,1)S(1)}, u32[]{:S(2)}, u32[]{:S(2)}) collective-permute-start(bf16[2,128,1024]{2,1,0:T(8,128)(2,1)} %get-tuple-element.7), channel_id=1, source_target_pairs={{0,96},{96,0},{32,64},{64,32},{1,97},{97,1},{33,65},{65,33},{2,98}... | collective-permute-start | bytes 1572872 | tf_op jit(solution)/shard_map/ppermute | solution.py:431
  53.8 11.5 %collective-permute-start.3 = (bf16[2,128,1024]{2,1,0:T(8,128)(2,1)}, bf16[2,128,1024]{2,1,0:T(8,128)(2,1)S(1)}, u32[]{:S(2)}, u32[]{:S(2)}) collective-permute-start(bf16[2,128,1024]{2,1,0:T(8,128)(2,1)} %get-tuple-element.8), channel_id=1, source_target_pairs={{0,32},{32,0},{64,96},{96,64},{1,33},{33,1},{65,97},{97,65},{2,34}... | collective-permute-start | bytes 1572872 | tf_op jit(solution)/shard_map/ppermute | solution.py:432
  65.0 0.8 copy-start.7
  65.8 0.8 copy-start.8
  71.1 8.4 %copy-start.2 = (bf16[16,128,384]{2,1,0:T(8,128)(2,1)}, bf16[16,128,384]{2,1,0:T(8,128)(2,1)S(1)}, u32[]{:S(2)}) copy-start(bf16[16,128,384]{2,1,0:T(8,128)(2,1)S(1)} %all-to-all-done.1) | copy-start | bytes 4718596
  71.2 20.0 %all-to-all-start.3 = ((bf16[16,256,128]{2,1,0:T(8,128)(2,1)}), bf16[16,256,128]{2,1,0:T(8,128)(2,1)S(1)}, u32[]{:S(2)}, u32[]{:S(2)}) async-start(bf16[16,256,128]{2,1,0:T(8,128)(2,1)} %bitcast.32), calls=%async_computation.3 | async-start | bytes 2097152 | tf_op jit(solution)/shard_map/all_to_all | solution.py:469
  79.6 18.2 %collective-permute-start.6 = (bf16[2048,128]{1,0:T(8,128)(2,1)S(1)}, bf16[2048,128]{1,0:T(8,128)(2,1)}, u32[]{:S(2)}, u32[]{:S(2)}) collective-permute-start(bf16[2048,128]{1,0:T(8,128)(2,1)S(1)} %slice.32), channel_id=1, source_target_pairs={{0,16},{16,0},{1,17},{17,1},{2,18},{18,2},{3,19},{19,3},{4,20},{20... | collective-permute-start | bytes 1572872 | tf_op jit(solution)/shard_map/ppermute | solution.py:455
  91.2 23.4 %copy-start.6 = (bf16[16,256,128]{2,1,0:T(8,128)(2,1)}, bf16[16,256,128]{2,1,0:T(8,128)(2,1)S(1)}, u32[]{:S(2)}) copy-start(bf16[16,256,128]{2,1,0:T(8,128)(2,1)S(1)} %all-to-all-done.3) | copy-start | bytes 3145732
  91.2 23.4 %collective-permute-start.4 = (bf16[4096,128]{1,0:T(8,128)(2,1)S(1)}, bf16[4096,128]{1,0:T(8,128)(2,1)S(1)}, u32[]{:S(2)}, u32[]{:S(2)}) collective-permute-start(bf16[4096,128]{1,0:T(8,128)(2,1)S(1)} %bitcast.39), channel_id=1, source_target_pairs={{0,16},{16,0},{1,17},{17,1},{2,18},{18,2},{3,19},{19,3},{4,20},{20... | collective-permute-start | bytes 3145736 | tf_op jit(solution)/shard_map/ppermute | solution.py:470
  114.6 1.0 copy-start.13
  141.2 22.5 %all-to-all-start.4 = ((bf16[16,128,256]{2,1,0:T(8,128)(2,1)}), bf16[16,128,256]{2,1,0:T(8,128)(2,1)S(1)}, u32[]{:S(2)}, u32[]{:S(2)}) async-start(bf16[16,128,256]{2,1,0:T(8,128)(2,1)} %bitcast.41), calls=%async_computation.4 | async-start | bytes 2097152 | tf_op jit(solution)/shard_map/all_to_all | solution.py:473
  163.7 2.5 %copy-start.1 = (bf16[16,128,256]{2,1,0:T(8,128)(2,1)}, bf16[16,128,256]{2,1,0:T(8,128)(2,1)S(1)}, u32[]{:S(2)}) copy-start(bf16[16,128,256]{2,1,0:T(8,128)(2,1)S(1)} %all-to-all-done.4) | copy-start | bytes 3145732
  163.7 2.5 %collective-permute-start.7 = (bf16[8,128,256]{2,1,0:T(8,128)(2,1)S(1)}, bf16[8,128,256]{2,1,0:T(8,128)(2,1)S(1)}, u32[]{:S(2)}, u32[]{:S(2)}) collective-permute-start(bf16[8,128,256]{2,1,0:T(8,128)(2,1)S(1)} %dynamic-slice_bitcast_fusion), channel_id=1, source_target_pairs={{0,16},{16,0},{1,17},{17,1},{2,18},{18,2},{3,19},{19,3},{4,20},{20... | collective-permute-start | bytes 1572872 | tf_op jit(solution)/shard_map/ppermute | solution.py:477
  166.2 0.8 copy-start.9

commit v3 on v2

--- a/solution.py
+++ b/solution.py
@@ -105,65 +105,93 @@
     )(q, k, v, cosine, sine)
 
 
-def relay_kernel(plan, a_own, b_own, a_got, b_got, a_out, b_out):
-    item = pl.program_id(0)
-    a_out[...] = jnp.where(plan[2, item] > 0, a_own[...], a_got[...])
-    b_out[...] = jnp.where(plan[3, item] > 0, b_own[...], b_got[...])
+def relay_kernel(plan, own, a_got, b_got, a_out, b_out, sems):
+    half = a_got.shape[1]
+    for item in range(2):
+        a, b = plan[0, item], plan[1, item]
+        own_a, own_b = plan[2, item] > 0, plan[3, item] > 0
+        a_to, b_to = a_out.at[item], b_out.at[item]
+        a_sem, b_sem = sems.at[2 * item], sems.at[2 * item + 1]
+
+        @pl.when(own_a)
+        def _():
+            pltpu.make_async_copy(own.at[a, pl.ds(0, half)], a_to, a_sem).start()
+
+        @pl.when(jnp.logical_not(own_a))
+        def _():
+            pltpu.make_async_copy(a_got.at[a], a_to, a_sem).start()
+
+        @pl.when(own_b)
+        def _():
+            pltpu.make_async_copy(own.at[b, pl.ds(half, half)], b_to, b_sem).start()
+
+        @pl.when(jnp.logical_not(own_b))
+        def _():
+            pltpu.make_async_copy(b_got.at[b], b_to, b_sem).start()
+
+    for item in range(2):
+        pltpu.make_async_copy(a_got.at[0], a_out.at[item], sems.at[2 * item]).wait()
+        pltpu.make_async_copy(b_got.at[0], b_out.at[item], sems.at[2 * item + 1]).wait()
 
 
 def relay(plan, items, a_got, b_got):
-    rows, width = a_got.shape[1:]
-    block = (1, rows, width)
+    whole = pl.BlockSpec(memory_space=pl.ANY)
     return pl.pallas_call(
         relay_kernel,
-        out_shape=[jax.ShapeDtypeStruct((2, rows, width), jnp.bfloat16)] * 2,
+        out_shape=[jax.ShapeDtypeStruct(a_got.shape, jnp.bfloat16)] * 2,
         grid_spec=pltpu.PrefetchScalarGridSpec(
             num_scalar_prefetch=1,
-            grid=(2,),
-            in_specs=[
-                pl.BlockSpec(block, lambda i, plan: (plan[0, i], 0, 0)),
-                pl.BlockSpec(block, lambda i, plan: (plan[1, i], 1, 0)),
-                pl.BlockSpec(block, lambda i, plan: (plan[0, i], 0, 0)),
-                pl.BlockSpec(block, lambda i, plan: (plan[1, i], 0, 0)),
-            ],
-            out_specs=[pl.BlockSpec(block, lambda i, plan: (i, 0, 0))] * 2,
-        ),
+            grid=(1,),
+            in_specs=[whole] * 3,
+            out_specs=[whole] * 2,
+            scratch_shapes=[pltpu.SemaphoreType.DMA((4,))],
+        ),
+        cost_estimate=pl.CostEstimate(flops=0, bytes_accessed=2 << 20, transcendentals=0),
         name="relay",
-    )(plan, items, items, a_got, b_got)
-
-
-def settle_kernel(plan, own, a_one, b_one, a_two, b_two, out):
-    pack = pl.program_id(0)
+    )(plan, items, a_got, b_got)
+
+
+def settle_kernel(plan, own, a_one, b_one, a_two, b_two, a_out, b_out, sems):
     half = a_one.shape[1]
-    mine = plan[1, pack] == 0
-    a = jnp.where(mine, own[0, :half], jnp.where(plan[1, pack] == 1, a_one[0], a_two[0]))
-    b = jnp.where(mine, own[0, half:], jnp.where(plan[1, pack] == 2, b_one[0], b_two[0]))
-    for e in range(out.shape[1]):
-        out[0, e, :half] = a[:, e * HD : e * HD + HD]
-        out[0, e, half:] = b[:, e * HD : e * HD + HD]
+
+    def spread(when, source, target, pack, side):
+        @pl.when(when)
+        def _():
+            for e in range(KVH):
+                pltpu.make_async_copy(
+                    source.at[:, pl.ds(e * HD, HD)], target.at[pack, e], sems.at[pack, side, e]
+                ).start()
+
+    for pack in range(2):
+        item, chip = plan[0, pack], plan[1, pack]
+        spread(chip == 0, own.at[item, pl.ds(0, half)], a_out, pack, 0)
+        spread(chip == 1, a_one.at[item], a_out, pack, 0)
+        spread(chip >= 2, a_two.at[pack], a_out, pack, 0)
+        spread(chip == 0, own.at[item, pl.ds(half, half)], b_out, pack, 1)
+        spread(chip == 2, b_one.at[item], b_out, pack, 1)
+        spread((chip == 1) | (chip == 3), b_two.at[pack], b_out, pack, 1)
+    for pack in range(2):
+        for side, target in enumerate((a_out, b_out)):
+            for e in range(KVH):
+                pltpu.make_async_copy(
+                    a_two.at[0, :, pl.ds(0, HD)], target.at[pack, e], sems.at[pack, side, e]
+                ).wait()
 
 
 def settle(plan, items, a_one, b_one, a_two, b_two):
-    rows, width = a_one.shape[1:]
-    part = width // 2
-    block = (1, rows, part)
+    whole = pl.BlockSpec(memory_space=pl.ANY)
+    shape = (2, KVH, a_one.shape[1], HD)
     return pl.pallas_call(
         settle_kernel,
-        out_shape=jax.ShapeDtypeStruct((2, KVH, 2 * rows, HD), jnp.bfloat16),
+        out_shape=[jax.ShapeDtypeStruct(shape, jnp.bfloat16)] * 2,
         grid_spec=pltpu.PrefetchScalarGridSpec(
             num_scalar_prefetch=1,
-            grid=(2, 2),
-            in_specs=[
-                pl.BlockSpec((1, 2 * rows, part), lambda i, j, plan: (plan[0, i], 0, j)),
-                pl.BlockSpec(block, lambda i, j, plan: (plan[0, i], 0, j)),
-                pl.BlockSpec(block, lambda i, j, plan: (plan[0, i], 0, j)),
-                pl.BlockSpec(block, lambda i, j, plan: (i, 0, j)),
-                pl.BlockSpec(block, lambda i, j, plan: (i, 0, j)),
-            ],
-            out_specs=pl.BlockSpec(
-                (1, KVH // 2, 2 * rows, HD), lambda i, j, plan: (i, j, 0, 0)
-            ),
-        ),
+            grid=(1,),
+            in_specs=[whole] * 5,
+            out_specs=[whole] * 2,
+            scratch_shapes=[pltpu.SemaphoreType.DMA((2, 2, KVH))],
+        ),
+        cost_estimate=pl.CostEstimate(flops=0, bytes_accessed=2 << 20, transcendentals=0),
         name="settle",
     )(plan, items, a_one, b_one, a_two, b_two)
 
@@ -202,6 +230,13 @@
     va[:, HD:] = jnp.ones_like(k_side)
 
 
+def put(o_ref, total, side):
+    rows = o_ref.shape[1]
+    for head in range(o_ref.shape[0]):
+        o_ref[head, :, :HD] = total[head * rows : head * rows + rows]
+        o_ref[head, :, HD:] = side[head * rows : head * rows + rows]
+
+
 def pack_kernel(
     core, seen, q_ref, mine_ref, other_ref, qb_ref, kb_ref, o_ref, qa, ka, va, top, acc
 ):
@@ -231,19 +266,18 @@
         def body(kj, carry):
             @pl.when(seen[qi, kj] > 0)
             def _():
-                at = pl.multiple_of(kj * CK, CK)
-                part = jnp.exp2(score(qa, ka, at, CK) * SCALE).astype(jnp.bfloat16)
+                at = pl.multiple_of(kj * BQ, BQ)
+                part = jnp.exp2(score(qa, ka, at, BQ) * SCALE).astype(jnp.bfloat16)
                 acc[...] += jnp.dot(
-                    part, va[pl.ds(at, CK), :], preferred_element_type=jnp.float32
+                    part, va[pl.ds(at, BQ), :], preferred_element_type=jnp.float32
                 )
 
             return carry
 
-        lax.fori_loop(0, qi * (BQ // CK), body, 0)
+        lax.fori_loop(0, qi, body, 0)
         kept = qa[:, HD:].astype(jnp.float32)
         shift_kept = jnp.sum(jnp.where(lane == SEGS, kept, 0.0), axis=1, keepdims=True)
-        o_ref[:, :HD] = acc[:, :HD]
-        o_ref[:, HD:] = jnp.where(lane == 1, shift_kept, acc[:, HD:])
+        put(o_ref, acc[:, :HD], jnp.where(lane == 1, shift_kept, acc[:, HD:]))
 
     run(ceiling(q_rows, top[0:1, 0:1]))
 
@@ -266,7 +300,7 @@
     once = dict(pipeline_mode=pl.Buffered(1))
     return pl.pallas_call(
         pack_kernel,
-        out_shape=jax.ShapeDtypeStruct((2 * pack, 2 * HD), jnp.float32),
+        out_shape=jax.ShapeDtypeStruct((2, pack, 2 * HD), jnp.float32),
         grid_spec=pltpu.PrefetchScalarGridSpec(
             num_scalar_prefetch=2,
             grid=(pack // BQ,),
@@ -277,7 +311,7 @@
                 pl.BlockSpec((BQ, HD), lambda i, *_: (i, 0)),
                 pl.BlockSpec((pack, HD), lambda i, *_: (0, 0), **once),
             ],
-            out_specs=pl.BlockSpec((2 * BQ, 2 * HD), lambda i, *_: (i, 0)),
+            out_specs=pl.BlockSpec((2, BQ, 2 * HD), lambda i, *_: (0, i, 0)),
             scratch_shapes=[
                 pltpu.VMEM((2 * BQ, 2 * HD), jnp.bfloat16),
                 pltpu.VMEM((pack, 2 * HD), jnp.bfloat16),
@@ -294,27 +328,46 @@
     )(core, seen, arrived, arrived, other, q_side, k_side)
 
 
-def stem_kernel(core, q_ref, mine_ref, other_ref, part_ref, o_ref, qa, ka, va, top, acc):
-    stem = ka.shape[0]
+def stem_kernel(last, core, q_ref, mine_ref, other_ref, part_ref, o_ref, qa, top, acc):
+    stem = mine_ref.shape[0]
+    heads, rows = part_ref.shape[:2]
     lane = lax.broadcasted_iota(jnp.int32, (1, HD), 1)
+    first = core[0] == 0
+    side = jnp.broadcast_to(jnp.where(lane == SEGS, -1.0, 0.0).astype(jnp.bfloat16), (CK, HD))
+    ones = jnp.ones((CK, HD), jnp.bfloat16)
+
+    def keys(at):
+        here = pl.ds(at, CK)
+        return jnp.where(first, mine_ref[here, :], other_ref[here, :])
 
     @pl.when(pl.program_id(0) == 0)
     def _():
-        side = jnp.broadcast_to(jnp.where(lane == SEGS, -1.0, 0.0).astype(jnp.bfloat16), (stem, HD))
-        fill(core[0], mine_ref, other_ref, side, ka, va)
-        top[...] = longest(ka, stem)
-
-    q_rows = stacked(q_ref)
+        def body(step, most):
+            wide = keys(pl.multiple_of(step * CK, CK)).astype(jnp.float32)
+            norms = jnp.sum(wide * wide, axis=1, keepdims=True)
+            return jnp.maximum(most, jnp.max(norms, axis=0, keepdims=True))
+
+        most = lax.fori_loop(0, stem // CK, body, jnp.zeros((1, 1), jnp.float32))
+        top[...] = jnp.broadcast_to(jnp.sqrt(most), (8, HD))
+
+    q_rows = jnp.concatenate([q_ref[:, h * HD : h * HD + HD] for h in range(heads)], axis=0)
     qa[:, :HD] = q_rows
+
+    def scores(at):
+        wide = jnp.concatenate([keys(at), side], axis=1)
+        return lax.dot_general(qa[...], wide, NT, preferred_element_type=jnp.float32)
 
     def run(shift):
         qa[:, HD:] = jnp.where(lane == SEGS, shift, 0.0).astype(jnp.bfloat16)
         total = None
-        held = score(qa, ka, 0, CK)
+        held = scores(0)
         for at in range(0, stem, CK):
-            ahead = score(qa, ka, at + CK, CK) if at + CK < stem else None
+            ahead = scores(at + CK) if at + CK < stem else None
             weights = jnp.exp2(held * SCALE).astype(jnp.bfloat16)
-            part = jnp.dot(weights, va[at : at + CK, :], preferred_element_type=jnp.float32)
+            here = pl.ds(at, CK)
+            wide = jnp.where(first, other_ref[here, :], mine_ref[here, :])
+            wide = jnp.concatenate([wide, ones], axis=1)
+            part = jnp.dot(weights, wide, preferred_element_type=jnp.float32)
             total = part if total is None else total + part
             held = ahead
         acc[...] = total
@@ -322,14 +375,19 @@
     def finish():
         kept = qa[:, HD:].astype(jnp.float32)
         shift = jnp.sum(jnp.where(lane == SEGS, kept, 0.0), axis=1, keepdims=True)
-        before = part_ref[:, HD + 1 : HD + 2]
+        part = jnp.concatenate([part_ref[h] for h in range(heads)], axis=0)
+        before = part[:, HD + 1 : HD + 2]
         most = jnp.maximum(shift, before)
         new = jnp.exp2((shift - most) * SCALE)
         old = jnp.exp2((before - most) * SCALE)
-        total = acc[:, HD : HD + 1] * new + part_ref[:, HD : HD + 1] * old
-        mixed = ((acc[:, :HD] * new + part_ref[:, :HD] * old) / total).astype(jnp.bfloat16)
-        o_ref[:, :HD] = mixed[:BQ]
-        o_ref[:, HD:] = mixed[BQ:]
+        total = acc[:, HD : HD + 1] * new + part[:, HD : HD + 1] * old
+        mixed = acc[:, :HD] * new + part[:, :HD] * old
+        if last:
+            mixed = (mixed / total).astype(jnp.bfloat16)
+            for h in range(heads):
+                o_ref[:, h * HD : h * HD + HD] = mixed[h * rows : h * rows + rows]
+        else:
+            put(o_ref, mixed, jnp.where(lane == 1, most, total))
 
     run(ceiling(q_rows, top[0:1, 0:1]))
     finish()
@@ -339,60 +397,71 @@
         qa[:, HD:] = jnp.zeros_like(q_rows)
 
         def body(step, most):
-            part = score(qa, ka, pl.multiple_of(step * BQ, BQ), BQ)
+            part = scores(pl.multiple_of(step * CK, CK))
             return jnp.maximum(most, jnp.max(part, axis=1, keepdims=True))
 
-        low = jnp.full((2 * BQ, 1), BARRED, jnp.float32)
-        run(lax.fori_loop(0, stem // BQ, body, low))
+        low = jnp.full((heads * rows, 1), BARRED, jnp.float32)
+        run(lax.fori_loop(0, stem // CK, body, low))
         finish()
 
 
-def stem_part(core, arrived, mine, other, before):
+def stem_part(core, arrived, mine, other, before, head=None):
     pack = arrived.shape[0]
     stem = mine.shape[0]
+    heads = 2 if head is None else 1
+    rows = 2 * BQ // heads
+    at = head or 0
     once = dict(pipeline_mode=pl.Buffered(1))
+    part = pl.BlockSpec((heads, rows, 2 * HD), lambda i, *_: (at, i, 0))
+    if head is None:
+        shape, spec = jax.ShapeDtypeStruct((2, pack, 2 * HD), jnp.float32), part
+    else:
+        shape = jax.ShapeDtypeStruct((pack, HD), jnp.bfloat16)
+        spec = pl.BlockSpec((rows, HD), lambda i, *_: (i, 0))
     return pl.pallas_call(
-        stem_kernel,
-        out_shape=jax.ShapeDtypeStruct((pack, 2 * HD), jnp.bfloat16),
+        functools.partial(stem_kernel, head is not None),
+        out_shape=shape,
         grid_spec=pltpu.PrefetchScalarGridSpec(
             num_scalar_prefetch=1,
-            grid=(pack // BQ,),
+            grid=(pack // rows,),
             in_specs=[
-                pl.BlockSpec((BQ, 2 * HD), lambda i, *_: (i, 0)),
+                pl.BlockSpec((rows, heads * HD), lambda i, *_: (i, at)),
                 pl.BlockSpec((stem, HD), lambda i, *_: (0, 0), **once),
                 pl.BlockSpec((stem, HD), lambda i, *_: (0, 0), **once),
-                pl.BlockSpec((2 * BQ, 2 * HD), lambda i, *_: (i, 0)),
+                part,
             ],
-            out_specs=pl.BlockSpec((BQ, 2 * HD), lambda i, *_: (i, 0)),
+            out_specs=spec,
             scratch_shapes=[
                 pltpu.VMEM((2 * BQ, 2 * HD), jnp.bfloat16),
-                pltpu.VMEM((stem, 2 * HD), jnp.bfloat16),
-                pltpu.VMEM((stem, 2 * HD), jnp.bfloat16),
                 pltpu.VMEM((8, HD), jnp.float32),
                 pltpu.VMEM((2 * BQ, 2 * HD), jnp.float32),
             ],
         ),
         compiler_params=pltpu.CompilerParams(vmem_limit_bytes=ROOM),
         cost_estimate=pl.CostEstimate(
-            flops=8 * pack * stem * HD, bytes_accessed=8 << 20, transcendentals=2 * pack * stem
+            flops=4 * heads * pack * stem * HD,
+            bytes_accessed=8 << 20,
+            transcendentals=heads * pack * stem,
         ),
         name="stem_part",
     )(core, arrived, mine, other, before)
 
 
-def gather_kernel(core, mine_ref, other_ref, o_ref):
+def gather_kernel(core, mine_a, mine_b, other_ref, o_ref):
     first = core[0] == 0
-    for e in range(mine_ref.shape[1]):
-        mine = mine_ref[0, e]
-        other = other_ref[e]
-        at = 4 * HD * e
-        o_ref[:, at : at + 2 * HD] = jnp.where(first, mine, other)
-        o_ref[:, at + 2 * HD : at + 4 * HD] = jnp.where(first, other, mine)
-
-
-def gather(core, mine, other):
-    tok = mine.shape[2]
+    for e in range(mine_a.shape[1]):
+        for head, mine_ref in enumerate((mine_a, mine_b)):
+            mine = mine_ref[0, e]
+            other = other_ref[head, e]
+            at = 4 * HD * e + HD * head
+            o_ref[:, at : at + HD] = jnp.where(first, mine, other)
+            o_ref[:, at + 2 * HD : at + 3 * HD] = jnp.where(first, other, mine)
+
+
+def gather(core, mine_a, mine_b, other):
+    tok = mine_a.shape[2]
     heads = KVH // 2
+    mine = pl.BlockSpec((1, heads, tok, HD), lambda i, core: (core[0], i, 0, 0))
     return pl.pallas_call(
         gather_kernel,
         out_shape=jax.ShapeDtypeStruct((tok, H * HD), jnp.bfloat16),
@@ -400,13 +469,14 @@
             num_scalar_prefetch=1,
             grid=(2,),
             in_specs=[
-                pl.BlockSpec((1, heads, tok, 2 * HD), lambda i, core: (core[0], i, 0, 0)),
-                pl.BlockSpec((heads, tok, 2 * HD), lambda i, core: (i, 0, 0)),
+                mine,
+                mine,
+                pl.BlockSpec((2, heads, tok, HD), lambda i, core: (0, i, 0, 0)),
             ],
             out_specs=pl.BlockSpec((tok, H * HD // 2), lambda i, core: (0, i)),
         ),
         name="gather",
-    )(core, mine, other)
+    )(core, mine_a, mine_b, other)
 
 
 def shards(queries, keys, values, stem_kv, seg_ids, seg_parent, stem_owner):
@@ -422,19 +492,9 @@
     near, far = x ^ 1, 3 - x
     a_one = lax.ppermute(items[:, :half], "x", NEAR)
     b_one = lax.ppermute(items[:, half:], "x", FAR)
-    follow = stem_owner.reshape(4, 2)
-    for_far, for_near, for_us = follow[far], follow[near], follow[x]
-    plan = jnp.stack(
-        [for_far % 2, for_near % 2, (for_far // 2 == x) * 1, (for_near // 2 == x) * 1]
-    ).astype(jnp.int32)
-    a_send, b_send = relay(plan, items, a_one, b_one)
-    a_two = lax.ppermute(a_send, "x", FAR)
-    b_two = lax.ppermute(b_send, "x", NEAR)
-    chip = for_us // 2
-    source = jnp.where(chip == x, 0, jnp.where(chip == near, 1, jnp.where(chip == far, 2, 3)))
-    stems = settle(
-        jnp.stack([for_us % 2, source]).astype(jnp.int32), items, a_one, b_one, a_two, b_two
-    ).reshape(16, 2 * half, HD)
+    queries, seg_ids, seg_parent, _ = lax.optimization_barrier(
+        (queries, seg_ids, seg_parent, items)
+    )
 
     linked = ancestry(seg_parent[0])
     places = token_places(seg_ids[0], linked)
@@ -448,6 +508,20 @@
         jnp.concatenate([cosine, cosine], axis=1),
         jnp.concatenate([-sine, sine], axis=1),
     )
+
+    a_one, b_one, sent = lax.optimization_barrier((a_one, b_one, sent))
+    follow = stem_owner.reshape(4, 2)
+    for_far, for_near, for_us = follow[far], follow[near], follow[x]
+    plan = jnp.stack(
+        [for_far % 2, for_near % 2, (for_far // 2 == x) * 1, (for_near // 2 == x) * 1]
+    ).astype(jnp.int32)
+    a_send, b_send = relay(plan, items, a_one, b_one)
+    a_two = lax.ppermute(a_send, "x", FAR)
+    b_two = lax.ppermute(b_send, "x", NEAR)
+
+    sent, a_send, seg_ids, seg_parent = lax.optimization_barrier(
+        (sent, a_send, seg_ids, seg_parent)
+    )
     crossed = lax.all_to_all(sent, "core", split_axis=0, concat_axis=0, tiled=True)
     arrived = lax.all_to_all(
         crossed.reshape(16, tok, 3 * HD), SEQ, split_axis=0, concat_axis=0, tiled=True
@@ -462,19 +536,37 @@
     q_side = jnp.dot(onehot, barred, precision=lax.Precision.HIGHEST).astype(jnp.bfloat16)
     k_side = jnp.where(jnp.arange(HD)[None, :] == SEGS, -1.0, onehot).astype(jnp.bfloat16)
     q_has = onehot.reshape(pack_len // BQ, BQ, HD).max(axis=1)[:, :SEGS]
-    k_has = onehot.reshape(pack_len // CK, CK, HD).max(axis=1)[:, :SEGS]
-    seen = (q_has @ reach @ k_has.T > 0.5).astype(jnp.int32)
-
-    before = pack_part(core_row, seen, arrived, pair, q_side, k_side)
-    mine = lax.all_to_all(stems, SEQ, split_axis=0, concat_axis=0, tiled=True).reshape(STEM, HD)
-    other = lax.ppermute(mine, "core", FLIP)
-    mixed = stem_part(core_row, arrived, mine, other, before)
-
-    back = lax.all_to_all(
-        mixed.reshape(16, tok, 2 * HD), SEQ, split_axis=0, concat_axis=0, tiled=True
-    ).reshape(2, KVH, tok, 2 * HD)
-    away = lax.dynamic_index_in_dim(back, 1 - core, 0, keepdims=False)
-    return gather(core_row, back, lax.ppermute(away, "core", FLIP))[None]
+    seen = (q_has @ reach @ q_has.T > 0.5).astype(jnp.int32)
+
+    chip = for_us // 2
+    source = jnp.where(chip == x, 0, jnp.where(chip == near, 1, jnp.where(chip == far, 2, 3)))
+    a_stem, b_stem = settle(
+        jnp.stack([for_us % 2, source]).astype(jnp.int32), items, a_one, b_one, a_two, b_two
+    )
+
+    def to_heads(part):
+        part = part.reshape(16, half, HD)
+        part = lax.all_to_all(part, SEQ, split_axis=0, concat_axis=0, tiled=True)
+        return part.reshape(16 * half, HD)
+
+    a_mine = to_heads(a_stem)
+    arrived, pair, _ = lax.optimization_barrier((arrived, pair, a_stem))
+    partial = pack_part(core_row, seen, arrived, pair, q_side, k_side)
+    a_mine, partial, b_stem = lax.optimization_barrier((a_mine, partial, b_stem))
+    b_mine = to_heads(b_stem)
+    partial = stem_part(core_row, arrived, a_mine, lax.ppermute(a_mine, "core", FLIP), partial)
+    b_other = lax.ppermute(b_mine, "core", FLIP)
+    backs = []
+    for head in range(2):
+        mixed = stem_part(core_row, arrived, b_mine, b_other, partial, head)
+        back = lax.all_to_all(
+            mixed.reshape(16, tok, HD), SEQ, split_axis=0, concat_axis=0, tiled=True
+        )
+        backs.append(back.reshape(2, KVH, tok, HD))
+    away = jnp.stack(
+        [lax.dynamic_index_in_dim(back, 1 - core, 0, keepdims=False) for back in backs]
+    )
+    return gather(core_row, backs[0], backs[1], lax.ppermute(away, "core", FLIP))[None]
 
 
 def solution(mesh):

time: 170 us -> 242 us (1.42)
  Pallas kernels: 57.8 us -> 127 us
  starting transfers between devices: 32.8 us -> 39.6 us
    pallas_call x4 -> x6, Pallas kernels: 49.9 us -> 119 us  [the longest x3 36.9 us: stem_part(): pl.pallas_call(functools.partial(stem_kernel, head is not None), out_shap...]
    all_to_all x1, waiting for transfers between devices: 0.01 us -> 22.2 us  [shards(): lax.all_to_all(crossed.reshape(16, tok, 3 * HD), SEQ, split_axis=0, conca...]
    ppermute x1, waiting for transfers between devices: 10.6 us -> 0.01 us  [shards(): a_two = lax.ppermute(a_send, 'x', FAR)]
    all_to_all x2 -> x4, starting transfers between devices: 9.74 us -> 19.3 us  [the longest x2 10.2 us: to_heads(): part = lax.all_to_all(part, SEQ, split_axis=0, concat_axis=0, tiled=True)]
    ppermute x1, waiting for transfers between devices: 7.4 us -> 0.83 us  [shards(): a_one = lax.ppermute(items[:, :half], 'x', NEAR)]
    all_to_all x2 -> x4, waiting for transfers between devices: 27 us -> 22 us  [the longest x2 11.8 us: shards(): lax.all_to_all(mixed.reshape(16, tok, HD), SEQ, split_axis=0, concat_axis...]
    all_to_all x1, blocking collectives: 9.02 us -> 5.87 us  [shards(): lax.all_to_all(sent, 'core', split_axis=0, concat_axis=0, tiled=True)]
    ppermute x2 -> x3, starting transfers between devices: 5.6 us -> 4.13 us  [the longest x1 1.81 us: shards(): lax.ppermute(away, 'core', FLIP)]
  transfers between devices with their start and end apart: 11 -> 14, of which waited for: 7 -> 7; matrix products, arithmetic and copies ran while one was open for 4% -> 3% of each run, Pallas kernels for 14% -> 34%
where the time goes in v3:
time: 242 us; the launch traced here: 241 us
  Pallas kernels  127 us (52%)
  waiting for transfers between devices  48.7 us (20%)
  starting transfers between devices  39.6 us (16%)
  blocking collectives  12.6 us (5%)
  local copies, waits for them, and re-layouts  4.53 us (2%)
  other arithmetic  4.3 us (2%)
  matrix products  3.6 us (1%)
    pallas_call x3, Pallas kernels, stem_part(): pl.pallas_call(functools.partial(stem_kernel, head is not None), out_shap...  36.9 us
    pallas_call x1, Pallas kernels, settle(): pl.pallas_call(settle_kernel, out_shape=[jax.ShapeDtypeStruct(shape, jnp....  33.9 us
    pallas_call x1, Pallas kernels, relay(): pl.pallas_call(relay_kernel, out_shape=[jax.ShapeDtypeStruct(a_got.shape,...  33.6 us
    all_to_all x1, waiting for transfers between devices, shards(): lax.all_to_all(crossed.reshape(16, tok, 3 * HD), SEQ, split_axis=0, conca...  22.2 us
    pallas_call x1, Pallas kernels, pack_part(): pl.pallas_call(pack_kernel, out_shape=jax.ShapeDtypeStruct((2, pack, 2 *...  14.9 us
    all_to_all x2, waiting for transfers between devices, shards(): lax.all_to_all(mixed.reshape(16, tok, HD), SEQ, split_axis=0, concat_axis...  11.8 us
    all_to_all x2, starting transfers between devices, to_heads(): part = lax.all_to_all(part, SEQ, split_axis=0, concat_axis=0, tiled=True)  10.2 us
    all_to_all x2, waiting for transfers between devices, to_heads(): part = lax.all_to_all(part, SEQ, split_axis=0, concat_axis=0, tiled=True)  10.2 us
  transfers between devices with their start and end apart: 14, of which 7 were waited for; matrix products, arithmetic and copies ran while one was open for 3% of the time, Pallas kernels for 34%

profile of v3, /device:TPU:1, one launch (start us, length us, event | category | flops | bytes accessed | tf_op | source)
XLA Modules:
  0.0 240.8 jit_solution(11783919148383062807)
XLA Ops:
  0.0 6.7 %all_to_all.35.own = bf16[2,256,1024]{2,1,0:T(8,128)(2,1)S(1)} all-to-all(bf16[2,256,1024]{2,1,0:T(8,128)(2,1)} %bitcast.46), channel_id=1, replica_groups=mesh['x'=4,'core'=2,'z'=4,'y'=4] {'core'}, dimensions={0} | all-to-all | bytes 2097152 | tf_op jit(solution)/shard_map/all_to_all | solution.py:490
  6.7 1.0 fusion.24
  7.8 1.3 collective-permute-start
  9.1 1.8 collective-permute-start.1
  13.4 5.8 %turn.1 = bf16[2,8,128,384]{3,2,1,0:T(8,128)(2,1)} custom-call(bf16[128,4096]{1,0:T(8,128)(2,1)} %bitcast.45, bf16[128,1024]{1,0:T(8,128)(2,1)} %bitcast.55, bf16[128,1024]{1,0:T(8,128)(2,1)} %bitcast.56, f32[128,128]{1,0:T(8,128)} %get-tuple-element.64.cos_ref, f32[128,128]{1,0:T(8,128)} %get-tuple-element.65.sin_ref), custom_call_target="tpu_custom_call" | custom-call | tf_op jit(solution)/shard_map/turn/pallas_call | solution.py:92
  20.4 0.8 collective-permute-done.a_got.a_one
  21.2 2.2 collective-permute-done.1.b_got.b_one
  23.4 33.6 %relay.1 = (bf16[2,128,1024]{2,1,0:T(8,128)(2,1)}, bf16[2,128,1024]{2,1,0:T(8,128)(2,1)}) custom-call(s32[4,2]{1,0:T(4,128)} %pad_add_fusion.1.plan, bf16[2,256,1024]{2,1,0:T(8,128)(2,1)} %copy-done, bf16[2,128,1024]{2,1,0:T(8,128)(2,1)} %copy-done.5, bf16[2,128,1024]{2,1,0:T(8,128)(2,1)} %collective-permute-done.1.b_got.b_one), custom_call_target="tpu_custom_call" | custom-call | bytes 2097152 | tf_op jit(solution)/shard_map/relay/pallas_call | solution.py:139
  57.0 1.6 collective-permute-start.5
  58.6 1.8 collective-permute-start.3
  60.5 5.9 %all_to_all.36 = bf16[2,8,128,384]{3,2,1,0:T(8,128)(2,1)} all-to-all(bf16[2,8,128,384]{3,2,1,0:T(8,128)(2,1)S(1)} %copy-done.1), channel_id=1, replica_groups=mesh['x'=4,'core'=2,'z'=4,'y'=4] {'core'}, dimensions={0} | all-to-all | bytes 3145728 | tf_op jit(solution)/shard_map/all_to_all | solution.py:525
  66.3 7.8 %all-to-all-start.2 = ((bf16[16,128,384]{2,1,0:T(8,128)(2,1)}), bf16[16,128,384]{2,1,0:T(8,128)(2,1)S(1)}, u32[]{:S(2)}, u32[]{:S(2)}) async-start(bf16[16,128,384]{2,1,0:T(8,128)(2,1)} %bitcast.34), calls=%async_computation.2 | async-start | bytes 3145728 | tf_op jit(solution)/shard_map/all_to_all | solution.py:526
  74.6 1.1 select_convert_fusion.kb_ref
  75.9 22.2 %all-to-all-done.2 = bf16[16,128,384]{2,1,0:T(8,128)(2,1)S(1)} async-done(((bf16[16,128,384]{2,1,0:T(8,128)(2,1)}), bf16[16,128,384]{2,1,0:T(8,128)(2,1)S(1)}, u32[]{:S(2)}, u32[]{:S(2)}) %all-to-all-start.2) | async-done | bytes 1572896 | tf_op jit(solution)/shard_map/all_to_all | solution.py:526
  98.1 1.9 collective-permute-start.2
  100.3 1.5 convolution_convert_fusion.qb_ref
  101.9 33.9 %settle.1 = (bf16[2,8,128,128]{3,2,1,0:T(8,128)(2,1)}, bf16[2,8,128,128]{3,2,1,0:T(8,128)(2,1)}) custom-call(s32[2,2]{1,0:T(2,128)} %pad_add_fusion.2.plan, bf16[2,256,1024]{2,1,0:T(8,128)(2,1)} %copy-done, bf16[2,128,1024]{2,1,0:T(8,128)(2,1)} %copy-done.5, bf16[2,128,1024]{2,1,0:T(8,128)(2,1)} %collective-permute-done.1.b_got.b_one, ...), custom_call_target="tpu_custom_call" | custom-call | bytes 2097152 | tf_op jit(solution)/shard_map/settle/pallas_call | solution.py:184
  135.7 3.6 %all-to-all-start.3 = ((bf16[16,128,128]{2,1,0:T(8,128)(2,1)}), bf16[16,128,128]{2,1,0:T(8,128)(2,1)S(1)}, u32[]{:S(2)}, u32[]{:S(2)}) async-start(bf16[16,128,128]{2,1,0:T(8,128)(2,1)} %bitcast.52), calls=%async_computation.3 | async-start | bytes 1048576 | tf_op jit(solution)/shard_map/all_to_all | solution.py:549
  140.9 14.9 %pack_part.1.part_ref = f32[2,2048,256]{2,1,0:T(8,128)} custom-call(s32[1]{0:T(128)} %bitcast.core, s32[4,4]{1,0:T(4,128)} %fusion.8.seen, bf16[2048,384]{1,0:T(8,128)(2,1)} %bitcast.40, bf16[2048,384]{1,0:T(8,128)(2,1)} %bitcast.41, bf16[2048,128]{1,0:T(8,128)(2,1)} %copy-done.13, bf16[2048,128]{1,0:T(8,128)(2,1)} %convolution_convert_fusion.qb_ref, ...), custom_call_target="tpu_custom_call" | custom-call | flops 4294967296 | bytes 8388608 | tf_op jit(solution)/shard_map/pack_part/pallas_call | solution.py:301
  155.8 6.6 %all-to-all-start.4 = ((bf16[16,128,128]{2,1,0:T(8,128)(2,1)}), bf16[16,128,128]{2,1,0:T(8,128)(2,1)S(1)}, u32[]{:S(2)}, u32[]{:S(2)}) async-start(bf16[16,128,128]{2,1,0:T(8,128)(2,1)} %bitcast.14), calls=%async_computation.4 | async-start | bytes 1048576 | tf_op jit(solution)/shard_map/all_to_all | solution.py:549
  163.1 10.2 %all-to-all-done.4 = bf16[16,128,128]{2,1,0:T(8,128)(2,1)S(1)} async-done(((bf16[16,128,128]{2,1,0:T(8,128)(2,1)}), bf16[16,128,128]{2,1,0:T(8,128)(2,1)S(1)}, u32[]{:S(2)}, u32[]{:S(2)}) %all-to-all-start.4) | async-done | bytes 524320 | tf_op jit(solution)/shard_map/all_to_all | solution.py:549
  173.3 1.7 collective-permute-start.6
  175.8 17.0 %stem_part.3.part_ref = f32[2,2048,256]{2,1,0:T(8,128)} custom-call(s32[1]{0:T(128)} %bitcast.core, bf16[2048,384]{1,0:T(8,128)(2,1)} %bitcast.42, bf16[2048,128]{1,0:T(8,128)(2,1)} %bitcast.48, bf16[2048,128]{1,0:T(8,128)(2,1)} %copy-done.15, f32[2,2048,256]{2,1,0:T(8,128)} %pack_part.1.part_ref), custom_call_target="tpu_custom_call" | custom-call | flops 4294967296 | bytes 8388608 | tf_op jit(solution)/shard_map/stem_part/pallas_call | solution.py:421
  193.5 10.0 %stem_part.5 = bf16[2048,128]{1,0:T(8,128)(2,1)} custom-call(s32[1]{0:T(128)} %bitcast.core, bf16[2048,384]{1,0:T(8,128)(2,1)} %bitcast.43, bf16[2048,128]{1,0:T(8,128)(2,1)} %bitcast.50, bf16[2048,128]{1,0:T(8,128)(2,1)} %copy-done.14, f32[2,2048,256]{2,1,0:T(8,128)} %stem_part.3.part_ref), custom_call_target="tpu_custom_call" | custom-call | flops 2147483648 | bytes 8388608 | tf_op jit(solution)/shard_map/stem_part/pallas_call | solution.py:421
  203.5 3.8 %all-to-all-start.6 = ((bf16[16,128,128]{2,1,0:T(8,128)(2,1)}), bf16[16,128,128]{2,1,0:T(8,128)(2,1)S(1)}, u32[]{:S(2)}, u32[]{:S(2)}) async-start(bf16[16,128,128]{2,1,0:T(8,128)(2,1)} %bitcast.54), calls=%async_computation.6 | async-start | bytes 1048576 | tf_op jit(solution)/shard_map/all_to_all | solution.py:562
  207.3 10.0 %stem_part.4 = bf16[2048,128]{1,0:T(8,128)(2,1)} custom-call(s32[1]{0:T(128)} %bitcast.core, bf16[2048,384]{1,0:T(8,128)(2,1)} %bitcast.44, bf16[2048,128]{1,0:T(8,128)(2,1)} %bitcast.51, bf16[2048,128]{1,0:T(8,128)(2,1)} %copy-done.14, f32[2,2048,256]{2,1,0:T(8,128)} %stem_part.3.part_ref), custom_call_target="tpu_custom_call" | custom-call | flops 2147483648 | bytes 8388608 | tf_op jit(solution)/shard_map/stem_part/pallas_call | solution.py:421
  217.3 1.1 all-to-all-done.6
  218.4 5.3 %all-to-all-start.5 = ((bf16[16,128,128]{2,1,0:T(8,128)(2,1)}), bf16[16,128,128]{2,1,0:T(8,128)(2,1)S(1)}, u32[]{:S(2)}, u32[]{:S(2)}) async-start(bf16[16,128,128]{2,1,0:T(8,128)(2,1)} %bitcast.53), calls=%async_computation.5 | async-start | bytes 1048576 | tf_op jit(solution)/shard_map/all_to_all | solution.py:562
  223.7 10.7 %all-to-all-done.5 = bf16[16,128,128]{2,1,0:T(8,128)(2,1)S(1)} async-done(((bf16[16,128,128]{2,1,0:T(8,128)(2,1)}), bf16[16,128,128]{2,1,0:T(8,128)(2,1)S(1)}, u32[]{:S(2)}, u32[]{:S(2)}) %all-to-all-start.5) | async-done | bytes 524320 | tf_op jit(solution)/shard_map/all_to_all | solution.py:562
  234.6 1.8 collective-permute-start.8
  236.4 1.5 collective-permute-done.8.other_ref
  238.7 2.1 gather.1
  (75 shorter events, 9.4 us)
Async XLA Ops:
  6.7 12.5 %copy-start = (bf16[2,256,1024]{2,1,0:T(8,128)(2,1)}, bf16[2,256,1024]{2,1,0:T(8,128)(2,1)S(1)}, u32[]{:S(2)}) copy-start(bf16[2,256,1024]{2,1,0:T(8,128)(2,1)S(1)} %all_to_all.35.own) | copy-start | bytes 3145732
  6.7 4.2 %copy-start.9 = (s32[1,2048]{1,0:T(1,128)S(1)}, s32[1,2048]{1,0:T(1,128)}, u32[]{:S(2)}) copy-start(s32[1,2048]{1,0:T(1,128)} %param.12) | copy-start | bytes 24580
  6.7 4.3 %copy-start.10 = (s32[1,16]{1,0:T(1,128)S(1)}, s32[1,16]{1,0:T(1,128)}, u32[]{:S(2)}) copy-start(s32[1,16]{1,0:T(1,128)} %param.13) | copy-start | bytes 196
  6.7 5.1 %copy-start.12 = (s32[8]{0:T(128)S(1)}, s32[8]{0:T(128)}, u32[]{:S(2)}) copy-start(s32[8]{0:T(128)} %param.14) | copy-start | bytes 100
  6.7 5.5 %copy-start.11 = (f32[64]{0:T(128)S(1)}, f32[64]{0:T(128)}, u32[]{:S(2)}) copy-start(f32[64]{0:T(128)} %constant.123.clone) | copy-start | bytes 772
  7.8 13.4 %collective-permute-start = (bf16[2,128,1024]{2,1,0:T(8,128)(2,1)}, bf16[2,128,1024]{2,1,0:T(8,128)(2,1)S(1)}, u32[]{:S(2)}, u32[]{:S(2)}) collective-permute-start(bf16[2,128,1024]{2,1,0:T(8,128)(2,1)} %get-tuple-element.48), channel_id=1, source_target_pairs={{0,32},{32,0},{64,96},{96,64},{1,33},{33,1},{65,97},{97,65},{2,34}... | collective-permute-start | bytes 1572872 | tf_op jit(solution)/shard_map/ppermute | solution.py:493
  9.1 14.3 %collective-permute-start.1 = (bf16[2,128,1024]{2,1,0:T(8,128)(2,1)}, bf16[2,128,1024]{2,1,0:T(8,128)(2,1)}, u32[]{:S(2)}, u32[]{:S(2)}) collective-permute-start(bf16[2,128,1024]{2,1,0:T(8,128)(2,1)} %get-tuple-element.47), channel_id=1, source_target_pairs={{0,96},{96,0},{32,64},{64,32},{1,97},{97,1},{33,65},{65,33},{2,98}... | collective-permute-start | bytes 1572872 | tf_op jit(solution)/shard_map/ppermute | solution.py:494
  19.2 41.3 %copy-start.1 = (bf16[2,8,128,384]{3,2,1,0:T(8,128)(2,1)S(1)}, bf16[2,8,128,384]{3,2,1,0:T(8,128)(2,1)}, u32[]{:S(2)}) copy-start(bf16[2,8,128,384]{3,2,1,0:T(8,128)(2,1)} %turn.1) | copy-start | bytes 4718596
  21.2 2.2 copy-start.5
  57.0 17.1 %collective-permute-start.5 = (s32[2064]{0:T(1024)S(1)}, s32[2064]{0:T(1024)S(1)}, u32[]{:S(2)}, u32[]{:S(2)}) collective-permute-start(s32[2064]{0:T(1024)S(1)} %pad_add_fusion), channel_id=1, source_target_pairs={{0,16},{16,0},{1,17},{17,1},{2,18},{18,2},{3,19},{19,3},{4,20},{20... | collective-permute-start | bytes 24776 | tf_op jit(solution)/shard_map/ppermute | solution.py:532
  58.6 43.2 %collective-permute-start.3 = (bf16[2,128,1024]{2,1,0:T(8,128)(2,1)}, bf16[2,128,1024]{2,1,0:T(8,128)(2,1)}, u32[]{:S(2)}, u32[]{:S(2)}) collective-permute-start(bf16[2,128,1024]{2,1,0:T(8,128)(2,1)} %get-tuple-element.29), channel_id=1, source_target_pairs={{0,96},{96,0},{32,64},{64,32},{1,97},{97,1},{33,65},{65,33},{2,98}... | collective-permute-start | bytes 1572872 | tf_op jit(solution)/shard_map/ppermute | solution.py:519
  60.5 41.4 %collective-permute-start.4 = (bf16[2,128,1024]{2,1,0:T(8,128)(2,1)}, bf16[2,128,1024]{2,1,0:T(8,128)(2,1)}, u32[]{:S(2)}, u32[]{:S(2)}) collective-permute-start(bf16[2,128,1024]{2,1,0:T(8,128)(2,1)} %get-tuple-element.31), channel_id=1, source_target_pairs={{0,32},{32,0},{64,96},{96,64},{1,33},{33,1},{65,97},{97,65},{2,34}... | collective-permute-start | bytes 1572872 | tf_op jit(solution)/shard_map/ppermute | solution.py:520
  66.3 31.7 %all-to-all-start.2 = ((bf16[16,128,384]{2,1,0:T(8,128)(2,1)}), bf16[16,128,384]{2,1,0:T(8,128)(2,1)S(1)}, u32[]{:S(2)}, u32[]{:S(2)}) async-start(bf16[16,128,384]{2,1,0:T(8,128)(2,1)} %bitcast.34), calls=%async_computation.2 | async-start | bytes 3145728 | tf_op jit(solution)/shard_map/all_to_all | solution.py:526
  98.1 37.7 %copy-start.4 = (bf16[16,128,384]{2,1,0:T(8,128)(2,1)}, bf16[16,128,384]{2,1,0:T(8,128)(2,1)S(1)}, u32[]{:S(2)}) copy-start(bf16[16,128,384]{2,1,0:T(8,128)(2,1)S(1)} %all-to-all-done.2) | copy-start | bytes 4718596
  98.1 42.0 %collective-permute-start.2 = (bf16[2048,128]{1,0:T(8,128)(2,1)S(1)}, bf16[2048,128]{1,0:T(8,128)(2,1)S(1)}, u32[]{:S(2)}, u32[]{:S(2)}) collective-permute-start(bf16[2048,128]{1,0:T(8,128)(2,1)S(1)} %slice.26), channel_id=1, source_target_pairs={{0,16},{16,0},{1,17},{17,1},{2,18},{18,2},{3,19},{19,3},{4,20},{20... | collective-permute-start | bytes 1572872 | tf_op jit(solution)/shard_map/ppermute | solution.py:529
  135.7 20.1 %all-to-all-start.3 = ((bf16[16,128,128]{2,1,0:T(8,128)(2,1)}), bf16[16,128,128]{2,1,0:T(8,128)(2,1)S(1)}, u32[]{:S(2)}, u32[]{:S(2)}) async-start(bf16[16,128,128]{2,1,0:T(8,128)(2,1)} %bitcast.52), calls=%async_computation.3 | async-start | bytes 1048576 | tf_op jit(solution)/shard_map/all_to_all | solution.py:549
  140.1 0.8 copy-start.13
  155.8 19.1 %copy-start.6 = (bf16[16,128,128]{2,1,0:T(8,128)(2,1)}, bf16[16,128,128]{2,1,0:T(8,128)(2,1)S(1)}, u32[]{:S(2)}) copy-start(bf16[16,128,128]{2,1,0:T(8,128)(2,1)S(1)} %all-to-all-done.3) | copy-start | bytes 1572868
  155.8 17.4 %all-to-all-start.4 = ((bf16[16,128,128]{2,1,0:T(8,128)(2,1)}), bf16[16,128,128]{2,1,0:T(8,128)(2,1)S(1)}, u32[]{:S(2)}, u32[]{:S(2)}) async-start(bf16[16,128,128]{2,1,0:T(8,128)(2,1)} %bitcast.14), calls=%async_computation.4 | async-start | bytes 1048576 | tf_op jit(solution)/shard_map/all_to_all | solution.py:549
  162.5 12.5 %collective-permute-start.7 = (bf16[2048,128]{1,0:T(8,128)(2,1)S(1)}, bf16[2048,128]{1,0:T(8,128)(2,1)S(1)}, u32[]{:S(2)}, u32[]{:S(2)}) collective-permute-start(bf16[2048,128]{1,0:T(8,128)(2,1)S(1)} %bitcast.47), channel_id=1, source_target_pairs={{0,16},{16,0},{1,17},{17,1},{2,18},{18,2},{3,19},{19,3},{4,20},{20... | collective-permute-start | bytes 1572872 | tf_op jit(solution)/shard_map/ppermute | solution.py:557
  173.3 19.5 %copy-start.7 = (bf16[16,128,128]{2,1,0:T(8,128)(2,1)}, bf16[16,128,128]{2,1,0:T(8,128)(2,1)S(1)}, u32[]{:S(2)}) copy-start(bf16[16,128,128]{2,1,0:T(8,128)(2,1)S(1)} %all-to-all-done.4) | copy-start | bytes 1572868
  173.3 19.5 %collective-permute-start.6 = (bf16[2048,128]{1,0:T(8,128)(2,1)S(1)}, bf16[2048,128]{1,0:T(8,128)(2,1)S(1)}, u32[]{:S(2)}, u32[]{:S(2)}) collective-permute-start(bf16[2048,128]{1,0:T(8,128)(2,1)S(1)} %bitcast.49), channel_id=1, source_target_pairs={{0,16},{16,0},{1,17},{17,1},{2,18},{18,2},{3,19},{19,3},{4,20},{20... | collective-permute-start | bytes 1572872 | tf_op jit(solution)/shard_map/ppermute | solution.py:558
  175.0 0.8 copy-start.15
  192.7 0.8 copy-start.14
  203.5 14.9 %all-to-all-start.6 = ((bf16[16,128,128]{2,1,0:T(8,128)(2,1)}), bf16[16,128,128]{2,1,0:T(8,128)(2,1)S(1)}, u32[]{:S(2)}, u32[]{:S(2)}) async-start(bf16[16,128,128]{2,1,0:T(8,128)(2,1)} %bitcast.54), calls=%async_computation.6 | async-start | bytes 1048576 | tf_op jit(solution)/shard_map/all_to_all | solution.py:562
  218.4 16.1 %copy-start.2 = (bf16[16,128,128]{2,1,0:T(8,128)(2,1)}, bf16[16,128,128]{2,1,0:T(8,128)(2,1)S(1)}, u32[]{:S(2)}) copy-start(bf16[16,128,128]{2,1,0:T(8,128)(2,1)S(1)} %all-to-all-done.6) | copy-start | bytes 1572868
  218.4 16.1 %all-to-all-start.5 = ((bf16[16,128,128]{2,1,0:T(8,128)(2,1)}), bf16[16,128,128]{2,1,0:T(8,128)(2,1)S(1)}, u32[]{:S(2)}, u32[]{:S(2)}) async-start(bf16[16,128,128]{2,1,0:T(8,128)(2,1)} %bitcast.53), calls=%async_computation.5 | async-start | bytes 1048576 | tf_op jit(solution)/shard_map/all_to_all | solution.py:562
  234.5 3.4 %copy-start.3 = (bf16[16,128,128]{2,1,0:T(8,128)(2,1)}, bf16[16,128,128]{2,1,0:T(8,128)(2,1)S(1)}, u32[]{:S(2)}) copy-start(bf16[16,128,128]{2,1,0:T(8,128)(2,1)S(1)} %all-to-all-done.5) | copy-start | bytes 1572868
  234.6 3.3 %collective-permute-start.8 = (bf16[2,8,128,128]{3,2,1,0:T(8,128)(2,1)S(1)}, bf16[2,8,128,128]{3,2,1,0:T(8,128)(2,1)S(1)}, u32[]{:S(2)}, u32[]{:S(2)}) collective-permute-start(bf16[2,8,128,128]{3,2,1,0:T(8,128)(2,1)S(1)} %pad_maximum_fusion), channel_id=1, source_target_pairs={{0,16},{16,0},{1,17},{17,1},{2,18},{18,2},{3,19},{19,3},{4,20},{20... | collective-permute-start | bytes 1572872 | tf_op jit(solution)/shard_map/ppermute | solution.py:569
  237.9 0.8 copy-start.8

commit v4 on v2

--- a/solution.py
+++ b/solution.py
@@ -1,4 +1,3 @@
-import functools
 import math
 
 import jax
@@ -202,6 +201,13 @@
     va[:, HD:] = jnp.ones_like(k_side)
 
 
+def put(o_ref, total, side):
+    rows = o_ref.shape[1]
+    for head in range(o_ref.shape[0]):
+        o_ref[head, :, :HD] = total[head * rows : head * rows + rows]
+        o_ref[head, :, HD:] = side[head * rows : head * rows + rows]
+
+
 def pack_kernel(
     core, seen, q_ref, mine_ref, other_ref, qb_ref, kb_ref, o_ref, qa, ka, va, top, acc
 ):
@@ -231,19 +237,18 @@
         def body(kj, carry):
             @pl.when(seen[qi, kj] > 0)
             def _():
-                at = pl.multiple_of(kj * CK, CK)
-                part = jnp.exp2(score(qa, ka, at, CK) * SCALE).astype(jnp.bfloat16)
+                at = pl.multiple_of(kj * BQ, BQ)
+                part = jnp.exp2(score(qa, ka, at, BQ) * SCALE).astype(jnp.bfloat16)
                 acc[...] += jnp.dot(
-                    part, va[pl.ds(at, CK), :], preferred_element_type=jnp.float32
+                    part, va[pl.ds(at, BQ), :], preferred_element_type=jnp.float32
                 )
 
             return carry
 
-        lax.fori_loop(0, qi * (BQ // CK), body, 0)
+        lax.fori_loop(0, qi, body, 0)
         kept = qa[:, HD:].astype(jnp.float32)
         shift_kept = jnp.sum(jnp.where(lane == SEGS, kept, 0.0), axis=1, keepdims=True)
-        o_ref[:, :HD] = acc[:, :HD]
-        o_ref[:, HD:] = jnp.where(lane == 1, shift_kept, acc[:, HD:])
+        put(o_ref, acc[:, :HD], jnp.where(lane == 1, shift_kept, acc[:, HD:]))
 
     run(ceiling(q_rows, top[0:1, 0:1]))
 
@@ -266,7 +271,7 @@
     once = dict(pipeline_mode=pl.Buffered(1))
     return pl.pallas_call(
         pack_kernel,
-        out_shape=jax.ShapeDtypeStruct((2 * pack, 2 * HD), jnp.float32),
+        out_shape=jax.ShapeDtypeStruct((2, pack, 2 * HD), jnp.float32),
         grid_spec=pltpu.PrefetchScalarGridSpec(
             num_scalar_prefetch=2,
             grid=(pack // BQ,),
@@ -277,7 +282,7 @@
                 pl.BlockSpec((BQ, HD), lambda i, *_: (i, 0)),
                 pl.BlockSpec((pack, HD), lambda i, *_: (0, 0), **once),
             ],
-            out_specs=pl.BlockSpec((2 * BQ, 2 * HD), lambda i, *_: (i, 0)),
+            out_specs=pl.BlockSpec((2, BQ, 2 * HD), lambda i, *_: (0, i, 0)),
             scratch_shapes=[
                 pltpu.VMEM((2 * BQ, 2 * HD), jnp.bfloat16),
                 pltpu.VMEM((pack, 2 * HD), jnp.bfloat16),
@@ -294,27 +299,46 @@
     )(core, seen, arrived, arrived, other, q_side, k_side)
 
 
-def stem_kernel(core, q_ref, mine_ref, other_ref, part_ref, o_ref, qa, ka, va, top, acc):
-    stem = ka.shape[0]
+def stem_kernel(core, q_ref, mine_ref, other_ref, part_ref, o_ref, qa, top, acc):
+    stem = mine_ref.shape[0]
+    heads, rows = part_ref.shape[:2]
     lane = lax.broadcasted_iota(jnp.int32, (1, HD), 1)
+    first = core[0] == 0
+    side = jnp.broadcast_to(jnp.where(lane == SEGS, -1.0, 0.0).astype(jnp.bfloat16), (CK, HD))
+    ones = jnp.ones((CK, HD), jnp.bfloat16)
+
+    def keys(at):
+        here = pl.ds(at, CK)
+        return jnp.where(first, mine_ref[here, :], other_ref[here, :])
 
     @pl.when(pl.program_id(0) == 0)
     def _():
-        side = jnp.broadcast_to(jnp.where(lane == SEGS, -1.0, 0.0).astype(jnp.bfloat16), (stem, HD))
-        fill(core[0], mine_ref, other_ref, side, ka, va)
-        top[...] = longest(ka, stem)
-
-    q_rows = stacked(q_ref)
+        def body(step, most):
+            wide = keys(pl.multiple_of(step * CK, CK)).astype(jnp.float32)
+            norms = jnp.sum(wide * wide, axis=1, keepdims=True)
+            return jnp.maximum(most, jnp.max(norms, axis=0, keepdims=True))
+
+        most = lax.fori_loop(0, stem // CK, body, jnp.zeros((1, 1), jnp.float32))
+        top[...] = jnp.broadcast_to(jnp.sqrt(most), (8, HD))
+
+    q_rows = jnp.concatenate([q_ref[:, h * HD : h * HD + HD] for h in range(heads)], axis=0)
     qa[:, :HD] = q_rows
+
+    def scores(at):
+        wide = jnp.concatenate([keys(at), side], axis=1)
+        return lax.dot_general(qa[...], wide, NT, preferred_element_type=jnp.float32)
 
     def run(shift):
         qa[:, HD:] = jnp.where(lane == SEGS, shift, 0.0).astype(jnp.bfloat16)
         total = None
-        held = score(qa, ka, 0, CK)
+        held = scores(0)
         for at in range(0, stem, CK):
-            ahead = score(qa, ka, at + CK, CK) if at + CK < stem else None
+            ahead = scores(at + CK) if at + CK < stem else None
             weights = jnp.exp2(held * SCALE).astype(jnp.bfloat16)
-            part = jnp.dot(weights, va[at : at + CK, :], preferred_element_type=jnp.float32)
+            here = pl.ds(at, CK)
+            wide = jnp.where(first, other_ref[here, :], mine_ref[here, :])
+            wide = jnp.concatenate([wide, ones], axis=1)
+            part = jnp.dot(weights, wide, preferred_element_type=jnp.float32)
             total = part if total is None else total + part
             held = ahead
         acc[...] = total
@@ -322,14 +346,15 @@
     def finish():
         kept = qa[:, HD:].astype(jnp.float32)
         shift = jnp.sum(jnp.where(lane == SEGS, kept, 0.0), axis=1, keepdims=True)
-        before = part_ref[:, HD + 1 : HD + 2]
+        part = jnp.concatenate([part_ref[h] for h in range(heads)], axis=0)
+        before = part[:, HD + 1 : HD + 2]
         most = jnp.maximum(shift, before)
         new = jnp.exp2((shift - most) * SCALE)
         old = jnp.exp2((before - most) * SCALE)
-        total = acc[:, HD : HD + 1] * new + part_ref[:, HD : HD + 1] * old
-        mixed = ((acc[:, :HD] * new + part_ref[:, :HD] * old) / total).astype(jnp.bfloat16)
-        o_ref[:, :HD] = mixed[:BQ]
-        o_ref[:, HD:] = mixed[BQ:]
+        total = acc[:, HD : HD + 1] * new + part[:, HD : HD + 1] * old
+        mixed = (acc[:, :HD] * new + part[:, :HD] * old) / total
+        for h in range(heads):
+            o_ref[:, h * HD : h * HD + HD] = mixed[h * rows : h * rows + rows].astype(jnp.bfloat16)
 
     run(ceiling(q_rows, top[0:1, 0:1]))
     finish()
@@ -339,11 +364,11 @@
         qa[:, HD:] = jnp.zeros_like(q_rows)
 
         def body(step, most):
-            part = score(qa, ka, pl.multiple_of(step * BQ, BQ), BQ)
+            part = scores(pl.multiple_of(step * CK, CK))
             return jnp.maximum(most, jnp.max(part, axis=1, keepdims=True))
 
-        low = jnp.full((2 * BQ, 1), BARRED, jnp.float32)
-        run(lax.fori_loop(0, stem // BQ, body, low))
+        low = jnp.full((heads * rows, 1), BARRED, jnp.float32)
+        run(lax.fori_loop(0, stem // CK, body, low))
         finish()
 
 
@@ -361,20 +386,20 @@
                 pl.BlockSpec((BQ, 2 * HD), lambda i, *_: (i, 0)),
                 pl.BlockSpec((stem, HD), lambda i, *_: (0, 0), **once),
                 pl.BlockSpec((stem, HD), lambda i, *_: (0, 0), **once),
-                pl.BlockSpec((2 * BQ, 2 * HD), lambda i, *_: (i, 0)),
+                pl.BlockSpec((2, BQ, 2 * HD), lambda i, *_: (0, i, 0)),
             ],
             out_specs=pl.BlockSpec((BQ, 2 * HD), lambda i, *_: (i, 0)),
             scratch_shapes=[
                 pltpu.VMEM((2 * BQ, 2 * HD), jnp.bfloat16),
-                pltpu.VMEM((stem, 2 * HD), jnp.bfloat16),
-                pltpu.VMEM((stem, 2 * HD), jnp.bfloat16),
                 pltpu.VMEM((8, HD), jnp.float32),
                 pltpu.VMEM((2 * BQ, 2 * HD), jnp.float32),
             ],
         ),
         compiler_params=pltpu.CompilerParams(vmem_limit_bytes=ROOM),
         cost_estimate=pl.CostEstimate(
-            flops=8 * pack * stem * HD, bytes_accessed=8 << 20, transcendentals=2 * pack * stem
+            flops=8 * pack * stem * HD,
+            bytes_accessed=8 << 20,
+            transcendentals=2 * pack * stem,
         ),
         name="stem_part",
     )(core, arrived, mine, other, before)
@@ -422,19 +447,9 @@
     near, far = x ^ 1, 3 - x
     a_one = lax.ppermute(items[:, :half], "x", NEAR)
     b_one = lax.ppermute(items[:, half:], "x", FAR)
-    follow = stem_owner.reshape(4, 2)
-    for_far, for_near, for_us = follow[far], follow[near], follow[x]
-    plan = jnp.stack(
-        [for_far % 2, for_near % 2, (for_far // 2 == x) * 1, (for_near // 2 == x) * 1]
-    ).astype(jnp.int32)
-    a_send, b_send = relay(plan, items, a_one, b_one)
-    a_two = lax.ppermute(a_send, "x", FAR)
-    b_two = lax.ppermute(b_send, "x", NEAR)
-    chip = for_us // 2
-    source = jnp.where(chip == x, 0, jnp.where(chip == near, 1, jnp.where(chip == far, 2, 3)))
-    stems = settle(
-        jnp.stack([for_us % 2, source]).astype(jnp.int32), items, a_one, b_one, a_two, b_two
-    ).reshape(16, 2 * half, HD)
+    queries, seg_ids, seg_parent, _ = lax.optimization_barrier(
+        (queries, seg_ids, seg_parent, items)
+    )
 
     linked = ancestry(seg_parent[0])
     places = token_places(seg_ids[0], linked)
@@ -448,11 +463,25 @@
         jnp.concatenate([cosine, cosine], axis=1),
         jnp.concatenate([-sine, sine], axis=1),
     )
+
+    a_one, b_one, sent = lax.optimization_barrier((a_one, b_one, sent))
     crossed = lax.all_to_all(sent, "core", split_axis=0, concat_axis=0, tiled=True)
+    a_one, b_one, crossed = lax.optimization_barrier((a_one, b_one, crossed))
+
     arrived = lax.all_to_all(
         crossed.reshape(16, tok, 3 * HD), SEQ, split_axis=0, concat_axis=0, tiled=True
     ).reshape(pack_len, 3 * HD)
     pair = lax.ppermute(arrived[:, 2 * HD :], "core", FLIP)
+
+    follow = stem_owner.reshape(4, 2)
+    for_far, for_near, for_us = follow[far], follow[near], follow[x]
+    plan = jnp.stack(
+        [for_far % 2, for_near % 2, (for_far // 2 == x) * 1, (for_near // 2 == x) * 1]
+    ).astype(jnp.int32)
+    a_send, b_send = relay(plan, items, a_one, b_one)
+    a_two = lax.ppermute(a_send, "x", FAR)
+    b_two = lax.ppermute(b_send, "x", NEAR)
+    seg_ids, seg_parent, _ = lax.optimization_barrier((seg_ids, seg_parent, a_send))
 
     rows = jnp.concatenate([seg_ids[0], seg_parent[0]])
     rows = jnp.where(spot // KVH == core, rows, lax.ppermute(rows, "core", FLIP))
@@ -462,13 +491,19 @@
     q_side = jnp.dot(onehot, barred, precision=lax.Precision.HIGHEST).astype(jnp.bfloat16)
     k_side = jnp.where(jnp.arange(HD)[None, :] == SEGS, -1.0, onehot).astype(jnp.bfloat16)
     q_has = onehot.reshape(pack_len // BQ, BQ, HD).max(axis=1)[:, :SEGS]
-    k_has = onehot.reshape(pack_len // CK, CK, HD).max(axis=1)[:, :SEGS]
-    seen = (q_has @ reach @ k_has.T > 0.5).astype(jnp.int32)
-
-    before = pack_part(core_row, seen, arrived, pair, q_side, k_side)
+    seen = (q_has @ reach @ q_has.T > 0.5).astype(jnp.int32)
+
+    chip = for_us // 2
+    source = jnp.where(chip == x, 0, jnp.where(chip == near, 1, jnp.where(chip == far, 2, 3)))
+    stems = settle(
+        jnp.stack([for_us % 2, source]).astype(jnp.int32), items, a_one, b_one, a_two, b_two
+    ).reshape(16, 2 * half, HD)
     mine = lax.all_to_all(stems, SEQ, split_axis=0, concat_axis=0, tiled=True).reshape(STEM, HD)
+    arrived, pair, _ = lax.optimization_barrier((arrived, pair, stems))
+    partial = pack_part(core_row, seen, arrived, pair, q_side, k_side)
+    mine, partial = lax.optimization_barrier((mine, partial))
     other = lax.ppermute(mine, "core", FLIP)
-    mixed = stem_part(core_row, arrived, mine, other, before)
+    mixed = stem_part(core_row, arrived, mine, other, partial)
 
     back = lax.all_to_all(
         mixed.reshape(16, tok, 2 * HD), SEQ, split_axis=0, concat_axis=0, tiled=True

time: 170 us -> 152 us (0.89)
  waiting for transfers between devices: 48.7 us -> 38.8 us
  starting transfers between devices: 32.8 us -> 27.1 us
  other arithmetic: 6.64 us -> 4.25 us
  blocking collectives: 13.6 us -> 15.7 us
    all_to_all x1, waiting for transfers between devices: 0.01 us -> 12.3 us  [shards(): lax.all_to_all(crossed.reshape(16, tok, 3 * HD), SEQ, split_axis=0, conca...]
    all_to_all x1, waiting for transfers between devices: 8.19 us -> 0.01 us  [shards(): lax.all_to_all(stems, SEQ, split_axis=0, concat_axis=0, tiled=True)]
    ppermute x1, waiting for transfers between devices: 10.6 us -> 2.7 us  [shards(): a_two = lax.ppermute(a_send, 'x', FAR)]
    ppermute x1, waiting for transfers between devices: 7.4 us -> 0.49 us  [shards(): a_one = lax.ppermute(items[:, :half], 'x', NEAR)]
    ppermute x1, starting transfers between devices: 4.65 us -> 0.34 us  [shards(): other = lax.ppermute(mine, 'core', FLIP)]
    ppermute x1, waiting for transfers between devices: 0.01 us -> 2.58 us  [shards(): other = lax.ppermute(mine, 'core', FLIP)]
    all_to_all x1, starting transfers between devices: 3.65 us -> 6.03 us  [shards(): lax.all_to_all(mixed.reshape(16, tok, 2 * HD), SEQ, split_axis=0, concat_...]
    all_to_all x1, blocking collectives: 4.56 us -> 6.73 us  [shards(): lax.all_to_all(stem_kv[0], 'core', split_axis=0, concat_axis=0, tiled=True)]
  transfers between devices with their start and end apart: 11 -> 11, of which waited for: 7 -> 8; matrix products, arithmetic and copies ran while one was open for 4% -> 5% of each run, Pallas kernels for 14% -> 17%
where the time goes in v4:
time: 152 us; the launch traced here: 150 us
  Pallas kernels  57.2 us (38%)
  waiting for transfers between devices  38.8 us (26%)
  starting transfers between devices  27.1 us (18%)
  blocking collectives  15.7 us (10%)
  other arithmetic  4.25 us (3%)
  matrix products  3.6 us (2%)
  local copies, waits for them, and re-layouts  3.5 us (2%)
    pallas_call x1, Pallas kernels, stem_part(): pl.pallas_call(stem_kernel, out_shape=jax.ShapeDtypeStruct((pack, 2 * HD)...  26.8 us
    all_to_all x1, waiting for transfers between devices, shards(): lax.all_to_all(mixed.reshape(16, tok, 2 * HD), SEQ, split_axis=0, concat_...  16.8 us
    pallas_call x1, Pallas kernels, pack_part(): pl.pallas_call(pack_kernel, out_shape=jax.ShapeDtypeStruct((2, pack, 2 *...  14.9 us
    all_to_all x1, waiting for transfers between devices, shards(): lax.all_to_all(crossed.reshape(16, tok, 3 * HD), SEQ, split_axis=0, conca...  12.3 us
    all_to_all x1, blocking collectives, shards(): lax.all_to_all(sent, 'core', split_axis=0, concat_axis=0, tiled=True)  9.01 us
    all_to_all x1, starting transfers between devices, shards(): lax.all_to_all(crossed.reshape(16, tok, 3 * HD), SEQ, split_axis=0, conca...  7.77 us
    all_to_all x1, blocking collectives, shards(): lax.all_to_all(stem_kv[0], 'core', split_axis=0, concat_axis=0, tiled=True)  6.73 us
    all_to_all x1, starting transfers between devices, shards(): lax.all_to_all(mixed.reshape(16, tok, 2 * HD), SEQ, split_axis=0, concat_...  6.03 us
  transfers between devices with their start and end apart: 11, of which 8 were waited for; matrix products, arithmetic and copies ran while one was open for 5% of the time, Pallas kernels for 17%

profile of v4, /device:TPU:1, one launch (start us, length us, event | category | flops | bytes accessed | tf_op | source)
XLA Modules:
  0.0 150.4 jit_solution(8457699823732251370)
XLA Ops:
  0.0 6.7 %all_to_all.25.a_own.b_own.own = bf16[2,256,1024]{2,1,0:T(8,128)(2,1)S(1)} all-to-all(bf16[2,256,1024]{2,1,0:T(8,128)(2,1)} %bitcast.40), channel_id=1, replica_groups=mesh['x'=4,'core'=2,'z'=4,'y'=4] {'core'}, dimensions={0} | all-to-all | bytes 2097152 | tf_op jit(solution)/shard_map/all_to_all | solution.py:445
  6.8 1.4 collective-permute-start
  8.2 1.8 %collective-permute-start.1 = (bf16[2,128,1024]{2,1,0:T(8,128)(2,1)S(1)}, bf16[2,128,1024]{2,1,0:T(8,128)(2,1)S(1)}, u32[]{:S(2)}, u32[]{:S(2)}) collective-permute-start(bf16[2,128,1024]{2,1,0:T(8,128)(2,1)S(1)} %get-tuple-element.45), channel_id=1, source_target_pairs={{0,96},{96,0},{32,64},{64,32},{1,97},{97,1},{33,65},{65,33},{2,98}... | collective-permute-start | bytes 1572872 | tf_op jit(solution)/shard_map/ppermute | solution.py:449
  11.7 0.8 pad_maximum_fusion
  12.5 5.9 %turn.1 = bf16[2,8,128,384]{3,2,1,0:T(8,128)(2,1)} custom-call(bf16[128,4096]{1,0:T(8,128)(2,1)} %bitcast.39, bf16[128,1024]{1,0:T(8,128)(2,1)} %bitcast.44, bf16[128,1024]{1,0:T(8,128)(2,1)} %bitcast.45, f32[128,128]{1,0:T(8,128)} %get-tuple-element.60.cos_ref, f32[128,128]{1,0:T(8,128)} %get-tuple-element.61.sin_ref), custom_call_target="tpu_custom_call" | custom-call | tf_op jit(solution)/shard_map/turn/pallas_call | solution.py:91
  18.4 0.6 pad_add_fusion.2.plan
  18.9 0.6 pad_add_fusion.1.plan
  20.0 2.2 %collective-permute-done.1.b_got.b_one = bf16[2,128,1024]{2,1,0:T(8,128)(2,1)S(1)} collective-permute-done((bf16[2,128,1024]{2,1,0:T(8,128)(2,1)S(1)}, bf16[2,128,1024]{2,1,0:T(8,128)(2,1)S(1)}, u32[]{:S(2)}, u32[]{:S(2)}) %collective-permute-start.1) | collective-permute-done | bytes 524320 | tf_op jit(solution)/shard_map/ppermute | solution.py:449
  22.2 9.0 %all_to_all.26 = bf16[2,8,128,384]{3,2,1,0:T(8,128)(2,1)} all-to-all(bf16[2,8,128,384]{3,2,1,0:T(8,128)(2,1)} %turn.1), channel_id=1, replica_groups=mesh['x'=4,'core'=2,'z'=4,'y'=4] {'core'}, dimensions={0} | all-to-all | bytes 3145728 | tf_op jit(solution)/shard_map/all_to_all | solution.py:468
  31.2 3.0 %relay.1 = (bf16[2,128,1024]{2,1,0:T(8,128)(2,1)}, bf16[2,128,1024]{2,1,0:T(8,128)(2,1)}) custom-call(s32[4,2]{1,0:T(4,128)} %pad_add_fusion.1.plan, bf16[2,256,1024]{2,1,0:T(8,128)(2,1)} %copy-done, bf16[2,256,1024]{2,1,0:T(8,128)(2,1)} %copy-done, bf16[2,128,1024]{2,1,0:T(8,128)(2,1)} %copy-done.3, bf16[2,128,1024]{2,1,0:T(8,128)(2,1)} %copy-done.4), custom_call_target="tpu_custom_call" | custom-call | tf_op jit(solution)/shard_map/relay/pallas_call | solution.py:116
  34.7 1.8 %collective-permute-start.3 = (bf16[2,128,1024]{2,1,0:T(8,128)(2,1)}, bf16[2,128,1024]{2,1,0:T(8,128)(2,1)S(1)}, u32[]{:S(2)}, u32[]{:S(2)}) collective-permute-start(bf16[2,128,1024]{2,1,0:T(8,128)(2,1)} %get-tuple-element.31), channel_id=1, source_target_pairs={{0,96},{96,0},{32,64},{64,32},{1,97},{97,1},{33,65},{65,33},{2,98}... | collective-permute-start | bytes 1572872 | tf_op jit(solution)/shard_map/ppermute | solution.py:482
  36.5 7.8 %all-to-all-start.2 = ((bf16[16,128,384]{2,1,0:T(8,128)(2,1)}), bf16[16,128,384]{2,1,0:T(8,128)(2,1)S(1)}, u32[]{:S(2)}, u32[]{:S(2)}) async-start(bf16[16,128,384]{2,1,0:T(8,128)(2,1)} %bitcast.8), calls=%async_computation.2 | async-start | bytes 3145728 | tf_op jit(solution)/shard_map/all_to_all | solution.py:471
  45.2 1.5 %convolution_convert_fusion.qb_ref = bf16[2048,128]{1,0:T(8,128)(2,1)} fusion(s32[2048]{0:T(1024)S(1)} %slice.27, f32[16,16]{1,0:T(8,128)S(1)} %get-tuple-element.58), kind=kOutput, calls=%fused_computation | convolution fusion | flops 403177472 | bytes 533504 | tf_op jit(solution)/shard_map/dot_general | solution.py:491
  46.8 2.7 %collective-permute-done.3.a_two = bf16[2,128,1024]{2,1,0:T(8,128)(2,1)S(1)} collective-permute-done((bf16[2,128,1024]{2,1,0:T(8,128)(2,1)}, bf16[2,128,1024]{2,1,0:T(8,128)(2,1)S(1)}, u32[]{:S(2)}, u32[]{:S(2)}) %collective-permute-start.3) | collective-permute-done | bytes 524320 | tf_op jit(solution)/shard_map/ppermute | solution.py:482
  49.8 0.5 copy-done.6
  50.3 0.8 copy-done.7
  51.1 4.6 %settle.1 = bf16[2,8,256,128]{3,2,1,0:T(8,128)(2,1)} custom-call(s32[2,2]{1,0:T(2,128)} %pad_add_fusion.2.plan, bf16[2,256,1024]{2,1,0:T(8,128)(2,1)} %copy-done, bf16[2,128,1024]{2,1,0:T(8,128)(2,1)} %copy-done.3, bf16[2,128,1024]{2,1,0:T(8,128)(2,1)} %copy-done.4, bf16[2,128,1024]{2,1,0:T(8,128)(2,1)} %copy-done.6, bf16[2,128,1024]{2,1,0:T(8,128)(2,1)} %copy-done.7), custom_call_target="tpu_custom_call" | custom-call | tf_op jit(solution)/shard_map/settle/pallas_call | solution.py:149
  55.7 12.3 %all-to-all-done.2 = bf16[16,128,384]{2,1,0:T(8,128)(2,1)S(1)} async-done(((bf16[16,128,384]{2,1,0:T(8,128)(2,1)}), bf16[16,128,384]{2,1,0:T(8,128)(2,1)S(1)}, u32[]{:S(2)}, u32[]{:S(2)}) %all-to-all-start.2) | async-done | bytes 1572896 | tf_op jit(solution)/shard_map/all_to_all | solution.py:471
  68.0 4.2 %all-to-all-start.3 = ((bf16[16,256,128]{2,1,0:T(8,128)(2,1)}), bf16[16,256,128]{2,1,0:T(8,128)(2,1)S(1)}, u32[]{:S(2)}, u32[]{:S(2)}) async-start(bf16[16,256,128]{2,1,0:T(8,128)(2,1)} %bitcast.34), calls=%async_computation.3 | async-start | bytes 2097152 | tf_op jit(solution)/shard_map/all_to_all | solution.py:501
  72.3 1.4 collective-permute-start.2
  73.7 0.8 fusion.8.seen
  74.5 1.1 select_convert_fusion.kb_ref
  75.6 14.9 %pack_part.1.part_ref = f32[2,2048,256]{2,1,0:T(8,128)} custom-call(s32[1]{0:T(128)} %bitcast.core, s32[4,4]{1,0:T(4,128)} %fusion.8.seen, bf16[2048,384]{1,0:T(8,128)(2,1)} %bitcast.36, bf16[2048,384]{1,0:T(8,128)(2,1)} %bitcast.37, bf16[2048,128]{1,0:T(8,128)(2,1)} %collective-permute-done.2.other_ref, bf16[2048,128]{1,0:T(8,128)(2,1)} %convolution_convert_fusion.qb_ref, ...), custom_call_target="tpu_custom_call" | custom-call | flops 4294967296 | bytes 8388608 | tf_op jit(solution)/shard_map/pack_part/pallas_call | solution.py:272
  90.9 2.6 %collective-permute-done.6.other_ref = bf16[4096,128]{1,0:T(8,128)(2,1)S(1)} collective-permute-done((bf16[4096,128]{1,0:T(8,128)(2,1)S(1)}, bf16[4096,128]{1,0:T(8,128)(2,1)S(1)}, u32[]{:S(2)}, u32[]{:S(2)}) %collective-permute-start.6) | collective-permute-done | bytes 1048608 | tf_op jit(solution)/shard_map/ppermute | solution.py:505
  93.5 1.0 copy-done.13
  94.4 26.8 %stem_part.1 = bf16[2048,256]{1,0:T(8,128)(2,1)} custom-call(s32[1]{0:T(128)} %bitcast.core, bf16[2048,384]{1,0:T(8,128)(2,1)} %bitcast.38, bf16[4096,128]{1,0:T(8,128)(2,1)} %bitcast.42, bf16[4096,128]{1,0:T(8,128)(2,1)} %copy-done.13, f32[2,2048,256]{2,1,0:T(8,128)} %pack_part.1.part_ref), custom_call_target="tpu_custom_call" | custom-call | flops 8589934592 | bytes 8388608 | tf_op jit(solution)/shard_map/stem_part/pallas_call | solution.py:379
  121.2 6.0 %all-to-all-start.4 = ((bf16[16,128,256]{2,1,0:T(8,128)(2,1)}), bf16[16,128,256]{2,1,0:T(8,128)(2,1)S(1)}, u32[]{:S(2)}, u32[]{:S(2)}) async-start(bf16[16,128,256]{2,1,0:T(8,128)(2,1)} %bitcast.43), calls=%async_computation.4 | async-start | bytes 2097152 | tf_op jit(solution)/shard_map/all_to_all | solution.py:508
  127.3 16.8 %all-to-all-done.4 = bf16[16,128,256]{2,1,0:T(8,128)(2,1)S(1)} async-done(((bf16[16,128,256]{2,1,0:T(8,128)(2,1)}), bf16[16,128,256]{2,1,0:T(8,128)(2,1)S(1)}, u32[]{:S(2)}, u32[]{:S(2)}) %all-to-all-start.4) | async-done | bytes 1048608 | tf_op jit(solution)/shard_map/all_to_all | solution.py:508
  144.1 1.9 %collective-permute-start.7 = (bf16[8,128,256]{2,1,0:T(8,128)(2,1)S(1)}, bf16[8,128,256]{2,1,0:T(8,128)(2,1)S(1)}, u32[]{:S(2)}, u32[]{:S(2)}) collective-permute-start(bf16[8,128,256]{2,1,0:T(8,128)(2,1)S(1)} %dynamic-slice_bitcast_fusion), channel_id=1, source_target_pairs={{0,16},{16,0},{1,17},{17,1},{2,18},{18,2},{3,19},{19,3},{4,20},{20... | collective-permute-start | bytes 1572872 | tf_op jit(solution)/shard_map/ppermute | solution.py:512
  146.0 1.5 %collective-permute-done.7.other_ref = bf16[8,128,256]{2,1,0:T(8,128)(2,1)S(1)} collective-permute-done((bf16[8,128,256]{2,1,0:T(8,128)(2,1)S(1)}, bf16[8,128,256]{2,1,0:T(8,128)(2,1)S(1)}, u32[]{:S(2)}, u32[]{:S(2)}) %collective-permute-start.7) | collective-permute-done | bytes 524320 | tf_op jit(solution)/shard_map/ppermute | solution.py:512
  147.5 0.8 copy-done.8
  148.4 2.0 %gather.1 = bf16[128,4096]{1,0:T(8,128)(2,1)} custom-call(s32[1]{0:T(128)} %bitcast.core, bf16[2,8,128,256]{3,2,1,0:T(8,128)(2,1)} %bitcast.33, bf16[8,128,256]{2,1,0:T(8,128)(2,1)} %copy-done.8), custom_call_target="tpu_custom_call" | custom-call | tf_op jit(solution)/shard_map/gather/pallas_call | solution.py:421
  (61 shorter events, 4.4 us)
Async XLA Ops:
  6.7 11.6 %copy-start = (bf16[2,256,1024]{2,1,0:T(8,128)(2,1)}, bf16[2,256,1024]{2,1,0:T(8,128)(2,1)S(1)}, u32[]{:S(2)}) copy-start(bf16[2,256,1024]{2,1,0:T(8,128)(2,1)S(1)} %all_to_all.25.a_own.b_own.own) | copy-start | bytes 3145732
  6.7 3.3 %copy-start.9 = (s32[1,2048]{1,0:T(1,128)S(1)}, s32[1,2048]{1,0:T(1,128)}, u32[]{:S(2)}) copy-start(s32[1,2048]{1,0:T(1,128)} %param.12) | copy-start | bytes 24580
  6.7 3.4 %copy-start.10 = (s32[1,16]{1,0:T(1,128)S(1)}, s32[1,16]{1,0:T(1,128)}, u32[]{:S(2)}) copy-start(s32[1,16]{1,0:T(1,128)} %param.13) | copy-start | bytes 196
  6.7 4.2 %copy-start.12 = (s32[8]{0:T(128)S(1)}, s32[8]{0:T(128)}, u32[]{:S(2)}) copy-start(s32[8]{0:T(128)} %param.14) | copy-start | bytes 100
  6.7 4.6 %copy-start.11 = (f32[64]{0:T(128)S(1)}, f32[64]{0:T(128)}, u32[]{:S(2)}) copy-start(f32[64]{0:T(128)} %constant.121.clone) | copy-start | bytes 772
  6.8 13.2 %collective-permute-start = (bf16[2,128,1024]{2,1,0:T(8,128)(2,1)S(1)}, bf16[2,128,1024]{2,1,0:T(8,128)(2,1)S(1)}, u32[]{:S(2)}, u32[]{:S(2)}) collective-permute-start(bf16[2,128,1024]{2,1,0:T(8,128)(2,1)S(1)} %get-tuple-element.46), channel_id=1, source_target_pairs={{0,32},{32,0},{64,96},{96,64},{1,33},{33,1},{65,97},{97,65},{2,34}... | collective-permute-start | bytes 1572872 | tf_op jit(solution)/shard_map/ppermute | solution.py:448
  8.2 14.0 %collective-permute-start.1 = (bf16[2,128,1024]{2,1,0:T(8,128)(2,1)S(1)}, bf16[2,128,1024]{2,1,0:T(8,128)(2,1)S(1)}, u32[]{:S(2)}, u32[]{:S(2)}) collective-permute-start(bf16[2,128,1024]{2,1,0:T(8,128)(2,1)S(1)} %get-tuple-element.45), channel_id=1, source_target_pairs={{0,96},{96,0},{32,64},{64,32},{1,97},{97,1},{33,65},{65,33},{2,98}... | collective-permute-start | bytes 1572872 | tf_op jit(solution)/shard_map/ppermute | solution.py:449
  20.0 11.2 %copy-start.3 = (bf16[2,128,1024]{2,1,0:T(8,128)(2,1)}, bf16[2,128,1024]{2,1,0:T(8,128)(2,1)S(1)}, u32[]{:S(2)}) copy-start(bf16[2,128,1024]{2,1,0:T(8,128)(2,1)S(1)} %collective-permute-done.a_got.a_one) | copy-start | bytes 1572868
  22.2 9.0 %copy-start.4 = (bf16[2,128,1024]{2,1,0:T(8,128)(2,1)}, bf16[2,128,1024]{2,1,0:T(8,128)(2,1)S(1)}, u32[]{:S(2)}) copy-start(bf16[2,128,1024]{2,1,0:T(8,128)(2,1)S(1)} %collective-permute-done.1.b_got.b_one) | copy-start | bytes 1572868
  34.2 10.1 %collective-permute-start.5 = (s32[2064]{0:T(1024)S(1)}, s32[2064]{0:T(1024)S(1)}, u32[]{:S(2)}, u32[]{:S(2)}) collective-permute-start(s32[2064]{0:T(1024)S(1)} %pad_add_fusion), channel_id=1, source_target_pairs={{0,16},{16,0},{1,17},{17,1},{2,18},{18,2},{3,19},{19,3},{4,20},{20... | collective-permute-start | bytes 24776 | tf_op jit(solution)/shard_map/ppermute | solution.py:487
  34.7 14.8 %collective-permute-start.3 = (bf16[2,128,1024]{2,1,0:T(8,128)(2,1)}, bf16[2,128,1024]{2,1,0:T(8,128)(2,1)S(1)}, u32[]{:S(2)}, u32[]{:S(2)}) collective-permute-start(bf16[2,128,1024]{2,1,0:T(8,128)(2,1)} %get-tuple-element.31), channel_id=1, source_target_pairs={{0,96},{96,0},{32,64},{64,32},{1,97},{97,1},{33,65},{65,33},{2,98}... | collective-permute-start | bytes 1572872 | tf_op jit(solution)/shard_map/ppermute | solution.py:482
  36.5 13.3 %collective-permute-start.4 = (bf16[2,128,1024]{2,1,0:T(8,128)(2,1)}, bf16[2,128,1024]{2,1,0:T(8,128)(2,1)S(1)}, u32[]{:S(2)}, u32[]{:S(2)}) collective-permute-start(bf16[2,128,1024]{2,1,0:T(8,128)(2,1)} %get-tuple-element.32), channel_id=1, source_target_pairs={{0,32},{32,0},{64,96},{96,64},{1,33},{33,1},{65,97},{97,65},{2,34}... | collective-permute-start | bytes 1572872 | tf_op jit(solution)/shard_map/ppermute | solution.py:483
  36.5 31.5 %all-to-all-start.2 = ((bf16[16,128,384]{2,1,0:T(8,128)(2,1)}), bf16[16,128,384]{2,1,0:T(8,128)(2,1)S(1)}, u32[]{:S(2)}, u32[]{:S(2)}) async-start(bf16[16,128,384]{2,1,0:T(8,128)(2,1)} %bitcast.8), calls=%async_computation.2 | async-start | bytes 3145728 | tf_op jit(solution)/shard_map/all_to_all | solution.py:471
  49.5 0.8 copy-start.6
  50.3 0.8 copy-start.7
  68.0 4.2 %copy-start.2 = (bf16[16,128,384]{2,1,0:T(8,128)(2,1)}, bf16[16,128,384]{2,1,0:T(8,128)(2,1)S(1)}, u32[]{:S(2)}) copy-start(bf16[16,128,384]{2,1,0:T(8,128)(2,1)S(1)} %all-to-all-done.2) | copy-start | bytes 4718596
  68.0 22.5 %all-to-all-start.3 = ((bf16[16,256,128]{2,1,0:T(8,128)(2,1)}), bf16[16,256,128]{2,1,0:T(8,128)(2,1)S(1)}, u32[]{:S(2)}, u32[]{:S(2)}) async-start(bf16[16,256,128]{2,1,0:T(8,128)(2,1)} %bitcast.34), calls=%async_computation.3 | async-start | bytes 2097152 | tf_op jit(solution)/shard_map/all_to_all | solution.py:501
  72.3 3.4 %collective-permute-start.2 = (bf16[2048,128]{1,0:T(8,128)(2,1)S(1)}, bf16[2048,128]{1,0:T(8,128)(2,1)}, u32[]{:S(2)}, u32[]{:S(2)}) collective-permute-start(bf16[2048,128]{1,0:T(8,128)(2,1)S(1)} %slice.26), channel_id=1, source_target_pairs={{0,16},{16,0},{1,17},{17,1},{2,18},{18,2},{3,19},{19,3},{4,20},{20... | collective-permute-start | bytes 1572872 | tf_op jit(solution)/shard_map/ppermute | solution.py:474
  90.5 2.9 %copy-start.5 = (bf16[16,256,128]{2,1,0:T(8,128)(2,1)}, bf16[16,256,128]{2,1,0:T(8,128)(2,1)S(1)}, u32[]{:S(2)}) copy-start(bf16[16,256,128]{2,1,0:T(8,128)(2,1)S(1)} %all-to-all-done.3) | copy-start | bytes 3145732
  90.5 2.9 %collective-permute-start.6 = (bf16[4096,128]{1,0:T(8,128)(2,1)S(1)}, bf16[4096,128]{1,0:T(8,128)(2,1)S(1)}, u32[]{:S(2)}, u32[]{:S(2)}) collective-permute-start(bf16[4096,128]{1,0:T(8,128)(2,1)S(1)} %bitcast.41), channel_id=1, source_target_pairs={{0,16},{16,0},{1,17},{17,1},{2,18},{18,2},{3,19},{19,3},{4,20},{20... | collective-permute-start | bytes 3145736 | tf_op jit(solution)/shard_map/ppermute | solution.py:505
  93.5 1.0 copy-start.13
  121.2 22.8 %all-to-all-start.4 = ((bf16[16,128,256]{2,1,0:T(8,128)(2,1)}), bf16[16,128,256]{2,1,0:T(8,128)(2,1)S(1)}, u32[]{:S(2)}, u32[]{:S(2)}) async-start(bf16[16,128,256]{2,1,0:T(8,128)(2,1)} %bitcast.43), calls=%async_computation.4 | async-start | bytes 2097152 | tf_op jit(solution)/shard_map/all_to_all | solution.py:508
  144.0 3.5 %copy-start.1 = (bf16[16,128,256]{2,1,0:T(8,128)(2,1)}, bf16[16,128,256]{2,1,0:T(8,128)(2,1)S(1)}, u32[]{:S(2)}) copy-start(bf16[16,128,256]{2,1,0:T(8,128)(2,1)S(1)} %all-to-all-done.4) | copy-start | bytes 3145732
  144.1 3.5 %collective-permute-start.7 = (bf16[8,128,256]{2,1,0:T(8,128)(2,1)S(1)}, bf16[8,128,256]{2,1,0:T(8,128)(2,1)S(1)}, u32[]{:S(2)}, u32[]{:S(2)}) collective-permute-start(bf16[8,128,256]{2,1,0:T(8,128)(2,1)S(1)} %dynamic-slice_bitcast_fusion), channel_id=1, source_target_pairs={{0,16},{16,0},{1,17},{17,1},{2,18},{18,2},{3,19},{19,3},{4,20},{20... | collective-permute-start | bytes 1572872 | tf_op jit(solution)/shard_map/ppermute | solution.py:512
  147.5 0.8 copy-start.8

commit v5 on v4

--- a/solution.py
+++ b/solution.py
@@ -104,67 +104,91 @@
     )(q, k, v, cosine, sine)
 
 
-def relay_kernel(plan, a_own, b_own, a_got, b_got, a_out, b_out):
-    item = pl.program_id(0)
-    a_out[...] = jnp.where(plan[2, item] > 0, a_own[...], a_got[...])
-    b_out[...] = jnp.where(plan[3, item] > 0, b_own[...], b_got[...])
-
-
-def relay(plan, items, a_got, b_got):
-    rows, width = a_got.shape[1:]
-    block = (1, rows, width)
+def held_at(x, core, group):
+    chip = lax.div(group, 2)
+    here = chip == x
+    other = jnp.where(core == 0, NEAR_OF(x), FAR_OF(x))
+    own = jnp.where(here, 0, 1 + core)
+    mate = jnp.where(here, 3, 4)
+    found = jnp.where(lax.rem(group, 2) == core, own, mate)
+    return jnp.where(here | (chip == other), found, 5)
+
+
+def NEAR_OF(x):
+    return x + 1 - 2 * lax.rem(x, 2)
+
+
+def FAR_OF(x):
+    return 3 - x
+
+
+def swap_kernel(spot, own, a_one, b_one, out, sems):
+    core = spot[1]
+    pltpu.make_async_copy(own.at[1 - core], out.at[0], sems.at[0]).start()
+
+    @pl.when(core == 0)
+    def _():
+        pltpu.make_async_copy(b_one, out.at[1], sems.at[1]).start()
+
+    @pl.when(core != 0)
+    def _():
+        pltpu.make_async_copy(a_one, out.at[1], sems.at[1]).start()
+
+    for item in range(2):
+        pltpu.make_async_copy(b_one, out.at[item], sems.at[item]).wait()
+
+
+def relay_kernel(spot, owner, own, a_one, b_one, mate, out, sems):
+    x, core = spot[0], spot[1]
+    to = jnp.where(core == 0, FAR_OF(x), NEAR_OF(x))
+    for item in range(2):
+        code = held_at(x, core, owner[2 * to + item])
+        sources = (own.at[core], a_one, b_one, mate.at[0], mate.at[1])
+        for place, source in enumerate(sources):
+            chosen = code == place if place else (code == 0) | (code == 5)
+
+            @pl.when(chosen)
+            def _(source=source):
+                pltpu.make_async_copy(source, out.at[item], sems.at[item]).start()
+
+    for item in range(2):
+        pltpu.make_async_copy(a_one, out.at[item], sems.at[item]).wait()
+
+
+def settle_kernel(spot, owner, own, a_one, b_one, mate, two, out, sems):
+    x, core = spot[0], spot[1]
+    for pack in range(2):
+        code = held_at(x, core, owner[2 * x + pack])
+        sources = (own.at[core], a_one, b_one, mate.at[0], mate.at[1], two.at[pack])
+        for place, source in enumerate(sources):
+
+            @pl.when(code == place)
+            def _(source=source):
+                for e in range(KVH):
+                    pltpu.make_async_copy(
+                        source.at[:, pl.ds(e * HD, HD)], out.at[pack, e], sems.at[pack, e]
+                    ).start()
+
+    for pack in range(2):
+        for e in range(KVH):
+            pltpu.make_async_copy(
+                a_one.at[:, pl.ds(0, HD)], out.at[pack, e], sems.at[pack, e]
+            ).wait()
+
+
+def moved(kernel, shape, sems, scalars, arrays):
     return pl.pallas_call(
-        relay_kernel,
-        out_shape=[jax.ShapeDtypeStruct((2, rows, width), jnp.bfloat16)] * 2,
+        kernel,
+        out_shape=jax.ShapeDtypeStruct(shape, jnp.bfloat16),
         grid_spec=pltpu.PrefetchScalarGridSpec(
-            num_scalar_prefetch=1,
-            grid=(2,),
-            in_specs=[
-                pl.BlockSpec(block, lambda i, plan: (plan[0, i], 0, 0)),
-                pl.BlockSpec(block, lambda i, plan: (plan[1, i], 1, 0)),
-                pl.BlockSpec(block, lambda i, plan: (plan[0, i], 0, 0)),
-                pl.BlockSpec(block, lambda i, plan: (plan[1, i], 0, 0)),
-            ],
-            out_specs=[pl.BlockSpec(block, lambda i, plan: (i, 0, 0))] * 2,
+            num_scalar_prefetch=len(scalars),
+            grid=(1,),
+            in_specs=[pl.BlockSpec(memory_space=pl.ANY)] * len(arrays),
+            out_specs=pl.BlockSpec(shape, lambda *_: (0,) * len(shape)),
+            scratch_shapes=[pltpu.SemaphoreType.DMA(sems)],
         ),
-        name="relay",
-    )(plan, items, items, a_got, b_got)
-
-
-def settle_kernel(plan, own, a_one, b_one, a_two, b_two, out):
-    pack = pl.program_id(0)
-    half = a_one.shape[1]
-    mine = plan[1, pack] == 0
-    a = jnp.where(mine, own[0, :half], jnp.where(plan[1, pack] == 1, a_one[0], a_two[0]))
-    b = jnp.where(mine, own[0, half:], jnp.where(plan[1, pack] == 2, b_one[0], b_two[0]))
-    for e in range(out.shape[1]):
-        out[0, e, :half] = a[:, e * HD : e * HD + HD]
-        out[0, e, half:] = b[:, e * HD : e * HD + HD]
-
-
-def settle(plan, items, a_one, b_one, a_two, b_two):
-    rows, width = a_one.shape[1:]
-    part = width // 2
-    block = (1, rows, part)
-    return pl.pallas_call(
-        settle_kernel,
-        out_shape=jax.ShapeDtypeStruct((2, KVH, 2 * rows, HD), jnp.bfloat16),
-        grid_spec=pltpu.PrefetchScalarGridSpec(
-            num_scalar_prefetch=1,
-            grid=(2, 2),
-            in_specs=[
-                pl.BlockSpec((1, 2 * rows, part), lambda i, j, plan: (plan[0, i], 0, j)),
-                pl.BlockSpec(block, lambda i, j, plan: (plan[0, i], 0, j)),
-                pl.BlockSpec(block, lambda i, j, plan: (plan[0, i], 0, j)),
-                pl.BlockSpec(block, lambda i, j, plan: (i, 0, j)),
-                pl.BlockSpec(block, lambda i, j, plan: (i, 0, j)),
-            ],
-            out_specs=pl.BlockSpec(
-                (1, KVH // 2, 2 * rows, HD), lambda i, j, plan: (i, j, 0, 0)
-            ),
-        ),
-        name="settle",
-    )(plan, items, a_one, b_one, a_two, b_two)
+        name=kernel.__name__,
+    )(*scalars, *arrays)
 
 
 def longest(ref, rows):
@@ -441,15 +465,11 @@
     spot = lax.axis_index(SEQ)
     pack_len = tok * 16
     core_row = core[None].astype(jnp.int32)
-
-    items = lax.all_to_all(stem_kv[0], "core", split_axis=0, concat_axis=0, tiled=True)
-    half = items.shape[1] // 2
-    near, far = x ^ 1, 3 - x
-    a_one = lax.ppermute(items[:, :half], "x", NEAR)
-    b_one = lax.ppermute(items[:, half:], "x", FAR)
-    queries, seg_ids, seg_parent, _ = lax.optimization_barrier(
-        (queries, seg_ids, seg_parent, items)
-    )
+    here = jnp.stack([x, core]).astype(jnp.int32)
+
+    own = stem_kv[0]
+    a_one = lax.ppermute(own[0], "x", NEAR)
+    b_one = lax.ppermute(own[1], "x", FAR)
 
     linked = ancestry(seg_parent[0])
     places = token_places(seg_ids[0], linked)
@@ -465,23 +485,27 @@
     )
 
     a_one, b_one, sent = lax.optimization_barrier((a_one, b_one, sent))
+
+    passed = moved(swap_kernel, own.shape, (2,), (here,), (own, a_one, b_one))
+    mate = lax.ppermute(passed, "core", FLIP)
+    sent, passed = lax.optimization_barrier((sent, passed))
     crossed = lax.all_to_all(sent, "core", split_axis=0, concat_axis=0, tiled=True)
-    a_one, b_one, crossed = lax.optimization_barrier((a_one, b_one, crossed))
+    mate, crossed = lax.optimization_barrier((mate, crossed))
 
     arrived = lax.all_to_all(
         crossed.reshape(16, tok, 3 * HD), SEQ, split_axis=0, concat_axis=0, tiled=True
     ).reshape(pack_len, 3 * HD)
     pair = lax.ppermute(arrived[:, 2 * HD :], "core", FLIP)
 
-    follow = stem_owner.reshape(4, 2)
-    for_far, for_near, for_us = follow[far], follow[near], follow[x]
-    plan = jnp.stack(
-        [for_far % 2, for_near % 2, (for_far // 2 == x) * 1, (for_near // 2 == x) * 1]
-    ).astype(jnp.int32)
-    a_send, b_send = relay(plan, items, a_one, b_one)
-    a_two = lax.ppermute(a_send, "x", FAR)
-    b_two = lax.ppermute(b_send, "x", NEAR)
-    seg_ids, seg_parent, _ = lax.optimization_barrier((seg_ids, seg_parent, a_send))
+    wanted = moved(
+        relay_kernel, own.shape, (2,), (here, stem_owner), (own, a_one, b_one, mate)
+    )
+    two = lax.ppermute(
+        wanted,
+        ("x", "core"),
+        [(2 * i, 2 * j) for i, j in FAR] + [(2 * i + 1, 2 * j + 1) for i, j in NEAR],
+    )
+    seg_ids, seg_parent, _ = lax.optimization_barrier((seg_ids, seg_parent, wanted))
 
     rows = jnp.concatenate([seg_ids[0], seg_parent[0]])
     rows = jnp.where(spot // KVH == core, rows, lax.ppermute(rows, "core", FLIP))
@@ -493,11 +517,13 @@
     q_has = onehot.reshape(pack_len // BQ, BQ, HD).max(axis=1)[:, :SEGS]
     seen = (q_has @ reach @ q_has.T > 0.5).astype(jnp.int32)
 
-    chip = for_us // 2
-    source = jnp.where(chip == x, 0, jnp.where(chip == near, 1, jnp.where(chip == far, 2, 3)))
-    stems = settle(
-        jnp.stack([for_us % 2, source]).astype(jnp.int32), items, a_one, b_one, a_two, b_two
-    ).reshape(16, 2 * half, HD)
+    stems = moved(
+        settle_kernel,
+        (2, KVH, own.shape[1], HD),
+        (2, KVH),
+        (here, stem_owner),
+        (own, a_one, b_one, mate, two),
+    ).reshape(16, own.shape[1], HD)
     mine = lax.all_to_all(stems, SEQ, split_axis=0, concat_axis=0, tiled=True).reshape(STEM, HD)
     arrived, pair, _ = lax.optimization_barrier((arrived, pair, stems))
     partial = pack_part(core_row, seen, arrived, pair, q_side, k_side)

time: 152 us -> 150 us (0.987)
  the two profiles are of different devices: /device:TPU:1 before, /device:TPU:3 now
where the time goes in v5:
time: 150 us; the launch traced here: 149 us
  Pallas kernels  58.6 us (39%)
  waiting for transfers between devices  42.9 us (29%)
  starting transfers between devices  28.1 us (19%)
  local copies, waits for them, and re-layouts  6.09 us (4%)
  blocking collectives  5.48 us (4%)
  other arithmetic  3.7 us (2%)
  matrix products  3.6 us (2%)
    pallas_call x1, Pallas kernels, stem_part(): pl.pallas_call(stem_kernel, out_shape=jax.ShapeDtypeStruct((pack, 2 * HD)...  26.8 us
    all_to_all x1, waiting for transfers between devices, shards(): lax.all_to_all(crossed.reshape(16, tok, 3 * HD), SEQ, split_axis=0, conca...  17.4 us
    all_to_all x1, waiting for transfers between devices, shards(): lax.all_to_all(mixed.reshape(16, tok, 2 * HD), SEQ, split_axis=0, concat_...  16.8 us
    pallas_call x1, Pallas kernels, pack_part(): pl.pallas_call(pack_kernel, out_shape=jax.ShapeDtypeStruct((2, pack, 2 *...  14.9 us
    pallas_call x3, Pallas kernels, moved(): pl.pallas_call(kernel, out_shape=jax.ShapeDtypeStruct(shape, jnp.bfloat16...  9 us
    all_to_all x1, starting transfers between devices, shards(): lax.all_to_all(crossed.reshape(16, tok, 3 * HD), SEQ, split_axis=0, conca...  7.77 us
    all_to_all x1, starting transfers between devices, shards(): lax.all_to_all(mixed.reshape(16, tok, 2 * HD), SEQ, split_axis=0, concat_...  6.87 us
    pallas_call x1, Pallas kernels, turn(): pl.pallas_call(turn_kernel, out_shape=jax.ShapeDtypeStruct((2, KVH, tok,...  5.85 us
  transfers between devices with their start and end apart: 11, of which 7 were waited for; matrix products, arithmetic and copies ran while one was open for 5% of the time, Pallas kernels for 16%

profile of v5, /device:TPU:3, one launch (start us, length us, event | category | flops | bytes accessed | tf_op | source)
XLA Modules:
  0.0 148.7 jit_solution(7236822228088220618)
XLA Ops:
  0.0 1.3 slice_bitcast_fusion
  1.4 2.1 %collective-permute-start.1 = (bf16[256,1024]{1,0:T(8,128)(2,1)S(1)}, bf16[256,1024]{1,0:T(8,128)(2,1)S(1)}, u32[]{:S(2)}, u32[]{:S(2)}) collective-permute-start(bf16[256,1024]{1,0:T(8,128)(2,1)S(1)} %get-tuple-element.31), channel_id=1, source_target_pairs={{0,96},{96,0},{32,64},{64,32},{1,97},{97,1},{33,65},{65,33},{2,98}... | collective-permute-start | bytes 1572872 | tf_op jit(solution)/shard_map/ppermute | solution.py:472
  5.1 0.7 pad_maximum_fusion
  5.9 5.8 %turn.1 = bf16[2,8,128,384]{3,2,1,0:T(8,128)(2,1)} custom-call(bf16[128,4096]{1,0:T(8,128)(2,1)} %bitcast.47, bf16[128,1024]{1,0:T(8,128)(2,1)} %bitcast.51, bf16[128,1024]{1,0:T(8,128)(2,1)} %bitcast.52, f32[128,128]{1,0:T(8,128)} %get-tuple-element.40.cos_ref, f32[128,128]{1,0:T(8,128)} %get-tuple-element.41.sin_ref), custom_call_target="tpu_custom_call" | custom-call | tf_op jit(solution)/shard_map/turn/pallas_call | solution.py:91
  12.4 1.8 %collective-permute-done.a_one = bf16[256,1024]{1,0:T(8,128)(2,1)S(1)} collective-permute-done((bf16[256,1024]{1,0:T(8,128)(2,1)S(1)}, bf16[256,1024]{1,0:T(8,128)(2,1)S(1)}, u32[]{:S(2)}, u32[]{:S(2)}) %collective-permute-start) | collective-permute-done | bytes 524320 | tf_op jit(solution)/shard_map/ppermute | solution.py:471
  15.0 0.7 copy-done.3
  15.7 3.0 %swap_kernel.1 = bf16[2,256,1024]{2,1,0:T(8,128)(2,1)} custom-call(s32[2]{0:T(128)} %pad_add_fusion.1.spot, bf16[2,256,1024]{2,1,0:T(8,128)(2,1)} %bitcast.37, bf16[256,1024]{1,0:T(8,128)(2,1)} %copy-done.2, bf16[256,1024]{1,0:T(8,128)(2,1)} %copy-done.3), custom_call_target="tpu_custom_call" | custom-call | tf_op jit(solution)/shard_map/swap_kernel/pallas_call | solution.py:180
  18.7 1.6 %collective-permute-start.2 = (bf16[2,256,1024]{2,1,0:T(8,128)(2,1)}, bf16[2,256,1024]{2,1,0:T(8,128)(2,1)S(1)}, u32[]{:S(2)}, u32[]{:S(2)}) collective-permute-start(bf16[2,256,1024]{2,1,0:T(8,128)(2,1)} %swap_kernel.1), channel_id=1, source_target_pairs={{0,16},{16,0},{1,17},{17,1},{2,18},{18,2},{3,19},{19,3},{4,20},{20... | collective-permute-start | bytes 3145736 | tf_op jit(solution)/shard_map/ppermute | solution.py:490
  20.3 5.5 %all_to_all.20 = bf16[2,8,128,384]{3,2,1,0:T(8,128)(2,1)} all-to-all(bf16[2,8,128,384]{3,2,1,0:T(8,128)(2,1)S(1)} %copy-done.1), channel_id=1, replica_groups=mesh['x'=4,'core'=2,'z'=4,'y'=4] {'core'}, dimensions={0} | all-to-all | bytes 3145728 | tf_op jit(solution)/shard_map/all_to_all | solution.py:492
  25.8 1.0 copy-done.4
  26.7 2.9 %relay_kernel.1 = bf16[2,256,1024]{2,1,0:T(8,128)(2,1)} custom-call(s32[2]{0:T(128)} %pad_add_fusion.1.spot, s32[8]{0:T(128)} %owner.3, bf16[2,256,1024]{2,1,0:T(8,128)(2,1)} %bitcast.38, bf16[256,1024]{1,0:T(8,128)(2,1)} %copy-done.2, bf16[256,1024]{1,0:T(8,128)(2,1)} %copy-done.3, bf16[2,256,1024]{2,1,0:T(8,128)(2,1)} %copy-done.4), custom_call_target="tpu_custom_call" | custom-call | tf_op jit(solution)/shard_map/relay_kernel/pallas_call | solution.py:180
  30.1 2.0 %collective-permute-start.4 = (bf16[2,256,1024]{2,1,0:T(8,128)(2,1)}, bf16[2,256,1024]{2,1,0:T(8,128)(2,1)S(1)}, u32[]{:S(2)}, u32[]{:S(2)}) collective-permute-start(bf16[2,256,1024]{2,1,0:T(8,128)(2,1)} %relay_kernel.1), channel_id=1, source_target_pairs={{0,96},{96,0},{32,64},{64,32},{16,48},{48,16},{80,112},{112,80},{1... | collective-permute-start | bytes 3145736 | tf_op jit(solution)/shard_map/ppermute | solution.py:503
  32.1 7.8 %all-to-all-start.1 = ((bf16[16,128,384]{2,1,0:T(8,128)(2,1)}), bf16[16,128,384]{2,1,0:T(8,128)(2,1)S(1)}, u32[]{:S(2)}, u32[]{:S(2)}) async-start(bf16[16,128,384]{2,1,0:T(8,128)(2,1)} %bitcast.11), calls=%async_computation.1 | async-start | bytes 3145728 | tf_op jit(solution)/shard_map/all_to_all | solution.py:495
  40.9 1.5 %convolution_convert_fusion.qb_ref = bf16[2048,128]{1,0:T(8,128)(2,1)} fusion(s32[2048]{0:T(1024)S(1)} %slice.27, f32[16,16]{1,0:T(8,128)S(1)} %get-tuple-element.38), kind=kOutput, calls=%fused_computation | convolution fusion | flops 403177472 | bytes 533504 | tf_op jit(solution)/shard_map/dot_general | solution.py:515
  42.4 2.4 %collective-permute-done.4.two = bf16[2,256,1024]{2,1,0:T(8,128)(2,1)S(1)} collective-permute-done((bf16[2,256,1024]{2,1,0:T(8,128)(2,1)}, bf16[2,256,1024]{2,1,0:T(8,128)(2,1)S(1)}, u32[]{:S(2)}, u32[]{:S(2)}) %collective-permute-start.4) | collective-permute-done | bytes 1048608 | tf_op jit(solution)/shard_map/ppermute | solution.py:503
  44.8 1.0 copy-done.7
  45.8 3.1 %settle_kernel.1 = bf16[2,8,256,128]{3,2,1,0:T(8,128)(2,1)} custom-call(s32[2]{0:T(128)} %pad_add_fusion.1.spot, s32[8]{0:T(128)} %owner.3, bf16[2,256,1024]{2,1,0:T(8,128)(2,1)} %bitcast.39, bf16[256,1024]{1,0:T(8,128)(2,1)} %copy-done.2, bf16[256,1024]{1,0:T(8,128)(2,1)} %copy-done.3, bf16[2,256,1024]{2,1,0:T(8,128)(2,1)} %copy-done.4, ...), custom_call_target="tpu_custom_call" | custom-call | tf_op jit(solution)/shard_map/settle_kernel/pallas_call | solution.py:180
  48.9 17.4 %all-to-all-done.1 = bf16[16,128,384]{2,1,0:T(8,128)(2,1)S(1)} async-done(((bf16[16,128,384]{2,1,0:T(8,128)(2,1)}), bf16[16,128,384]{2,1,0:T(8,128)(2,1)S(1)}, u32[]{:S(2)}, u32[]{:S(2)}) %all-to-all-start.1) | async-done | bytes 1572896 | tf_op jit(solution)/shard_map/all_to_all | solution.py:495
  66.4 3.7 %all-to-all-start.2 = ((bf16[16,256,128]{2,1,0:T(8,128)(2,1)}), bf16[16,256,128]{2,1,0:T(8,128)(2,1)S(1)}, u32[]{:S(2)}, u32[]{:S(2)}) async-start(bf16[16,256,128]{2,1,0:T(8,128)(2,1)} %bitcast.42), calls=%async_computation.2 | async-start | bytes 2097152 | tf_op jit(solution)/shard_map/all_to_all | solution.py:527
  70.1 1.0 collective-permute-start.3
  71.1 0.8 fusion.8.seen
  71.9 1.1 select_convert_fusion.kb_ref
  73.1 14.9 %pack_part.1.part_ref = f32[2,2048,256]{2,1,0:T(8,128)} custom-call(s32[1]{0:T(128)} %bitcast.core, s32[4,4]{1,0:T(4,128)} %fusion.8.seen, bf16[2048,384]{1,0:T(8,128)(2,1)} %bitcast.44, bf16[2048,384]{1,0:T(8,128)(2,1)} %bitcast.45, bf16[2048,128]{1,0:T(8,128)(2,1)} %collective-permute-done.3.other_ref, bf16[2048,128]{1,0:T(8,128)(2,1)} %convolution_convert_fusion.qb_ref, ...), custom_call_target="tpu_custom_call" | custom-call | flops 4294967296 | bytes 8388608 | tf_op jit(solution)/shard_map/pack_part/pallas_call | solution.py:296
  88.6 2.4 %collective-permute-done.6.other_ref = bf16[4096,128]{1,0:T(8,128)(2,1)S(1)} collective-permute-done((bf16[4096,128]{1,0:T(8,128)(2,1)S(1)}, bf16[4096,128]{1,0:T(8,128)(2,1)S(1)}, u32[]{:S(2)}, u32[]{:S(2)}) %collective-permute-start.6) | collective-permute-done | bytes 1048608 | tf_op jit(solution)/shard_map/ppermute | solution.py:531
  90.9 1.0 copy-done.12
  91.9 26.8 %stem_part.1 = bf16[2048,256]{1,0:T(8,128)(2,1)} custom-call(s32[1]{0:T(128)} %bitcast.core, bf16[2048,384]{1,0:T(8,128)(2,1)} %bitcast.46, bf16[4096,128]{1,0:T(8,128)(2,1)} %bitcast.49, bf16[4096,128]{1,0:T(8,128)(2,1)} %copy-done.12, f32[2,2048,256]{2,1,0:T(8,128)} %pack_part.1.part_ref), custom_call_target="tpu_custom_call" | custom-call | flops 8589934592 | bytes 8388608 | tf_op jit(solution)/shard_map/stem_part/pallas_call | solution.py:403
  118.7 6.9 %all-to-all-start.3 = ((bf16[16,128,256]{2,1,0:T(8,128)(2,1)}), bf16[16,128,256]{2,1,0:T(8,128)(2,1)S(1)}, u32[]{:S(2)}, u32[]{:S(2)}) async-start(bf16[16,128,256]{2,1,0:T(8,128)(2,1)} %bitcast.50), calls=%async_computation.3 | async-start | bytes 2097152 | tf_op jit(solution)/shard_map/all_to_all | solution.py:534
  125.6 16.8 %all-to-all-done.3 = bf16[16,128,256]{2,1,0:T(8,128)(2,1)S(1)} async-done(((bf16[16,128,256]{2,1,0:T(8,128)(2,1)}), bf16[16,128,256]{2,1,0:T(8,128)(2,1)S(1)}, u32[]{:S(2)}, u32[]{:S(2)}) %all-to-all-start.3) | async-done | bytes 1048608 | tf_op jit(solution)/shard_map/all_to_all | solution.py:534
  142.4 1.9 %collective-permute-start.7 = (bf16[8,128,256]{2,1,0:T(8,128)(2,1)S(1)}, bf16[8,128,256]{2,1,0:T(8,128)(2,1)S(1)}, u32[]{:S(2)}, u32[]{:S(2)}) collective-permute-start(bf16[8,128,256]{2,1,0:T(8,128)(2,1)S(1)} %dynamic-slice_bitcast_fusion), channel_id=1, source_target_pairs={{0,16},{16,0},{1,17},{17,1},{2,18},{18,2},{3,19},{19,3},{4,20},{20... | collective-permute-start | bytes 1572872 | tf_op jit(solution)/shard_map/ppermute | solution.py:538
  144.3 1.5 %collective-permute-done.7.other_ref = bf16[8,128,256]{2,1,0:T(8,128)(2,1)S(1)} collective-permute-done((bf16[8,128,256]{2,1,0:T(8,128)(2,1)S(1)}, bf16[8,128,256]{2,1,0:T(8,128)(2,1)S(1)}, u32[]{:S(2)}, u32[]{:S(2)}) %collective-permute-start.7) | collective-permute-done | bytes 524320 | tf_op jit(solution)/shard_map/ppermute | solution.py:538
  145.9 0.8 copy-done.8
  146.7 2.0 %gather.1 = bf16[128,4096]{1,0:T(8,128)(2,1)} custom-call(s32[1]{0:T(128)} %bitcast.core, bf16[2,8,128,256]{3,2,1,0:T(8,128)(2,1)} %bitcast.41, bf16[8,128,256]{2,1,0:T(8,128)(2,1)} %copy-done.8), custom_call_target="tpu_custom_call" | custom-call | tf_op jit(solution)/shard_map/gather/pallas_call | solution.py:445
  (55 shorter events, 5.2 us)
Async XLA Ops:
  0.0 4.8 %copy-start.11 = (f32[64]{0:T(128)S(1)}, f32[64]{0:T(128)}, u32[]{:S(2)}) copy-start(f32[64]{0:T(128)} %constant.72.clone) | copy-start | bytes 772
  0.0 3.5 %copy-start.9 = (s32[1,2048]{1,0:T(1,128)S(1)}, s32[1,2048]{1,0:T(1,128)}, u32[]{:S(2)}) copy-start(s32[1,2048]{1,0:T(1,128)} %param.12) | copy-start | bytes 24580
  0.0 3.7 %copy-start.10 = (s32[1,16]{1,0:T(1,128)S(1)}, s32[1,16]{1,0:T(1,128)}, u32[]{:S(2)}) copy-start(s32[1,16]{1,0:T(1,128)} %param.13) | copy-start | bytes 196
  1.3 12.9 %collective-permute-start = (bf16[256,1024]{1,0:T(8,128)(2,1)S(1)}, bf16[256,1024]{1,0:T(8,128)(2,1)S(1)}, u32[]{:S(2)}, u32[]{:S(2)}) collective-permute-start(bf16[256,1024]{1,0:T(8,128)(2,1)S(1)} %get-tuple-element.32), channel_id=1, source_target_pairs={{0,32},{32,0},{64,96},{96,64},{1,33},{33,1},{65,97},{97,65},{2,34}... | collective-permute-start | bytes 1572872 | tf_op jit(solution)/shard_map/ppermute | solution.py:471
  1.4 13.4 %collective-permute-start.1 = (bf16[256,1024]{1,0:T(8,128)(2,1)S(1)}, bf16[256,1024]{1,0:T(8,128)(2,1)S(1)}, u32[]{:S(2)}, u32[]{:S(2)}) collective-permute-start(bf16[256,1024]{1,0:T(8,128)(2,1)S(1)} %get-tuple-element.31), channel_id=1, source_target_pairs={{0,96},{96,0},{32,64},{64,32},{1,97},{97,1},{33,65},{65,33},{2,98}... | collective-permute-start | bytes 1572872 | tf_op jit(solution)/shard_map/ppermute | solution.py:472
  14.2 0.8 copy-start.2
  14.9 0.8 copy-start.3
  15.7 4.6 %copy-start.1 = (bf16[2,8,128,384]{3,2,1,0:T(8,128)(2,1)S(1)}, bf16[2,8,128,384]{3,2,1,0:T(8,128)(2,1)}, u32[]{:S(2)}) copy-start(bf16[2,8,128,384]{3,2,1,0:T(8,128)(2,1)} %turn.1) | copy-start | bytes 4718596
  18.7 7.1 %collective-permute-start.2 = (bf16[2,256,1024]{2,1,0:T(8,128)(2,1)}, bf16[2,256,1024]{2,1,0:T(8,128)(2,1)S(1)}, u32[]{:S(2)}, u32[]{:S(2)}) collective-permute-start(bf16[2,256,1024]{2,1,0:T(8,128)(2,1)} %swap_kernel.1), channel_id=1, source_target_pairs={{0,16},{16,0},{1,17},{17,1},{2,18},{18,2},{3,19},{19,3},{4,20},{20... | collective-permute-start | bytes 3145736 | tf_op jit(solution)/shard_map/ppermute | solution.py:490
  25.8 1.0 copy-start.4
  29.7 10.2 %collective-permute-start.5 = (s32[2064]{0:T(1024)S(1)}, s32[2064]{0:T(1024)S(1)}, u32[]{:S(2)}, u32[]{:S(2)}) collective-permute-start(s32[2064]{0:T(1024)S(1)} %pad_add_fusion), channel_id=1, source_target_pairs={{0,16},{16,0},{1,17},{17,1},{2,18},{18,2},{3,19},{19,3},{4,20},{20... | collective-permute-start | bytes 24776 | tf_op jit(solution)/shard_map/ppermute | solution.py:511
  30.1 14.7 %collective-permute-start.4 = (bf16[2,256,1024]{2,1,0:T(8,128)(2,1)}, bf16[2,256,1024]{2,1,0:T(8,128)(2,1)S(1)}, u32[]{:S(2)}, u32[]{:S(2)}) collective-permute-start(bf16[2,256,1024]{2,1,0:T(8,128)(2,1)} %relay_kernel.1), channel_id=1, source_target_pairs={{0,96},{96,0},{32,64},{64,32},{16,48},{48,16},{80,112},{112,80},{1... | collective-permute-start | bytes 3145736 | tf_op jit(solution)/shard_map/ppermute | solution.py:503
  32.1 34.2 %all-to-all-start.1 = ((bf16[16,128,384]{2,1,0:T(8,128)(2,1)}), bf16[16,128,384]{2,1,0:T(8,128)(2,1)S(1)}, u32[]{:S(2)}, u32[]{:S(2)}) async-start(bf16[16,128,384]{2,1,0:T(8,128)(2,1)} %bitcast.11), calls=%async_computation.1 | async-start | bytes 3145728 | tf_op jit(solution)/shard_map/all_to_all | solution.py:495
  44.8 1.0 copy-start.7
  66.4 3.7 %copy-start.5 = (bf16[16,128,384]{2,1,0:T(8,128)(2,1)}, bf16[16,128,384]{2,1,0:T(8,128)(2,1)S(1)}, u32[]{:S(2)}) copy-start(bf16[16,128,384]{2,1,0:T(8,128)(2,1)S(1)} %all-to-all-done.1) | copy-start | bytes 4718596
  66.4 21.7 %all-to-all-start.2 = ((bf16[16,256,128]{2,1,0:T(8,128)(2,1)}), bf16[16,256,128]{2,1,0:T(8,128)(2,1)S(1)}, u32[]{:S(2)}, u32[]{:S(2)}) async-start(bf16[16,256,128]{2,1,0:T(8,128)(2,1)} %bitcast.42), calls=%async_computation.2 | async-start | bytes 2097152 | tf_op jit(solution)/shard_map/all_to_all | solution.py:527
  70.1 3.0 %collective-permute-start.3 = (bf16[2048,128]{1,0:T(8,128)(2,1)S(1)}, bf16[2048,128]{1,0:T(8,128)(2,1)}, u32[]{:S(2)}, u32[]{:S(2)}) collective-permute-start(bf16[2048,128]{1,0:T(8,128)(2,1)S(1)} %slice.26), channel_id=1, source_target_pairs={{0,16},{16,0},{1,17},{17,1},{2,18},{18,2},{3,19},{19,3},{4,20},{20... | collective-permute-start | bytes 1572872 | tf_op jit(solution)/shard_map/ppermute | solution.py:498
  88.0 2.9 %copy-start.6 = (bf16[16,256,128]{2,1,0:T(8,128)(2,1)}, bf16[16,256,128]{2,1,0:T(8,128)(2,1)S(1)}, u32[]{:S(2)}) copy-start(bf16[16,256,128]{2,1,0:T(8,128)(2,1)S(1)} %all-to-all-done.2) | copy-start | bytes 3145732
  88.0 2.9 %collective-permute-start.6 = (bf16[4096,128]{1,0:T(8,128)(2,1)S(1)}, bf16[4096,128]{1,0:T(8,128)(2,1)S(1)}, u32[]{:S(2)}, u32[]{:S(2)}) collective-permute-start(bf16[4096,128]{1,0:T(8,128)(2,1)S(1)} %bitcast.48), channel_id=1, source_target_pairs={{0,16},{16,0},{1,17},{17,1},{2,18},{18,2},{3,19},{19,3},{4,20},{20... | collective-permute-start | bytes 3145736 | tf_op jit(solution)/shard_map/ppermute | solution.py:531
  90.9 1.0 copy-start.12
  118.7 23.6 %all-to-all-start.3 = ((bf16[16,128,256]{2,1,0:T(8,128)(2,1)}), bf16[16,128,256]{2,1,0:T(8,128)(2,1)S(1)}, u32[]{:S(2)}, u32[]{:S(2)}) async-start(bf16[16,128,256]{2,1,0:T(8,128)(2,1)} %bitcast.50), calls=%async_computation.3 | async-start | bytes 2097152 | tf_op jit(solution)/shard_map/all_to_all | solution.py:534
  142.4 3.5 %copy-start = (bf16[16,128,256]{2,1,0:T(8,128)(2,1)}, bf16[16,128,256]{2,1,0:T(8,128)(2,1)S(1)}, u32[]{:S(2)}) copy-start(bf16[16,128,256]{2,1,0:T(8,128)(2,1)S(1)} %all-to-all-done.3) | copy-start | bytes 3145732
  142.4 3.5 %collective-permute-start.7 = (bf16[8,128,256]{2,1,0:T(8,128)(2,1)S(1)}, bf16[8,128,256]{2,1,0:T(8,128)(2,1)S(1)}, u32[]{:S(2)}, u32[]{:S(2)}) collective-permute-start(bf16[8,128,256]{2,1,0:T(8,128)(2,1)S(1)} %dynamic-slice_bitcast_fusion), channel_id=1, source_target_pairs={{0,16},{16,0},{1,17},{17,1},{2,18},{18,2},{3,19},{19,3},{4,20},{20... | collective-permute-start | bytes 1572872 | tf_op jit(solution)/shard_map/ppermute | solution.py:538
  145.9 0.8 copy-start.8

commit v6 on v5

--- a/solution.py
+++ b/solution.py
@@ -71,37 +71,57 @@
     )
 
 
-def turn_kernel(q_ref, k_ref, v_ref, cos_ref, sin_ref, o_ref):
-    cosine = cos_ref[...]
-    sine = sin_ref[...]
-
-    def turned(part):
-        wide = part.astype(jnp.float32)
-        return (wide * cosine + pltpu.roll(wide, HD // 2, 1) * sine).astype(jnp.bfloat16)
-
-    for head in range(4):
-        at = head % 2 * HD
-        o_ref[head // 2, 0, :, at : at + HD] = turned(q_ref[:, head * HD : head * HD + HD])
-    o_ref[0, 0, :, 2 * HD :] = turned(k_ref[...])
-    o_ref[1, 0, :, 2 * HD :] = v_ref[...]
-
-
-def turn(q, k, v, cosine, sine):
-    tok = q.shape[0]
+def turn_kernel(
+    spot, q_own, k_own, v_own, q_mate, k_mate, v_mate, cos_ref, sin_ref, o_ref
+):
+    core = spot[1]
+    pack = pl.program_id(0)
+
+    def run(place, q_ref, k_ref, v_ref):
+        cosine = cos_ref[place]
+        sine = sin_ref[place]
+
+        def turned(part):
+            wide = part.astype(jnp.float32)
+            return (wide * cosine + pltpu.roll(wide, HD // 2, 1) * sine).astype(jnp.bfloat16)
+
+        for e in range(KVH):
+            for head in range(2):
+                at = pl.multiple_of((4 * e + head + 2 * core) * HD, HD)
+                o_ref[0, e, :, head * HD : head * HD + HD] = turned(q_ref[:, pl.ds(at, HD)])
+            at = e * HD
+            o_ref[0, e, :, 2 * HD :] = jnp.where(
+                core == 0, turned(k_ref[:, at : at + HD]), v_ref[:, at : at + HD]
+            )
+
+    @pl.when(pack == core)
+    def _():
+        run(0, q_own, k_own, v_own)
+
+    @pl.when(pack != core)
+    def _():
+        run(1, q_mate, k_mate, v_mate)
+
+
+def turn(here, own, mate, cosine, sine):
+    tok = own[0].shape[0]
+    whole = [
+        pl.BlockSpec(part.shape, lambda i, here: (0, 0), pipeline_mode=pl.Buffered(1))
+        for part in own + mate
+    ]
+    table = pl.BlockSpec(cosine.shape, lambda i, here: (0, 0, 0), pipeline_mode=pl.Buffered(1))
     return pl.pallas_call(
         turn_kernel,
         out_shape=jax.ShapeDtypeStruct((2, KVH, tok, 3 * HD), jnp.bfloat16),
-        grid=(KVH,),
-        in_specs=[
-            pl.BlockSpec((tok, 4 * HD), lambda e: (0, e)),
-            pl.BlockSpec((tok, HD), lambda e: (0, e)),
-            pl.BlockSpec((tok, HD), lambda e: (0, e)),
-            pl.BlockSpec((tok, HD), lambda e: (0, 0)),
-            pl.BlockSpec((tok, HD), lambda e: (0, 0)),
-        ],
-        out_specs=pl.BlockSpec((2, 1, tok, 3 * HD), lambda e: (0, e, 0, 0)),
+        grid_spec=pltpu.PrefetchScalarGridSpec(
+            num_scalar_prefetch=1,
+            grid=(2,),
+            in_specs=whole + [table, table],
+            out_specs=pl.BlockSpec((1, KVH, tok, 3 * HD), lambda i, here: (i, 0, 0, 0)),
+        ),
+        compiler_params=pltpu.CompilerParams(vmem_limit_bytes=32 * 1024 * 1024),
         name="turn",
-    )(q, k, v, cosine, sine)
+    )(here, *own, *mate, cosine, sine)
 
 
 def held_at(x, core, group):
@@ -467,35 +487,35 @@
     core_row = core[None].astype(jnp.int32)
     here = jnp.stack([x, core]).astype(jnp.int32)
 
+    raw = (queries[0], keys[0], values[0])
+    rows = jnp.concatenate([seg_ids[0], seg_parent[0]])
+    rows_mate = lax.ppermute(rows, "core", FLIP)
+    raw_mate = tuple(lax.ppermute(part, "core", FLIP) for part in raw)
+
     own = stem_kv[0]
     a_one = lax.ppermute(own[0], "x", NEAR)
     b_one = lax.ppermute(own[1], "x", FAR)
 
-    linked = ancestry(seg_parent[0])
-    places = token_places(seg_ids[0], linked)
-    own_places = lax.dynamic_slice_in_dim(places, spot * tok, tok)
-    angles = own_places[:, None] * rotary_table()[None, :]
+    both = jnp.stack([rows, rows_mate])
+    linked = jax.vmap(ancestry)(both[:, pack_len:])
+    places = jax.vmap(token_places)(both[:, :pack_len], linked)
+    places = lax.dynamic_slice_in_dim(places, spot * tok, tok, axis=1)
+    angles = places[:, :, None] * rotary_table()[None, None, :]
     cosine, sine = jnp.cos(angles), jnp.sin(angles)
     sent = turn(
-        queries[0],
-        keys[0],
-        values[0],
-        jnp.concatenate([cosine, cosine], axis=1),
-        jnp.concatenate([-sine, sine], axis=1),
-    )
-
+        here,
+        raw,
+        raw_mate,
+        jnp.concatenate([cosine, cosine], axis=2),
+        jnp.concatenate([-sine, sine], axis=2),
+    )
+    arrived = lax.all_to_all(
+        sent.reshape(16, tok, 3 * HD), SEQ, split_axis=0, concat_axis=0, tiled=True
+    ).reshape(pack_len, 3 * HD)
     a_one, b_one, sent = lax.optimization_barrier((a_one, b_one, sent))
 
     passed = moved(swap_kernel, own.shape, (2,), (here,), (own, a_one, b_one))
     mate = lax.ppermute(passed, "core", FLIP)
-    sent, passed = lax.optimization_barrier((sent, passed))
-    crossed = lax.all_to_all(sent, "core", split_axis=0, concat_axis=0, tiled=True)
-    mate, crossed = lax.optimization_barrier((mate, crossed))
-
-    arrived = lax.all_to_all(
-        crossed.reshape(16, tok, 3 * HD), SEQ, split_axis=0, concat_axis=0, tiled=True
-    ).reshape(pack_len, 3 * HD)
-    pair = lax.ppermute(arrived[:, 2 * HD :], "core", FLIP)
 
     wanted = moved(
         relay_kernel, own.shape, (2,), (here, stem_owner), (own, a_one, b_one, mate)
@@ -505,11 +525,13 @@
         ("x", "core"),
         [(2 * i, 2 * j) for i, j in FAR] + [(2 * i + 1, 2 * j + 1) for i, j in NEAR],
     )
-    seg_ids, seg_parent, _ = lax.optimization_barrier((seg_ids, seg_parent, wanted))
-
-    rows = jnp.concatenate([seg_ids[0], seg_parent[0]])
-    rows = jnp.where(spot // KVH == core, rows, lax.ppermute(rows, "core", FLIP))
-    seg_row, reach = rows[:pack_len], ancestry(rows[pack_len:])
+    both, linked, _ = lax.optimization_barrier((both, linked, wanted))
+    two, arrived = lax.optimization_barrier((two, arrived))
+    pair = lax.ppermute(arrived[:, 2 * HD :], "core", FLIP)
+
+    ours = spot // KVH == core
+    seg_row = jnp.where(ours, both[0, :pack_len], both[1, :pack_len])
+    reach = jnp.where(ours, linked[0], linked[1])
     onehot = (seg_row[:, None] == jnp.arange(HD, dtype=jnp.int32)[None, :]).astype(jnp.float32)
     barred = jnp.pad(BARRED * (1.0 - reach), ((0, HD - SEGS), (0, HD - SEGS)))
     q_side = jnp.dot(onehot, barred, precision=lax.Precision.HIGHEST).astype(jnp.bfloat16)

time: 150 us -> 145 us (0.967)
  the two profiles are of different devices: /device:TPU:3 before, /device:TPU:1 now
where the time goes in v6:
time: 145 us
  Pallas kernels  55 us (38%)
  waiting for transfers between devices  46.9 us (32%)
  starting transfers between devices  29.7 us (20%)
  local copies, waits for them, and re-layouts  5.82 us (4%)
  other arithmetic  4.17 us (3%)
  matrix products  3.02 us (2%)
    pallas_call x1, Pallas kernels, stem_part(): pl.pallas_call(stem_kernel, out_shape=jax.ShapeDtypeStruct((pack, 2 * HD)...  26.8 us
    all_to_all x1, waiting for transfers between devices, shards(): lax.all_to_all(sent.reshape(16, tok, 3 * HD), SEQ, split_axis=0, concat_a...  18.5 us
    all_to_all x1, waiting for transfers between devices, shards(): lax.all_to_all(mixed.reshape(16, tok, 2 * HD), SEQ, split_axis=0, concat_...  16.3 us
    pallas_call x1, Pallas kernels, pack_part(): pl.pallas_call(pack_kernel, out_shape=jax.ShapeDtypeStruct((2, pack, 2 *...  14.9 us
    pallas_call x3, Pallas kernels, moved(): pl.pallas_call(kernel, out_shape=jax.ShapeDtypeStruct(shape, jnp.bfloat16...  8.85 us
    all_to_all x1, starting transfers between devices, shards(): lax.all_to_all(sent.reshape(16, tok, 3 * HD), SEQ, split_axis=0, concat_a...  7.77 us
    all_to_all x1, starting transfers between devices, shards(): lax.all_to_all(mixed.reshape(16, tok, 2 * HD), SEQ, split_axis=0, concat_...  6.38 us
    ppermute x1, waiting for transfers between devices, shards(): a_one = lax.ppermute(own[0], 'x', NEAR)  5.77 us
  transfers between devices with their start and end apart: 14, of which 6 were waited for; matrix products, arithmetic and copies ran while one was open for 7% of the time, Pallas kernels for 16%

profile of v6, /device:TPU:1, one launch (start us, length us, event | category | flops | bytes accessed | tf_op | source)
XLA Modules:
  0.0 144.8 jit_solution(17373321105240842757)
XLA Ops:
  0.0 0.7 pad_add_fusion.1
  0.7 1.4 collective-permute-start.5
  2.8 2.3 %slice_bitcast_fusion = (bf16[256,1024]{1,0:T(8,128)(2,1)}, bf16[256,1024]{1,0:T(8,128)(2,1)}) fusion(bf16[1,2,256,1024]{3,2,1,0:T(8,128)(2,1)} %param.11), kind=kLoop, calls=%fused_computation.27 | loop fusion | bytes 2097152 | tf_op jit(solution)/shard_map/squeeze | solution.py:497
  5.1 1.3 collective-permute-start
  6.6 1.8 %collective-permute-start.1 = (bf16[256,1024]{1,0:T(8,128)(2,1)}, bf16[256,1024]{1,0:T(8,128)(2,1)}, u32[]{:S(2)}, u32[]{:S(2)}) collective-permute-start(bf16[256,1024]{1,0:T(8,128)(2,1)} %get-tuple-element.29), channel_id=1, source_target_pairs={{0,96},{96,0},{32,64},{64,32},{1,97},{97,1},{33,65},{65,33},{2,98}... | collective-permute-start | bytes 1572872 | tf_op jit(solution)/shard_map/ppermute | solution.py:497
  10.5 2.4 %turn.1 = bf16[2,8,128,384]{3,2,1,0:T(8,128)(2,1)} custom-call(s32[2]{0:T(128)S(1)} %pad_add_fusion.2.spot, bf16[128,4096]{1,0:T(8,128)(2,1)S(1)} %bitcast.36, bf16[128,1024]{1,0:T(8,128)(2,1)S(1)} %bitcast.38, bf16[128,1024]{1,0:T(8,128)(2,1)S(1)} %bitcast.40, bf16[128,4096]{1,0:T(8,128)(2,1)S(1)} %collective-permute-done.2.q_mate, ...), custom_call_target="tpu_custom_call" | custom-call | tf_op jit(solution)/shard_map/turn/pallas_call | solution.py:113
  12.8 5.8 %collective-permute-done.a_one = bf16[256,1024]{1,0:T(8,128)(2,1)} collective-permute-done((bf16[256,1024]{1,0:T(8,128)(2,1)}, bf16[256,1024]{1,0:T(8,128)(2,1)}, u32[]{:S(2)}, u32[]{:S(2)}) %collective-permute-start) | collective-permute-done | bytes 524320 | tf_op jit(solution)/shard_map/ppermute | solution.py:496
  18.6 2.4 %collective-permute-done.1.b_one = bf16[256,1024]{1,0:T(8,128)(2,1)} collective-permute-done((bf16[256,1024]{1,0:T(8,128)(2,1)}, bf16[256,1024]{1,0:T(8,128)(2,1)}, u32[]{:S(2)}, u32[]{:S(2)}) %collective-permute-start.1) | collective-permute-done | bytes 524320 | tf_op jit(solution)/shard_map/ppermute | solution.py:497
  21.0 2.8 %swap_kernel.1 = bf16[2,256,1024]{2,1,0:T(8,128)(2,1)} custom-call(s32[2]{0:T(128)} %copy-done.3, bf16[2,256,1024]{2,1,0:T(8,128)(2,1)} %bitcast.41, bf16[256,1024]{1,0:T(8,128)(2,1)} %collective-permute-done.a_one, bf16[256,1024]{1,0:T(8,128)(2,1)} %collective-permute-done.1.b_one), custom_call_target="tpu_custom_call" | custom-call | tf_op jit(solution)/shard_map/swap_kernel/pallas_call | solution.py:200
  23.9 1.5 %collective-permute-start.6 = (bf16[2,256,1024]{2,1,0:T(8,128)(2,1)}, bf16[2,256,1024]{2,1,0:T(8,128)(2,1)S(1)}, u32[]{:S(2)}, u32[]{:S(2)}) collective-permute-start(bf16[2,256,1024]{2,1,0:T(8,128)(2,1)} %swap_kernel.1), channel_id=1, source_target_pairs={{0,16},{16,0},{1,17},{17,1},{2,18},{18,2},{3,19},{19,3},{4,20},{20... | collective-permute-start | bytes 3145736 | tf_op jit(solution)/shard_map/ppermute | solution.py:518
  25.4 7.8 %all-to-all-start = ((bf16[16,128,384]{2,1,0:T(8,128)(2,1)}), bf16[16,128,384]{2,1,0:T(8,128)(2,1)S(1)}, u32[]{:S(2)}, u32[]{:S(2)}) async-start(bf16[16,128,384]{2,1,0:T(8,128)(2,1)} %bitcast.10), calls=%async_computation | async-start | bytes 3145728 | tf_op jit(solution)/shard_map/all_to_all | solution.py:512
  33.3 1.0 copy-done.5
  34.2 2.9 %relay_kernel.1 = bf16[2,256,1024]{2,1,0:T(8,128)(2,1)} custom-call(s32[2]{0:T(128)} %copy-done.3, s32[8]{0:T(128)} %owner.3, bf16[2,256,1024]{2,1,0:T(8,128)(2,1)} %bitcast.42, bf16[256,1024]{1,0:T(8,128)(2,1)} %collective-permute-done.a_one, bf16[256,1024]{1,0:T(8,128)(2,1)} %collective-permute-done.1.b_one, bf16[2,256,1024]{2,1,0:T(8,128)(2,1)} %copy-done.5), custom_call_target="tpu_custom_call" | custom-call | tf_op jit(solution)/shard_map/relay_kernel/pallas_call | solution.py:200
  37.8 0.6 fusion.40
  38.7 1.5 %convolution_convert_fusion.qb_ref = bf16[2048,128]{1,0:T(8,128)(2,1)} fusion(s32[2048]{0:T(1024)S(1)} %bitcast.54, f32[16,16]{0,1:T(8,128)S(1)} %fusion.33), kind=kOutput, calls=%fused_computation | convolution fusion | flops 403177472 | bytes 533504 | tf_op jit(solution)/shard_map/dot_general | solution.py:537
  40.3 18.5 %all-to-all-done = bf16[16,128,384]{2,1,0:T(8,128)(2,1)S(1)} async-done(((bf16[16,128,384]{2,1,0:T(8,128)(2,1)}), bf16[16,128,384]{2,1,0:T(8,128)(2,1)S(1)}, u32[]{:S(2)}, u32[]{:S(2)}) %all-to-all-start) | async-done | bytes 1572896 | tf_op jit(solution)/shard_map/all_to_all | solution.py:512
  58.9 1.2 collective-permute-start.8
  60.1 3.1 %settle_kernel.1 = bf16[2,8,256,128]{3,2,1,0:T(8,128)(2,1)} custom-call(s32[2]{0:T(128)} %copy-done.3, s32[8]{0:T(128)} %owner.3, bf16[2,256,1024]{2,1,0:T(8,128)(2,1)} %bitcast.43, bf16[256,1024]{1,0:T(8,128)(2,1)} %collective-permute-done.a_one, bf16[256,1024]{1,0:T(8,128)(2,1)} %collective-permute-done.1.b_one, bf16[2,256,1024]{2,1,0:T(8,128)(2,1)} %copy-done.5, ...), custom_call_target="tpu_custom_call" | custom-call | tf_op jit(solution)/shard_map/settle_kernel/pallas_call | solution.py:200
  63.2 3.8 %all-to-all-start.1 = ((bf16[16,256,128]{2,1,0:T(8,128)(2,1)}), bf16[16,256,128]{2,1,0:T(8,128)(2,1)S(1)}, u32[]{:S(2)}, u32[]{:S(2)}) async-start(bf16[16,256,128]{2,1,0:T(8,128)(2,1)} %bitcast.46), calls=%async_computation.1 | async-start | bytes 2097152 | tf_op jit(solution)/shard_map/all_to_all | solution.py:549
  67.1 0.8 fusion.18.seen
  67.9 1.1 select_convert_fusion.kb_ref
  69.0 14.9 %pack_part.1.part_ref = f32[2,2048,256]{2,1,0:T(8,128)} custom-call(s32[1]{0:T(128)} %bitcast.core, s32[4,4]{1,0:T(4,128)} %fusion.18.seen, bf16[2048,384]{1,0:T(8,128)(2,1)} %bitcast.48, bf16[2048,384]{1,0:T(8,128)(2,1)} %bitcast.49, bf16[2048,128]{1,0:T(8,128)(2,1)} %collective-permute-done.8.other_ref, bf16[2048,128]{1,0:T(8,128)(2,1)} %convolution_convert_fusion.qb_ref, ...), custom_call_target="tpu_custom_call" | custom-call | flops 4294967296 | bytes 8388608 | tf_op jit(solution)/shard_map/pack_part/pallas_call | solution.py:316
  84.0 1.5 %collective-permute-start.9 = (bf16[4096,128]{1,0:T(8,128)(2,1)S(1)}, bf16[4096,128]{1,0:T(8,128)(2,1)S(1)}, u32[]{:S(2)}, u32[]{:S(2)}) collective-permute-start(bf16[4096,128]{1,0:T(8,128)(2,1)S(1)} %bitcast.51), channel_id=1, source_target_pairs={{0,16},{16,0},{1,17},{17,1},{2,18},{18,2},{3,19},{19,3},{4,20},{20... | collective-permute-start | bytes 3145736 | tf_op jit(solution)/shard_map/ppermute | solution.py:553
  85.4 2.3 %collective-permute-done.9.other_ref = bf16[4096,128]{1,0:T(8,128)(2,1)S(1)} collective-permute-done((bf16[4096,128]{1,0:T(8,128)(2,1)S(1)}, bf16[4096,128]{1,0:T(8,128)(2,1)S(1)}, u32[]{:S(2)}, u32[]{:S(2)}) %collective-permute-start.9) | collective-permute-done | bytes 1048608 | tf_op jit(solution)/shard_map/ppermute | solution.py:553
  87.7 1.0 copy-done.11
  88.7 26.8 %stem_part.1 = bf16[2048,256]{1,0:T(8,128)(2,1)} custom-call(s32[1]{0:T(128)} %bitcast.core, bf16[2048,384]{1,0:T(8,128)(2,1)} %bitcast.50, bf16[4096,128]{1,0:T(8,128)(2,1)} %bitcast.52, bf16[4096,128]{1,0:T(8,128)(2,1)} %copy-done.11, f32[2,2048,256]{2,1,0:T(8,128)} %pack_part.1.part_ref), custom_call_target="tpu_custom_call" | custom-call | flops 8589934592 | bytes 8388608 | tf_op jit(solution)/shard_map/stem_part/pallas_call | solution.py:423
  115.5 6.4 %all-to-all-start.2 = ((bf16[16,128,256]{2,1,0:T(8,128)(2,1)}), bf16[16,128,256]{2,1,0:T(8,128)(2,1)S(1)}, u32[]{:S(2)}, u32[]{:S(2)}) async-start(bf16[16,128,256]{2,1,0:T(8,128)(2,1)} %bitcast.53), calls=%async_computation.2 | async-start | bytes 2097152 | tf_op jit(solution)/shard_map/all_to_all | solution.py:556
  121.9 16.3 %all-to-all-done.2 = bf16[16,128,256]{2,1,0:T(8,128)(2,1)S(1)} async-done(((bf16[16,128,256]{2,1,0:T(8,128)(2,1)}), bf16[16,128,256]{2,1,0:T(8,128)(2,1)S(1)}, u32[]{:S(2)}, u32[]{:S(2)}) %all-to-all-start.2) | async-done | bytes 1048608 | tf_op jit(solution)/shard_map/all_to_all | solution.py:556
  138.3 2.2 %collective-permute-start.10 = (bf16[8,128,256]{2,1,0:T(8,128)(2,1)S(1)}, bf16[8,128,256]{2,1,0:T(8,128)(2,1)S(1)}, u32[]{:S(2)}, u32[]{:S(2)}) collective-permute-start(bf16[8,128,256]{2,1,0:T(8,128)(2,1)S(1)} %dynamic-slice_bitcast_fusion), channel_id=1, source_target_pairs={{0,16},{16,0},{1,17},{17,1},{2,18},{18,2},{3,19},{19,3},{4,20},{20... | collective-permute-start | bytes 1572872 | tf_op jit(solution)/shard_map/ppermute | solution.py:560
  140.5 1.5 %collective-permute-done.10.other_ref = bf16[8,128,256]{2,1,0:T(8,128)(2,1)S(1)} collective-permute-done((bf16[8,128,256]{2,1,0:T(8,128)(2,1)S(1)}, bf16[8,128,256]{2,1,0:T(8,128)(2,1)S(1)}, u32[]{:S(2)}, u32[]{:S(2)}) %collective-permute-start.10) | collective-permute-done | bytes 524320 | tf_op jit(solution)/shard_map/ppermute | solution.py:560
  142.0 0.8 copy-done.9
  142.8 2.0 %gather.1 = bf16[128,4096]{1,0:T(8,128)(2,1)} custom-call(s32[1]{0:T(128)} %bitcast.core, bf16[2,8,128,256]{3,2,1,0:T(8,128)(2,1)} %bitcast.45, bf16[8,128,256]{2,1,0:T(8,128)(2,1)} %copy-done.9), custom_call_target="tpu_custom_call" | custom-call | tf_op jit(solution)/shard_map/gather/pallas_call | solution.py:465
  (64 shorter events, 3.8 us)
Async XLA Ops:
  0.0 9.7 %copy-start.10 = (f32[64]{0:T(128)S(1)}, f32[64]{0:T(128)}, u32[]{:S(2)}) copy-start(f32[64]{0:T(128)} %constant.72.clone) | copy-start | bytes 772
  0.7 5.9 %collective-permute-start.5 = (s32[2064]{0:T(1024)S(1)}, s32[2064]{0:T(1024)S(1)}, u32[]{:S(2)}, u32[]{:S(2)}) collective-permute-start(s32[2064]{0:T(1024)S(1)} %pad_add_fusion.1), channel_id=1, source_target_pairs={{0,16},{16,0},{1,17},{17,1},{2,18},{18,2},{3,19},{19,3},{4,20},{20... | collective-permute-start | bytes 24776 | tf_op jit(solution)/shard_map/ppermute | solution.py:492
  2.2 8.3 %collective-permute-start.2 = (bf16[128,4096]{1,0:T(8,128)(2,1)}, bf16[128,4096]{1,0:T(8,128)(2,1)S(1)}, u32[]{:S(2)}, u32[]{:S(2)}) collective-permute-start(bf16[128,4096]{1,0:T(8,128)(2,1)} %bitcast.35), channel_id=1, source_target_pairs={{0,16},{16,0},{1,17},{17,1},{2,18},{18,2},{3,19},{19,3},{4,20},{20... | collective-permute-start | bytes 3145736 | tf_op jit(solution)/shard_map/ppermute | solution.py:493
  2.2 8.2 %collective-permute-start.3 = (bf16[128,1024]{1,0:T(8,128)(2,1)}, bf16[128,1024]{1,0:T(8,128)(2,1)S(1)}, u32[]{:S(2)}, u32[]{:S(2)}) collective-permute-start(bf16[128,1024]{1,0:T(8,128)(2,1)} %bitcast.37), channel_id=1, source_target_pairs={{0,16},{16,0},{1,17},{17,1},{2,18},{18,2},{3,19},{19,3},{4,20},{20... | collective-permute-start | bytes 786440 | tf_op jit(solution)/shard_map/ppermute | solution.py:493
  2.7 7.8 %copy-start = (bf16[1,128,4096]{2,1,0:T(8,128)(2,1)S(1)}, bf16[1,128,4096]{2,1,0:T(8,128)(2,1)}, u32[]{:S(2)}) copy-start(bf16[1,128,4096]{2,1,0:T(8,128)(2,1)} %param.8) | copy-start | bytes 3145732
  2.7 7.8 %copy-start.1 = (bf16[1,128,1024]{2,1,0:T(8,128)(2,1)S(1)}, bf16[1,128,1024]{2,1,0:T(8,128)(2,1)}, u32[]{:S(2)}) copy-start(bf16[1,128,1024]{2,1,0:T(8,128)(2,1)} %param.9) | copy-start | bytes 786436
  2.7 7.8 %copy-start.2 = (bf16[1,128,1024]{2,1,0:T(8,128)(2,1)S(1)}, bf16[1,128,1024]{2,1,0:T(8,128)(2,1)}, u32[]{:S(2)}) copy-start(bf16[1,128,1024]{2,1,0:T(8,128)(2,1)} %param.10) | copy-start | bytes 786436
  2.7 7.7 %collective-permute-start.4 = (bf16[128,1024]{1,0:T(8,128)(2,1)}, bf16[128,1024]{1,0:T(8,128)(2,1)S(1)}, u32[]{:S(2)}, u32[]{:S(2)}) collective-permute-start(bf16[128,1024]{1,0:T(8,128)(2,1)} %bitcast.39), channel_id=1, source_target_pairs={{0,16},{16,0},{1,17},{17,1},{2,18},{18,2},{3,19},{19,3},{4,20},{20... | collective-permute-start | bytes 786440 | tf_op jit(solution)/shard_map/ppermute | solution.py:493
  5.1 13.5 %collective-permute-start = (bf16[256,1024]{1,0:T(8,128)(2,1)}, bf16[256,1024]{1,0:T(8,128)(2,1)}, u32[]{:S(2)}, u32[]{:S(2)}) collective-permute-start(bf16[256,1024]{1,0:T(8,128)(2,1)} %get-tuple-element.30), channel_id=1, source_target_pairs={{0,32},{32,0},{64,96},{96,64},{1,33},{33,1},{65,97},{97,65},{2,34}... | collective-permute-start | bytes 1572872 | tf_op jit(solution)/shard_map/ppermute | solution.py:496
  6.5 6.3 %copy-start.3 = (s32[2]{0:T(128)}, s32[2]{0:T(128)S(1)}, u32[]{:S(2)}) copy-start(s32[2]{0:T(128)S(1)} %pad_add_fusion.2.spot) | copy-start | bytes 28
  6.6 14.4 %collective-permute-start.1 = (bf16[256,1024]{1,0:T(8,128)(2,1)}, bf16[256,1024]{1,0:T(8,128)(2,1)}, u32[]{:S(2)}, u32[]{:S(2)}) collective-permute-start(bf16[256,1024]{1,0:T(8,128)(2,1)} %get-tuple-element.29), channel_id=1, source_target_pairs={{0,96},{96,0},{32,64},{64,32},{1,97},{97,1},{33,65},{65,33},{2,98}... | collective-permute-start | bytes 1572872 | tf_op jit(solution)/shard_map/ppermute | solution.py:497
  23.9 9.4 %collective-permute-start.6 = (bf16[2,256,1024]{2,1,0:T(8,128)(2,1)}, bf16[2,256,1024]{2,1,0:T(8,128)(2,1)S(1)}, u32[]{:S(2)}, u32[]{:S(2)}) collective-permute-start(bf16[2,256,1024]{2,1,0:T(8,128)(2,1)} %swap_kernel.1), channel_id=1, source_target_pairs={{0,16},{16,0},{1,17},{17,1},{2,18},{18,2},{3,19},{19,3},{4,20},{20... | collective-permute-start | bytes 3145736 | tf_op jit(solution)/shard_map/ppermute | solution.py:518
  25.4 33.4 %all-to-all-start = ((bf16[16,128,384]{2,1,0:T(8,128)(2,1)}), bf16[16,128,384]{2,1,0:T(8,128)(2,1)S(1)}, u32[]{:S(2)}, u32[]{:S(2)}) async-start(bf16[16,128,384]{2,1,0:T(8,128)(2,1)} %bitcast.10), calls=%async_computation | async-start | bytes 3145728 | tf_op jit(solution)/shard_map/all_to_all | solution.py:512
  33.3 1.0 copy-start.5
  37.1 21.7 %collective-permute-start.7 = (bf16[2,256,1024]{2,1,0:T(8,128)(2,1)}, bf16[2,256,1024]{2,1,0:T(8,128)(2,1)S(1)}, u32[]{:S(2)}, u32[]{:S(2)}) collective-permute-start(bf16[2,256,1024]{2,1,0:T(8,128)(2,1)} %relay_kernel.1), channel_id=1, source_target_pairs={{0,96},{96,0},{32,64},{64,32},{16,48},{48,16},{80,112},{112,80},{1... | collective-permute-start | bytes 3145736 | tf_op jit(solution)/shard_map/ppermute | solution.py:523
  58.8 4.4 %copy-start.6 = (bf16[16,128,384]{2,1,0:T(8,128)(2,1)}, bf16[16,128,384]{2,1,0:T(8,128)(2,1)S(1)}, u32[]{:S(2)}) copy-start(bf16[16,128,384]{2,1,0:T(8,128)(2,1)S(1)} %all-to-all-done) | copy-start | bytes 4718596
  58.8 1.3 copy-start.8
  58.9 10.2 %collective-permute-start.8 = (bf16[2048,128]{1,0:T(8,128)(2,1)S(1)}, bf16[2048,128]{1,0:T(8,128)(2,1)}, u32[]{:S(2)}, u32[]{:S(2)}) collective-permute-start(bf16[2048,128]{1,0:T(8,128)(2,1)S(1)} %slice.36), channel_id=1, source_target_pairs={{0,16},{16,0},{1,17},{17,1},{2,18},{18,2},{3,19},{19,3},{4,20},{20... | collective-permute-start | bytes 1572872 | tf_op jit(solution)/shard_map/ppermute | solution.py:530
  63.2 20.7 %all-to-all-start.1 = ((bf16[16,256,128]{2,1,0:T(8,128)(2,1)}), bf16[16,256,128]{2,1,0:T(8,128)(2,1)S(1)}, u32[]{:S(2)}, u32[]{:S(2)}) async-start(bf16[16,256,128]{2,1,0:T(8,128)(2,1)} %bitcast.46), calls=%async_computation.1 | async-start | bytes 2097152 | tf_op jit(solution)/shard_map/all_to_all | solution.py:549
  83.9 3.8 %copy-start.7 = (bf16[16,256,128]{2,1,0:T(8,128)(2,1)}, bf16[16,256,128]{2,1,0:T(8,128)(2,1)S(1)}, u32[]{:S(2)}) copy-start(bf16[16,256,128]{2,1,0:T(8,128)(2,1)S(1)} %all-to-all-done.1) | copy-start | bytes 3145732
  84.0 3.8 %collective-permute-start.9 = (bf16[4096,128]{1,0:T(8,128)(2,1)S(1)}, bf16[4096,128]{1,0:T(8,128)(2,1)S(1)}, u32[]{:S(2)}, u32[]{:S(2)}) collective-permute-start(bf16[4096,128]{1,0:T(8,128)(2,1)S(1)} %bitcast.51), channel_id=1, source_target_pairs={{0,16},{16,0},{1,17},{17,1},{2,18},{18,2},{3,19},{19,3},{4,20},{20... | collective-permute-start | bytes 3145736 | tf_op jit(solution)/shard_map/ppermute | solution.py:553
  87.7 1.0 copy-start.11
  115.5 22.7 %all-to-all-start.2 = ((bf16[16,128,256]{2,1,0:T(8,128)(2,1)}), bf16[16,128,256]{2,1,0:T(8,128)(2,1)S(1)}, u32[]{:S(2)}, u32[]{:S(2)}) async-start(bf16[16,128,256]{2,1,0:T(8,128)(2,1)} %bitcast.53), calls=%async_computation.2 | async-start | bytes 2097152 | tf_op jit(solution)/shard_map/all_to_all | solution.py:556
  138.2 3.8 %copy-start.4 = (bf16[16,128,256]{2,1,0:T(8,128)(2,1)}, bf16[16,128,256]{2,1,0:T(8,128)(2,1)S(1)}, u32[]{:S(2)}) copy-start(bf16[16,128,256]{2,1,0:T(8,128)(2,1)S(1)} %all-to-all-done.2) | copy-start | bytes 3145732
  138.3 3.7 %collective-permute-start.10 = (bf16[8,128,256]{2,1,0:T(8,128)(2,1)S(1)}, bf16[8,128,256]{2,1,0:T(8,128)(2,1)S(1)}, u32[]{:S(2)}, u32[]{:S(2)}) collective-permute-start(bf16[8,128,256]{2,1,0:T(8,128)(2,1)S(1)} %dynamic-slice_bitcast_fusion), channel_id=1, source_target_pairs={{0,16},{16,0},{1,17},{17,1},{2,18},{18,2},{3,19},{19,3},{4,20},{20... | collective-permute-start | bytes 1572872 | tf_op jit(solution)/shard_map/ppermute | solution.py:560
  142.0 0.8 copy-start.9

commit v7 on v6

--- a/solution.py
+++ b/solution.py
@@ -24,6 +24,15 @@
 NEAR = [(0, 1), (1, 0), (2, 3), (3, 2)]
 FAR = [(0, 3), (3, 0), (1, 2), (2, 1)]
 SEQ = ("z", "y")
+
+
+def joint(step, crossed):
+    keys, values = (NEAR, FAR) if step == 0 else (FAR, NEAR)
+    return [(2 * i + crossed, 2 * j) for i, j in keys] + [
+        (2 * i + 1 - crossed, 2 * j + 1) for i, j in values
+    ]
+
+
 NT = (((1,), (1,)), ((), ()))
 ROOM = 56 * 1024 * 1024
 
@@ -126,61 +135,40 @@
 
 def held_at(x, core, group):
     chip = lax.div(group, 2)
-    here = chip == x
-    other = jnp.where(core == 0, NEAR_OF(x), FAR_OF(x))
-    own = jnp.where(here, 0, 1 + core)
-    mate = jnp.where(here, 3, 4)
-    found = jnp.where(lax.rem(group, 2) == core, own, mate)
-    return jnp.where(here | (chip == other), found, 5)
-
-
-def NEAR_OF(x):
+    other = jnp.where(core == 0, near_of(x), far_of(x))
+    found = jnp.where(lax.rem(group, 2) == core, 0, 2) + jnp.where(chip == x, 0, 1)
+    return jnp.where((chip == x) | (chip == other), found, 4)
+
+
+def near_of(x):
     return x + 1 - 2 * lax.rem(x, 2)
 
 
-def FAR_OF(x):
+def far_of(x):
     return 3 - x
 
 
-def swap_kernel(spot, own, a_one, b_one, out, sems):
-    core = spot[1]
-    pltpu.make_async_copy(own.at[1 - core], out.at[0], sems.at[0]).start()
-
-    @pl.when(core == 0)
-    def _():
-        pltpu.make_async_copy(b_one, out.at[1], sems.at[1]).start()
-
-    @pl.when(core != 0)
-    def _():
-        pltpu.make_async_copy(a_one, out.at[1], sems.at[1]).start()
-
-    for item in range(2):
-        pltpu.make_async_copy(b_one, out.at[item], sems.at[item]).wait()
-
-
-def relay_kernel(spot, owner, own, a_one, b_one, mate, out, sems):
+def relay_kernel(spot, owner, own, same, flip, cross, out, sems):
     x, core = spot[0], spot[1]
-    to = jnp.where(core == 0, FAR_OF(x), NEAR_OF(x))
+    to = jnp.where(core == 0, far_of(x), near_of(x))
     for item in range(2):
         code = held_at(x, core, owner[2 * to + item])
-        sources = (own.at[core], a_one, b_one, mate.at[0], mate.at[1])
-        for place, source in enumerate(sources):
-            chosen = code == place if place else (code == 0) | (code == 5)
+        for place, source in enumerate((own, same, flip, cross)):
+            chosen = code == place if place else (code == 0) | (code == 4)
 
             @pl.when(chosen)
             def _(source=source):
                 pltpu.make_async_copy(source, out.at[item], sems.at[item]).start()
 
     for item in range(2):
-        pltpu.make_async_copy(a_one, out.at[item], sems.at[item]).wait()
-
-
-def settle_kernel(spot, owner, own, a_one, b_one, mate, two, out, sems):
+        pltpu.make_async_copy(own, out.at[item], sems.at[item]).wait()
+
+
+def settle_kernel(spot, owner, own, same, flip, cross, two, out, sems):
     x, core = spot[0], spot[1]
     for pack in range(2):
         code = held_at(x, core, owner[2 * x + pack])
-        sources = (own.at[core], a_one, b_one, mate.at[0], mate.at[1], two.at[pack])
-        for place, source in enumerate(sources):
+        for place, source in enumerate((own, same, flip, cross, two.at[pack])):
 
             @pl.when(code == place)
             def _(source=source):
@@ -192,7 +180,7 @@
     for pack in range(2):
         for e in range(KVH):
             pltpu.make_async_copy(
-                a_one.at[:, pl.ds(0, HD)], out.at[pack, e], sems.at[pack, e]
+                own.at[:, pl.ds(0, HD)], out.at[pack, e], sems.at[pack, e]
             ).wait()
 
 
@@ -492,9 +480,12 @@
     rows_mate = lax.ppermute(rows, "core", FLIP)
     raw_mate = tuple(lax.ppermute(part, "core", FLIP) for part in raw)
 
-    own = stem_kv[0]
-    a_one = lax.ppermute(own[0], "x", NEAR)
-    b_one = lax.ppermute(own[1], "x", FAR)
+    stem = stem_kv[0]
+    own = lax.dynamic_index_in_dim(stem, core, 0, keepdims=False)
+    given = lax.dynamic_index_in_dim(stem, 1 - core, 0, keepdims=False)
+    same = lax.ppermute(own, ("x", "core"), joint(0, 0))
+    cross = lax.ppermute(given, ("x", "core"), joint(0, 1))
+    flip = lax.ppermute(given, "core", FLIP)
 
     both = jnp.stack([rows, rows_mate])
     linked = jax.vmap(ancestry)(both[:, pack_len:])
@@ -512,19 +503,11 @@
     arrived = lax.all_to_all(
         sent.reshape(16, tok, 3 * HD), SEQ, split_axis=0, concat_axis=0, tiled=True
     ).reshape(pack_len, 3 * HD)
-    a_one, b_one, sent = lax.optimization_barrier((a_one, b_one, sent))
-
-    passed = moved(swap_kernel, own.shape, (2,), (here,), (own, a_one, b_one))
-    mate = lax.ppermute(passed, "core", FLIP)
-
-    wanted = moved(
-        relay_kernel, own.shape, (2,), (here, stem_owner), (own, a_one, b_one, mate)
-    )
-    two = lax.ppermute(
-        wanted,
-        ("x", "core"),
-        [(2 * i, 2 * j) for i, j in FAR] + [(2 * i + 1, 2 * j + 1) for i, j in NEAR],
-    )
+    same, cross, flip, sent = lax.optimization_barrier((same, cross, flip, sent))
+
+    held = (own, same, flip, cross)
+    wanted = moved(relay_kernel, stem.shape, (2,), (here, stem_owner), held)
+    two = lax.ppermute(wanted, ("x", "core"), joint(1, 0))
     both, linked, _ = lax.optimization_barrier((both, linked, wanted))
     two, arrived = lax.optimization_barrier((two, arrived))
     pair = lax.ppermute(arrived[:, 2 * HD :], "core", FLIP)
@@ -541,11 +524,11 @@
 
     stems = moved(
         settle_kernel,
-        (2, KVH, own.shape[1], HD),
+        (2, KVH, stem.shape[1], HD),
         (2, KVH),
         (here, stem_owner),
-        (own, a_one, b_one, mate, two),
-    ).reshape(16, own.shape[1], HD)
+        held + (two,),
+    ).reshape(16, stem.shape[1], HD)
     mine = lax.all_to_all(stems, SEQ, split_axis=0, concat_axis=0, tiled=True).reshape(STEM, HD)
     arrived, pair, _ = lax.optimization_barrier((arrived, pair, stems))
     partial = pack_part(core_row, seen, arrived, pair, q_side, k_side)

time: 145 us -> 132 us (0.910)
  waiting for transfers between devices: 46.9 us -> 22.2 us
  blocking collectives: 0 us -> 24.3 us
  starting transfers between devices: 29.7 us -> 21.1 us
  Pallas kernels: 55 us -> 51.3 us
    all_to_all x0 -> x1, blocking collectives: none -> 24.3 us  [shards(): lax.all_to_all(mixed.reshape(16, tok, 2 * HD), SEQ, split_axis=0, concat_...]
    all_to_all x1 -> x0, waiting for transfers between devices: 16.3 us -> none  [shards(): lax.all_to_all(mixed.reshape(16, tok, 2 * HD), SEQ, split_axis=0, concat_...]
    all_to_all x1, waiting for transfers between devices: 18.5 us -> 7.17 us  [shards(): lax.all_to_all(sent.reshape(16, tok, 3 * HD), SEQ, split_axis=0, concat_a...]
    all_to_all x1 -> x0, starting transfers between devices: 6.38 us -> none  [shards(): lax.all_to_all(mixed.reshape(16, tok, 2 * HD), SEQ, split_axis=0, concat_...]
    pallas_call x3 -> x2, Pallas kernels: 8.85 us -> 5.99 us  [moved(): pl.pallas_call(kernel, out_shape=jax.ShapeDtypeStruct(shape, jnp.bfloat16...]
    ppermute x4, waiting for transfers between devices: 8.19 us -> 10.7 us  [the longest x1 10.7 us: shards(): two = lax.ppermute(wanted, ('x', 'core'), joint(1, 0))]
    ppermute x4, starting transfers between devices: 4.77 us -> 3.28 us  [the longest x1 1.41 us: shards(): flip = lax.ppermute(given, 'core', FLIP)]
  transfers between devices with their start and end apart: 14 -> 13, of which waited for: 6 -> 5; matrix products, arithmetic and copies ran while one was open for 7% -> 5% of each run, Pallas kernels for 16% -> 15%
where the time goes in v7:
time: 132 us; the launch traced here: 131 us
  Pallas kernels  51.3 us (39%)
  blocking collectives  24.3 us (18%)
  waiting for transfers between devices  22.2 us (17%)
  starting transfers between devices  21.1 us (16%)
  local copies, waits for them, and re-layouts  5.73 us (4%)
  other arithmetic  3.48 us (3%)
  matrix products  3.03 us (2%)
    pallas_call x1, Pallas kernels, stem_part(): pl.pallas_call(stem_kernel, out_shape=jax.ShapeDtypeStruct((pack, 2 * HD)...  26.8 us
    all_to_all x1, blocking collectives, shards(): lax.all_to_all(mixed.reshape(16, tok, 2 * HD), SEQ, split_axis=0, concat_...  24.3 us
    pallas_call x1, Pallas kernels, pack_part(): pl.pallas_call(pack_kernel, out_shape=jax.ShapeDtypeStruct((2, pack, 2 *...  14.1 us
    ppermute x1, waiting for transfers between devices, shards(): two = lax.ppermute(wanted, ('x', 'core'), joint(1, 0))  10.7 us
    all_to_all x1, starting transfers between devices, shards(): lax.all_to_all(sent.reshape(16, tok, 3 * HD), SEQ, split_axis=0, concat_a...  7.77 us
    all_to_all x1, waiting for transfers between devices, shards(): lax.all_to_all(sent.reshape(16, tok, 3 * HD), SEQ, split_axis=0, concat_a...  7.17 us
    pallas_call x2, Pallas kernels, moved(): pl.pallas_call(kernel, out_shape=jax.ShapeDtypeStruct(shape, jnp.bfloat16...  5.99 us
    all_to_all x1, starting transfers between devices, shards(): lax.all_to_all(stems, SEQ, split_axis=0, concat_axis=0, tiled=True)  3.75 us
  transfers between devices with their start and end apart: 13, of which 5 were waited for; matrix products, arithmetic and copies ran while one was open for 5% of the time, Pallas kernels for 15%

profile of v7, /device:TPU:1, one launch (start us, length us, event | category | flops | bytes accessed | tf_op | source)
XLA Modules:
  0.0 131.4 jit_solution(13343558103897367267)
XLA Ops:
  0.0 2.4 %dynamic-slice_bitcast_fusion.1 = (bf16[256,1024]{1,0:T(8,128)(2,1)}, bf16[256,1024]{1,0:T(8,128)(2,1)}) fusion(bf16[1,2,256,1024]{3,2,1,0:T(8,128)(2,1)} %param.11, s32[]{:T(128)S(6)} %select_n.52, s32[]{:T(128)S(6)} %select_n.51), kind=kLoop, calls=%fused_computation.27 | loop fusion | bytes 2097160 | tf_op jit(solution)/shard_map/jit(dynamic_index_in_dim)/squeeze | solution.py:485
  2.4 1.4 %collective-permute-start.2 = (bf16[256,1024]{1,0:T(8,128)(2,1)}, bf16[256,1024]{1,0:T(8,128)(2,1)}, u32[]{:S(2)}, u32[]{:S(2)}) collective-permute-start(bf16[256,1024]{1,0:T(8,128)(2,1)} %get-tuple-element.31), channel_id=1, source_target_pairs={{0,16},{16,0},{1,17},{17,1},{2,18},{18,2},{3,19},{19,3},{4,20},{20... | collective-permute-start | bytes 1572872 | tf_op jit(solution)/shard_map/ppermute | solution.py:488
  3.8 1.2 collective-permute-start.1
  5.0 1.9 %collective-permute-start.6 = (s32[2064]{0:T(1024)S(1)}, s32[2064]{0:T(1024)S(1)}, u32[]{:S(2)}, u32[]{:S(2)}) collective-permute-start(s32[2064]{0:T(1024)S(1)} %pad_add_fusion.1), channel_id=1, source_target_pairs={{0,16},{16,0},{1,17},{17,1},{2,18},{18,2},{3,19},{19,3},{4,20},{20... | collective-permute-start | bytes 24776 | tf_op jit(solution)/shard_map/ppermute | solution.py:480
  7.0 0.4 collective-permute-start.5
  7.7 0.3 collective-permute-start.3
  9.3 0.3 collective-permute-start
  9.7 0.5 fusion.23
  10.4 2.4 %turn.1 = bf16[2,8,128,384]{3,2,1,0:T(8,128)(2,1)} custom-call(s32[2]{0:T(128)S(1)} %pad_add_fusion.2.spot, bf16[128,4096]{1,0:T(8,128)(2,1)S(1)} %bitcast.35, bf16[128,1024]{1,0:T(8,128)(2,1)S(1)} %bitcast.37, bf16[128,1024]{1,0:T(8,128)(2,1)S(1)} %bitcast.39, bf16[128,4096]{1,0:T(8,128)(2,1)S(1)} %collective-permute-done.3.q_mate, ...), custom_call_target="tpu_custom_call" | custom-call | tf_op jit(solution)/shard_map/turn/pallas_call | solution.py:122
  12.8 7.8 %all-to-all-start = ((bf16[16,128,384]{2,1,0:T(8,128)(2,1)}), bf16[16,128,384]{2,1,0:T(8,128)(2,1)S(1)}, u32[]{:S(2)}, u32[]{:S(2)}) async-start(bf16[16,128,384]{2,1,0:T(8,128)(2,1)} %bitcast.9), calls=%async_computation | async-start | bytes 3145728 | tf_op jit(solution)/shard_map/all_to_all | solution.py:503
  20.6 2.9 %relay_kernel.1 = bf16[2,256,1024]{2,1,0:T(8,128)(2,1)} custom-call(s32[2]{0:T(128)} %copy-done.3, s32[8]{0:T(128)} %owner.3, bf16[256,1024]{1,0:T(8,128)(2,1)} %get-tuple-element.32.own, bf16[256,1024]{1,0:T(8,128)(2,1)} %collective-permute-done.same, bf16[256,1024]{1,0:T(8,128)(2,1)} %collective-permute-done.2.flip, ...), custom_call_target="tpu_custom_call" | custom-call | tf_op jit(solution)/shard_map/relay_kernel/pallas_call | solution.py:188
  23.9 0.6 broadcast.78
  24.5 0.6 fusion.42
  25.1 0.3 convert_reduce_fusion
  25.5 1.5 %convolution_convert_fusion.qb_ref = bf16[2048,128]{1,0:T(8,128)(2,1)} fusion(s32[2048]{0:T(1024)S(1)} %bitcast.50, f32[16,16]{0,1:T(8,128)S(1)} %fusion.33), kind=kOutput, calls=%fused_computation | convolution fusion | flops 403177472 | bytes 533504 | tf_op jit(solution)/shard_map/dot_general | solution.py:520
  27.0 10.7 %collective-permute-done.7.two = bf16[2,256,1024]{2,1,0:T(8,128)(2,1)S(1)} collective-permute-done((bf16[2,256,1024]{2,1,0:T(8,128)(2,1)}, bf16[2,256,1024]{2,1,0:T(8,128)(2,1)S(1)}, u32[]{:S(2)}, u32[]{:S(2)}) %collective-permute-start.7) | collective-permute-done | bytes 1048608 | tf_op jit(solution)/shard_map/ppermute | solution.py:510
  37.8 7.2 %all-to-all-done = bf16[16,128,384]{2,1,0:T(8,128)(2,1)S(1)} async-done(((bf16[16,128,384]{2,1,0:T(8,128)(2,1)}), bf16[16,128,384]{2,1,0:T(8,128)(2,1)S(1)}, u32[]{:S(2)}, u32[]{:S(2)}) %all-to-all-start) | async-done | bytes 1572896 | tf_op jit(solution)/shard_map/all_to_all | solution.py:503
  45.0 3.1 %settle_kernel.1 = bf16[2,8,256,128]{3,2,1,0:T(8,128)(2,1)} custom-call(s32[2]{0:T(128)} %copy-done.3, s32[8]{0:T(128)} %owner.3, bf16[256,1024]{1,0:T(8,128)(2,1)} %get-tuple-element.32.own, bf16[256,1024]{1,0:T(8,128)(2,1)} %collective-permute-done.same, bf16[256,1024]{1,0:T(8,128)(2,1)} %collective-permute-done.2.flip, ...), custom_call_target="tpu_custom_call" | custom-call | tf_op jit(solution)/shard_map/settle_kernel/pallas_call | solution.py:188
  48.1 3.8 %all-to-all-start.1 = ((bf16[16,256,128]{2,1,0:T(8,128)(2,1)}), bf16[16,256,128]{2,1,0:T(8,128)(2,1)S(1)}, u32[]{:S(2)}, u32[]{:S(2)}) async-start(bf16[16,256,128]{2,1,0:T(8,128)(2,1)} %bitcast.42), calls=%async_computation.1 | async-start | bytes 2097152 | tf_op jit(solution)/shard_map/all_to_all | solution.py:532
  51.9 1.6 %collective-permute-start.8 = (bf16[2048,128]{1,0:T(8,128)(2,1)S(1)}, bf16[2048,128]{1,0:T(8,128)(2,1)S(1)}, u32[]{:S(2)}, u32[]{:S(2)}) collective-permute-start(bf16[2048,128]{1,0:T(8,128)(2,1)S(1)} %slice.26), channel_id=1, source_target_pairs={{0,16},{16,0},{1,17},{17,1},{2,18},{18,2},{3,19},{19,3},{4,20},{20... | collective-permute-start | bytes 1572872 | tf_op jit(solution)/shard_map/ppermute | solution.py:513
  53.5 0.8 fusion.18.seen
  54.3 1.1 select_convert_fusion.kb_ref
  55.4 0.8 copy-done.13
  56.2 14.1 %pack_part.1.part_ref = f32[2,2048,256]{2,1,0:T(8,128)} custom-call(s32[1]{0:T(128)} %bitcast.core, s32[4,4]{1,0:T(4,128)} %fusion.18.seen, bf16[2048,384]{1,0:T(8,128)(2,1)} %bitcast.44, bf16[2048,384]{1,0:T(8,128)(2,1)} %bitcast.45, bf16[2048,128]{1,0:T(8,128)(2,1)} %copy-done.13, bf16[2048,128]{1,0:T(8,128)(2,1)} %convolution_convert_fusion.qb_ref, ...), custom_call_target="tpu_custom_call" | custom-call | flops 4294967296 | bytes 8388608 | tf_op jit(solution)/shard_map/pack_part/pallas_call | solution.py:304
  70.6 2.6 %collective-permute-done.9.other_ref = bf16[4096,128]{1,0:T(8,128)(2,1)S(1)} collective-permute-done((bf16[4096,128]{1,0:T(8,128)(2,1)S(1)}, bf16[4096,128]{1,0:T(8,128)(2,1)S(1)}, u32[]{:S(2)}, u32[]{:S(2)}) %collective-permute-start.9) | collective-permute-done | bytes 1048608 | tf_op jit(solution)/shard_map/ppermute | solution.py:536
  73.3 1.0 copy-done.12
  74.3 26.8 %stem_part.1 = bf16[2048,256]{1,0:T(8,128)(2,1)} custom-call(s32[1]{0:T(128)} %bitcast.core, bf16[2048,384]{1,0:T(8,128)(2,1)} %bitcast.46, bf16[4096,128]{1,0:T(8,128)(2,1)} %bitcast.48, bf16[4096,128]{1,0:T(8,128)(2,1)} %copy-done.12, f32[2,2048,256]{2,1,0:T(8,128)} %pack_part.1.part_ref), custom_call_target="tpu_custom_call" | custom-call | flops 8589934592 | bytes 8388608 | tf_op jit(solution)/shard_map/stem_part/pallas_call | solution.py:411
  101.0 24.3 %all_to_all.15 = bf16[16,128,256]{2,1,0:T(8,128)(2,1)S(1)} all-to-all(bf16[16,128,256]{2,1,0:T(8,128)(2,1)} %bitcast.49), channel_id=1, replica_groups=mesh['x'=4,'core'=2,'z'=4,'y'=4] {'z','y'}, dimensions={0} | all-to-all | bytes 2097152 | tf_op jit(solution)/shard_map/all_to_all | solution.py:539
  125.4 1.6 %collective-permute-start.10 = (bf16[8,128,256]{2,1,0:T(8,128)(2,1)S(1)}, bf16[8,128,256]{2,1,0:T(8,128)(2,1)S(1)}, u32[]{:S(2)}, u32[]{:S(2)}) collective-permute-start(bf16[8,128,256]{2,1,0:T(8,128)(2,1)S(1)} %dynamic-slice_bitcast_fusion), channel_id=1, source_target_pairs={{0,16},{16,0},{1,17},{17,1},{2,18},{18,2},{3,19},{19,3},{4,20},{20... | collective-permute-start | bytes 1572872 | tf_op jit(solution)/shard_map/ppermute | solution.py:543
  127.0 1.5 %collective-permute-done.10.other_ref = bf16[8,128,256]{2,1,0:T(8,128)(2,1)S(1)} collective-permute-done((bf16[8,128,256]{2,1,0:T(8,128)(2,1)S(1)}, bf16[8,128,256]{2,1,0:T(8,128)(2,1)S(1)}, u32[]{:S(2)}, u32[]{:S(2)}) %collective-permute-start.10) | collective-permute-done | bytes 524320 | tf_op jit(solution)/shard_map/ppermute | solution.py:543
  128.6 0.8 copy-done.8
  129.4 2.0 %gather.1 = bf16[128,4096]{1,0:T(8,128)(2,1)} custom-call(s32[1]{0:T(128)} %bitcast.core, bf16[2,8,128,256]{3,2,1,0:T(8,128)(2,1)} %bitcast.41, bf16[8,128,256]{2,1,0:T(8,128)(2,1)} %copy-done.8), custom_call_target="tpu_custom_call" | custom-call | tf_op jit(solution)/shard_map/gather/pallas_call | solution.py:453
  (66 shorter events, 2.6 us)
Async XLA Ops:
  0.0 9.7 %copy-start.10 = (f32[64]{0:T(128)S(1)}, f32[64]{0:T(128)}, u32[]{:S(2)}) copy-start(f32[64]{0:T(128)} %constant.81.clone) | copy-start | bytes 772
  0.0 5.0 %copy-start.11 = (s32[1,16]{1,0:T(1,128)S(1)}, s32[1,16]{1,0:T(1,128)}, u32[]{:S(2)}) copy-start(s32[1,16]{1,0:T(1,128)} %param.13) | copy-start | bytes 196
  0.0 5.0 %copy-start.9 = (s32[1,2048]{1,0:T(1,128)S(1)}, s32[1,2048]{1,0:T(1,128)}, u32[]{:S(2)}) copy-start(s32[1,2048]{1,0:T(1,128)} %param.12) | copy-start | bytes 24580
  0.0 6.9 %copy-start.1 = (bf16[1,128,1024]{2,1,0:T(8,128)(2,1)S(1)}, bf16[1,128,1024]{2,1,0:T(8,128)(2,1)}, u32[]{:S(2)}) copy-start(bf16[1,128,1024]{2,1,0:T(8,128)(2,1)} %param.9) | copy-start | bytes 786436
  0.0 7.0 %copy-start.2 = (bf16[1,128,1024]{2,1,0:T(8,128)(2,1)S(1)}, bf16[1,128,1024]{2,1,0:T(8,128)(2,1)}, u32[]{:S(2)}) copy-start(bf16[1,128,1024]{2,1,0:T(8,128)(2,1)} %param.10) | copy-start | bytes 786436
  0.0 7.7 %copy-start = (bf16[1,128,4096]{2,1,0:T(8,128)(2,1)S(1)}, bf16[1,128,4096]{2,1,0:T(8,128)(2,1)}, u32[]{:S(2)}) copy-start(bf16[1,128,4096]{2,1,0:T(8,128)(2,1)} %param.8) | copy-start | bytes 3145732
  2.4 18.2 %collective-permute-start.2 = (bf16[256,1024]{1,0:T(8,128)(2,1)}, bf16[256,1024]{1,0:T(8,128)(2,1)}, u32[]{:S(2)}, u32[]{:S(2)}) collective-permute-start(bf16[256,1024]{1,0:T(8,128)(2,1)} %get-tuple-element.31), channel_id=1, source_target_pairs={{0,16},{16,0},{1,17},{17,1},{2,18},{18,2},{3,19},{19,3},{4,20},{20... | collective-permute-start | bytes 1572872 | tf_op jit(solution)/shard_map/ppermute | solution.py:488
  3.8 16.8 %collective-permute-start.1 = (bf16[256,1024]{1,0:T(8,128)(2,1)}, bf16[256,1024]{1,0:T(8,128)(2,1)}, u32[]{:S(2)}, u32[]{:S(2)}) collective-permute-start(bf16[256,1024]{1,0:T(8,128)(2,1)} %get-tuple-element.31), channel_id=1, source_target_pairs={{16,32},{48,0},{80,96},{112,64},{0,112},{96,16},{32,80},{64,48},{1... | collective-permute-start | bytes 1572872 | tf_op jit(solution)/shard_map/ppermute | solution.py:487
  5.0 2.7 %collective-permute-start.6 = (s32[2064]{0:T(1024)S(1)}, s32[2064]{0:T(1024)S(1)}, u32[]{:S(2)}, u32[]{:S(2)}) collective-permute-start(s32[2064]{0:T(1024)S(1)} %pad_add_fusion.1), channel_id=1, source_target_pairs={{0,16},{16,0},{1,17},{17,1},{2,18},{18,2},{3,19},{19,3},{4,20},{20... | collective-permute-start | bytes 24776 | tf_op jit(solution)/shard_map/ppermute | solution.py:480
  6.9 2.5 %collective-permute-start.4 = (bf16[128,1024]{1,0:T(8,128)(2,1)S(1)}, bf16[128,1024]{1,0:T(8,128)(2,1)S(1)}, u32[]{:S(2)}, u32[]{:S(2)}) collective-permute-start(bf16[128,1024]{1,0:T(8,128)(2,1)S(1)} %bitcast.36), channel_id=1, source_target_pairs={{0,16},{16,0},{1,17},{17,1},{2,18},{18,2},{3,19},{19,3},{4,20},{20... | collective-permute-start | bytes 786440 | tf_op jit(solution)/shard_map/ppermute | solution.py:481
  7.0 3.4 %collective-permute-start.5 = (bf16[128,1024]{1,0:T(8,128)(2,1)S(1)}, bf16[128,1024]{1,0:T(8,128)(2,1)S(1)}, u32[]{:S(2)}, u32[]{:S(2)}) collective-permute-start(bf16[128,1024]{1,0:T(8,128)(2,1)S(1)} %bitcast.38), channel_id=1, source_target_pairs={{0,16},{16,0},{1,17},{17,1},{2,18},{18,2},{3,19},{19,3},{4,20},{20... | collective-permute-start | bytes 786440 | tf_op jit(solution)/shard_map/ppermute | solution.py:481
  7.5 5.3 %copy-start.3 = (s32[2]{0:T(128)}, s32[2]{0:T(128)S(1)}, u32[]{:S(2)}) copy-start(s32[2]{0:T(128)S(1)} %pad_add_fusion.2.spot) | copy-start | bytes 28
  7.7 2.7 %collective-permute-start.3 = (bf16[128,4096]{1,0:T(8,128)(2,1)S(1)}, bf16[128,4096]{1,0:T(8,128)(2,1)S(1)}, u32[]{:S(2)}, u32[]{:S(2)}) collective-permute-start(bf16[128,4096]{1,0:T(8,128)(2,1)S(1)} %bitcast.34), channel_id=1, source_target_pairs={{0,16},{16,0},{1,17},{17,1},{2,18},{18,2},{3,19},{19,3},{4,20},{20... | collective-permute-start | bytes 3145736 | tf_op jit(solution)/shard_map/ppermute | solution.py:481
  9.3 11.3 %collective-permute-start = (bf16[256,1024]{1,0:T(8,128)(2,1)}, bf16[256,1024]{1,0:T(8,128)(2,1)}, u32[]{:S(2)}, u32[]{:S(2)}) collective-permute-start(bf16[256,1024]{1,0:T(8,128)(2,1)} %get-tuple-element.32.own), channel_id=1, source_target_pairs={{0,32},{32,0},{64,96},{96,64},{16,112},{112,16},{48,80},{80,48},{1... | collective-permute-start | bytes 1572872 | tf_op jit(solution)/shard_map/ppermute | solution.py:486
  12.8 32.1 %all-to-all-start = ((bf16[16,128,384]{2,1,0:T(8,128)(2,1)}), bf16[16,128,384]{2,1,0:T(8,128)(2,1)S(1)}, u32[]{:S(2)}, u32[]{:S(2)}) async-start(bf16[16,128,384]{2,1,0:T(8,128)(2,1)} %bitcast.9), calls=%async_computation | async-start | bytes 3145728 | tf_op jit(solution)/shard_map/all_to_all | solution.py:503
  23.5 14.2 %collective-permute-start.7 = (bf16[2,256,1024]{2,1,0:T(8,128)(2,1)}, bf16[2,256,1024]{2,1,0:T(8,128)(2,1)S(1)}, u32[]{:S(2)}, u32[]{:S(2)}) collective-permute-start(bf16[2,256,1024]{2,1,0:T(8,128)(2,1)} %relay_kernel.1), channel_id=1, source_target_pairs={{0,96},{96,0},{32,64},{64,32},{16,48},{48,16},{80,112},{112,80},{1... | collective-permute-start | bytes 3145736 | tf_op jit(solution)/shard_map/ppermute | solution.py:510
  37.8 7.2 %copy-start.6 = (bf16[2,256,1024]{2,1,0:T(8,128)(2,1)}, bf16[2,256,1024]{2,1,0:T(8,128)(2,1)S(1)}, u32[]{:S(2)}) copy-start(bf16[2,256,1024]{2,1,0:T(8,128)(2,1)S(1)} %collective-permute-done.7.two) | copy-start | bytes 3145732
  44.9 6.9 %copy-start.5 = (bf16[16,128,384]{2,1,0:T(8,128)(2,1)}, bf16[16,128,384]{2,1,0:T(8,128)(2,1)S(1)}, u32[]{:S(2)}) copy-start(bf16[16,128,384]{2,1,0:T(8,128)(2,1)S(1)} %all-to-all-done) | copy-start | bytes 4718596
  48.1 22.2 %all-to-all-start.1 = ((bf16[16,256,128]{2,1,0:T(8,128)(2,1)}), bf16[16,256,128]{2,1,0:T(8,128)(2,1)S(1)}, u32[]{:S(2)}, u32[]{:S(2)}) async-start(bf16[16,256,128]{2,1,0:T(8,128)(2,1)} %bitcast.42), calls=%async_computation.1 | async-start | bytes 2097152 | tf_op jit(solution)/shard_map/all_to_all | solution.py:532
  51.9 3.5 %collective-permute-start.8 = (bf16[2048,128]{1,0:T(8,128)(2,1)S(1)}, bf16[2048,128]{1,0:T(8,128)(2,1)S(1)}, u32[]{:S(2)}, u32[]{:S(2)}) collective-permute-start(bf16[2048,128]{1,0:T(8,128)(2,1)S(1)} %slice.26), channel_id=1, source_target_pairs={{0,16},{16,0},{1,17},{17,1},{2,18},{18,2},{3,19},{19,3},{4,20},{20... | collective-permute-start | bytes 1572872 | tf_op jit(solution)/shard_map/ppermute | solution.py:513
  55.4 0.8 copy-start.13
  70.3 3.0 %copy-start.7 = (bf16[16,256,128]{2,1,0:T(8,128)(2,1)}, bf16[16,256,128]{2,1,0:T(8,128)(2,1)S(1)}, u32[]{:S(2)}) copy-start(bf16[16,256,128]{2,1,0:T(8,128)(2,1)S(1)} %all-to-all-done.1) | copy-start | bytes 3145732
  70.3 3.0 %collective-permute-start.9 = (bf16[4096,128]{1,0:T(8,128)(2,1)S(1)}, bf16[4096,128]{1,0:T(8,128)(2,1)S(1)}, u32[]{:S(2)}, u32[]{:S(2)}) collective-permute-start(bf16[4096,128]{1,0:T(8,128)(2,1)S(1)} %bitcast.47), channel_id=1, source_target_pairs={{0,16},{16,0},{1,17},{17,1},{2,18},{18,2},{3,19},{19,3},{4,20},{20... | collective-permute-start | bytes 3145736 | tf_op jit(solution)/shard_map/ppermute | solution.py:536
  73.3 1.0 copy-start.12
  125.3 3.2 %copy-start.4 = (bf16[16,128,256]{2,1,0:T(8,128)(2,1)}, bf16[16,128,256]{2,1,0:T(8,128)(2,1)S(1)}, u32[]{:S(2)}) copy-start(bf16[16,128,256]{2,1,0:T(8,128)(2,1)S(1)} %all_to_all.15) | copy-start | bytes 3145732
  125.4 3.2 %collective-permute-start.10 = (bf16[8,128,256]{2,1,0:T(8,128)(2,1)S(1)}, bf16[8,128,256]{2,1,0:T(8,128)(2,1)S(1)}, u32[]{:S(2)}, u32[]{:S(2)}) collective-permute-start(bf16[8,128,256]{2,1,0:T(8,128)(2,1)S(1)} %dynamic-slice_bitcast_fusion), channel_id=1, source_target_pairs={{0,16},{16,0},{1,17},{17,1},{2,18},{18,2},{3,19},{19,3},{4,20},{20... | collective-permute-start | bytes 1572872 | tf_op jit(solution)/shard_map/ppermute | solution.py:543
  128.6 0.8 copy-start.8

commit v8 on v7

--- a/solution.py
+++ b/solution.py
@@ -17,6 +17,7 @@
 BARRED = -1e30
 BQ = 512
 CK = 256
+WIDE = 1024
 SCALE = HD**-0.5 * math.log2(math.e)
 SHIFT = 70.0 / SCALE
 TINY = 2.0**-16
@@ -199,49 +200,49 @@
     )(*scalars, *arrays)
 
 
-def longest(ref, rows):
-    most = jnp.zeros((1, 1), jnp.float32)
-    for at in range(0, rows, 512):
-        wide = ref[at : at + 512, :HD].astype(jnp.float32)
-        norms = jnp.sum(wide * wide, axis=1, keepdims=True)
-        most = jnp.maximum(most, jnp.max(norms, axis=0, keepdims=True))
-    return jnp.broadcast_to(jnp.sqrt(most), (8, HD))
-
-
-def stacked(q_ref):
-    return jnp.concatenate([q_ref[:, :HD], q_ref[:, HD : 2 * HD]], axis=0)
+def flipped_dot(left, right):
+    return lax.dot_general(left, right, NT, preferred_element_type=jnp.float32)
+
+
+def fill(core, mine_ref, other_ref, ka, vt, top):
+    first = core == 0
+    best = jnp.zeros((8, BQ), jnp.float32)
+    for at in range(0, mine_ref.shape[0], BQ):
+        mine = mine_ref[at : at + BQ, :]
+        other = other_ref[at : at + BQ, :]
+        key = jnp.where(first, mine, other)
+        ka[at : at + BQ, :HD] = key
+        vt[:HD, at : at + BQ] = jnp.where(first, other, mine).T
+        wide = key.astype(jnp.float32)
+        squares = (wide * wide).astype(jnp.bfloat16)
+        best = jnp.maximum(best, flipped_dot(jnp.ones((8, HD), jnp.bfloat16), squares))
+    vt[HD:, :] = jnp.ones_like(vt[HD:, :])
+    longest = jnp.max(jnp.max(best, axis=1, keepdims=True), axis=0, keepdims=True)
+    top[...] = jnp.broadcast_to(jnp.sqrt(longest), (8, HD))
+
+
+def stacked(ref):
+    return jnp.concatenate([ref[:, :HD], ref[:, HD : 2 * HD]], axis=0)
 
 
 def ceiling(rows, top):
     wide = rows.astype(jnp.float32)
-    return jnp.sqrt(jnp.sum(wide * wide, axis=1, keepdims=True)) * top * 1.02 - SHIFT
-
-
-def score(qa, ref, start, size):
-    return lax.dot_general(
-        qa[...], ref[pl.ds(start, size), :], NT, preferred_element_type=jnp.float32
-    )
-
-
-def fill(core, mine_ref, other_ref, k_side, ka, va):
-    mine = mine_ref[...]
-    other = other_ref[...]
-    first = core == 0
-    ka[:, :HD] = jnp.where(first, mine, other)
-    va[:, :HD] = jnp.where(first, other, mine)
-    ka[:, HD:] = k_side
-    va[:, HD:] = jnp.ones_like(k_side)
-
-
-def put(o_ref, total, side):
-    rows = o_ref.shape[1]
-    for head in range(o_ref.shape[0]):
-        o_ref[head, :, :HD] = total[head * rows : head * rows + rows]
-        o_ref[head, :, HD:] = side[head * rows : head * rows + rows]
+    squares = (wide * wide).astype(jnp.bfloat16)
+    norms = jnp.dot(squares, jnp.ones((HD, HD), jnp.bfloat16), preferred_element_type=jnp.float32)
+    return jnp.sqrt(norms) * top * 1.02 - SHIFT
+
+
+def shift_row(qa):
+    pick = lax.broadcasted_iota(jnp.int32, (8, 2 * HD), 1) == HD + SEGS
+    return flipped_dot(pick.astype(jnp.float32).astype(jnp.bfloat16), qa[...])
+
+
+def down(row):
+    return jnp.broadcast_to(row, (HD, row.shape[1])).T
 
 
 def pack_kernel(
-    core, seen, q_ref, mine_ref, other_ref, qb_ref, kb_ref, o_ref, qa, ka, va, top, acc
+    core, seen, q_ref, mine_ref, other_ref, qb_ref, kb_ref, o_ref, qa, ka, vt, top, acc
 ):
     qi = pl.program_id(0)
     rows = 2 * BQ
@@ -249,53 +250,56 @@
 
     @pl.when(qi == 0)
     def _():
-        fill(core[0], mine_ref, other_ref, kb_ref[...], ka, va)
-        top[...] = longest(ka, ka.shape[0])
+        fill(core[0], mine_ref, other_ref, ka, vt, top)
+        ka[:, HD:] = kb_ref[...]
 
     q_rows = stacked(q_ref)
     qa[:, :HD] = q_rows
     side = jnp.concatenate([qb_ref[...], qb_ref[...]], axis=0).astype(jnp.float32)
-    row = lax.broadcasted_iota(jnp.int32, (rows, BQ), 0)
-    ahead = lax.broadcasted_iota(jnp.int32, (rows, BQ), 1) > jnp.where(row >= BQ, row - BQ, row)
+    query = lax.broadcasted_iota(jnp.int32, (BQ, rows), 1)
+    ahead = lax.broadcasted_iota(jnp.int32, (BQ, rows), 0) > jnp.where(
+        query >= BQ, query - BQ, query
+    )
     here = pl.multiple_of(qi * BQ, BQ)
+
+    def scores(at):
+        return flipped_dot(ka[pl.ds(at, BQ), :], qa[...])
+
+    def mixed(at, weights):
+        return jnp.dot(
+            vt[:, pl.ds(at, BQ)],
+            weights.astype(jnp.bfloat16),
+            preferred_element_type=jnp.float32,
+        )
 
     def run(shift):
         qa[:, HD:] = jnp.where(lane == SEGS, shift, side).astype(jnp.bfloat16)
-        weights = jnp.where(ahead, 0.0, jnp.exp2(score(qa, ka, here, BQ) * SCALE))
-        acc[...] = jnp.dot(
-            weights.astype(jnp.bfloat16), va[pl.ds(here, BQ), :], preferred_element_type=jnp.float32
-        )
+        acc[...] = mixed(here, jnp.where(ahead, 0.0, jnp.exp2(scores(here) * SCALE)))
 
         def body(kj, carry):
             @pl.when(seen[qi, kj] > 0)
             def _():
                 at = pl.multiple_of(kj * BQ, BQ)
-                part = jnp.exp2(score(qa, ka, at, BQ) * SCALE).astype(jnp.bfloat16)
-                acc[...] += jnp.dot(
-                    part, va[pl.ds(at, BQ), :], preferred_element_type=jnp.float32
-                )
+                acc[...] += mixed(at, jnp.exp2(scores(at) * SCALE))
 
             return carry
 
         lax.fori_loop(0, qi, body, 0)
-        kept = qa[:, HD:].astype(jnp.float32)
-        shift_kept = jnp.sum(jnp.where(lane == SEGS, kept, 0.0), axis=1, keepdims=True)
-        put(o_ref, acc[:, :HD], jnp.where(lane == 1, shift_kept, acc[:, HD:]))
+        o_ref[0, : HD + 8] = acc[...]
+        o_ref[0, HD + 8 :] = shift_row(qa)
 
     run(ceiling(q_rows, top[0:1, 0:1]))
 
-    @pl.when(jnp.min(acc[:, HD:]) < TINY)
+    @pl.when(jnp.min(acc[HD:, :]) < TINY)
     def _():
         qa[:, HD:] = side.astype(jnp.bfloat16)
-        most = jnp.max(
-            jnp.where(ahead, BARRED, score(qa, ka, here, BQ)), axis=1, keepdims=True
-        )
+        most = jnp.max(jnp.where(ahead, BARRED, scores(here)), axis=0, keepdims=True)
 
         def body(kj, most):
-            part = score(qa, ka, pl.multiple_of(kj * BQ, BQ), BQ)
-            return jnp.maximum(most, jnp.max(part, axis=1, keepdims=True))
-
-        run(lax.fori_loop(0, qi, body, most))
+            part = scores(pl.multiple_of(kj * BQ, BQ))
+            return jnp.maximum(most, jnp.max(part, axis=0, keepdims=True))
+
+        run(down(lax.fori_loop(0, qi, body, most)))
 
 
 def pack_part(core, seen, arrived, other, q_side, k_side):
@@ -303,7 +307,7 @@
     once = dict(pipeline_mode=pl.Buffered(1))
     return pl.pallas_call(
         pack_kernel,
-        out_shape=jax.ShapeDtypeStruct((2, pack, 2 * HD), jnp.float32),
+        out_shape=jax.ShapeDtypeStruct((pack // BQ, HD + 16, 2 * BQ), jnp.float32),
         grid_spec=pltpu.PrefetchScalarGridSpec(
             num_scalar_prefetch=2,
             grid=(pack // BQ,),
@@ -314,13 +318,13 @@
                 pl.BlockSpec((BQ, HD), lambda i, *_: (i, 0)),
                 pl.BlockSpec((pack, HD), lambda i, *_: (0, 0), **once),
             ],
-            out_specs=pl.BlockSpec((2, BQ, 2 * HD), lambda i, *_: (0, i, 0)),
+            out_specs=pl.BlockSpec((1, HD + 16, 2 * BQ), lambda i, *_: (i, 0, 0)),
             scratch_shapes=[
                 pltpu.VMEM((2 * BQ, 2 * HD), jnp.bfloat16),
                 pltpu.VMEM((pack, 2 * HD), jnp.bfloat16),
-                pltpu.VMEM((pack, 2 * HD), jnp.bfloat16),
+                pltpu.VMEM((HD + 8, pack), jnp.bfloat16),
                 pltpu.VMEM((8, HD), jnp.float32),
-                pltpu.VMEM((2 * BQ, 2 * HD), jnp.float32),
+                pltpu.VMEM((HD + 8, 2 * BQ), jnp.float32),
             ],
         ),
         compiler_params=pltpu.CompilerParams(vmem_limit_bytes=ROOM),
@@ -331,76 +335,63 @@
     )(core, seen, arrived, arrived, other, q_side, k_side)
 
 
-def stem_kernel(core, q_ref, mine_ref, other_ref, part_ref, o_ref, qa, top, acc):
-    stem = mine_ref.shape[0]
-    heads, rows = part_ref.shape[:2]
+def stem_kernel(core, q_ref, mine_ref, other_ref, part_ref, o_ref, qa, ka, vt, top, acc):
+    stem = ka.shape[0]
     lane = lax.broadcasted_iota(jnp.int32, (1, HD), 1)
-    first = core[0] == 0
     side = jnp.broadcast_to(jnp.where(lane == SEGS, -1.0, 0.0).astype(jnp.bfloat16), (CK, HD))
-    ones = jnp.ones((CK, HD), jnp.bfloat16)
-
-    def keys(at):
-        here = pl.ds(at, CK)
-        return jnp.where(first, mine_ref[here, :], other_ref[here, :])
 
     @pl.when(pl.program_id(0) == 0)
     def _():
-        def body(step, most):
-            wide = keys(pl.multiple_of(step * CK, CK)).astype(jnp.float32)
-            norms = jnp.sum(wide * wide, axis=1, keepdims=True)
-            return jnp.maximum(most, jnp.max(norms, axis=0, keepdims=True))
-
-        most = lax.fori_loop(0, stem // CK, body, jnp.zeros((1, 1), jnp.float32))
-        top[...] = jnp.broadcast_to(jnp.sqrt(most), (8, HD))
-
-    q_rows = jnp.concatenate([q_ref[:, h * HD : h * HD + HD] for h in range(heads)], axis=0)
+        fill(core[0], mine_ref, other_ref, ka, vt, top)
+
+    q_rows = stacked(q_ref)
     qa[:, :HD] = q_rows
 
     def scores(at):
-        wide = jnp.concatenate([keys(at), side], axis=1)
-        return lax.dot_general(qa[...], wide, NT, preferred_element_type=jnp.float32)
+        return flipped_dot(jnp.concatenate([ka[pl.ds(at, CK), :], side], axis=1), qa[...])
 
     def run(shift):
         qa[:, HD:] = jnp.where(lane == SEGS, shift, 0.0).astype(jnp.bfloat16)
-        total = None
+        total, weights = None, []
         held = scores(0)
         for at in range(0, stem, CK):
             ahead = scores(at + CK) if at + CK < stem else None
-            weights = jnp.exp2(held * SCALE).astype(jnp.bfloat16)
-            here = pl.ds(at, CK)
-            wide = jnp.where(first, other_ref[here, :], mine_ref[here, :])
-            wide = jnp.concatenate([wide, ones], axis=1)
-            part = jnp.dot(weights, wide, preferred_element_type=jnp.float32)
-            total = part if total is None else total + part
+            weights.append(jnp.exp2(held * SCALE).astype(jnp.bfloat16))
+            if len(weights) * CK == WIDE:
+                part = jnp.dot(
+                    vt[:, at + CK - WIDE : at + CK],
+                    jnp.concatenate(weights, axis=0),
+                    preferred_element_type=jnp.float32,
+                )
+                total = part if total is None else total + part
+                weights = []
             held = ahead
         acc[...] = total
 
     def finish():
-        kept = qa[:, HD:].astype(jnp.float32)
-        shift = jnp.sum(jnp.where(lane == SEGS, kept, 0.0), axis=1, keepdims=True)
-        part = jnp.concatenate([part_ref[h] for h in range(heads)], axis=0)
-        before = part[:, HD + 1 : HD + 2]
+        shift = shift_row(qa)[:1]
+        before = part_ref[0, HD + 8 : HD + 9]
         most = jnp.maximum(shift, before)
         new = jnp.exp2((shift - most) * SCALE)
         old = jnp.exp2((before - most) * SCALE)
-        total = acc[:, HD : HD + 1] * new + part[:, HD : HD + 1] * old
-        mixed = (acc[:, :HD] * new + part[:, :HD] * old) / total
-        for h in range(heads):
-            o_ref[:, h * HD : h * HD + HD] = mixed[h * rows : h * rows + rows].astype(jnp.bfloat16)
+        total = acc[HD : HD + 1] * new + part_ref[0, HD : HD + 1] * old
+        out = (acc[:HD] * (new / total) + part_ref[0, :HD] * (old / total)).T
+        o_ref[:, :HD] = out[:BQ].astype(jnp.bfloat16)
+        o_ref[:, HD:] = out[BQ:].astype(jnp.bfloat16)
 
     run(ceiling(q_rows, top[0:1, 0:1]))
     finish()
 
-    @pl.when(jnp.min(acc[:, HD:]) < TINY)
+    @pl.when(jnp.min(acc[HD:, :]) < TINY)
     def _():
         qa[:, HD:] = jnp.zeros_like(q_rows)
 
         def body(step, most):
             part = scores(pl.multiple_of(step * CK, CK))
-            return jnp.maximum(most, jnp.max(part, axis=1, keepdims=True))
-
-        low = jnp.full((heads * rows, 1), BARRED, jnp.float32)
-        run(lax.fori_loop(0, stem // CK, body, low))
+            return jnp.maximum(most, jnp.max(part, axis=0, keepdims=True))
+
+        low = jnp.full((1, 2 * BQ), BARRED, jnp.float32)
+        run(down(lax.fori_loop(0, stem // CK, body, low)))
         finish()
 
 
@@ -418,20 +409,20 @@
                 pl.BlockSpec((BQ, 2 * HD), lambda i, *_: (i, 0)),
                 pl.BlockSpec((stem, HD), lambda i, *_: (0, 0), **once),
                 pl.BlockSpec((stem, HD), lambda i, *_: (0, 0), **once),
-                pl.BlockSpec((2, BQ, 2 * HD), lambda i, *_: (0, i, 0)),
+                pl.BlockSpec((1, HD + 16, 2 * BQ), lambda i, *_: (i, 0, 0)),
             ],
             out_specs=pl.BlockSpec((BQ, 2 * HD), lambda i, *_: (i, 0)),
             scratch_shapes=[
                 pltpu.VMEM((2 * BQ, 2 * HD), jnp.bfloat16),
+                pltpu.VMEM((stem, HD), jnp.bfloat16),
+                pltpu.VMEM((HD + 8, stem), jnp.bfloat16),
                 pltpu.VMEM((8, HD), jnp.float32),
-                pltpu.VMEM((2 * BQ, 2 * HD), jnp.float32),
+                pltpu.VMEM((HD + 8, 2 * BQ), jnp.float32),
             ],
         ),
         compiler_params=pltpu.CompilerParams(vmem_limit_bytes=ROOM),
         cost_estimate=pl.CostEstimate(
-            flops=8 * pack * stem * HD,
-            bytes_accessed=8 << 20,
-            transcendentals=2 * pack * stem,
+            flops=8 * pack * stem * HD, bytes_accessed=8 << 20, transcendentals=2 * pack * stem
         ),
         name="stem_part",
     )(core, arrived, mine, other, before)
@@ -509,7 +500,6 @@
     wanted = moved(relay_kernel, stem.shape, (2,), (here, stem_owner), held)
     two = lax.ppermute(wanted, ("x", "core"), joint(1, 0))
     both, linked, _ = lax.optimization_barrier((both, linked, wanted))
-    two, arrived = lax.optimization_barrier((two, arrived))
     pair = lax.ppermute(arrived[:, 2 * HD :], "core", FLIP)
 
     ours = spot // KVH == core

time: 132 us -> 121 us (0.917)
  Pallas kernels: 51.3 us -> 42.6 us
  blocking collectives: 24.3 us -> 20.4 us
    pallas_call x1, Pallas kernels: 26.8 us -> 20.2 us  [stem_part(): pl.pallas_call(stem_kernel, out_shape=jax.ShapeDtypeStruct((pack, 2 * HD)...]
    all_to_all x1, blocking collectives: 24.3 us -> 20.4 us  [shards(): lax.all_to_all(mixed.reshape(16, tok, 2 * HD), SEQ, split_axis=0, concat_...]
    pallas_call x1, Pallas kernels: 14.1 us -> 12 us  [pack_part(): pl.pallas_call(pack_kernel, out_shape=jax.ShapeDtypeStruct((pack // BQ, H...]
    ppermute x1, starting transfers between devices: 0.31 us -> 2.08 us  [shards(): other = lax.ppermute(mine, 'core', FLIP)]
    ppermute x1, starting transfers between devices: 1.85 us -> 0.09 us  [shards(): rows_mate = lax.ppermute(rows, 'core', FLIP)]
    all_to_all x1, waiting for transfers between devices: 0.01 us -> 1.64 us  [shards(): lax.all_to_all(stems, SEQ, split_axis=0, concat_axis=0, tiled=True)]
    all_to_all x1, waiting for transfers between devices: 7.17 us -> 5.65 us  [shards(): lax.all_to_all(sent.reshape(16, tok, 3 * HD), SEQ, split_axis=0, concat_a...]
    ppermute x1, starting transfers between devices: 1.2 us -> 2.6 us  [shards(): cross = lax.ppermute(given, ('x', 'core'), joint(0, 1))]
  transfers between devices with their start and end apart: 13 -> 13, of which waited for: 5 -> 7; matrix products, arithmetic and copies ran while one was open for 5% -> 6% of each run, Pallas kernels for 15% -> 17%
where the time goes in v8:
time: 121 us; the launch traced here: 120 us
  Pallas kernels  42.6 us (35%)
  waiting for transfers between devices  22.8 us (19%)
  starting transfers between devices  22.1 us (18%)
  blocking collectives  20.4 us (17%)
  local copies, waits for them, and re-layouts  5.84 us (5%)
  other arithmetic  3.44 us (3%)
  matrix products  2.99 us (2%)
    all_to_all x1, blocking collectives, shards(): lax.all_to_all(mixed.reshape(16, tok, 2 * HD), SEQ, split_axis=0, concat_...  20.4 us
    pallas_call x1, Pallas kernels, stem_part(): pl.pallas_call(stem_kernel, out_shape=jax.ShapeDtypeStruct((pack, 2 * HD)...  20.2 us
    pallas_call x1, Pallas kernels, pack_part(): pl.pallas_call(pack_kernel, out_shape=jax.ShapeDtypeStruct((pack // BQ, H...  12 us
    ppermute x1, waiting for transfers between devices, shards(): two = lax.ppermute(wanted, ('x', 'core'), joint(1, 0))  10.8 us
    all_to_all x1, starting transfers between devices, shards(): lax.all_to_all(sent.reshape(16, tok, 3 * HD), SEQ, split_axis=0, concat_a...  7.77 us
    pallas_call x2, Pallas kernels, moved(): pl.pallas_call(kernel, out_shape=jax.ShapeDtypeStruct(shape, jnp.bfloat16...  5.97 us
    all_to_all x1, waiting for transfers between devices, shards(): lax.all_to_all(sent.reshape(16, tok, 3 * HD), SEQ, split_axis=0, concat_a...  5.65 us
    all_to_all x1, starting transfers between devices, shards(): lax.all_to_all(stems, SEQ, split_axis=0, concat_axis=0, tiled=True)  3.65 us
  transfers between devices with their start and end apart: 13, of which 7 were waited for; matrix products, arithmetic and copies ran while one was open for 6% of the time, Pallas kernels for 17%

profile of v8, /device:TPU:1, one launch (start us, length us, event | category | flops | bytes accessed | tf_op | source)
XLA Modules:
  0.0 120.4 jit_solution(13182871491725366684)
XLA Ops:
  0.0 2.4 %dynamic-slice_bitcast_fusion.1 = (bf16[256,1024]{1,0:T(8,128)(2,1)}, bf16[256,1024]{1,0:T(8,128)(2,1)}) fusion(bf16[1,2,256,1024]{3,2,1,0:T(8,128)(2,1)} %param.11, s32[]{:T(128)S(6)} %select_n.53, s32[]{:T(128)S(6)} %select_n.52), kind=kLoop, calls=%fused_computation.27 | loop fusion | bytes 2097160 | tf_op jit(solution)/shard_map/jit(dynamic_index_in_dim)/squeeze | solution.py:476
  2.4 2.6 %collective-permute-start.6 = (bf16[256,1024]{1,0:T(8,128)(2,1)}, bf16[256,1024]{1,0:T(8,128)(2,1)}, u32[]{:S(2)}, u32[]{:S(2)}) collective-permute-start(bf16[256,1024]{1,0:T(8,128)(2,1)} %get-tuple-element.27), channel_id=1, source_target_pairs={{16,32},{48,0},{80,96},{112,64},{0,112},{96,16},{32,80},{64,48},{1... | collective-permute-start | bytes 1572872 | tf_op jit(solution)/shard_map/ppermute | solution.py:478
  5.0 1.1 collective-permute-start.7
  6.2 0.5 collective-permute-start
  7.0 0.7 collective-permute-done.3
  9.5 1.1 collective-permute-start.5
  10.6 0.5 fusion.23
  11.3 2.4 %turn.1 = bf16[2,8,128,384]{3,2,1,0:T(8,128)(2,1)} custom-call(s32[2]{0:T(128)S(1)} %pad_add_fusion.2.spot, bf16[128,4096]{1,0:T(8,128)(2,1)S(1)} %bitcast.35, bf16[128,1024]{1,0:T(8,128)(2,1)S(1)} %bitcast.37, bf16[128,1024]{1,0:T(8,128)(2,1)S(1)} %bitcast.39, bf16[128,4096]{1,0:T(8,128)(2,1)S(1)} %collective-permute-done.q_mate, ...), custom_call_target="tpu_custom_call" | custom-call | tf_op jit(solution)/shard_map/turn/pallas_call | solution.py:123
  13.7 7.8 %all-to-all-start = ((bf16[16,128,384]{2,1,0:T(8,128)(2,1)}), bf16[16,128,384]{2,1,0:T(8,128)(2,1)S(1)}, u32[]{:S(2)}, u32[]{:S(2)}) async-start(bf16[16,128,384]{2,1,0:T(8,128)(2,1)} %bitcast.7), calls=%async_computation | async-start | bytes 3145728 | tf_op jit(solution)/shard_map/all_to_all | solution.py:494
  21.6 2.9 %relay_kernel.1 = bf16[2,256,1024]{2,1,0:T(8,128)(2,1)} custom-call(s32[2]{0:T(128)} %copy-done.3, s32[8]{0:T(128)} %owner.3, bf16[256,1024]{1,0:T(8,128)(2,1)} %get-tuple-element.28.own, bf16[256,1024]{1,0:T(8,128)(2,1)} %collective-permute-done.5.same, bf16[256,1024]{1,0:T(8,128)(2,1)} %collective-permute-done.7.flip, ...), custom_call_target="tpu_custom_call" | custom-call | tf_op jit(solution)/shard_map/relay_kernel/pallas_call | solution.py:189
  24.9 0.5 broadcast.78
  25.4 0.6 fusion.42
  26.4 1.5 %convolution_convert_fusion.qb_ref = bf16[2048,128]{1,0:T(8,128)(2,1)} fusion(s32[2048]{0:T(1024)S(1)} %bitcast.50, f32[16,16]{0,1:T(8,128)S(1)} %fusion.33), kind=kOutput, calls=%fused_computation | convolution fusion | flops 403177472 | bytes 533504 | tf_op jit(solution)/shard_map/dot_general | solution.py:510
  27.9 10.8 %collective-permute-done.8.two = bf16[2,256,1024]{2,1,0:T(8,128)(2,1)S(1)} collective-permute-done((bf16[2,256,1024]{2,1,0:T(8,128)(2,1)}, bf16[2,256,1024]{2,1,0:T(8,128)(2,1)S(1)}, u32[]{:S(2)}, u32[]{:S(2)}) %collective-permute-start.8) | collective-permute-done | bytes 1048608 | tf_op jit(solution)/shard_map/ppermute | solution.py:501
  38.7 1.0 copy-done.6
  39.7 3.1 %settle_kernel.1 = bf16[2,8,256,128]{3,2,1,0:T(8,128)(2,1)} custom-call(s32[2]{0:T(128)} %copy-done.3, s32[8]{0:T(128)} %owner.3, bf16[256,1024]{1,0:T(8,128)(2,1)} %get-tuple-element.28.own, bf16[256,1024]{1,0:T(8,128)(2,1)} %collective-permute-done.5.same, bf16[256,1024]{1,0:T(8,128)(2,1)} %collective-permute-done.7.flip, ...), custom_call_target="tpu_custom_call" | custom-call | tf_op jit(solution)/shard_map/settle_kernel/pallas_call | solution.py:189
  42.8 5.6 %all-to-all-done = bf16[16,128,384]{2,1,0:T(8,128)(2,1)S(1)} async-done(((bf16[16,128,384]{2,1,0:T(8,128)(2,1)}), bf16[16,128,384]{2,1,0:T(8,128)(2,1)S(1)}, u32[]{:S(2)}, u32[]{:S(2)}) %all-to-all-start) | async-done | bytes 1572896 | tf_op jit(solution)/shard_map/all_to_all | solution.py:494
  48.4 3.7 %all-to-all-start.1 = ((bf16[16,256,128]{2,1,0:T(8,128)(2,1)}), bf16[16,256,128]{2,1,0:T(8,128)(2,1)S(1)}, u32[]{:S(2)}, u32[]{:S(2)}) async-start(bf16[16,256,128]{2,1,0:T(8,128)(2,1)} %bitcast.42), calls=%async_computation.1 | async-start | bytes 2097152 | tf_op jit(solution)/shard_map/all_to_all | solution.py:522
  52.2 0.7 collective-permute-start.4
  52.9 0.8 fusion.18.seen
  53.7 1.1 select_convert_fusion.kb_ref
  54.8 12.0 %pack_part.1.part_ref = f32[4,144,1024]{2,1,0:T(8,128)} custom-call(s32[1]{0:T(128)} %bitcast.core, s32[4,4]{1,0:T(4,128)} %fusion.18.seen, bf16[2048,384]{1,0:T(8,128)(2,1)} %bitcast.44, bf16[2048,384]{1,0:T(8,128)(2,1)} %bitcast.45, bf16[2048,128]{1,0:T(8,128)(2,1)} %collective-permute-done.4.other_ref, bf16[2048,128]{1,0:T(8,128)(2,1)} %convolution_convert_fusion.qb_ref, ...), custom_call_target="tpu_custom_call" | custom-call | flops 4294967296 | bytes 8388608 | tf_op jit(solution)/shard_map/pack_part/pallas_call | solution.py:308
  66.8 1.6 %all-to-all-done.1 = bf16[16,256,128]{2,1,0:T(8,128)(2,1)S(1)} async-done(((bf16[16,256,128]{2,1,0:T(8,128)(2,1)}), bf16[16,256,128]{2,1,0:T(8,128)(2,1)S(1)}, u32[]{:S(2)}, u32[]{:S(2)}) %all-to-all-start.1) | async-done | bytes 1048608 | tf_op jit(solution)/shard_map/all_to_all | solution.py:522
  68.4 2.1 %collective-permute-start.9 = (bf16[4096,128]{1,0:T(8,128)(2,1)S(1)}, bf16[4096,128]{1,0:T(8,128)(2,1)S(1)}, u32[]{:S(2)}, u32[]{:S(2)}) collective-permute-start(bf16[4096,128]{1,0:T(8,128)(2,1)S(1)} %bitcast.47), channel_id=1, source_target_pairs={{0,16},{16,0},{1,17},{17,1},{2,18},{18,2},{3,19},{19,3},{4,20},{20... | collective-permute-start | bytes 3145736 | tf_op jit(solution)/shard_map/ppermute | solution.py:526
  70.5 2.3 %collective-permute-done.9.other_ref = bf16[4096,128]{1,0:T(8,128)(2,1)S(1)} collective-permute-done((bf16[4096,128]{1,0:T(8,128)(2,1)S(1)}, bf16[4096,128]{1,0:T(8,128)(2,1)S(1)}, u32[]{:S(2)}, u32[]{:S(2)}) %collective-permute-start.9) | collective-permute-done | bytes 1048608 | tf_op jit(solution)/shard_map/ppermute | solution.py:526
  72.8 1.0 copy-done.12
  73.8 20.2 %stem_part.1 = bf16[2048,256]{1,0:T(8,128)(2,1)} custom-call(s32[1]{0:T(128)} %bitcast.core, bf16[2048,384]{1,0:T(8,128)(2,1)} %bitcast.46, bf16[4096,128]{1,0:T(8,128)(2,1)} %bitcast.48, bf16[4096,128]{1,0:T(8,128)(2,1)} %copy-done.12, f32[4,144,1024]{2,1,0:T(8,128)} %pack_part.1.part_ref), custom_call_target="tpu_custom_call" | custom-call | flops 8589934592 | bytes 8388608 | tf_op jit(solution)/shard_map/stem_part/pallas_call | solution.py:402
  94.0 20.4 %all_to_all.15 = bf16[16,128,256]{2,1,0:T(8,128)(2,1)S(1)} all-to-all(bf16[16,128,256]{2,1,0:T(8,128)(2,1)} %bitcast.49), channel_id=1, replica_groups=mesh['x'=4,'core'=2,'z'=4,'y'=4] {'z','y'}, dimensions={0} | all-to-all | bytes 2097152 | tf_op jit(solution)/shard_map/all_to_all | solution.py:529
  114.4 1.6 %collective-permute-start.10 = (bf16[8,128,256]{2,1,0:T(8,128)(2,1)S(1)}, bf16[8,128,256]{2,1,0:T(8,128)(2,1)S(1)}, u32[]{:S(2)}, u32[]{:S(2)}) collective-permute-start(bf16[8,128,256]{2,1,0:T(8,128)(2,1)S(1)} %dynamic-slice_bitcast_fusion), channel_id=1, source_target_pairs={{0,16},{16,0},{1,17},{17,1},{2,18},{18,2},{3,19},{19,3},{4,20},{20... | collective-permute-start | bytes 1572872 | tf_op jit(solution)/shard_map/ppermute | solution.py:533
  116.0 1.5 %collective-permute-done.10.other_ref = bf16[8,128,256]{2,1,0:T(8,128)(2,1)S(1)} collective-permute-done((bf16[8,128,256]{2,1,0:T(8,128)(2,1)S(1)}, bf16[8,128,256]{2,1,0:T(8,128)(2,1)S(1)}, u32[]{:S(2)}, u32[]{:S(2)}) %collective-permute-start.10) | collective-permute-done | bytes 524320 | tf_op jit(solution)/shard_map/ppermute | solution.py:533
  117.6 0.8 copy-done.8
  118.4 2.0 %gather.1 = bf16[128,4096]{1,0:T(8,128)(2,1)} custom-call(s32[1]{0:T(128)} %bitcast.core, bf16[2,8,128,256]{3,2,1,0:T(8,128)(2,1)} %bitcast.41, bf16[8,128,256]{2,1,0:T(8,128)(2,1)} %copy-done.8), custom_call_target="tpu_custom_call" | custom-call | tf_op jit(solution)/shard_map/gather/pallas_call | solution.py:444
  (64 shorter events, 3.2 us)
Async XLA Ops:
  0.0 10.6 %copy-start.10 = (f32[64]{0:T(128)S(1)}, f32[64]{0:T(128)}, u32[]{:S(2)}) copy-start(f32[64]{0:T(128)} %constant.81.clone) | copy-start | bytes 772
  0.0 6.1 %copy-start.9 = (s32[1,2048]{1,0:T(1,128)S(1)}, s32[1,2048]{1,0:T(1,128)}, u32[]{:S(2)}) copy-start(s32[1,2048]{1,0:T(1,128)} %param.12) | copy-start | bytes 24580
  0.0 6.1 %copy-start.11 = (s32[1,16]{1,0:T(1,128)S(1)}, s32[1,16]{1,0:T(1,128)}, u32[]{:S(2)}) copy-start(s32[1,16]{1,0:T(1,128)} %param.13) | copy-start | bytes 196
  0.0 6.2 %copy-start = (bf16[1,128,4096]{2,1,0:T(8,128)(2,1)S(1)}, bf16[1,128,4096]{2,1,0:T(8,128)(2,1)}, u32[]{:S(2)}) copy-start(bf16[1,128,4096]{2,1,0:T(8,128)(2,1)} %param.8) | copy-start | bytes 3145732
  0.0 6.7 %copy-start.1 = (bf16[1,128,1024]{2,1,0:T(8,128)(2,1)S(1)}, bf16[1,128,1024]{2,1,0:T(8,128)(2,1)}, u32[]{:S(2)}) copy-start(bf16[1,128,1024]{2,1,0:T(8,128)(2,1)} %param.9) | copy-start | bytes 786436
  0.0 7.6 %copy-start.2 = (bf16[1,128,1024]{2,1,0:T(8,128)(2,1)S(1)}, bf16[1,128,1024]{2,1,0:T(8,128)(2,1)}, u32[]{:S(2)}) copy-start(bf16[1,128,1024]{2,1,0:T(8,128)(2,1)} %param.10) | copy-start | bytes 786436
  2.4 19.2 %collective-permute-start.6 = (bf16[256,1024]{1,0:T(8,128)(2,1)}, bf16[256,1024]{1,0:T(8,128)(2,1)}, u32[]{:S(2)}, u32[]{:S(2)}) collective-permute-start(bf16[256,1024]{1,0:T(8,128)(2,1)} %get-tuple-element.27), channel_id=1, source_target_pairs={{16,32},{48,0},{80,96},{112,64},{0,112},{96,16},{32,80},{64,48},{1... | collective-permute-start | bytes 1572872 | tf_op jit(solution)/shard_map/ppermute | solution.py:478
  5.0 16.6 %collective-permute-start.7 = (bf16[256,1024]{1,0:T(8,128)(2,1)}, bf16[256,1024]{1,0:T(8,128)(2,1)}, u32[]{:S(2)}, u32[]{:S(2)}) collective-permute-start(bf16[256,1024]{1,0:T(8,128)(2,1)} %get-tuple-element.27), channel_id=1, source_target_pairs={{0,16},{16,0},{1,17},{17,1},{2,18},{18,2},{3,19},{19,3},{4,20},{20... | collective-permute-start | bytes 1572872 | tf_op jit(solution)/shard_map/ppermute | solution.py:479
  6.1 1.5 %collective-permute-start.3 = (s32[2064]{0:T(1024)S(1)}, s32[2064]{0:T(1024)S(1)}, u32[]{:S(2)}, u32[]{:S(2)}) collective-permute-start(s32[2064]{0:T(1024)S(1)} %pad_add_fusion.1), channel_id=1, source_target_pairs={{0,16},{16,0},{1,17},{17,1},{2,18},{18,2},{3,19},{19,3},{4,20},{20... | collective-permute-start | bytes 24776 | tf_op jit(solution)/shard_map/ppermute | solution.py:471
  6.2 5.1 %collective-permute-start = (bf16[128,4096]{1,0:T(8,128)(2,1)S(1)}, bf16[128,4096]{1,0:T(8,128)(2,1)S(1)}, u32[]{:S(2)}, u32[]{:S(2)}) collective-permute-start(bf16[128,4096]{1,0:T(8,128)(2,1)S(1)} %bitcast.34), channel_id=1, source_target_pairs={{0,16},{16,0},{1,17},{17,1},{2,18},{18,2},{3,19},{19,3},{4,20},{20... | collective-permute-start | bytes 3145736 | tf_op jit(solution)/shard_map/ppermute | solution.py:472
  6.7 2.8 %collective-permute-start.1 = (bf16[128,1024]{1,0:T(8,128)(2,1)S(1)}, bf16[128,1024]{1,0:T(8,128)(2,1)S(1)}, u32[]{:S(2)}, u32[]{:S(2)}) collective-permute-start(bf16[128,1024]{1,0:T(8,128)(2,1)S(1)} %bitcast.36), channel_id=1, source_target_pairs={{0,16},{16,0},{1,17},{17,1},{2,18},{18,2},{3,19},{19,3},{4,20},{20... | collective-permute-start | bytes 786440 | tf_op jit(solution)/shard_map/ppermute | solution.py:472
  6.9 6.8 %copy-start.3 = (s32[2]{0:T(128)}, s32[2]{0:T(128)S(1)}, u32[]{:S(2)}) copy-start(s32[2]{0:T(128)S(1)} %pad_add_fusion.2.spot) | copy-start | bytes 28
  7.7 3.6 %collective-permute-start.2 = (bf16[128,1024]{1,0:T(8,128)(2,1)S(1)}, bf16[128,1024]{1,0:T(8,128)(2,1)S(1)}, u32[]{:S(2)}, u32[]{:S(2)}) collective-permute-start(bf16[128,1024]{1,0:T(8,128)(2,1)S(1)} %bitcast.38), channel_id=1, source_target_pairs={{0,16},{16,0},{1,17},{17,1},{2,18},{18,2},{3,19},{19,3},{4,20},{20... | collective-permute-start | bytes 786440 | tf_op jit(solution)/shard_map/ppermute | solution.py:472
  9.5 12.0 %collective-permute-start.5 = (bf16[256,1024]{1,0:T(8,128)(2,1)}, bf16[256,1024]{1,0:T(8,128)(2,1)}, u32[]{:S(2)}, u32[]{:S(2)}) collective-permute-start(bf16[256,1024]{1,0:T(8,128)(2,1)} %get-tuple-element.28.own), channel_id=1, source_target_pairs={{0,32},{32,0},{64,96},{96,64},{16,112},{112,16},{48,80},{80,48},{1... | collective-permute-start | bytes 1572872 | tf_op jit(solution)/shard_map/ppermute | solution.py:477
  13.7 34.7 %all-to-all-start = ((bf16[16,128,384]{2,1,0:T(8,128)(2,1)}), bf16[16,128,384]{2,1,0:T(8,128)(2,1)S(1)}, u32[]{:S(2)}, u32[]{:S(2)}) async-start(bf16[16,128,384]{2,1,0:T(8,128)(2,1)} %bitcast.7), calls=%async_computation | async-start | bytes 3145728 | tf_op jit(solution)/shard_map/all_to_all | solution.py:494
  24.5 14.2 %collective-permute-start.8 = (bf16[2,256,1024]{2,1,0:T(8,128)(2,1)}, bf16[2,256,1024]{2,1,0:T(8,128)(2,1)S(1)}, u32[]{:S(2)}, u32[]{:S(2)}) collective-permute-start(bf16[2,256,1024]{2,1,0:T(8,128)(2,1)} %relay_kernel.1), channel_id=1, source_target_pairs={{0,96},{96,0},{32,64},{64,32},{16,48},{48,16},{80,112},{112,80},{1... | collective-permute-start | bytes 3145736 | tf_op jit(solution)/shard_map/ppermute | solution.py:501
  38.7 1.0 copy-start.6
  48.4 3.7 %copy-start.5 = (bf16[16,128,384]{2,1,0:T(8,128)(2,1)}, bf16[16,128,384]{2,1,0:T(8,128)(2,1)S(1)}, u32[]{:S(2)}) copy-start(bf16[16,128,384]{2,1,0:T(8,128)(2,1)S(1)} %all-to-all-done) | copy-start | bytes 4718596
  48.4 20.0 %all-to-all-start.1 = ((bf16[16,256,128]{2,1,0:T(8,128)(2,1)}), bf16[16,256,128]{2,1,0:T(8,128)(2,1)S(1)}, u32[]{:S(2)}, u32[]{:S(2)}) async-start(bf16[16,256,128]{2,1,0:T(8,128)(2,1)} %bitcast.42), calls=%async_computation.1 | async-start | bytes 2097152 | tf_op jit(solution)/shard_map/all_to_all | solution.py:522
  52.2 2.7 %collective-permute-start.4 = (bf16[2048,128]{1,0:T(8,128)(2,1)S(1)}, bf16[2048,128]{1,0:T(8,128)(2,1)}, u32[]{:S(2)}, u32[]{:S(2)}) collective-permute-start(bf16[2048,128]{1,0:T(8,128)(2,1)S(1)} %slice.36), channel_id=1, source_target_pairs={{0,16},{16,0},{1,17},{17,1},{2,18},{18,2},{3,19},{19,3},{4,20},{20... | collective-permute-start | bytes 1572872 | tf_op jit(solution)/shard_map/ppermute | solution.py:503
  68.4 4.4 %copy-start.7 = (bf16[16,256,128]{2,1,0:T(8,128)(2,1)}, bf16[16,256,128]{2,1,0:T(8,128)(2,1)S(1)}, u32[]{:S(2)}) copy-start(bf16[16,256,128]{2,1,0:T(8,128)(2,1)S(1)} %all-to-all-done.1) | copy-start | bytes 3145732
  68.4 4.4 %collective-permute-start.9 = (bf16[4096,128]{1,0:T(8,128)(2,1)S(1)}, bf16[4096,128]{1,0:T(8,128)(2,1)S(1)}, u32[]{:S(2)}, u32[]{:S(2)}) collective-permute-start(bf16[4096,128]{1,0:T(8,128)(2,1)S(1)} %bitcast.47), channel_id=1, source_target_pairs={{0,16},{16,0},{1,17},{17,1},{2,18},{18,2},{3,19},{19,3},{4,20},{20... | collective-permute-start | bytes 3145736 | tf_op jit(solution)/shard_map/ppermute | solution.py:526
  72.8 1.0 copy-start.12
  114.3 3.2 %copy-start.4 = (bf16[16,128,256]{2,1,0:T(8,128)(2,1)}, bf16[16,128,256]{2,1,0:T(8,128)(2,1)S(1)}, u32[]{:S(2)}) copy-start(bf16[16,128,256]{2,1,0:T(8,128)(2,1)S(1)} %all_to_all.15) | copy-start | bytes 3145732
  114.4 3.2 %collective-permute-start.10 = (bf16[8,128,256]{2,1,0:T(8,128)(2,1)S(1)}, bf16[8,128,256]{2,1,0:T(8,128)(2,1)S(1)}, u32[]{:S(2)}, u32[]{:S(2)}) collective-permute-start(bf16[8,128,256]{2,1,0:T(8,128)(2,1)S(1)} %dynamic-slice_bitcast_fusion), channel_id=1, source_target_pairs={{0,16},{16,0},{1,17},{17,1},{2,18},{18,2},{3,19},{19,3},{4,20},{20... | collective-permute-start | bytes 1572872 | tf_op jit(solution)/shard_map/ppermute | solution.py:533
  117.6 0.8 copy-start.8

commit v9 on v8

--- a/solution.py
+++ b/solution.py
@@ -35,7 +35,7 @@
 
 
 NT = (((1,), (1,)), ((), ()))
-ROOM = 56 * 1024 * 1024
+ROOM = 127 * 512 * 1024
 
 
 def rotary_table():
@@ -149,53 +149,63 @@
     return 3 - x
 
 
-def relay_kernel(spot, owner, own, same, flip, cross, out, sems):
+def relay_kernel(spot, owner, own, same, flip, cross, out, hold, sems):
     x, core = spot[0], spot[1]
     to = jnp.where(core == 0, far_of(x), near_of(x))
-    for item in range(2):
-        code = held_at(x, core, owner[2 * to + item])
-        for place, source in enumerate((own, same, flip, cross)):
-            chosen = code == place if place else (code == 0) | (code == 4)
+    half = own.shape[0] // 2
+    parts = [(item, pl.ds(side * half, half), 2 * item + side) for item in range(2) for side in range(2)]
+    codes = [held_at(x, core, owner[2 * to + item]) for item in range(2)]
+    for item, rows, place in parts:
+        for at, source in enumerate((own, same, flip, cross)):
+            chosen = codes[item] == at if at else (codes[item] == 0) | (codes[item] == 4)
 
             @pl.when(chosen)
             def _(source=source):
-                pltpu.make_async_copy(source, out.at[item], sems.at[item]).start()
-
-    for item in range(2):
-        pltpu.make_async_copy(own, out.at[item], sems.at[item]).wait()
-
-
-def settle_kernel(spot, owner, own, same, flip, cross, two, out, sems):
+                pltpu.make_async_copy(source.at[rows], hold.at[item, rows], sems.at[0, place]).start()
+
+    for item, rows, place in parts:
+        pltpu.make_async_copy(own.at[rows], hold.at[item, rows], sems.at[0, place]).wait()
+        pltpu.make_async_copy(hold.at[item, rows], out.at[item, rows], sems.at[1, place]).start()
+    for item, rows, place in parts:
+        pltpu.make_async_copy(hold.at[item, rows], out.at[item, rows], sems.at[1, place]).wait()
+
+
+def settle_kernel(spot, owner, own, same, flip, cross, two, out, hold, sems):
     x, core = spot[0], spot[1]
+    parts = [(pack, e) for pack in range(2) for e in range(KVH)]
     for pack in range(2):
         code = held_at(x, core, owner[2 * x + pack])
-        for place, source in enumerate((own, same, flip, cross, two.at[pack])):
-
-            @pl.when(code == place)
+        for at, source in enumerate((own, same, flip, cross, two.at[pack])):
+
+            @pl.when(code == at)
             def _(source=source):
                 for e in range(KVH):
                     pltpu.make_async_copy(
-                        source.at[:, pl.ds(e * HD, HD)], out.at[pack, e], sems.at[pack, e]
+                        source.at[:, pl.ds(e * HD, HD)], hold.at[pack, e], sems.at[0, pack, e]
                     ).start()
 
-    for pack in range(2):
-        for e in range(KVH):
-            pltpu.make_async_copy(
-                own.at[:, pl.ds(0, HD)], out.at[pack, e], sems.at[pack, e]
-            ).wait()
+    for pack, e in parts:
+        pltpu.make_async_copy(
+            own.at[:, pl.ds(0, HD)], hold.at[pack, e], sems.at[0, pack, e]
+        ).wait()
+        pltpu.make_async_copy(hold.at[pack, e], out.at[pack, e], sems.at[1, pack, e]).start()
+    for pack, e in parts:
+        pltpu.make_async_copy(hold.at[pack, e], out.at[pack, e], sems.at[1, pack, e]).wait()
 
 
 def moved(kernel, shape, sems, scalars, arrays):
+    whole = pl.BlockSpec(memory_space=pl.ANY)
     return pl.pallas_call(
         kernel,
         out_shape=jax.ShapeDtypeStruct(shape, jnp.bfloat16),
         grid_spec=pltpu.PrefetchScalarGridSpec(
             num_scalar_prefetch=len(scalars),
             grid=(1,),
-            in_specs=[pl.BlockSpec(memory_space=pl.ANY)] * len(arrays),
-            out_specs=pl.BlockSpec(shape, lambda *_: (0,) * len(shape)),
-            scratch_shapes=[pltpu.SemaphoreType.DMA(sems)],
-        ),
+            in_specs=[whole] * len(arrays),
+            out_specs=whole,
+            scratch_shapes=[pltpu.VMEM(shape, jnp.bfloat16), pltpu.SemaphoreType.DMA(sems)],
+        ),
+        compiler_params=pltpu.CompilerParams(vmem_limit_bytes=ROOM),
         name=kernel.__name__,
     )(*scalars, *arrays)
 
@@ -453,6 +463,7 @@
             ],
             out_specs=pl.BlockSpec((tok, H * HD // 2), lambda i, core: (0, i)),
         ),
+        compiler_params=pltpu.CompilerParams(vmem_limit_bytes=ROOM),
         name="gather",
     )(core, mine, other)
 
@@ -497,7 +508,7 @@
     same, cross, flip, sent = lax.optimization_barrier((same, cross, flip, sent))
 
     held = (own, same, flip, cross)
-    wanted = moved(relay_kernel, stem.shape, (2,), (here, stem_owner), held)
+    wanted = moved(relay_kernel, stem.shape, (2, 4), (here, stem_owner), held)
     two = lax.ppermute(wanted, ("x", "core"), joint(1, 0))
     both, linked, _ = lax.optimization_barrier((both, linked, wanted))
     pair = lax.ppermute(arrived[:, 2 * HD :], "core", FLIP)
@@ -515,7 +526,7 @@
     stems = moved(
         settle_kernel,
         (2, KVH, stem.shape[1], HD),
-        (2, KVH),
+        (2, 2, KVH),
         (here, stem_owner),
         held + (two,),
     ).reshape(16, stem.shape[1], HD)

time: 121 us -> 122 us (level)
    unnamed x26 -> x16, local copies, waits for them, and re-layouts: 2.8 us -> 1 us
    all_to_all x1, waiting for transfers between devices: 5.65 us -> 6.97 us  [shards(): lax.all_to_all(sent.reshape(16, tok, 3 * HD), SEQ, split_axis=0, concat_a...]
  transfers between devices with their start and end apart: 13 -> 13, of which waited for: 7 -> 7; matrix products, arithmetic and copies ran while one was open for 6% -> 7% of each run, Pallas kernels for 17% -> 16%
where the time goes in v9:
time: 122 us
  Pallas kernels  41.5 us (34%)
  waiting for transfers between devices  23.9 us (20%)
  starting transfers between devices  23.1 us (19%)
  blocking collectives  21 us (17%)
  local copies, waits for them, and re-layouts  5.18 us (4%)
  other arithmetic  3.58 us (3%)
  matrix products  2.98 us (2%)
    all_to_all x1, blocking collectives, shards(): lax.all_to_all(mixed.reshape(16, tok, 2 * HD), SEQ, split_axis=0, concat_...  21 us
    pallas_call x1, Pallas kernels, stem_part(): pl.pallas_call(stem_kernel, out_shape=jax.ShapeDtypeStruct((pack, 2 * HD)...  20.2 us
    pallas_call x1, Pallas kernels, pack_part(): pl.pallas_call(pack_kernel, out_shape=jax.ShapeDtypeStruct((pack // BQ, H...  11.3 us
    ppermute x1, waiting for transfers between devices, shards(): two = lax.ppermute(wanted, ('x', 'core'), joint(1, 0))  10.5 us
    all_to_all x1, starting transfers between devices, shards(): lax.all_to_all(sent.reshape(16, tok, 3 * HD), SEQ, split_axis=0, concat_a...  7.81 us
    all_to_all x1, waiting for transfers between devices, shards(): lax.all_to_all(sent.reshape(16, tok, 3 * HD), SEQ, split_axis=0, concat_a...  6.97 us
    pallas_call x2, Pallas kernels, moved(): pl.pallas_call(kernel, out_shape=jax.ShapeDtypeStruct(shape, jnp.bfloat16...  5.55 us
    all_to_all x1, starting transfers between devices, shards(): lax.all_to_all(stems, SEQ, split_axis=0, concat_axis=0, tiled=True)  4.33 us
  transfers between devices with their start and end apart: 13, of which 7 were waited for; matrix products, arithmetic and copies ran while one was open for 7% of the time, Pallas kernels for 16%

profile of v9, /device:TPU:1, one launch (start us, length us, event | category | flops | bytes accessed | tf_op | source)
XLA Modules:
  0.0 121.6 jit_solution(9333284859835421403)
XLA Ops:
  0.0 2.4 %dynamic-slice_bitcast_fusion.1 = (bf16[256,1024]{1,0:T(8,128)(2,1)}, bf16[256,1024]{1,0:T(8,128)(2,1)}) fusion(bf16[1,2,256,1024]{3,2,1,0:T(8,128)(2,1)} %param.11, s32[]{:T(128)S(6)} %select_n.53, s32[]{:T(128)S(6)} %select_n.52), kind=kLoop, calls=%fused_computation.27 | loop fusion | bytes 2097160 | tf_op jit(solution)/shard_map/jit(dynamic_index_in_dim)/squeeze | solution.py:487
  2.4 2.6 %collective-permute-start.6 = (bf16[256,1024]{1,0:T(8,128)(2,1)}, bf16[256,1024]{1,0:T(8,128)(2,1)}, u32[]{:S(2)}, u32[]{:S(2)}) collective-permute-start(bf16[256,1024]{1,0:T(8,128)(2,1)} %get-tuple-element.27), channel_id=1, source_target_pairs={{16,32},{48,0},{80,96},{112,64},{0,112},{96,16},{32,80},{64,48},{1... | collective-permute-start | bytes 1572872 | tf_op jit(solution)/shard_map/ppermute | solution.py:489
  5.0 1.1 collective-permute-start.7
  6.2 0.5 collective-permute-start
  7.0 0.7 collective-permute-done.3
  9.5 1.1 collective-permute-start.5
  10.6 0.5 fusion.23
  11.3 2.4 %turn.1 = bf16[2,8,128,384]{3,2,1,0:T(8,128)(2,1)} custom-call(s32[2]{0:T(128)S(1)} %pad_add_fusion.2.spot, bf16[128,4096]{1,0:T(8,128)(2,1)S(1)} %bitcast.35, bf16[128,1024]{1,0:T(8,128)(2,1)S(1)} %bitcast.37, bf16[128,1024]{1,0:T(8,128)(2,1)S(1)} %bitcast.39, bf16[128,4096]{1,0:T(8,128)(2,1)S(1)} %collective-permute-done.q_mate, ...), custom_call_target="tpu_custom_call" | custom-call | tf_op jit(solution)/shard_map/turn/pallas_call | solution.py:123
  13.7 7.8 %all-to-all-start = ((bf16[16,128,384]{2,1,0:T(8,128)(2,1)}), bf16[16,128,384]{2,1,0:T(8,128)(2,1)}, u32[]{:S(2)}, u32[]{:S(2)}) async-start(bf16[16,128,384]{2,1,0:T(8,128)(2,1)} %bitcast.7), calls=%async_computation | async-start | bytes 3145728 | tf_op jit(solution)/shard_map/all_to_all | solution.py:505
  21.6 2.7 %relay_kernel.1 = bf16[2,256,1024]{2,1,0:T(8,128)(2,1)} custom-call(s32[2]{0:T(128)} %copy-done.3, s32[8]{0:T(128)} %owner.3, bf16[256,1024]{1,0:T(8,128)(2,1)} %get-tuple-element.28.own, bf16[256,1024]{1,0:T(8,128)(2,1)} %collective-permute-done.5.same, bf16[256,1024]{1,0:T(8,128)(2,1)} %collective-permute-done.7.flip, ...), custom_call_target="tpu_custom_call" | custom-call | tf_op jit(solution)/shard_map/relay_kernel/pallas_call | solution.py:198
  24.3 0.6 collective-permute-start.8
  25.0 0.6 broadcast.78
  25.6 0.7 fusion.42
  26.7 1.5 %convolution_convert_fusion.qb_ref = bf16[2048,128]{1,0:T(8,128)(2,1)} fusion(s32[2048]{0:T(1024)S(1)} %bitcast.44, f32[16,16]{0,1:T(8,128)S(1)} %fusion.33), kind=kOutput, calls=%fused_computation | convolution fusion | flops 403177472 | bytes 533504 | tf_op jit(solution)/shard_map/dot_general | solution.py:521
  28.2 10.5 %collective-permute-done.8.two = bf16[2,256,1024]{2,1,0:T(8,128)(2,1)} collective-permute-done((bf16[2,256,1024]{2,1,0:T(8,128)(2,1)}, bf16[2,256,1024]{2,1,0:T(8,128)(2,1)}, u32[]{:S(2)}, u32[]{:S(2)}) %collective-permute-start.8) | collective-permute-done | bytes 1048608 | tf_op jit(solution)/shard_map/ppermute | solution.py:512
  38.7 2.9 %settle_kernel.1 = bf16[2,8,256,128]{3,2,1,0:T(8,128)(2,1)} custom-call(s32[2]{0:T(128)} %copy-done.3, s32[8]{0:T(128)} %owner.3, bf16[256,1024]{1,0:T(8,128)(2,1)} %get-tuple-element.28.own, bf16[256,1024]{1,0:T(8,128)(2,1)} %collective-permute-done.5.same, bf16[256,1024]{1,0:T(8,128)(2,1)} %collective-permute-done.7.flip, ...), custom_call_target="tpu_custom_call" | custom-call | tf_op jit(solution)/shard_map/settle_kernel/pallas_call | solution.py:198
  41.5 7.0 %all-to-all-done = bf16[16,128,384]{2,1,0:T(8,128)(2,1)} async-done(((bf16[16,128,384]{2,1,0:T(8,128)(2,1)}), bf16[16,128,384]{2,1,0:T(8,128)(2,1)}, u32[]{:S(2)}, u32[]{:S(2)}) %all-to-all-start) | async-done | bytes 1572896 | tf_op jit(solution)/shard_map/all_to_all | solution.py:505
  48.5 4.3 %all-to-all-start.1 = ((bf16[16,256,128]{2,1,0:T(8,128)(2,1)}), bf16[16,256,128]{2,1,0:T(8,128)(2,1)}, u32[]{:S(2)}, u32[]{:S(2)}) async-start(bf16[16,256,128]{2,1,0:T(8,128)(2,1)} %bitcast.42), calls=%async_computation.1 | async-start | bytes 2097152 | tf_op jit(solution)/shard_map/all_to_all | solution.py:533
  52.9 1.1 slice.36
  53.9 0.7 collective-permute-start.4
  54.7 0.8 fusion.18.seen
  55.5 1.2 select_convert_fusion.kb_ref
  56.6 11.3 %pack_part.1.part_ref = f32[4,144,1024]{2,1,0:T(8,128)} custom-call(s32[1]{0:T(128)} %bitcast.core, s32[4,4]{1,0:T(4,128)} %fusion.18.seen, bf16[2048,384]{1,0:T(8,128)(2,1)} %bitcast.8.q_ref.mine_ref, bf16[2048,384]{1,0:T(8,128)(2,1)} %bitcast.8.q_ref.mine_ref, bf16[2048,128]{1,0:T(8,128)(2,1)} %collective-permute-done.4.other_ref, ...), custom_call_target="tpu_custom_call" | custom-call | flops 4294967296 | bytes 8388608 | tf_op jit(solution)/shard_map/pack_part/pallas_call | solution.py:318
  68.0 1.2 %all-to-all-done.1 = bf16[16,256,128]{2,1,0:T(8,128)(2,1)} async-done(((bf16[16,256,128]{2,1,0:T(8,128)(2,1)}), bf16[16,256,128]{2,1,0:T(8,128)(2,1)}, u32[]{:S(2)}, u32[]{:S(2)}) %all-to-all-start.1) | async-done | bytes 1048608 | tf_op jit(solution)/shard_map/all_to_all | solution.py:533
  69.2 2.1 %collective-permute-start.9 = (bf16[4096,128]{1,0:T(8,128)(2,1)}, bf16[4096,128]{1,0:T(8,128)(2,1)}, u32[]{:S(2)}, u32[]{:S(2)}) collective-permute-start(bf16[4096,128]{1,0:T(8,128)(2,1)} %bitcast.12.mine_ref), channel_id=1, source_target_pairs={{0,16},{16,0},{1,17},{17,1},{2,18},{18,2},{3,19},{19,3},{4,20},{20... | collective-permute-start | bytes 3145736 | tf_op jit(solution)/shard_map/ppermute | solution.py:537
  71.3 2.6 %collective-permute-done.9.other_ref = bf16[4096,128]{1,0:T(8,128)(2,1)} collective-permute-done((bf16[4096,128]{1,0:T(8,128)(2,1)}, bf16[4096,128]{1,0:T(8,128)(2,1)}, u32[]{:S(2)}, u32[]{:S(2)}) %collective-permute-start.9) | collective-permute-done | bytes 1048608 | tf_op jit(solution)/shard_map/ppermute | solution.py:537
  73.9 20.2 %stem_part.1 = bf16[2048,256]{1,0:T(8,128)(2,1)} custom-call(s32[1]{0:T(128)} %bitcast.core, bf16[2048,384]{1,0:T(8,128)(2,1)} %bitcast.8.q_ref.mine_ref, bf16[4096,128]{1,0:T(8,128)(2,1)} %bitcast.12.mine_ref, bf16[4096,128]{1,0:T(8,128)(2,1)} %collective-permute-done.9.other_ref, f32[4,144,1024]{2,1,0:T(8,128)} %pack_part.1.part_ref), custom_call_target="tpu_custom_call" | custom-call | flops 8589934592 | bytes 8388608 | tf_op jit(solution)/shard_map/stem_part/pallas_call | solution.py:412
  94.1 21.0 %all_to_all.15 = bf16[16,128,256]{2,1,0:T(8,128)(2,1)S(1)} all-to-all(bf16[16,128,256]{2,1,0:T(8,128)(2,1)} %bitcast.43), channel_id=1, replica_groups=mesh['x'=4,'core'=2,'z'=4,'y'=4] {'z','y'}, dimensions={0} | all-to-all | bytes 2097152 | tf_op jit(solution)/shard_map/all_to_all | solution.py:540
  115.2 1.0 copy-done.4
  116.2 1.6 %collective-permute-start.10 = (bf16[8,128,256]{2,1,0:T(8,128)(2,1)S(1)}, bf16[8,128,256]{2,1,0:T(8,128)(2,1)}, u32[]{:S(2)}, u32[]{:S(2)}) collective-permute-start(bf16[8,128,256]{2,1,0:T(8,128)(2,1)S(1)} %dynamic-slice_bitcast_fusion), channel_id=1, source_target_pairs={{0,16},{16,0},{1,17},{17,1},{2,18},{18,2},{3,19},{19,3},{4,20},{20... | collective-permute-start | bytes 1572872 | tf_op jit(solution)/shard_map/ppermute | solution.py:544
  117.8 1.7 %collective-permute-done.10.other_ref = bf16[8,128,256]{2,1,0:T(8,128)(2,1)} collective-permute-done((bf16[8,128,256]{2,1,0:T(8,128)(2,1)S(1)}, bf16[8,128,256]{2,1,0:T(8,128)(2,1)}, u32[]{:S(2)}, u32[]{:S(2)}) %collective-permute-start.10) | collective-permute-done | bytes 524320 | tf_op jit(solution)/shard_map/ppermute | solution.py:544
  119.5 2.0 %gather.1 = bf16[128,4096]{1,0:T(8,128)(2,1)} custom-call(s32[1]{0:T(128)} %bitcast.core, bf16[2,8,128,256]{3,2,1,0:T(8,128)(2,1)} %bitcast.41, bf16[8,128,256]{2,1,0:T(8,128)(2,1)} %collective-permute-done.10.other_ref), custom_call_target="tpu_custom_call" | custom-call | tf_op jit(solution)/shard_map/gather/pallas_call | solution.py:454
  (54 shorter events, 2.8 us)
Async XLA Ops:
  0.0 10.6 %copy-start.6 = (f32[64]{0:T(128)S(1)}, f32[64]{0:T(128)}, u32[]{:S(2)}) copy-start(f32[64]{0:T(128)} %constant.81.clone) | copy-start | bytes 772
  0.0 6.1 %copy-start.5 = (s32[1,2048]{1,0:T(1,128)S(1)}, s32[1,2048]{1,0:T(1,128)}, u32[]{:S(2)}) copy-start(s32[1,2048]{1,0:T(1,128)} %param.12) | copy-start | bytes 24580
  0.0 6.1 %copy-start.7 = (s32[1,16]{1,0:T(1,128)S(1)}, s32[1,16]{1,0:T(1,128)}, u32[]{:S(2)}) copy-start(s32[1,16]{1,0:T(1,128)} %param.13) | copy-start | bytes 196
  0.0 6.2 %copy-start = (bf16[1,128,4096]{2,1,0:T(8,128)(2,1)S(1)}, bf16[1,128,4096]{2,1,0:T(8,128)(2,1)}, u32[]{:S(2)}) copy-start(bf16[1,128,4096]{2,1,0:T(8,128)(2,1)} %param.8) | copy-start | bytes 3145732
  0.0 6.7 %copy-start.1 = (bf16[1,128,1024]{2,1,0:T(8,128)(2,1)S(1)}, bf16[1,128,1024]{2,1,0:T(8,128)(2,1)}, u32[]{:S(2)}) copy-start(bf16[1,128,1024]{2,1,0:T(8,128)(2,1)} %param.9) | copy-start | bytes 786436
  0.0 7.6 %copy-start.2 = (bf16[1,128,1024]{2,1,0:T(8,128)(2,1)S(1)}, bf16[1,128,1024]{2,1,0:T(8,128)(2,1)}, u32[]{:S(2)}) copy-start(bf16[1,128,1024]{2,1,0:T(8,128)(2,1)} %param.10) | copy-start | bytes 786436
  2.4 19.2 %collective-permute-start.6 = (bf16[256,1024]{1,0:T(8,128)(2,1)}, bf16[256,1024]{1,0:T(8,128)(2,1)}, u32[]{:S(2)}, u32[]{:S(2)}) collective-permute-start(bf16[256,1024]{1,0:T(8,128)(2,1)} %get-tuple-element.27), channel_id=1, source_target_pairs={{16,32},{48,0},{80,96},{112,64},{0,112},{96,16},{32,80},{64,48},{1... | collective-permute-start | bytes 1572872 | tf_op jit(solution)/shard_map/ppermute | solution.py:489
  5.0 16.6 %collective-permute-start.7 = (bf16[256,1024]{1,0:T(8,128)(2,1)}, bf16[256,1024]{1,0:T(8,128)(2,1)}, u32[]{:S(2)}, u32[]{:S(2)}) collective-permute-start(bf16[256,1024]{1,0:T(8,128)(2,1)} %get-tuple-element.27), channel_id=1, source_target_pairs={{0,16},{16,0},{1,17},{17,1},{2,18},{18,2},{3,19},{19,3},{4,20},{20... | collective-permute-start | bytes 1572872 | tf_op jit(solution)/shard_map/ppermute | solution.py:490
  6.1 1.5 %collective-permute-start.3 = (s32[2064]{0:T(1024)S(1)}, s32[2064]{0:T(1024)S(1)}, u32[]{:S(2)}, u32[]{:S(2)}) collective-permute-start(s32[2064]{0:T(1024)S(1)} %pad_add_fusion.1), channel_id=1, source_target_pairs={{0,16},{16,0},{1,17},{17,1},{2,18},{18,2},{3,19},{19,3},{4,20},{20... | collective-permute-start | bytes 24776 | tf_op jit(solution)/shard_map/ppermute | solution.py:482
  6.2 5.1 %collective-permute-start = (bf16[128,4096]{1,0:T(8,128)(2,1)S(1)}, bf16[128,4096]{1,0:T(8,128)(2,1)S(1)}, u32[]{:S(2)}, u32[]{:S(2)}) collective-permute-start(bf16[128,4096]{1,0:T(8,128)(2,1)S(1)} %bitcast.34), channel_id=1, source_target_pairs={{0,16},{16,0},{1,17},{17,1},{2,18},{18,2},{3,19},{19,3},{4,20},{20... | collective-permute-start | bytes 3145736 | tf_op jit(solution)/shard_map/ppermute | solution.py:483
  6.7 2.8 %collective-permute-start.1 = (bf16[128,1024]{1,0:T(8,128)(2,1)S(1)}, bf16[128,1024]{1,0:T(8,128)(2,1)S(1)}, u32[]{:S(2)}, u32[]{:S(2)}) collective-permute-start(bf16[128,1024]{1,0:T(8,128)(2,1)S(1)} %bitcast.36), channel_id=1, source_target_pairs={{0,16},{16,0},{1,17},{17,1},{2,18},{18,2},{3,19},{19,3},{4,20},{20... | collective-permute-start | bytes 786440 | tf_op jit(solution)/shard_map/ppermute | solution.py:483
  6.9 6.8 %copy-start.3 = (s32[2]{0:T(128)}, s32[2]{0:T(128)S(1)}, u32[]{:S(2)}) copy-start(s32[2]{0:T(128)S(1)} %pad_add_fusion.2.spot) | copy-start | bytes 28
  7.7 3.6 %collective-permute-start.2 = (bf16[128,1024]{1,0:T(8,128)(2,1)S(1)}, bf16[128,1024]{1,0:T(8,128)(2,1)S(1)}, u32[]{:S(2)}, u32[]{:S(2)}) collective-permute-start(bf16[128,1024]{1,0:T(8,128)(2,1)S(1)} %bitcast.38), channel_id=1, source_target_pairs={{0,16},{16,0},{1,17},{17,1},{2,18},{18,2},{3,19},{19,3},{4,20},{20... | collective-permute-start | bytes 786440 | tf_op jit(solution)/shard_map/ppermute | solution.py:483
  9.5 12.1 %collective-permute-start.5 = (bf16[256,1024]{1,0:T(8,128)(2,1)}, bf16[256,1024]{1,0:T(8,128)(2,1)}, u32[]{:S(2)}, u32[]{:S(2)}) collective-permute-start(bf16[256,1024]{1,0:T(8,128)(2,1)} %get-tuple-element.28.own), channel_id=1, source_target_pairs={{0,32},{32,0},{64,96},{96,64},{16,112},{112,16},{48,80},{80,48},{1... | collective-permute-start | bytes 1572872 | tf_op jit(solution)/shard_map/ppermute | solution.py:488
  13.7 34.8 %all-to-all-start = ((bf16[16,128,384]{2,1,0:T(8,128)(2,1)}), bf16[16,128,384]{2,1,0:T(8,128)(2,1)}, u32[]{:S(2)}, u32[]{:S(2)}) async-start(bf16[16,128,384]{2,1,0:T(8,128)(2,1)} %bitcast.7), calls=%async_computation | async-start | bytes 3145728 | tf_op jit(solution)/shard_map/all_to_all | solution.py:505
  24.3 14.3 %collective-permute-start.8 = (bf16[2,256,1024]{2,1,0:T(8,128)(2,1)}, bf16[2,256,1024]{2,1,0:T(8,128)(2,1)}, u32[]{:S(2)}, u32[]{:S(2)}) collective-permute-start(bf16[2,256,1024]{2,1,0:T(8,128)(2,1)} %relay_kernel.1), channel_id=1, source_target_pairs={{0,96},{96,0},{32,64},{64,32},{16,48},{48,16},{80,112},{112,80},{1... | collective-permute-start | bytes 3145736 | tf_op jit(solution)/shard_map/ppermute | solution.py:512
  48.5 20.7 %all-to-all-start.1 = ((bf16[16,256,128]{2,1,0:T(8,128)(2,1)}), bf16[16,256,128]{2,1,0:T(8,128)(2,1)}, u32[]{:S(2)}, u32[]{:S(2)}) async-start(bf16[16,256,128]{2,1,0:T(8,128)(2,1)} %bitcast.42), calls=%async_computation.1 | async-start | bytes 2097152 | tf_op jit(solution)/shard_map/all_to_all | solution.py:533
  53.9 2.7 %collective-permute-start.4 = (bf16[2048,128]{1,0:T(8,128)(2,1)S(1)}, bf16[2048,128]{1,0:T(8,128)(2,1)}, u32[]{:S(2)}, u32[]{:S(2)}) collective-permute-start(bf16[2048,128]{1,0:T(8,128)(2,1)S(1)} %slice.36), channel_id=1, source_target_pairs={{0,16},{16,0},{1,17},{17,1},{2,18},{18,2},{3,19},{19,3},{4,20},{20... | collective-permute-start | bytes 1572872 | tf_op jit(solution)/shard_map/ppermute | solution.py:514
  69.2 4.7 %collective-permute-start.9 = (bf16[4096,128]{1,0:T(8,128)(2,1)}, bf16[4096,128]{1,0:T(8,128)(2,1)}, u32[]{:S(2)}, u32[]{:S(2)}) collective-permute-start(bf16[4096,128]{1,0:T(8,128)(2,1)} %bitcast.12.mine_ref), channel_id=1, source_target_pairs={{0,16},{16,0},{1,17},{17,1},{2,18},{18,2},{3,19},{19,3},{4,20},{20... | collective-permute-start | bytes 3145736 | tf_op jit(solution)/shard_map/ppermute | solution.py:537
  115.2 1.0 copy-start.4
  116.2 3.3 %collective-permute-start.10 = (bf16[8,128,256]{2,1,0:T(8,128)(2,1)S(1)}, bf16[8,128,256]{2,1,0:T(8,128)(2,1)}, u32[]{:S(2)}, u32[]{:S(2)}) collective-permute-start(bf16[8,128,256]{2,1,0:T(8,128)(2,1)S(1)} %dynamic-slice_bitcast_fusion), channel_id=1, source_target_pairs={{0,16},{16,0},{1,17},{17,1},{2,18},{18,2},{3,19},{19,3},{4,20},{20... | collective-permute-start | bytes 1572872 | tf_op jit(solution)/shard_map/ppermute | solution.py:544

commit v10 on v9

--- a/solution.py
+++ b/solution.py
@@ -1,3 +1,4 @@
+import functools
 import math
 
 import jax
@@ -152,8 +153,7 @@
 def relay_kernel(spot, owner, own, same, flip, cross, out, hold, sems):
     x, core = spot[0], spot[1]
     to = jnp.where(core == 0, far_of(x), near_of(x))
-    half = own.shape[0] // 2
-    parts = [(item, pl.ds(side * half, half), 2 * item + side) for item in range(2) for side in range(2)]
+    parts = [(item, side, 2 * item + side) for item in range(2) for side in range(2)]
     codes = [held_at(x, core, owner[2 * to + item]) for item in range(2)]
     for item, rows, place in parts:
         for at, source in enumerate((own, same, flip, cross)):
@@ -181,12 +181,12 @@
             def _(source=source):
                 for e in range(KVH):
                     pltpu.make_async_copy(
-                        source.at[:, pl.ds(e * HD, HD)], hold.at[pack, e], sems.at[0, pack, e]
+                        source.at[:, :, pl.ds(e * HD, HD)], hold.at[pack, e], sems.at[0, pack, e]
                     ).start()
 
     for pack, e in parts:
         pltpu.make_async_copy(
-            own.at[:, pl.ds(0, HD)], hold.at[pack, e], sems.at[0, pack, e]
+            own.at[:, :, pl.ds(0, HD)], hold.at[pack, e], sems.at[0, pack, e]
         ).wait()
         pltpu.make_async_copy(hold.at[pack, e], out.at[pack, e], sems.at[1, pack, e]).start()
     for pack, e in parts:
@@ -214,6 +214,16 @@
     return lax.dot_general(left, right, NT, preferred_element_type=jnp.float32)
 
 
+def norms_of(key):
+    wide = key.astype(jnp.float32)
+    return flipped_dot(jnp.ones((8, HD), jnp.bfloat16), (wide * wide).astype(jnp.bfloat16))
+
+
+def longest(best):
+    most = jnp.max(jnp.max(best, axis=1, keepdims=True), axis=0, keepdims=True)
+    return jnp.broadcast_to(jnp.sqrt(most), (8, HD))
+
+
 def fill(core, mine_ref, other_ref, ka, vt, top):
     first = core == 0
     best = jnp.zeros((8, BQ), jnp.float32)
@@ -223,12 +233,9 @@
         key = jnp.where(first, mine, other)
         ka[at : at + BQ, :HD] = key
         vt[:HD, at : at + BQ] = jnp.where(first, other, mine).T
-        wide = key.astype(jnp.float32)
-        squares = (wide * wide).astype(jnp.bfloat16)
-        best = jnp.maximum(best, flipped_dot(jnp.ones((8, HD), jnp.bfloat16), squares))
+        best = jnp.maximum(best, norms_of(key))
     vt[HD:, :] = jnp.ones_like(vt[HD:, :])
-    longest = jnp.max(jnp.max(best, axis=1, keepdims=True), axis=0, keepdims=True)
-    top[...] = jnp.broadcast_to(jnp.sqrt(longest), (8, HD))
+    top[...] = longest(best)
 
 
 def stacked(ref):
@@ -345,14 +352,23 @@
     )(core, seen, arrived, arrived, other, q_side, k_side)
 
 
-def stem_kernel(core, q_ref, mine_ref, other_ref, part_ref, o_ref, qa, ka, vt, top, acc):
+def stem_kernel(last, q_ref, kv_ref, part_ref, o_ref, qa, ka, vt, top, acc):
     stem = ka.shape[0]
     lane = lax.broadcasted_iota(jnp.int32, (1, HD), 1)
     side = jnp.broadcast_to(jnp.where(lane == SEGS, -1.0, 0.0).astype(jnp.bfloat16), (CK, HD))
 
     @pl.when(pl.program_id(0) == 0)
     def _():
-        fill(core[0], mine_ref, other_ref, ka, vt, top)
+        owners, _, rows, _ = kv_ref.shape
+        best = jnp.zeros((8, rows), jnp.float32)
+        for owner in range(owners):
+            here = slice(owner * rows, owner * rows + rows)
+            key = kv_ref[owner, 0]
+            ka[here, :] = key
+            vt[:HD, here] = kv_ref[owner, 1].T
+            best = jnp.maximum(best, norms_of(key))
+        vt[HD:, :] = jnp.ones_like(vt[HD:, :])
+        top[...] = longest(best)
 
     q_rows = stacked(q_ref)
     qa[:, :HD] = q_rows
@@ -384,10 +400,14 @@
         most = jnp.maximum(shift, before)
         new = jnp.exp2((shift - most) * SCALE)
         old = jnp.exp2((before - most) * SCALE)
-        total = acc[HD : HD + 1] * new + part_ref[0, HD : HD + 1] * old
-        out = (acc[:HD] * (new / total) + part_ref[0, :HD] * (old / total)).T
-        o_ref[:, :HD] = out[:BQ].astype(jnp.bfloat16)
-        o_ref[:, HD:] = out[BQ:].astype(jnp.bfloat16)
+        if last:
+            total = acc[HD : HD + 1] * new + part_ref[0, HD : HD + 1] * old
+            out = (acc[:HD] * (new / total) + part_ref[0, :HD] * (old / total)).T
+            o_ref[:, :HD] = out[:BQ].astype(jnp.bfloat16)
+            o_ref[:, HD:] = out[BQ:].astype(jnp.bfloat16)
+        else:
+            o_ref[0, : HD + 8] = acc[...] * new + part_ref[0, : HD + 8] * old
+            o_ref[0, HD + 8 :] = jnp.broadcast_to(most, (8, 2 * BQ))
 
     run(ceiling(q_rows, top[0:1, 0:1]))
     finish()
@@ -405,67 +425,70 @@
         finish()
 
 
-def stem_part(core, arrived, mine, other, before):
+def stem_part(last, arrived, kv, before):
     pack = arrived.shape[0]
-    stem = mine.shape[0]
-    once = dict(pipeline_mode=pl.Buffered(1))
+    stem = kv.shape[0] * kv.shape[2]
+    part = pl.BlockSpec((1, HD + 16, 2 * BQ), lambda i: (i, 0, 0))
+    rows = pl.BlockSpec((BQ, 2 * HD), lambda i: (i, 0))
     return pl.pallas_call(
-        stem_kernel,
-        out_shape=jax.ShapeDtypeStruct((pack, 2 * HD), jnp.bfloat16),
-        grid_spec=pltpu.PrefetchScalarGridSpec(
-            num_scalar_prefetch=1,
-            grid=(pack // BQ,),
-            in_specs=[
-                pl.BlockSpec((BQ, 2 * HD), lambda i, *_: (i, 0)),
-                pl.BlockSpec((stem, HD), lambda i, *_: (0, 0), **once),
-                pl.BlockSpec((stem, HD), lambda i, *_: (0, 0), **once),
-                pl.BlockSpec((1, HD + 16, 2 * BQ), lambda i, *_: (i, 0, 0)),
-            ],
-            out_specs=pl.BlockSpec((BQ, 2 * HD), lambda i, *_: (i, 0)),
-            scratch_shapes=[
-                pltpu.VMEM((2 * BQ, 2 * HD), jnp.bfloat16),
-                pltpu.VMEM((stem, HD), jnp.bfloat16),
-                pltpu.VMEM((HD + 8, stem), jnp.bfloat16),
-                pltpu.VMEM((8, HD), jnp.float32),
-                pltpu.VMEM((HD + 8, 2 * BQ), jnp.float32),
-            ],
-        ),
+        functools.partial(stem_kernel, last),
+        out_shape=jax.ShapeDtypeStruct((pack, 2 * HD), jnp.bfloat16)
+        if last
+        else jax.ShapeDtypeStruct(before.shape, jnp.float32),
+        grid=(pack // BQ,),
+        in_specs=[
+            rows,
+            pl.BlockSpec(kv.shape, lambda i: (0, 0, 0, 0), pipeline_mode=pl.Buffered(1)),
+            part,
+        ],
+        out_specs=rows if last else part,
+        scratch_shapes=[
+            pltpu.VMEM((2 * BQ, 2 * HD), jnp.bfloat16),
+            pltpu.VMEM((stem, HD), jnp.bfloat16),
+            pltpu.VMEM((HD + 8, stem), jnp.bfloat16),
+            pltpu.VMEM((8, HD), jnp.float32),
+            pltpu.VMEM((HD + 8, 2 * BQ), jnp.float32),
+        ],
         compiler_params=pltpu.CompilerParams(vmem_limit_bytes=ROOM),
         cost_estimate=pl.CostEstimate(
             flops=8 * pack * stem * HD, bytes_accessed=8 << 20, transcendentals=2 * pack * stem
         ),
         name="stem_part",
-    )(core, arrived, mine, other, before)
-
-
-def gather_kernel(core, mine_ref, other_ref, o_ref):
-    first = core[0] == 0
-    for e in range(mine_ref.shape[1]):
-        mine = mine_ref[0, e]
-        other = other_ref[e]
-        at = 4 * HD * e
-        o_ref[:, at : at + 2 * HD] = jnp.where(first, mine, other)
-        o_ref[:, at + 2 * HD : at + 4 * HD] = jnp.where(first, other, mine)
-
-
-def gather(core, mine, other):
-    tok = mine.shape[2]
-    heads = KVH // 2
+    )(arrived, kv, before)
+
+
+def gather_kernel(slot, part_ref, *rest):
+    out, sems = rest[-2:]
+    part = part_ref.at[0]
+    spots = [
+        out.at[:, pl.ds(pl.multiple_of((2 * e + slot[1]) * 2 * HD, 2 * HD), 2 * HD)]
+        for e in range(KVH)
+    ]
+    for e, spot in enumerate(spots):
+        pltpu.make_async_copy(part.at[e], spot, sems.at[e]).start()
+    for e, spot in enumerate(spots):
+        pltpu.make_async_copy(part.at[e], spot, sems.at[e]).wait()
+
+
+def gather(slot, part, done=None):
+    tok = part.shape[2]
+    whole = pl.BlockSpec(memory_space=pl.ANY)
     return pl.pallas_call(
         gather_kernel,
         out_shape=jax.ShapeDtypeStruct((tok, H * HD), jnp.bfloat16),
         grid_spec=pltpu.PrefetchScalarGridSpec(
             num_scalar_prefetch=1,
-            grid=(2,),
+            grid=(1,),
             in_specs=[
-                pl.BlockSpec((1, heads, tok, 2 * HD), lambda i, core: (core[0], i, 0, 0)),
-                pl.BlockSpec((heads, tok, 2 * HD), lambda i, core: (i, 0, 0)),
-            ],
-            out_specs=pl.BlockSpec((tok, H * HD // 2), lambda i, core: (0, i)),
+                pl.BlockSpec((1, KVH, tok, 2 * HD), lambda i, slot: (slot[0], 0, 0, 0)),
+            ]
+            + ([] if done is None else [whole]),
+            out_specs=whole,
+            scratch_shapes=[pltpu.SemaphoreType.DMA((KVH,))],
         ),
-        compiler_params=pltpu.CompilerParams(vmem_limit_bytes=ROOM),
+        input_output_aliases={} if done is None else {2: 0},
         name="gather",
-    )(core, mine, other)
+    )(slot, part, *(() if done is None else (done,)))
 
 
 def shards(queries, keys, values, stem_kv, seg_ids, seg_parent, stem_owner):
@@ -483,8 +506,9 @@
     raw_mate = tuple(lax.ppermute(part, "core", FLIP) for part in raw)
 
     stem = stem_kv[0]
-    own = lax.dynamic_index_in_dim(stem, core, 0, keepdims=False)
-    given = lax.dynamic_index_in_dim(stem, 1 - core, 0, keepdims=False)
+    half = stem.shape[1] // 2
+    own = lax.dynamic_slice_in_dim(stem, core * half, half, axis=1)
+    given = lax.dynamic_slice_in_dim(stem, (1 - core) * half, half, axis=1)
     same = lax.ppermute(own, ("x", "core"), joint(0, 0))
     cross = lax.ppermute(given, ("x", "core"), joint(0, 1))
     flip = lax.ppermute(given, "core", FLIP)
@@ -508,7 +532,7 @@
     same, cross, flip, sent = lax.optimization_barrier((same, cross, flip, sent))
 
     held = (own, same, flip, cross)
-    wanted = moved(relay_kernel, stem.shape, (2, 4), (here, stem_owner), held)
+    wanted = moved(relay_kernel, (2,) + own.shape, (2, 4), (here, stem_owner), held)
     two = lax.ppermute(wanted, ("x", "core"), joint(1, 0))
     both, linked, _ = lax.optimization_barrier((both, linked, wanted))
     pair = lax.ppermute(arrived[:, 2 * HD :], "core", FLIP)
@@ -525,23 +549,25 @@
 
     stems = moved(
         settle_kernel,
-        (2, KVH, stem.shape[1], HD),
+        (2, KVH, 2, half, HD),
         (2, 2, KVH),
         (here, stem_owner),
         held + (two,),
-    ).reshape(16, stem.shape[1], HD)
-    mine = lax.all_to_all(stems, SEQ, split_axis=0, concat_axis=0, tiled=True).reshape(STEM, HD)
+    ).reshape(16, 2, half, HD)
+    mine = lax.all_to_all(stems, SEQ, split_axis=0, concat_axis=0, tiled=True)
     arrived, pair, _ = lax.optimization_barrier((arrived, pair, stems))
     partial = pack_part(core_row, seen, arrived, pair, q_side, k_side)
     mine, partial = lax.optimization_barrier((mine, partial))
     other = lax.ppermute(mine, "core", FLIP)
-    mixed = stem_part(core_row, arrived, mine, other, partial)
+    partial = stem_part(False, arrived, mine, partial)
+    mixed = stem_part(True, arrived, other, partial)
 
     back = lax.all_to_all(
         mixed.reshape(16, tok, 2 * HD), SEQ, split_axis=0, concat_axis=0, tiled=True
     ).reshape(2, KVH, tok, 2 * HD)
-    away = lax.dynamic_index_in_dim(back, 1 - core, 0, keepdims=False)
-    return gather(core_row, back, lax.ppermute(away, "core", FLIP))[None]
+    away = lax.ppermute(lax.dynamic_slice_in_dim(back, 1 - core, 1), "core", FLIP)
+    out = gather(jnp.stack([core, core]).astype(jnp.int32), back)
+    return gather(jnp.stack([0 * core, 1 - core]).astype(jnp.int32), away, out)[None]
 
 
 def solution(mesh):

time: 122 us -> 128 us (1.049)
  blocking collectives: 21 us -> 0 us
  waiting for transfers between devices: 23.9 us -> 35.8 us
  Pallas kernels: 41.5 us -> 49.9 us
  starting transfers between devices: 23.1 us -> 27.2 us
  other arithmetic: 3.58 us -> 5.54 us
    all_to_all x1 -> x0, blocking collectives: 21 us -> none  [shards(): lax.all_to_all(mixed.reshape(16, tok, 2 * HD), SEQ, split_axis=0, concat_...]
    all_to_all x1 -> x2, waiting for transfers between devices: 1.25 us -> 16.9 us  [the longest x1 16.2 us: shards(): lax.all_to_all(mixed.reshape(16, tok, 2 * HD), SEQ, split_axis=0, concat_...]
    pallas_call x1 -> x2, Pallas kernels: 20.2 us -> 24.7 us  [stem_part(): pl.pallas_call(functools.partial(stem_kernel, last), out_shape=jax.ShapeD...]
    all_to_all x1 -> x2, starting transfers between devices: 4.33 us -> 8.48 us  [the longest x1 4.34 us: shards(): mine = lax.all_to_all(stems, SEQ, split_axis=0, concat_axis=0, tiled=True)]
    pallas_call x1 -> x2, Pallas kernels: 2.05 us -> 5.1 us  [gather(): pl.pallas_call(gather_kernel, out_shape=jax.ShapeDtypeStruct((tok, H * HD...]
    ppermute x1, waiting for transfers between devices: 2.63 us -> 0.01 us  [shards(): other = lax.ppermute(mine, 'core', FLIP)]
    dynamic_slice x0 -> x2, local copies, waits for them, and re-layouts: none -> 2.4 us  [the longest x1 2.37 us: shards(): given = lax.dynamic_slice_in_dim(stem, (1 - core) * half, half, axis=1)]
    squeeze x2 -> x0, local copies, waits for them, and re-layouts: 2.4 us -> none  [the longest x1 2.37 us: shards(): given = lax.dynamic_index_in_dim(stem, 1 - core, 0, keepdims=False)]
  transfers between devices with their start and end apart: 13 -> 14, of which waited for: 7 -> 6; matrix products, arithmetic and copies ran while one was open for 7% -> 8% of each run, Pallas kernels for 16% -> 27%
where the time goes in v10:
time: 128 us; the launch traced here: 127 us
  Pallas kernels  49.9 us (39%)
  waiting for transfers between devices  35.8 us (28%)
  starting transfers between devices  27.2 us (21%)
  other arithmetic  5.54 us (4%)
  local copies, waits for them, and re-layouts  4.97 us (4%)
  matrix products  3 us (2%)
    pallas_call x2, Pallas kernels, stem_part(): pl.pallas_call(functools.partial(stem_kernel, last), out_shape=jax.ShapeD...  24.7 us
    all_to_all x1, waiting for transfers between devices, shards(): lax.all_to_all(mixed.reshape(16, tok, 2 * HD), SEQ, split_axis=0, concat_...  16.2 us
    pallas_call x1, Pallas kernels, pack_part(): pl.pallas_call(pack_kernel, out_shape=jax.ShapeDtypeStruct((pack // BQ, H...  11.9 us
    ppermute x1, waiting for transfers between devices, shards(): two = lax.ppermute(wanted, ('x', 'core'), joint(1, 0))  10.9 us
    all_to_all x1, starting transfers between devices, shards(): lax.all_to_all(sent.reshape(16, tok, 3 * HD), SEQ, split_axis=0, concat_a...  7.81 us
    all_to_all x1, waiting for transfers between devices, shards(): lax.all_to_all(sent.reshape(16, tok, 3 * HD), SEQ, split_axis=0, concat_a...  6.81 us
    pallas_call x2, Pallas kernels, moved(): pl.pallas_call(kernel, out_shape=jax.ShapeDtypeStruct(shape, jnp.bfloat16...  5.71 us
    pallas_call x2, Pallas kernels, gather(): pl.pallas_call(gather_kernel, out_shape=jax.ShapeDtypeStruct((tok, H * HD...  5.1 us
  transfers between devices with their start and end apart: 14, of which 6 were waited for; matrix products, arithmetic and copies ran while one was open for 8% of the time, Pallas kernels for 27%

profile of v10, /device:TPU:1, one launch (start us, length us, event | category | flops | bytes accessed | tf_op | source)
XLA Modules:
  0.0 126.9 jit_solution(13801841509117225251)
XLA Ops:
  0.0 2.4 %dynamic-slice_bitcast_fusion = (bf16[2,128,1024]{2,1,0:T(8,128)(2,1)}, bf16[2,128,1024]{2,1,0:T(8,128)(2,1)}) fusion(bf16[1,2,256,1024]{3,2,1,0:T(8,128)(2,1)} %param.11, s32[]{:T(128)S(6)} %select_n.53, s32[]{:T(128)S(6)} %select_n.52), kind=kLoop, calls=%fused_computation.26 | loop fusion | bytes 2097160 | tf_op jit(solution)/shard_map/dynamic_slice | solution.py:511
  2.4 2.6 %collective-permute-start.6 = (bf16[2,128,1024]{2,1,0:T(8,128)(2,1)}, bf16[2,128,1024]{2,1,0:T(8,128)(2,1)}, u32[]{:S(2)}, u32[]{:S(2)}) collective-permute-start(bf16[2,128,1024]{2,1,0:T(8,128)(2,1)} %get-tuple-element.27), channel_id=1, source_target_pairs={{16,32},{48,0},{80,96},{112,64},{0,112},{96,16},{32,80},{64,48},{1... | collective-permute-start | bytes 1572872 | tf_op jit(solution)/shard_map/ppermute | solution.py:513
  5.0 1.1 collective-permute-start.7
  6.1 0.7 pad_add_fusion.1
  9.4 0.8 collective-permute-done.1.k_mate
  10.2 1.1 collective-permute-start.5
  12.0 2.4 %turn.1 = bf16[2,8,128,384]{3,2,1,0:T(8,128)(2,1)} custom-call(s32[2]{0:T(128)S(1)} %pad_add_fusion.3.spot, bf16[128,4096]{1,0:T(8,128)(2,1)S(1)} %bitcast.33, bf16[128,1024]{1,0:T(8,128)(2,1)S(1)} %bitcast.35, bf16[128,1024]{1,0:T(8,128)(2,1)S(1)} %bitcast.37, bf16[128,4096]{1,0:T(8,128)(2,1)S(1)} %collective-permute-done.q_mate, ...), custom_call_target="tpu_custom_call" | custom-call | tf_op jit(solution)/shard_map/turn/pallas_call | solution.py:124
  14.4 7.8 %all-to-all-start = ((bf16[16,128,384]{2,1,0:T(8,128)(2,1)}), bf16[16,128,384]{2,1,0:T(8,128)(2,1)}, u32[]{:S(2)}, u32[]{:S(2)}) async-start(bf16[16,128,384]{2,1,0:T(8,128)(2,1)} %bitcast.8), calls=%async_computation | async-start | bytes 3145728 | tf_op jit(solution)/shard_map/all_to_all | solution.py:529
  22.3 2.8 %relay_kernel.1 = bf16[2,2,128,1024]{3,2,1,0:T(8,128)(2,1)} custom-call(s32[2]{0:T(128)} %copy-done.3, s32[8]{0:T(128)} %owner.3, bf16[2,128,1024]{2,1,0:T(8,128)(2,1)} %get-tuple-element.28.own, bf16[2,128,1024]{2,1,0:T(8,128)(2,1)} %collective-permute-done.5.same, bf16[2,128,1024]{2,1,0:T(8,128)(2,1)} %collective-permute-done.7.flip, ...), custom_call_target="tpu_custom_call" | custom-call | tf_op jit(solution)/shard_map/relay_kernel/pallas_call | solution.py:198
  26.0 0.7 fusion.42
  27.1 1.5 %convolution_convert_fusion.qb_ref = bf16[2048,128]{1,0:T(8,128)(2,1)} fusion(s32[2048]{0:T(1024)S(1)} %bitcast.42, f32[16,16]{0,1:T(8,128)S(1)} %fusion.33), kind=kOutput, calls=%fused_computation | convolution fusion | flops 403177472 | bytes 533504 | tf_op jit(solution)/shard_map/dot_general | solution.py:545
  28.6 10.9 %collective-permute-done.8.two = bf16[2,2,128,1024]{3,2,1,0:T(8,128)(2,1)} collective-permute-done((bf16[2,2,128,1024]{3,2,1,0:T(8,128)(2,1)}, bf16[2,2,128,1024]{3,2,1,0:T(8,128)(2,1)}, u32[]{:S(2)}, u32[]{:S(2)}) %collective-permute-start.8) | collective-permute-done | bytes 1048608 | tf_op jit(solution)/shard_map/ppermute | solution.py:536
  39.5 2.9 %settle_kernel.1 = bf16[2,8,2,128,128]{4,3,2,1,0:T(8,128)(2,1)} custom-call(s32[2]{0:T(128)} %copy-done.3, s32[8]{0:T(128)} %owner.3, bf16[2,128,1024]{2,1,0:T(8,128)(2,1)} %get-tuple-element.28.own, bf16[2,128,1024]{2,1,0:T(8,128)(2,1)} %collective-permute-done.5.same, bf16[2,128,1024]{2,1,0:T(8,128)(2,1)} %collective-permute-done.7.flip, ...), custom_call_target="tpu_custom_call" | custom-call | tf_op jit(solution)/shard_map/settle_kernel/pallas_call | solution.py:198
  42.4 6.8 %all-to-all-done = bf16[16,128,384]{2,1,0:T(8,128)(2,1)} async-done(((bf16[16,128,384]{2,1,0:T(8,128)(2,1)}), bf16[16,128,384]{2,1,0:T(8,128)(2,1)}, u32[]{:S(2)}, u32[]{:S(2)}) %all-to-all-start) | async-done | bytes 1572896 | tf_op jit(solution)/shard_map/all_to_all | solution.py:529
  49.2 4.3 %all-to-all-start.1 = ((bf16[16,2,128,128]{3,2,1,0:T(8,128)(2,1)}), bf16[16,2,128,128]{3,2,1,0:T(8,128)(2,1)}, u32[]{:S(2)}, u32[]{:S(2)}) async-start(bf16[16,2,128,128]{3,2,1,0:T(8,128)(2,1)} %bitcast.40), calls=%async_computation.1 | async-start | bytes 2097152 | tf_op jit(solution)/shard_map/all_to_all | solution.py:557
  53.6 1.1 slice.36
  54.6 0.7 collective-permute-start.4
  55.4 0.8 fusion.18.seen
  56.2 1.1 select_convert_fusion.kb_ref
  57.3 11.9 %pack_part.1.part_ref = f32[4,144,1024]{2,1,0:T(8,128)} custom-call(s32[1]{0:T(128)} %bitcast.2.core, s32[4,4]{1,0:T(4,128)} %fusion.18.seen, bf16[2048,384]{1,0:T(8,128)(2,1)} %bitcast.9.q_ref.mine_ref, bf16[2048,384]{1,0:T(8,128)(2,1)} %bitcast.9.q_ref.mine_ref, bf16[2048,128]{1,0:T(8,128)(2,1)} %collective-permute-done.4.other_ref, ...), custom_call_target="tpu_custom_call" | custom-call | flops 4294967296 | bytes 8388608 | tf_op jit(solution)/shard_map/pack_part/pallas_call | solution.py:325
  69.3 0.6 all-to-all-done.1.kv_ref
  69.9 2.1 %collective-permute-start.9 = (bf16[16,2,128,128]{3,2,1,0:T(8,128)(2,1)}, bf16[16,2,128,128]{3,2,1,0:T(8,128)(2,1)}, u32[]{:S(2)}, u32[]{:S(2)}) collective-permute-start(bf16[16,2,128,128]{3,2,1,0:T(8,128)(2,1)} %all-to-all-done.1.kv_ref), channel_id=1, source_target_pairs={{0,16},{16,0},{1,17},{17,1},{2,18},{18,2},{3,19},{19,3},{4,20},{20... | collective-permute-start | bytes 3145736 | tf_op jit(solution)/shard_map/ppermute | solution.py:561
  72.0 12.3 %stem_part.2.part_ref = f32[4,144,1024]{2,1,0:T(8,128)} custom-call(bf16[2048,384]{1,0:T(8,128)(2,1)} %bitcast.9.q_ref.mine_ref, bf16[16,2,128,128]{3,2,1,0:T(8,128)(2,1)} %all-to-all-done.1.kv_ref, f32[4,144,1024]{2,1,0:T(8,128)} %pack_part.1.part_ref), custom_call_target="tpu_custom_call" | custom-call | flops 4294967296 | bytes 8388608 | tf_op jit(solution)/shard_map/stem_part/pallas_call | solution.py:433
  84.3 12.5 %stem_part.3 = bf16[2048,256]{1,0:T(8,128)(2,1)} custom-call(bf16[2048,384]{1,0:T(8,128)(2,1)} %bitcast.9.q_ref.mine_ref, bf16[16,2,128,128]{3,2,1,0:T(8,128)(2,1)} %collective-permute-done.9.kv_ref, f32[4,144,1024]{2,1,0:T(8,128)} %stem_part.2.part_ref), custom_call_target="tpu_custom_call" | custom-call | flops 4294967296 | bytes 8388608 | tf_op jit(solution)/shard_map/stem_part/pallas_call | solution.py:433
  96.8 4.1 %all-to-all-start.2 = ((bf16[16,128,256]{2,1,0:T(8,128)(2,1)}), bf16[16,128,256]{2,1,0:T(8,128)(2,1)S(1)}, u32[]{:S(2)}, u32[]{:S(2)}) async-start(bf16[16,128,256]{2,1,0:T(8,128)(2,1)} %bitcast.41), calls=%async_computation.2 | async-start | bytes 2097152 | tf_op jit(solution)/shard_map/all_to_all | solution.py:565
  100.9 16.2 %all-to-all-done.2 = bf16[16,128,256]{2,1,0:T(8,128)(2,1)S(1)} async-done(((bf16[16,128,256]{2,1,0:T(8,128)(2,1)}), bf16[16,128,256]{2,1,0:T(8,128)(2,1)S(1)}, u32[]{:S(2)}, u32[]{:S(2)}) %all-to-all-start.2) | async-done | bytes 1048608 | tf_op jit(solution)/shard_map/all_to_all | solution.py:565
  117.2 2.3 %collective-permute-start.10 = (bf16[1,8,128,256]{3,2,1,0:T(8,128)(2,1)S(1)}, bf16[1,8,128,256]{3,2,1,0:T(8,128)(2,1)S(1)}, u32[]{:S(2)}, u32[]{:S(2)}) collective-permute-start(bf16[1,8,128,256]{3,2,1,0:T(8,128)(2,1)S(1)} %constant_dynamic-slice_fusion.1), channel_id=1, source_target_pairs={{0,16},{16,0},{1,17},{17,1},{2,18},{18,2},{3,19},{19,3},{4,20},{20... | collective-permute-start | bytes 1572872 | tf_op jit(solution)/shard_map/ppermute | solution.py:568
  119.6 0.6 pad_add_fusion.4.slot
  120.2 0.6 pad_add_fusion.2.slot
  120.8 2.6 %gather.2.rest_0_ = bf16[128,4096]{1,0:T(8,128)(2,1)} custom-call(s32[2]{0:T(128)} %pad_add_fusion.4.slot, bf16[2,8,128,256]{3,2,1,0:T(8,128)(2,1)} %bitcast.39), custom_call_target="tpu_custom_call" | custom-call | tf_op jit(solution)/shard_map/gather/pallas_call | solution.py:476
  123.4 0.8 copy-done.5
  124.2 2.6 %gather.3 = bf16[128,4096]{1,0:T(8,128)(2,1)} custom-call(s32[2]{0:T(128)} %pad_add_fusion.2.slot, bf16[1,8,128,256]{3,2,1,0:T(8,128)(2,1)} %copy-done.5, bf16[128,4096]{1,0:T(8,128)(2,1)} %gather.2.rest_0_), custom_call_target="tpu_custom_call", output_to_operand_aliasing={{}: (2, {})} | custom-call | tf_op jit(solution)/shard_map/gather/pallas_call | solution.py:476
  (57 shorter events, 4.5 us)
Async XLA Ops:
  0.0 11.3 %copy-start.6 = (f32[64]{0:T(128)S(1)}, f32[64]{0:T(128)}, u32[]{:S(2)}) copy-start(f32[64]{0:T(128)} %constant.75.clone) | copy-start | bytes 772
  0.0 12.0 %copy-start = (bf16[1,128,4096]{2,1,0:T(8,128)(2,1)S(1)}, bf16[1,128,4096]{2,1,0:T(8,128)(2,1)}, u32[]{:S(2)}) copy-start(bf16[1,128,4096]{2,1,0:T(8,128)(2,1)} %param.8) | copy-start | bytes 3145732
  0.0 12.0 %copy-start.1 = (bf16[1,128,1024]{2,1,0:T(8,128)(2,1)S(1)}, bf16[1,128,1024]{2,1,0:T(8,128)(2,1)}, u32[]{:S(2)}) copy-start(bf16[1,128,1024]{2,1,0:T(8,128)(2,1)} %param.9) | copy-start | bytes 786436
  0.0 12.0 %copy-start.2 = (bf16[1,128,1024]{2,1,0:T(8,128)(2,1)S(1)}, bf16[1,128,1024]{2,1,0:T(8,128)(2,1)}, u32[]{:S(2)}) copy-start(bf16[1,128,1024]{2,1,0:T(8,128)(2,1)} %param.10) | copy-start | bytes 786436
  2.4 19.9 %collective-permute-start.6 = (bf16[2,128,1024]{2,1,0:T(8,128)(2,1)}, bf16[2,128,1024]{2,1,0:T(8,128)(2,1)}, u32[]{:S(2)}, u32[]{:S(2)}) collective-permute-start(bf16[2,128,1024]{2,1,0:T(8,128)(2,1)} %get-tuple-element.27), channel_id=1, source_target_pairs={{16,32},{48,0},{80,96},{112,64},{0,112},{96,16},{32,80},{64,48},{1... | collective-permute-start | bytes 1572872 | tf_op jit(solution)/shard_map/ppermute | solution.py:513
  5.0 17.3 %collective-permute-start.7 = (bf16[2,128,1024]{2,1,0:T(8,128)(2,1)}, bf16[2,128,1024]{2,1,0:T(8,128)(2,1)}, u32[]{:S(2)}, u32[]{:S(2)}) collective-permute-start(bf16[2,128,1024]{2,1,0:T(8,128)(2,1)} %get-tuple-element.27), channel_id=1, source_target_pairs={{0,16},{16,0},{1,17},{17,1},{2,18},{18,2},{3,19},{19,3},{4,20},{20... | collective-permute-start | bytes 1572872 | tf_op jit(solution)/shard_map/ppermute | solution.py:514
  6.8 1.2 collective-permute-start.3
  6.8 5.2 %collective-permute-start = (bf16[128,4096]{1,0:T(8,128)(2,1)}, bf16[128,4096]{1,0:T(8,128)(2,1)S(1)}, u32[]{:S(2)}, u32[]{:S(2)}) collective-permute-start(bf16[128,4096]{1,0:T(8,128)(2,1)} %bitcast.32), channel_id=1, source_target_pairs={{0,16},{16,0},{1,17},{17,1},{2,18},{18,2},{3,19},{19,3},{4,20},{20... | collective-permute-start | bytes 3145736 | tf_op jit(solution)/shard_map/ppermute | solution.py:506
  7.3 2.9 %collective-permute-start.1 = (bf16[128,1024]{1,0:T(8,128)(2,1)}, bf16[128,1024]{1,0:T(8,128)(2,1)S(1)}, u32[]{:S(2)}, u32[]{:S(2)}) collective-permute-start(bf16[128,1024]{1,0:T(8,128)(2,1)} %bitcast.34), channel_id=1, source_target_pairs={{0,16},{16,0},{1,17},{17,1},{2,18},{18,2},{3,19},{19,3},{4,20},{20... | collective-permute-start | bytes 786440 | tf_op jit(solution)/shard_map/ppermute | solution.py:506
  7.4 7.0 %copy-start.3 = (s32[2]{0:T(128)}, s32[2]{0:T(128)S(1)}, u32[]{:S(2)}) copy-start(s32[2]{0:T(128)S(1)} %pad_add_fusion.3.spot) | copy-start | bytes 28
  8.0 4.0 %collective-permute-start.2 = (bf16[128,1024]{1,0:T(8,128)(2,1)}, bf16[128,1024]{1,0:T(8,128)(2,1)S(1)}, u32[]{:S(2)}, u32[]{:S(2)}) collective-permute-start(bf16[128,1024]{1,0:T(8,128)(2,1)} %bitcast.36), channel_id=1, source_target_pairs={{0,16},{16,0},{1,17},{17,1},{2,18},{18,2},{3,19},{19,3},{4,20},{20... | collective-permute-start | bytes 786440 | tf_op jit(solution)/shard_map/ppermute | solution.py:506
  10.2 12.1 %collective-permute-start.5 = (bf16[2,128,1024]{2,1,0:T(8,128)(2,1)}, bf16[2,128,1024]{2,1,0:T(8,128)(2,1)}, u32[]{:S(2)}, u32[]{:S(2)}) collective-permute-start(bf16[2,128,1024]{2,1,0:T(8,128)(2,1)} %get-tuple-element.28.own), channel_id=1, source_target_pairs={{0,32},{32,0},{64,96},{96,64},{16,112},{112,16},{48,80},{80,48},{1... | collective-permute-start | bytes 1572872 | tf_op jit(solution)/shard_map/ppermute | solution.py:512
  14.4 34.8 %all-to-all-start = ((bf16[16,128,384]{2,1,0:T(8,128)(2,1)}), bf16[16,128,384]{2,1,0:T(8,128)(2,1)}, u32[]{:S(2)}, u32[]{:S(2)}) async-start(bf16[16,128,384]{2,1,0:T(8,128)(2,1)} %bitcast.8), calls=%async_computation | async-start | bytes 3145728 | tf_op jit(solution)/shard_map/all_to_all | solution.py:529
  25.2 14.3 %collective-permute-start.8 = (bf16[2,2,128,1024]{3,2,1,0:T(8,128)(2,1)}, bf16[2,2,128,1024]{3,2,1,0:T(8,128)(2,1)}, u32[]{:S(2)}, u32[]{:S(2)}) collective-permute-start(bf16[2,2,128,1024]{3,2,1,0:T(8,128)(2,1)} %relay_kernel.1), channel_id=1, source_target_pairs={{0,96},{96,0},{32,64},{64,32},{16,48},{48,16},{80,112},{112,80},{1... | collective-permute-start | bytes 3145736 | tf_op jit(solution)/shard_map/ppermute | solution.py:536
  49.2 20.7 %all-to-all-start.1 = ((bf16[16,2,128,128]{3,2,1,0:T(8,128)(2,1)}), bf16[16,2,128,128]{3,2,1,0:T(8,128)(2,1)}, u32[]{:S(2)}, u32[]{:S(2)}) async-start(bf16[16,2,128,128]{3,2,1,0:T(8,128)(2,1)} %bitcast.40), calls=%async_computation.1 | async-start | bytes 2097152 | tf_op jit(solution)/shard_map/all_to_all | solution.py:557
  54.6 2.7 %collective-permute-start.4 = (bf16[2048,128]{1,0:T(8,128)(2,1)S(1)}, bf16[2048,128]{1,0:T(8,128)(2,1)}, u32[]{:S(2)}, u32[]{:S(2)}) collective-permute-start(bf16[2048,128]{1,0:T(8,128)(2,1)S(1)} %slice.36), channel_id=1, source_target_pairs={{0,16},{16,0},{1,17},{17,1},{2,18},{18,2},{3,19},{19,3},{4,20},{20... | collective-permute-start | bytes 1572872 | tf_op jit(solution)/shard_map/ppermute | solution.py:538
  69.9 14.4 %collective-permute-start.9 = (bf16[16,2,128,128]{3,2,1,0:T(8,128)(2,1)}, bf16[16,2,128,128]{3,2,1,0:T(8,128)(2,1)}, u32[]{:S(2)}, u32[]{:S(2)}) collective-permute-start(bf16[16,2,128,128]{3,2,1,0:T(8,128)(2,1)} %all-to-all-done.1.kv_ref), channel_id=1, source_target_pairs={{0,16},{16,0},{1,17},{17,1},{2,18},{18,2},{3,19},{19,3},{4,20},{20... | collective-permute-start | bytes 3145736 | tf_op jit(solution)/shard_map/ppermute | solution.py:561
  96.8 20.4 %all-to-all-start.2 = ((bf16[16,128,256]{2,1,0:T(8,128)(2,1)}), bf16[16,128,256]{2,1,0:T(8,128)(2,1)S(1)}, u32[]{:S(2)}, u32[]{:S(2)}) async-start(bf16[16,128,256]{2,1,0:T(8,128)(2,1)} %bitcast.41), calls=%async_computation.2 | async-start | bytes 2097152 | tf_op jit(solution)/shard_map/all_to_all | solution.py:565
  117.2 3.6 %copy-start.4 = (bf16[16,128,256]{2,1,0:T(8,128)(2,1)}, bf16[16,128,256]{2,1,0:T(8,128)(2,1)S(1)}, u32[]{:S(2)}) copy-start(bf16[16,128,256]{2,1,0:T(8,128)(2,1)S(1)} %all-to-all-done.2) | copy-start | bytes 3145732
  117.2 6.2 %collective-permute-start.10 = (bf16[1,8,128,256]{3,2,1,0:T(8,128)(2,1)S(1)}, bf16[1,8,128,256]{3,2,1,0:T(8,128)(2,1)S(1)}, u32[]{:S(2)}, u32[]{:S(2)}) collective-permute-start(bf16[1,8,128,256]{3,2,1,0:T(8,128)(2,1)S(1)} %constant_dynamic-slice_fusion.1), channel_id=1, source_target_pairs={{0,16},{16,0},{1,17},{17,1},{2,18},{18,2},{3,19},{19,3},{4,20},{20... | collective-permute-start | bytes 1572872 | tf_op jit(solution)/shard_map/ppermute | solution.py:568
  123.4 0.8 copy-start.5

commit v11 on v9

--- a/solution.py
+++ b/solution.py
@@ -16,6 +16,7 @@
 SEGS = 16
 BARRED = -1e30
 BQ = 512
+SPAN = 2
 CK = 256
 WIDE = 1024
 SCALE = HD**-0.5 * math.log2(math.e)
@@ -35,7 +36,8 @@
 
 
 NT = (((1,), (1,)), ((), ()))
-ROOM = 127 * 512 * 1024
+ROOM = 56 * 1024 * 1024
+FULL = 127 * 512 * 1024
 
 
 def rotary_table():
@@ -205,7 +207,7 @@
             out_specs=whole,
             scratch_shapes=[pltpu.VMEM(shape, jnp.bfloat16), pltpu.SemaphoreType.DMA(sems)],
         ),
-        compiler_params=pltpu.CompilerParams(vmem_limit_bytes=ROOM),
+        compiler_params=pltpu.CompilerParams(vmem_limit_bytes=FULL),
         name=kernel.__name__,
     )(*scalars, *arrays)
 
@@ -354,7 +356,8 @@
     def _():
         fill(core[0], mine_ref, other_ref, ka, vt, top)
 
-    q_rows = stacked(q_ref)
+    blocks = part_ref.shape[0]
+    q_rows = jnp.concatenate([stacked(q_ref.at[pl.ds(b * BQ, BQ)]) for b in range(blocks)], axis=0)
     qa[:, :HD] = q_rows
 
     def scores(at):
@@ -379,15 +382,18 @@
         acc[...] = total
 
     def finish():
-        shift = shift_row(qa)[:1]
-        before = part_ref[0, HD + 8 : HD + 9]
-        most = jnp.maximum(shift, before)
-        new = jnp.exp2((shift - most) * SCALE)
-        old = jnp.exp2((before - most) * SCALE)
-        total = acc[HD : HD + 1] * new + part_ref[0, HD : HD + 1] * old
-        out = (acc[:HD] * (new / total) + part_ref[0, :HD] * (old / total)).T
-        o_ref[:, :HD] = out[:BQ].astype(jnp.bfloat16)
-        o_ref[:, HD:] = out[BQ:].astype(jnp.bfloat16)
+        shifts = shift_row(qa)[:1]
+        for b in range(blocks):
+            here = slice(b * 2 * BQ, (b + 1) * 2 * BQ)
+            shift = shifts[:, here]
+            before = part_ref[b, HD + 8 : HD + 9]
+            most = jnp.maximum(shift, before)
+            new = jnp.exp2((shift - most) * SCALE)
+            old = jnp.exp2((before - most) * SCALE)
+            total = acc[HD : HD + 1, here] * new + part_ref[b, HD : HD + 1] * old
+            out = (acc[:HD, here] * (new / total) + part_ref[b, :HD] * (old / total)).T
+            o_ref[b * BQ : (b + 1) * BQ, :HD] = out[:BQ].astype(jnp.bfloat16)
+            o_ref[b * BQ : (b + 1) * BQ, HD:] = out[BQ:].astype(jnp.bfloat16)
 
     run(ceiling(q_rows, top[0:1, 0:1]))
     finish()
@@ -400,7 +406,7 @@
             part = scores(pl.multiple_of(step * CK, CK))
             return jnp.maximum(most, jnp.max(part, axis=0, keepdims=True))
 
-        low = jnp.full((1, 2 * BQ), BARRED, jnp.float32)
+        low = jnp.full((1, q_rows.shape[0]), BARRED, jnp.float32)
         run(down(lax.fori_loop(0, stem // CK, body, low)))
         finish()
 
@@ -414,23 +420,23 @@
         out_shape=jax.ShapeDtypeStruct((pack, 2 * HD), jnp.bfloat16),
         grid_spec=pltpu.PrefetchScalarGridSpec(
             num_scalar_prefetch=1,
-            grid=(pack // BQ,),
+            grid=(pack // (SPAN * BQ),),
             in_specs=[
-                pl.BlockSpec((BQ, 2 * HD), lambda i, *_: (i, 0)),
+                pl.BlockSpec((SPAN * BQ, 2 * HD), lambda i, *_: (i, 0)),
                 pl.BlockSpec((stem, HD), lambda i, *_: (0, 0), **once),
                 pl.BlockSpec((stem, HD), lambda i, *_: (0, 0), **once),
-                pl.BlockSpec((1, HD + 16, 2 * BQ), lambda i, *_: (i, 0, 0)),
+                pl.BlockSpec((SPAN, HD + 16, 2 * BQ), lambda i, *_: (i, 0, 0)),
             ],
-            out_specs=pl.BlockSpec((BQ, 2 * HD), lambda i, *_: (i, 0)),
+            out_specs=pl.BlockSpec((SPAN * BQ, 2 * HD), lambda i, *_: (i, 0)),
             scratch_shapes=[
-                pltpu.VMEM((2 * BQ, 2 * HD), jnp.bfloat16),
+                pltpu.VMEM((2 * SPAN * BQ, 2 * HD), jnp.bfloat16),
                 pltpu.VMEM((stem, HD), jnp.bfloat16),
                 pltpu.VMEM((HD + 8, stem), jnp.bfloat16),
                 pltpu.VMEM((8, HD), jnp.float32),
-                pltpu.VMEM((HD + 8, 2 * BQ), jnp.float32),
+                pltpu.VMEM((HD + 8, 2 * SPAN * BQ), jnp.float32),
             ],
         ),
-        compiler_params=pltpu.CompilerParams(vmem_limit_bytes=ROOM),
+        compiler_params=pltpu.CompilerParams(vmem_limit_bytes=FULL),
         cost_estimate=pl.CostEstimate(
             flops=8 * pack * stem * HD, bytes_accessed=8 << 20, transcendentals=2 * pack * stem
         ),
@@ -438,32 +444,49 @@
     )(core, arrived, mine, other, before)
 
 
-def gather_kernel(core, mine_ref, other_ref, o_ref):
+def gather_kernel(core, mine_ref, other_ref, o_ref, mine, other, sems):
+    step = pl.program_id(0)
+    heads = KVH // 2
+
+    def copies(part):
+        rows = pl.ds(part * heads, heads)
+        return (
+            pltpu.make_async_copy(mine_ref.at[core[0], rows], mine.at[rows], sems.at[0, part]),
+            pltpu.make_async_copy(other_ref.at[rows], other.at[rows], sems.at[1, part]),
+        )
+
+    @pl.when(step == 0)
+    def _():
+        for copy in copies(0) + copies(1):
+            copy.start()
+
+    for copy in copies(step):
+        copy.wait()
     first = core[0] == 0
-    for e in range(mine_ref.shape[1]):
-        mine = mine_ref[0, e]
-        other = other_ref[e]
+    for e in range(heads):
+        own, got = mine[step * heads + e], other[step * heads + e]
         at = 4 * HD * e
-        o_ref[:, at : at + 2 * HD] = jnp.where(first, mine, other)
-        o_ref[:, at + 2 * HD : at + 4 * HD] = jnp.where(first, other, mine)
+        o_ref[:, at : at + 2 * HD] = jnp.where(first, own, got)
+        o_ref[:, at + 2 * HD : at + 4 * HD] = jnp.where(first, got, own)
 
 
 def gather(core, mine, other):
     tok = mine.shape[2]
-    heads = KVH // 2
+    whole = pl.BlockSpec(memory_space=pl.ANY)
     return pl.pallas_call(
         gather_kernel,
         out_shape=jax.ShapeDtypeStruct((tok, H * HD), jnp.bfloat16),
         grid_spec=pltpu.PrefetchScalarGridSpec(
             num_scalar_prefetch=1,
             grid=(2,),
-            in_specs=[
-                pl.BlockSpec((1, heads, tok, 2 * HD), lambda i, core: (core[0], i, 0, 0)),
-                pl.BlockSpec((heads, tok, 2 * HD), lambda i, core: (i, 0, 0)),
+            in_specs=[whole, whole],
+            out_specs=pl.BlockSpec((tok, H * HD // 2), lambda i, core: (0, i)),
+            scratch_shapes=[
+                pltpu.VMEM(other.shape, jnp.bfloat16),
+                pltpu.VMEM(other.shape, jnp.bfloat16),
+                pltpu.SemaphoreType.DMA((2, 2)),
             ],
-            out_specs=pl.BlockSpec((tok, H * HD // 2), lambda i, core: (0, i)),
-        ),
-        compiler_params=pltpu.CompilerParams(vmem_limit_bytes=ROOM),
+        ),
         name="gather",
     )(core, mine, other)
 

time: 122 us -> 123 us (level)
  local copies, waits for them, and re-layouts: 5.18 us -> 6.68 us
  waiting for transfers between devices: 23.9 us -> 22.6 us
    unnamed x16 -> x22, local copies, waits for them, and re-layouts: 1 us -> 2.6 us
    all_to_all x1, waiting for transfers between devices: 1.25 us -> 0.01 us  [shards(): lax.all_to_all(stems, SEQ, split_axis=0, concat_axis=0, tiled=True)]
  transfers between devices with their start and end apart: 13 -> 13, of which waited for: 7 -> 6; matrix products, arithmetic and copies ran while one was open for 7% -> 7% of each run, Pallas kernels for 16% -> 16%
where the time goes in v11:
time: 123 us; the launch traced here: 122 us
  Pallas kernels  41.9 us (34%)
  waiting for transfers between devices  22.6 us (18%)
  starting transfers between devices  22 us (18%)
  blocking collectives  21.9 us (18%)
  local copies, waits for them, and re-layouts  6.68 us (5%)
  other arithmetic  3.51 us (3%)
  matrix products  3 us (2%)
    all_to_all x1, blocking collectives, shards(): lax.all_to_all(mixed.reshape(16, tok, 2 * HD), SEQ, split_axis=0, concat_...  21.9 us
    pallas_call x1, Pallas kernels, stem_part(): pl.pallas_call(stem_kernel, out_shape=jax.ShapeDtypeStruct((pack, 2 * HD)...  20 us
    pallas_call x1, Pallas kernels, pack_part(): pl.pallas_call(pack_kernel, out_shape=jax.ShapeDtypeStruct((pack // BQ, H...  11.9 us
    ppermute x1, waiting for transfers between devices, shards(): two = lax.ppermute(wanted, ('x', 'core'), joint(1, 0))  10.8 us
    all_to_all x1, starting transfers between devices, shards(): lax.all_to_all(sent.reshape(16, tok, 3 * HD), SEQ, split_axis=0, concat_a...  7.81 us
    all_to_all x1, waiting for transfers between devices, shards(): lax.all_to_all(sent.reshape(16, tok, 3 * HD), SEQ, split_axis=0, concat_a...  6.96 us
    pallas_call x2, Pallas kernels, moved(): pl.pallas_call(kernel, out_shape=jax.ShapeDtypeStruct(shape, jnp.bfloat16...  5.56 us
    all_to_all x1, starting transfers between devices, shards(): lax.all_to_all(stems, SEQ, split_axis=0, concat_axis=0, tiled=True)  3.66 us
  transfers between devices with their start and end apart: 13, of which 6 were waited for; matrix products, arithmetic and copies ran while one was open for 7% of the time, Pallas kernels for 16%

profile of v11, /device:TPU:1, one launch (start us, length us, event | category | flops | bytes accessed | tf_op | source)
XLA Modules:
  0.0 122.1 jit_solution(17860329587595828633)
XLA Ops:
  0.0 2.3 %dynamic-slice_bitcast_fusion.1 = (bf16[256,1024]{1,0:T(8,128)(2,1)}, bf16[256,1024]{1,0:T(8,128)(2,1)}) fusion(bf16[1,2,256,1024]{3,2,1,0:T(8,128)(2,1)} %param.11, s32[]{:T(128)S(6)} %select_n.53, s32[]{:T(128)S(6)} %select_n.52), kind=kLoop, calls=%fused_computation.27 | loop fusion | bytes 2097160 | tf_op jit(solution)/shard_map/jit(dynamic_index_in_dim)/squeeze | solution.py:510
  2.4 2.6 %collective-permute-start.6 = (bf16[256,1024]{1,0:T(8,128)(2,1)}, bf16[256,1024]{1,0:T(8,128)(2,1)}, u32[]{:S(2)}, u32[]{:S(2)}) collective-permute-start(bf16[256,1024]{1,0:T(8,128)(2,1)} %get-tuple-element.27), channel_id=1, source_target_pairs={{16,32},{48,0},{80,96},{112,64},{0,112},{96,16},{32,80},{64,48},{1... | collective-permute-start | bytes 1572872 | tf_op jit(solution)/shard_map/ppermute | solution.py:512
  5.0 1.1 collective-permute-start.7
  6.2 0.5 collective-permute-start
  7.0 0.7 collective-permute-done.3
  9.5 1.1 collective-permute-start.5
  10.6 0.5 fusion.23
  11.3 2.4 %turn.1 = bf16[2,8,128,384]{3,2,1,0:T(8,128)(2,1)} custom-call(s32[2]{0:T(128)S(1)} %pad_add_fusion.2.spot, bf16[128,4096]{1,0:T(8,128)(2,1)S(1)} %bitcast.35, bf16[128,1024]{1,0:T(8,128)(2,1)S(1)} %bitcast.37, bf16[128,1024]{1,0:T(8,128)(2,1)S(1)} %bitcast.39, bf16[128,4096]{1,0:T(8,128)(2,1)S(1)} %collective-permute-done.q_mate, ...), custom_call_target="tpu_custom_call" | custom-call | tf_op jit(solution)/shard_map/turn/pallas_call | solution.py:125
  13.7 7.8 %all-to-all-start = ((bf16[16,128,384]{2,1,0:T(8,128)(2,1)}), bf16[16,128,384]{2,1,0:T(8,128)(2,1)}, u32[]{:S(2)}, u32[]{:S(2)}) async-start(bf16[16,128,384]{2,1,0:T(8,128)(2,1)} %bitcast.7), calls=%async_computation | async-start | bytes 3145728 | tf_op jit(solution)/shard_map/all_to_all | solution.py:528
  21.6 2.7 %relay_kernel.1 = bf16[2,256,1024]{2,1,0:T(8,128)(2,1)} custom-call(s32[2]{0:T(128)} %copy-done.3, s32[8]{0:T(128)} %owner.3, bf16[256,1024]{1,0:T(8,128)(2,1)} %get-tuple-element.28.own, bf16[256,1024]{1,0:T(8,128)(2,1)} %collective-permute-done.5.same, bf16[256,1024]{1,0:T(8,128)(2,1)} %collective-permute-done.7.flip, ...), custom_call_target="tpu_custom_call" | custom-call | tf_op jit(solution)/shard_map/relay_kernel/pallas_call | solution.py:200
  24.7 0.5 broadcast.78
  25.2 0.6 fusion.42
  26.3 1.5 %convolution_convert_fusion.qb_ref = bf16[2048,128]{1,0:T(8,128)(2,1)} fusion(s32[2048]{0:T(1024)S(1)} %bitcast.46, f32[16,16]{0,1:T(8,128)S(1)} %fusion.33), kind=kOutput, calls=%fused_computation | convolution fusion | flops 403177472 | bytes 533504 | tf_op jit(solution)/shard_map/dot_general | solution.py:544
  27.8 10.8 %collective-permute-done.8.two = bf16[2,256,1024]{2,1,0:T(8,128)(2,1)} collective-permute-done((bf16[2,256,1024]{2,1,0:T(8,128)(2,1)}, bf16[2,256,1024]{2,1,0:T(8,128)(2,1)}, u32[]{:S(2)}, u32[]{:S(2)}) %collective-permute-start.8) | collective-permute-done | bytes 1048608 | tf_op jit(solution)/shard_map/ppermute | solution.py:535
  38.6 2.9 %settle_kernel.1 = bf16[2,8,256,128]{3,2,1,0:T(8,128)(2,1)} custom-call(s32[2]{0:T(128)} %copy-done.3, s32[8]{0:T(128)} %owner.3, bf16[256,1024]{1,0:T(8,128)(2,1)} %get-tuple-element.28.own, bf16[256,1024]{1,0:T(8,128)(2,1)} %collective-permute-done.5.same, bf16[256,1024]{1,0:T(8,128)(2,1)} %collective-permute-done.7.flip, ...), custom_call_target="tpu_custom_call" | custom-call | tf_op jit(solution)/shard_map/settle_kernel/pallas_call | solution.py:200
  41.5 7.0 %all-to-all-done = bf16[16,128,384]{2,1,0:T(8,128)(2,1)} async-done(((bf16[16,128,384]{2,1,0:T(8,128)(2,1)}), bf16[16,128,384]{2,1,0:T(8,128)(2,1)}, u32[]{:S(2)}, u32[]{:S(2)}) %all-to-all-start) | async-done | bytes 1572896 | tf_op jit(solution)/shard_map/all_to_all | solution.py:528
  48.5 3.7 %all-to-all-start.1 = ((bf16[16,256,128]{2,1,0:T(8,128)(2,1)}), bf16[16,256,128]{2,1,0:T(8,128)(2,1)S(1)}, u32[]{:S(2)}, u32[]{:S(2)}) async-start(bf16[16,256,128]{2,1,0:T(8,128)(2,1)} %bitcast.42), calls=%async_computation.1 | async-start | bytes 2097152 | tf_op jit(solution)/shard_map/all_to_all | solution.py:556
  52.2 1.1 slice.36
  53.2 0.7 collective-permute-start.4
  54.0 0.8 fusion.18.seen
  54.8 1.2 select_convert_fusion.kb_ref
  55.9 0.8 copy-done.10
  56.7 11.9 %pack_part.1.part_ref = f32[4,144,1024]{2,1,0:T(8,128)} custom-call(s32[1]{0:T(128)} %bitcast.core, s32[4,4]{1,0:T(4,128)} %fusion.18.seen, bf16[2048,384]{1,0:T(8,128)(2,1)} %bitcast.8.q_ref.mine_ref, bf16[2048,384]{1,0:T(8,128)(2,1)} %bitcast.8.q_ref.mine_ref, bf16[2048,128]{1,0:T(8,128)(2,1)} %copy-done.10, ...), custom_call_target="tpu_custom_call" | custom-call | flops 4294967296 | bytes 8388608 | tf_op jit(solution)/shard_map/pack_part/pallas_call | solution.py:320
  68.7 1.0 copy-done.5
  69.6 1.9 %collective-permute-start.9 = (bf16[4096,128]{1,0:T(8,128)(2,1)S(1)}, bf16[4096,128]{1,0:T(8,128)(2,1)}, u32[]{:S(2)}, u32[]{:S(2)}) collective-permute-start(bf16[4096,128]{1,0:T(8,128)(2,1)S(1)} %bitcast.43), channel_id=1, source_target_pairs={{0,16},{16,0},{1,17},{17,1},{2,18},{18,2},{3,19},{19,3},{4,20},{20... | collective-permute-start | bytes 3145736 | tf_op jit(solution)/shard_map/ppermute | solution.py:560
  71.6 2.4 %collective-permute-done.9.other_ref = bf16[4096,128]{1,0:T(8,128)(2,1)} collective-permute-done((bf16[4096,128]{1,0:T(8,128)(2,1)S(1)}, bf16[4096,128]{1,0:T(8,128)(2,1)}, u32[]{:S(2)}, u32[]{:S(2)}) %collective-permute-start.9) | collective-permute-done | bytes 1048608 | tf_op jit(solution)/shard_map/ppermute | solution.py:560
  74.0 20.0 %stem_part.1 = bf16[2048,256]{1,0:T(8,128)(2,1)} custom-call(s32[1]{0:T(128)} %bitcast.core, bf16[2048,384]{1,0:T(8,128)(2,1)} %bitcast.8.q_ref.mine_ref, bf16[4096,128]{1,0:T(8,128)(2,1)} %bitcast.44, bf16[4096,128]{1,0:T(8,128)(2,1)} %collective-permute-done.9.other_ref, f32[4,144,1024]{2,1,0:T(8,128)} %pack_part.1.part_ref), custom_call_target="tpu_custom_call" | custom-call | flops 8589934592 | bytes 8388608 | tf_op jit(solution)/shard_map/stem_part/pallas_call | solution.py:418
  94.0 21.9 %all_to_all.15 = bf16[16,128,256]{2,1,0:T(8,128)(2,1)S(1)} all-to-all(bf16[16,128,256]{2,1,0:T(8,128)(2,1)} %bitcast.45), channel_id=1, replica_groups=mesh['x'=4,'core'=2,'z'=4,'y'=4] {'z','y'}, dimensions={0} | all-to-all | bytes 2097152 | tf_op jit(solution)/shard_map/all_to_all | solution.py:563
  115.9 1.6 %collective-permute-start.10 = (bf16[8,128,256]{2,1,0:T(8,128)(2,1)S(1)}, bf16[8,128,256]{2,1,0:T(8,128)(2,1)S(1)}, u32[]{:S(2)}, u32[]{:S(2)}) collective-permute-start(bf16[8,128,256]{2,1,0:T(8,128)(2,1)S(1)} %dynamic-slice_bitcast_fusion), channel_id=1, source_target_pairs={{0,16},{16,0},{1,17},{17,1},{2,18},{18,2},{3,19},{19,3},{4,20},{20... | collective-permute-start | bytes 1572872 | tf_op jit(solution)/shard_map/ppermute | solution.py:567
  117.5 1.5 %collective-permute-done.10.other_ref = bf16[8,128,256]{2,1,0:T(8,128)(2,1)S(1)} collective-permute-done((bf16[8,128,256]{2,1,0:T(8,128)(2,1)S(1)}, bf16[8,128,256]{2,1,0:T(8,128)(2,1)S(1)}, u32[]{:S(2)}, u32[]{:S(2)}) %collective-permute-start.10) | collective-permute-done | bytes 524320 | tf_op jit(solution)/shard_map/ppermute | solution.py:567
  119.1 0.8 copy-done.6
  119.9 2.1 %gather.1 = bf16[128,4096]{1,0:T(8,128)(2,1)} custom-call(s32[1]{0:T(128)} %bitcast.core, bf16[2,8,128,256]{3,2,1,0:T(8,128)(2,1)} %bitcast.41, bf16[8,128,256]{2,1,0:T(8,128)(2,1)} %copy-done.6), custom_call_target="tpu_custom_call" | custom-call | tf_op jit(solution)/shard_map/gather/pallas_call | solution.py:476
  (60 shorter events, 3.2 us)
Async XLA Ops:
  0.0 10.6 %copy-start.8 = (f32[64]{0:T(128)S(1)}, f32[64]{0:T(128)}, u32[]{:S(2)}) copy-start(f32[64]{0:T(128)} %constant.81.clone) | copy-start | bytes 772
  0.0 6.1 %copy-start.7 = (s32[1,2048]{1,0:T(1,128)S(1)}, s32[1,2048]{1,0:T(1,128)}, u32[]{:S(2)}) copy-start(s32[1,2048]{1,0:T(1,128)} %param.12) | copy-start | bytes 24580
  0.0 6.1 %copy-start.9 = (s32[1,16]{1,0:T(1,128)S(1)}, s32[1,16]{1,0:T(1,128)}, u32[]{:S(2)}) copy-start(s32[1,16]{1,0:T(1,128)} %param.13) | copy-start | bytes 196
  0.0 6.2 %copy-start = (bf16[1,128,4096]{2,1,0:T(8,128)(2,1)S(1)}, bf16[1,128,4096]{2,1,0:T(8,128)(2,1)}, u32[]{:S(2)}) copy-start(bf16[1,128,4096]{2,1,0:T(8,128)(2,1)} %param.8) | copy-start | bytes 3145732
  0.0 6.7 %copy-start.1 = (bf16[1,128,1024]{2,1,0:T(8,128)(2,1)S(1)}, bf16[1,128,1024]{2,1,0:T(8,128)(2,1)}, u32[]{:S(2)}) copy-start(bf16[1,128,1024]{2,1,0:T(8,128)(2,1)} %param.9) | copy-start | bytes 786436
  0.0 7.6 %copy-start.2 = (bf16[1,128,1024]{2,1,0:T(8,128)(2,1)S(1)}, bf16[1,128,1024]{2,1,0:T(8,128)(2,1)}, u32[]{:S(2)}) copy-start(bf16[1,128,1024]{2,1,0:T(8,128)(2,1)} %param.10) | copy-start | bytes 786436
  2.4 19.2 %collective-permute-start.6 = (bf16[256,1024]{1,0:T(8,128)(2,1)}, bf16[256,1024]{1,0:T(8,128)(2,1)}, u32[]{:S(2)}, u32[]{:S(2)}) collective-permute-start(bf16[256,1024]{1,0:T(8,128)(2,1)} %get-tuple-element.27), channel_id=1, source_target_pairs={{16,32},{48,0},{80,96},{112,64},{0,112},{96,16},{32,80},{64,48},{1... | collective-permute-start | bytes 1572872 | tf_op jit(solution)/shard_map/ppermute | solution.py:512
  5.0 16.6 %collective-permute-start.7 = (bf16[256,1024]{1,0:T(8,128)(2,1)}, bf16[256,1024]{1,0:T(8,128)(2,1)}, u32[]{:S(2)}, u32[]{:S(2)}) collective-permute-start(bf16[256,1024]{1,0:T(8,128)(2,1)} %get-tuple-element.27), channel_id=1, source_target_pairs={{0,16},{16,0},{1,17},{17,1},{2,18},{18,2},{3,19},{19,3},{4,20},{20... | collective-permute-start | bytes 1572872 | tf_op jit(solution)/shard_map/ppermute | solution.py:513
  6.1 1.5 %collective-permute-start.3 = (s32[2064]{0:T(1024)S(1)}, s32[2064]{0:T(1024)S(1)}, u32[]{:S(2)}, u32[]{:S(2)}) collective-permute-start(s32[2064]{0:T(1024)S(1)} %pad_add_fusion.1), channel_id=1, source_target_pairs={{0,16},{16,0},{1,17},{17,1},{2,18},{18,2},{3,19},{19,3},{4,20},{20... | collective-permute-start | bytes 24776 | tf_op jit(solution)/shard_map/ppermute | solution.py:505
  6.2 5.1 %collective-permute-start = (bf16[128,4096]{1,0:T(8,128)(2,1)S(1)}, bf16[128,4096]{1,0:T(8,128)(2,1)S(1)}, u32[]{:S(2)}, u32[]{:S(2)}) collective-permute-start(bf16[128,4096]{1,0:T(8,128)(2,1)S(1)} %bitcast.34), channel_id=1, source_target_pairs={{0,16},{16,0},{1,17},{17,1},{2,18},{18,2},{3,19},{19,3},{4,20},{20... | collective-permute-start | bytes 3145736 | tf_op jit(solution)/shard_map/ppermute | solution.py:506
  6.7 2.8 %collective-permute-start.1 = (bf16[128,1024]{1,0:T(8,128)(2,1)S(1)}, bf16[128,1024]{1,0:T(8,128)(2,1)S(1)}, u32[]{:S(2)}, u32[]{:S(2)}) collective-permute-start(bf16[128,1024]{1,0:T(8,128)(2,1)S(1)} %bitcast.36), channel_id=1, source_target_pairs={{0,16},{16,0},{1,17},{17,1},{2,18},{18,2},{3,19},{19,3},{4,20},{20... | collective-permute-start | bytes 786440 | tf_op jit(solution)/shard_map/ppermute | solution.py:506
  6.9 6.8 %copy-start.3 = (s32[2]{0:T(128)}, s32[2]{0:T(128)S(1)}, u32[]{:S(2)}) copy-start(s32[2]{0:T(128)S(1)} %pad_add_fusion.2.spot) | copy-start | bytes 28
  7.7 3.6 %collective-permute-start.2 = (bf16[128,1024]{1,0:T(8,128)(2,1)S(1)}, bf16[128,1024]{1,0:T(8,128)(2,1)S(1)}, u32[]{:S(2)}, u32[]{:S(2)}) collective-permute-start(bf16[128,1024]{1,0:T(8,128)(2,1)S(1)} %bitcast.38), channel_id=1, source_target_pairs={{0,16},{16,0},{1,17},{17,1},{2,18},{18,2},{3,19},{19,3},{4,20},{20... | collective-permute-start | bytes 786440 | tf_op jit(solution)/shard_map/ppermute | solution.py:506
  9.5 12.1 %collective-permute-start.5 = (bf16[256,1024]{1,0:T(8,128)(2,1)}, bf16[256,1024]{1,0:T(8,128)(2,1)}, u32[]{:S(2)}, u32[]{:S(2)}) collective-permute-start(bf16[256,1024]{1,0:T(8,128)(2,1)} %get-tuple-element.28.own), channel_id=1, source_target_pairs={{0,32},{32,0},{64,96},{96,64},{16,112},{112,16},{48,80},{80,48},{1... | collective-permute-start | bytes 1572872 | tf_op jit(solution)/shard_map/ppermute | solution.py:511
  13.7 34.8 %all-to-all-start = ((bf16[16,128,384]{2,1,0:T(8,128)(2,1)}), bf16[16,128,384]{2,1,0:T(8,128)(2,1)}, u32[]{:S(2)}, u32[]{:S(2)}) async-start(bf16[16,128,384]{2,1,0:T(8,128)(2,1)} %bitcast.7), calls=%async_computation | async-start | bytes 3145728 | tf_op jit(solution)/shard_map/all_to_all | solution.py:528
  24.3 14.3 %collective-permute-start.8 = (bf16[2,256,1024]{2,1,0:T(8,128)(2,1)}, bf16[2,256,1024]{2,1,0:T(8,128)(2,1)}, u32[]{:S(2)}, u32[]{:S(2)}) collective-permute-start(bf16[2,256,1024]{2,1,0:T(8,128)(2,1)} %relay_kernel.1), channel_id=1, source_target_pairs={{0,96},{96,0},{32,64},{64,32},{16,48},{48,16},{80,112},{112,80},{1... | collective-permute-start | bytes 3145736 | tf_op jit(solution)/shard_map/ppermute | solution.py:535
  48.5 20.1 %all-to-all-start.1 = ((bf16[16,256,128]{2,1,0:T(8,128)(2,1)}), bf16[16,256,128]{2,1,0:T(8,128)(2,1)S(1)}, u32[]{:S(2)}, u32[]{:S(2)}) async-start(bf16[16,256,128]{2,1,0:T(8,128)(2,1)} %bitcast.42), calls=%async_computation.1 | async-start | bytes 2097152 | tf_op jit(solution)/shard_map/all_to_all | solution.py:556
  53.2 2.7 %collective-permute-start.4 = (bf16[2048,128]{1,0:T(8,128)(2,1)S(1)}, bf16[2048,128]{1,0:T(8,128)(2,1)S(1)}, u32[]{:S(2)}, u32[]{:S(2)}) collective-permute-start(bf16[2048,128]{1,0:T(8,128)(2,1)S(1)} %slice.36), channel_id=1, source_target_pairs={{0,16},{16,0},{1,17},{17,1},{2,18},{18,2},{3,19},{19,3},{4,20},{20... | collective-permute-start | bytes 1572872 | tf_op jit(solution)/shard_map/ppermute | solution.py:537
  55.9 0.8 copy-start.10
  68.6 1.0 copy-start.5
  69.6 4.4 %collective-permute-start.9 = (bf16[4096,128]{1,0:T(8,128)(2,1)S(1)}, bf16[4096,128]{1,0:T(8,128)(2,1)}, u32[]{:S(2)}, u32[]{:S(2)}) collective-permute-start(bf16[4096,128]{1,0:T(8,128)(2,1)S(1)} %bitcast.43), channel_id=1, source_target_pairs={{0,16},{16,0},{1,17},{17,1},{2,18},{18,2},{3,19},{19,3},{4,20},{20... | collective-permute-start | bytes 3145736 | tf_op jit(solution)/shard_map/ppermute | solution.py:560
  115.9 3.2 %copy-start.4 = (bf16[16,128,256]{2,1,0:T(8,128)(2,1)}, bf16[16,128,256]{2,1,0:T(8,128)(2,1)S(1)}, u32[]{:S(2)}) copy-start(bf16[16,128,256]{2,1,0:T(8,128)(2,1)S(1)} %all_to_all.15) | copy-start | bytes 3145732
  115.9 3.2 %collective-permute-start.10 = (bf16[8,128,256]{2,1,0:T(8,128)(2,1)S(1)}, bf16[8,128,256]{2,1,0:T(8,128)(2,1)S(1)}, u32[]{:S(2)}, u32[]{:S(2)}) collective-permute-start(bf16[8,128,256]{2,1,0:T(8,128)(2,1)S(1)} %dynamic-slice_bitcast_fusion), channel_id=1, source_target_pairs={{0,16},{16,0},{1,17},{17,1},{2,18},{18,2},{3,19},{19,3},{4,20},{20... | collective-permute-start | bytes 1572872 | tf_op jit(solution)/shard_map/ppermute | solution.py:567
  119.1 0.8 copy-start.6

commit v12 on v9

--- a/solution.py
+++ b/solution.py
@@ -35,7 +35,8 @@
 
 
 NT = (((1,), (1,)), ((), ()))
-ROOM = 127 * 512 * 1024
+ROOM = 56 * 1024 * 1024
+FULL = 127 * 512 * 1024
 
 
 def rotary_table():
@@ -205,7 +206,7 @@
             out_specs=whole,
             scratch_shapes=[pltpu.VMEM(shape, jnp.bfloat16), pltpu.SemaphoreType.DMA(sems)],
         ),
-        compiler_params=pltpu.CompilerParams(vmem_limit_bytes=ROOM),
+        compiler_params=pltpu.CompilerParams(vmem_limit_bytes=FULL),
         name=kernel.__name__,
     )(*scalars, *arrays)
 
@@ -408,7 +409,6 @@
 def stem_part(core, arrived, mine, other, before):
     pack = arrived.shape[0]
     stem = mine.shape[0]
-    once = dict(pipeline_mode=pl.Buffered(1))
     return pl.pallas_call(
         stem_kernel,
         out_shape=jax.ShapeDtypeStruct((pack, 2 * HD), jnp.bfloat16),
@@ -417,8 +417,8 @@
             grid=(pack // BQ,),
             in_specs=[
                 pl.BlockSpec((BQ, 2 * HD), lambda i, *_: (i, 0)),
-                pl.BlockSpec((stem, HD), lambda i, *_: (0, 0), **once),
-                pl.BlockSpec((stem, HD), lambda i, *_: (0, 0), **once),
+                pl.BlockSpec(memory_space=pltpu.VMEM),
+                pl.BlockSpec(memory_space=pltpu.VMEM),
                 pl.BlockSpec((1, HD + 16, 2 * BQ), lambda i, *_: (i, 0, 0)),
             ],
             out_specs=pl.BlockSpec((BQ, 2 * HD), lambda i, *_: (i, 0)),
@@ -430,42 +430,43 @@
                 pltpu.VMEM((HD + 8, 2 * BQ), jnp.float32),
             ],
         ),
-        compiler_params=pltpu.CompilerParams(vmem_limit_bytes=ROOM),
+        compiler_params=pltpu.CompilerParams(vmem_limit_bytes=48 * 1024 * 1024),
         cost_estimate=pl.CostEstimate(
             flops=8 * pack * stem * HD, bytes_accessed=8 << 20, transcendentals=2 * pack * stem
         ),
         name="stem_part",
-    )(core, arrived, mine, other, before)
+    )(core, arrived, inside(mine), inside(other), before)
 
 
 def gather_kernel(core, mine_ref, other_ref, o_ref):
+    step = pl.program_id(0)
+    heads = KVH // 2
     first = core[0] == 0
-    for e in range(mine_ref.shape[1]):
-        mine = mine_ref[0, e]
-        other = other_ref[e]
+    for e in range(heads):
+        own, got = mine_ref[core[0], step * heads + e], other_ref[step * heads + e]
         at = 4 * HD * e
-        o_ref[:, at : at + 2 * HD] = jnp.where(first, mine, other)
-        o_ref[:, at + 2 * HD : at + 4 * HD] = jnp.where(first, other, mine)
+        o_ref[:, at : at + 2 * HD] = jnp.where(first, own, got)
+        o_ref[:, at + 2 * HD : at + 4 * HD] = jnp.where(first, got, own)
+
+
+def inside(part):
+    return pltpu.with_memory_space_constraint(part, pltpu.VMEM)
 
 
 def gather(core, mine, other):
     tok = mine.shape[2]
-    heads = KVH // 2
+    whole = pl.BlockSpec(memory_space=pltpu.VMEM)
     return pl.pallas_call(
         gather_kernel,
         out_shape=jax.ShapeDtypeStruct((tok, H * HD), jnp.bfloat16),
         grid_spec=pltpu.PrefetchScalarGridSpec(
             num_scalar_prefetch=1,
             grid=(2,),
-            in_specs=[
-                pl.BlockSpec((1, heads, tok, 2 * HD), lambda i, core: (core[0], i, 0, 0)),
-                pl.BlockSpec((heads, tok, 2 * HD), lambda i, core: (i, 0, 0)),
-            ],
+            in_specs=[whole, whole],
             out_specs=pl.BlockSpec((tok, H * HD // 2), lambda i, core: (0, i)),
         ),
-        compiler_params=pltpu.CompilerParams(vmem_limit_bytes=ROOM),
         name="gather",
-    )(core, mine, other)
+    )(core, inside(mine), inside(other))
 
 
 def shards(queries, keys, values, stem_kv, seg_ids, seg_parent, stem_owner):

time: 122 us -> 118 us (0.967)
  Pallas kernels: 41.5 us -> 39.1 us
  waiting for transfers between devices: 23.9 us -> 22.6 us
    pallas_call x1, Pallas kernels: 20.2 us -> 18.8 us  [stem_part(): pl.pallas_call(stem_kernel, out_shape=jax.ShapeDtypeStruct((pack, 2 * HD)...]
where the time goes in v12:
time: 118 us
  Pallas kernels  39.1 us (33%)
  waiting for transfers between devices  22.6 us (19%)
  starting transfers between devices  22.4 us (19%)
  blocking collectives  21.7 us (18%)
  local copies, waits for them, and re-layouts  4.98 us (4%)
  other arithmetic  3.56 us (3%)
  matrix products  3 us (3%)
    all_to_all x1, blocking collectives, shards(): lax.all_to_all(mixed.reshape(16, tok, 2 * HD), SEQ, split_axis=0, concat_...  21.7 us
    pallas_call x1, Pallas kernels, stem_part(): pl.pallas_call(stem_kernel, out_shape=jax.ShapeDtypeStruct((pack, 2 * HD)...  18.8 us
    pallas_call x1, Pallas kernels, pack_part(): pl.pallas_call(pack_kernel, out_shape=jax.ShapeDtypeStruct((pack // BQ, H...  11.3 us
    ppermute x1, waiting for transfers between devices, shards(): two = lax.ppermute(wanted, ('x', 'core'), joint(1, 0))  10.5 us
    all_to_all x1, starting transfers between devices, shards(): lax.all_to_all(sent.reshape(16, tok, 3 * HD), SEQ, split_axis=0, concat_a...  7.81 us
    all_to_all x1, waiting for transfers between devices, shards(): lax.all_to_all(sent.reshape(16, tok, 3 * HD), SEQ, split_axis=0, concat_a...  6.97 us
    pallas_call x2, Pallas kernels, moved(): pl.pallas_call(kernel, out_shape=jax.ShapeDtypeStruct(shape, jnp.bfloat16...  5.56 us
    all_to_all x1, starting transfers between devices, shards(): lax.all_to_all(stems, SEQ, split_axis=0, concat_axis=0, tiled=True)  3.66 us
  transfers between devices with their start and end apart: 13, of which 7 were waited for; matrix products, arithmetic and copies ran while one was open for 7% of the time, Pallas kernels for 16%

profile of v12, /device:TPU:1, one launch (start us, length us, event | category | flops | bytes accessed | tf_op | source)
XLA Modules:
  0.0 117.7 jit_solution(5094575837218579632)
XLA Ops:
  0.0 2.4 %dynamic-slice_bitcast_fusion.1 = (bf16[256,1024]{1,0:T(8,128)(2,1)}, bf16[256,1024]{1,0:T(8,128)(2,1)}) fusion(bf16[1,2,256,1024]{3,2,1,0:T(8,128)(2,1)} %param.11, s32[]{:T(128)S(6)} %select_n.53, s32[]{:T(128)S(6)} %select_n.52), kind=kLoop, calls=%fused_computation.27 | loop fusion | bytes 2097160 | tf_op jit(solution)/shard_map/jit(dynamic_index_in_dim)/squeeze | solution.py:488
  2.4 2.6 %collective-permute-start.6 = (bf16[256,1024]{1,0:T(8,128)(2,1)}, bf16[256,1024]{1,0:T(8,128)(2,1)}, u32[]{:S(2)}, u32[]{:S(2)}) collective-permute-start(bf16[256,1024]{1,0:T(8,128)(2,1)} %get-tuple-element.27), channel_id=1, source_target_pairs={{16,32},{48,0},{80,96},{112,64},{0,112},{96,16},{32,80},{64,48},{1... | collective-permute-start | bytes 1572872 | tf_op jit(solution)/shard_map/ppermute | solution.py:490
  5.0 1.1 collective-permute-start.7
  6.2 0.5 collective-permute-start
  7.0 0.7 collective-permute-done.3
  9.5 1.1 collective-permute-start.5
  10.6 0.5 fusion.23
  11.3 2.4 %turn.1 = bf16[2,8,128,384]{3,2,1,0:T(8,128)(2,1)} custom-call(s32[2]{0:T(128)S(1)} %pad_add_fusion.2.spot, bf16[128,4096]{1,0:T(8,128)(2,1)S(1)} %bitcast.37, bf16[128,1024]{1,0:T(8,128)(2,1)S(1)} %bitcast.42, bf16[128,1024]{1,0:T(8,128)(2,1)S(1)} %bitcast.44, bf16[128,4096]{1,0:T(8,128)(2,1)S(1)} %collective-permute-done.q_mate, ...), custom_call_target="tpu_custom_call" | custom-call | tf_op jit(solution)/shard_map/turn/pallas_call | solution.py:124
  13.7 7.8 %all-to-all-start = ((bf16[16,128,384]{2,1,0:T(8,128)(2,1)}), bf16[16,128,384]{2,1,0:T(8,128)(2,1)}, u32[]{:S(2)}, u32[]{:S(2)}) async-start(bf16[16,128,384]{2,1,0:T(8,128)(2,1)} %bitcast.7), calls=%async_computation | async-start | bytes 3145728 | tf_op jit(solution)/shard_map/all_to_all | solution.py:506
  21.6 2.7 %relay_kernel.1 = bf16[2,256,1024]{2,1,0:T(8,128)(2,1)} custom-call(s32[2]{0:T(128)} %copy-done.3, s32[8]{0:T(128)} %owner.3, bf16[256,1024]{1,0:T(8,128)(2,1)} %get-tuple-element.28.own, bf16[256,1024]{1,0:T(8,128)(2,1)} %collective-permute-done.5.same, bf16[256,1024]{1,0:T(8,128)(2,1)} %collective-permute-done.7.flip, ...), custom_call_target="tpu_custom_call" | custom-call | tf_op jit(solution)/shard_map/relay_kernel/pallas_call | solution.py:199
  24.3 0.6 collective-permute-start.8
  25.0 0.6 broadcast.78
  25.5 0.7 fusion.42
  26.6 1.5 %convolution_convert_fusion.qb_ref = bf16[2048,128]{1,0:T(8,128)(2,1)} fusion(s32[2048]{0:T(1024)S(1)} %bitcast.46, f32[16,16]{0,1:T(8,128)S(1)} %fusion.33), kind=kOutput, calls=%fused_computation | convolution fusion | flops 403177472 | bytes 533504 | tf_op jit(solution)/shard_map/dot_general | solution.py:522
  28.2 10.5 %collective-permute-done.8.two = bf16[2,256,1024]{2,1,0:T(8,128)(2,1)} collective-permute-done((bf16[2,256,1024]{2,1,0:T(8,128)(2,1)}, bf16[2,256,1024]{2,1,0:T(8,128)(2,1)}, u32[]{:S(2)}, u32[]{:S(2)}) %collective-permute-start.8) | collective-permute-done | bytes 1048608 | tf_op jit(solution)/shard_map/ppermute | solution.py:513
  38.6 2.9 %settle_kernel.1 = bf16[2,8,256,128]{3,2,1,0:T(8,128)(2,1)} custom-call(s32[2]{0:T(128)} %copy-done.3, s32[8]{0:T(128)} %owner.3, bf16[256,1024]{1,0:T(8,128)(2,1)} %get-tuple-element.28.own, bf16[256,1024]{1,0:T(8,128)(2,1)} %collective-permute-done.5.same, bf16[256,1024]{1,0:T(8,128)(2,1)} %collective-permute-done.7.flip, ...), custom_call_target="tpu_custom_call" | custom-call | tf_op jit(solution)/shard_map/settle_kernel/pallas_call | solution.py:199
  41.5 7.0 %all-to-all-done = bf16[16,128,384]{2,1,0:T(8,128)(2,1)} async-done(((bf16[16,128,384]{2,1,0:T(8,128)(2,1)}), bf16[16,128,384]{2,1,0:T(8,128)(2,1)}, u32[]{:S(2)}, u32[]{:S(2)}) %all-to-all-start) | async-done | bytes 1572896 | tf_op jit(solution)/shard_map/all_to_all | solution.py:506
  48.5 3.7 %all-to-all-start.1 = ((bf16[16,256,128]{2,1,0:T(8,128)(2,1)}), bf16[16,256,128]{2,1,0:T(8,128)(2,1)S(1)}, u32[]{:S(2)}, u32[]{:S(2)}) async-start(bf16[16,256,128]{2,1,0:T(8,128)(2,1)} %bitcast.45), calls=%async_computation.1 | async-start | bytes 2097152 | tf_op jit(solution)/shard_map/all_to_all | solution.py:534
  52.2 1.1 slice.36
  53.2 0.7 collective-permute-start.4
  54.0 0.8 fusion.18.seen
  54.8 1.1 select_convert_fusion.kb_ref
  55.9 0.8 copy-done.7
  56.7 11.3 %pack_part.1.part_ref = f32[4,144,1024]{2,1,0:T(8,128)} custom-call(s32[1]{0:T(128)} %bitcast.core, s32[4,4]{1,0:T(4,128)} %fusion.18.seen, bf16[2048,384]{1,0:T(8,128)(2,1)} %bitcast.8.q_ref.mine_ref, bf16[2048,384]{1,0:T(8,128)(2,1)} %bitcast.8.q_ref.mine_ref, bf16[2048,128]{1,0:T(8,128)(2,1)} %copy-done.7, ...), custom_call_target="tpu_custom_call" | custom-call | flops 4294967296 | bytes 8388608 | tf_op jit(solution)/shard_map/pack_part/pallas_call | solution.py:319
  68.0 0.4 all-to-all-done.1
  68.5 2.1 %collective-permute-start.9 = (bf16[4096,128]{1,0:T(8,128)(2,1)S(1)}, bf16[4096,128]{1,0:T(8,128)(2,1)S(1)}, u32[]{:S(2)}, u32[]{:S(2)}) collective-permute-start(bf16[4096,128]{1,0:T(8,128)(2,1)S(1)} %bitcast.38), channel_id=1, source_target_pairs={{0,16},{16,0},{1,17},{17,1},{2,18},{18,2},{3,19},{19,3},{4,20},{20... | collective-permute-start | bytes 3145736 | tf_op jit(solution)/shard_map/ppermute | solution.py:538
  70.6 2.3 %collective-permute-done.9.other_ref = bf16[4096,128]{1,0:T(8,128)(2,1)S(1)} collective-permute-done((bf16[4096,128]{1,0:T(8,128)(2,1)S(1)}, bf16[4096,128]{1,0:T(8,128)(2,1)S(1)}, u32[]{:S(2)}, u32[]{:S(2)}) %collective-permute-start.9) | collective-permute-done | bytes 1048608 | tf_op jit(solution)/shard_map/ppermute | solution.py:538
  72.9 18.8 %stem_part.1 = bf16[2048,256]{1,0:T(8,128)(2,1)S(1)} custom-call(s32[1]{0:T(128)} %bitcast.core, bf16[2048,384]{1,0:T(8,128)(2,1)} %bitcast.8.q_ref.mine_ref, bf16[4096,128]{1,0:T(8,128)(2,1)S(1)} %bitcast.39, bf16[4096,128]{1,0:T(8,128)(2,1)S(1)} %collective-permute-done.9.other_ref, f32[4,144,1024]{2,1,0:T(8,128)} %pack_part.1.part_ref), custom_call_target="tpu_custom_call" | custom-call | flops 8589934592 | bytes 8388608 | tf_op jit(solution)/shard_map/stem_part/pallas_call | solution.py:412
  91.7 21.7 %all_to_all.15 = bf16[16,128,256]{2,1,0:T(8,128)(2,1)S(1)} all-to-all(bf16[16,128,256]{2,1,0:T(8,128)(2,1)S(1)} %bitcast.40), channel_id=1, replica_groups=mesh['x'=4,'core'=2,'z'=4,'y'=4] {'z','y'}, dimensions={0} | all-to-all | bytes 2097152 | tf_op jit(solution)/shard_map/all_to_all | solution.py:541
  113.5 1.6 %collective-permute-start.10 = (bf16[8,128,256]{2,1,0:T(8,128)(2,1)S(1)}, bf16[8,128,256]{2,1,0:T(8,128)(2,1)S(1)}, u32[]{:S(2)}, u32[]{:S(2)}) collective-permute-start(bf16[8,128,256]{2,1,0:T(8,128)(2,1)S(1)} %dynamic-slice_bitcast_fusion), channel_id=1, source_target_pairs={{0,16},{16,0},{1,17},{17,1},{2,18},{18,2},{3,19},{19,3},{4,20},{20... | collective-permute-start | bytes 1572872 | tf_op jit(solution)/shard_map/ppermute | solution.py:545
  115.1 1.5 %collective-permute-done.10.other_ref = bf16[8,128,256]{2,1,0:T(8,128)(2,1)S(1)} collective-permute-done((bf16[8,128,256]{2,1,0:T(8,128)(2,1)S(1)}, bf16[8,128,256]{2,1,0:T(8,128)(2,1)S(1)}, u32[]{:S(2)}, u32[]{:S(2)}) %collective-permute-start.10) | collective-permute-done | bytes 524320 | tf_op jit(solution)/shard_map/ppermute | solution.py:545
  116.6 1.0 gather.1
  (54 shorter events, 2.8 us)
Async XLA Ops:
  0.0 10.6 %copy-start.5 = (f32[64]{0:T(128)S(1)}, f32[64]{0:T(128)}, u32[]{:S(2)}) copy-start(f32[64]{0:T(128)} %constant.81.clone) | copy-start | bytes 772
  0.0 6.1 %copy-start.4 = (s32[1,2048]{1,0:T(1,128)S(1)}, s32[1,2048]{1,0:T(1,128)}, u32[]{:S(2)}) copy-start(s32[1,2048]{1,0:T(1,128)} %param.12) | copy-start | bytes 24580
  0.0 6.1 %copy-start.6 = (s32[1,16]{1,0:T(1,128)S(1)}, s32[1,16]{1,0:T(1,128)}, u32[]{:S(2)}) copy-start(s32[1,16]{1,0:T(1,128)} %param.13) | copy-start | bytes 196
  0.0 6.2 %copy-start = (bf16[1,128,4096]{2,1,0:T(8,128)(2,1)S(1)}, bf16[1,128,4096]{2,1,0:T(8,128)(2,1)}, u32[]{:S(2)}) copy-start(bf16[1,128,4096]{2,1,0:T(8,128)(2,1)} %param.8) | copy-start | bytes 3145732
  0.0 6.7 %copy-start.1 = (bf16[1,128,1024]{2,1,0:T(8,128)(2,1)S(1)}, bf16[1,128,1024]{2,1,0:T(8,128)(2,1)}, u32[]{:S(2)}) copy-start(bf16[1,128,1024]{2,1,0:T(8,128)(2,1)} %param.9) | copy-start | bytes 786436
  0.0 7.6 %copy-start.2 = (bf16[1,128,1024]{2,1,0:T(8,128)(2,1)S(1)}, bf16[1,128,1024]{2,1,0:T(8,128)(2,1)}, u32[]{:S(2)}) copy-start(bf16[1,128,1024]{2,1,0:T(8,128)(2,1)} %param.10) | copy-start | bytes 786436
  2.4 19.2 %collective-permute-start.6 = (bf16[256,1024]{1,0:T(8,128)(2,1)}, bf16[256,1024]{1,0:T(8,128)(2,1)}, u32[]{:S(2)}, u32[]{:S(2)}) collective-permute-start(bf16[256,1024]{1,0:T(8,128)(2,1)} %get-tuple-element.27), channel_id=1, source_target_pairs={{16,32},{48,0},{80,96},{112,64},{0,112},{96,16},{32,80},{64,48},{1... | collective-permute-start | bytes 1572872 | tf_op jit(solution)/shard_map/ppermute | solution.py:490
  5.0 16.6 %collective-permute-start.7 = (bf16[256,1024]{1,0:T(8,128)(2,1)}, bf16[256,1024]{1,0:T(8,128)(2,1)}, u32[]{:S(2)}, u32[]{:S(2)}) collective-permute-start(bf16[256,1024]{1,0:T(8,128)(2,1)} %get-tuple-element.27), channel_id=1, source_target_pairs={{0,16},{16,0},{1,17},{17,1},{2,18},{18,2},{3,19},{19,3},{4,20},{20... | collective-permute-start | bytes 1572872 | tf_op jit(solution)/shard_map/ppermute | solution.py:491
  6.1 1.5 %collective-permute-start.3 = (s32[2064]{0:T(1024)S(1)}, s32[2064]{0:T(1024)S(1)}, u32[]{:S(2)}, u32[]{:S(2)}) collective-permute-start(s32[2064]{0:T(1024)S(1)} %pad_add_fusion.1), channel_id=1, source_target_pairs={{0,16},{16,0},{1,17},{17,1},{2,18},{18,2},{3,19},{19,3},{4,20},{20... | collective-permute-start | bytes 24776 | tf_op jit(solution)/shard_map/ppermute | solution.py:483
  6.2 5.1 %collective-permute-start = (bf16[128,4096]{1,0:T(8,128)(2,1)S(1)}, bf16[128,4096]{1,0:T(8,128)(2,1)S(1)}, u32[]{:S(2)}, u32[]{:S(2)}) collective-permute-start(bf16[128,4096]{1,0:T(8,128)(2,1)S(1)} %bitcast.36), channel_id=1, source_target_pairs={{0,16},{16,0},{1,17},{17,1},{2,18},{18,2},{3,19},{19,3},{4,20},{20... | collective-permute-start | bytes 3145736 | tf_op jit(solution)/shard_map/ppermute | solution.py:484
  6.7 2.8 %collective-permute-start.1 = (bf16[128,1024]{1,0:T(8,128)(2,1)S(1)}, bf16[128,1024]{1,0:T(8,128)(2,1)S(1)}, u32[]{:S(2)}, u32[]{:S(2)}) collective-permute-start(bf16[128,1024]{1,0:T(8,128)(2,1)S(1)} %bitcast.41), channel_id=1, source_target_pairs={{0,16},{16,0},{1,17},{17,1},{2,18},{18,2},{3,19},{19,3},{4,20},{20... | collective-permute-start | bytes 786440 | tf_op jit(solution)/shard_map/ppermute | solution.py:484
  6.9 6.8 %copy-start.3 = (s32[2]{0:T(128)}, s32[2]{0:T(128)S(1)}, u32[]{:S(2)}) copy-start(s32[2]{0:T(128)S(1)} %pad_add_fusion.2.spot) | copy-start | bytes 28
  7.7 3.6 %collective-permute-start.2 = (bf16[128,1024]{1,0:T(8,128)(2,1)S(1)}, bf16[128,1024]{1,0:T(8,128)(2,1)S(1)}, u32[]{:S(2)}, u32[]{:S(2)}) collective-permute-start(bf16[128,1024]{1,0:T(8,128)(2,1)S(1)} %bitcast.43), channel_id=1, source_target_pairs={{0,16},{16,0},{1,17},{17,1},{2,18},{18,2},{3,19},{19,3},{4,20},{20... | collective-permute-start | bytes 786440 | tf_op jit(solution)/shard_map/ppermute | solution.py:484
  9.5 12.0 %collective-permute-start.5 = (bf16[256,1024]{1,0:T(8,128)(2,1)}, bf16[256,1024]{1,0:T(8,128)(2,1)}, u32[]{:S(2)}, u32[]{:S(2)}) collective-permute-start(bf16[256,1024]{1,0:T(8,128)(2,1)} %get-tuple-element.28.own), channel_id=1, source_target_pairs={{0,32},{32,0},{64,96},{96,64},{16,112},{112,16},{48,80},{80,48},{1... | collective-permute-start | bytes 1572872 | tf_op jit(solution)/shard_map/ppermute | solution.py:489
  13.7 34.8 %all-to-all-start = ((bf16[16,128,384]{2,1,0:T(8,128)(2,1)}), bf16[16,128,384]{2,1,0:T(8,128)(2,1)}, u32[]{:S(2)}, u32[]{:S(2)}) async-start(bf16[16,128,384]{2,1,0:T(8,128)(2,1)} %bitcast.7), calls=%async_computation | async-start | bytes 3145728 | tf_op jit(solution)/shard_map/all_to_all | solution.py:506
  24.3 14.3 %collective-permute-start.8 = (bf16[2,256,1024]{2,1,0:T(8,128)(2,1)}, bf16[2,256,1024]{2,1,0:T(8,128)(2,1)}, u32[]{:S(2)}, u32[]{:S(2)}) collective-permute-start(bf16[2,256,1024]{2,1,0:T(8,128)(2,1)} %relay_kernel.1), channel_id=1, source_target_pairs={{0,96},{96,0},{32,64},{64,32},{16,48},{48,16},{80,112},{112,80},{1... | collective-permute-start | bytes 3145736 | tf_op jit(solution)/shard_map/ppermute | solution.py:513
  48.5 20.0 %all-to-all-start.1 = ((bf16[16,256,128]{2,1,0:T(8,128)(2,1)}), bf16[16,256,128]{2,1,0:T(8,128)(2,1)S(1)}, u32[]{:S(2)}, u32[]{:S(2)}) async-start(bf16[16,256,128]{2,1,0:T(8,128)(2,1)} %bitcast.45), calls=%async_computation.1 | async-start | bytes 2097152 | tf_op jit(solution)/shard_map/all_to_all | solution.py:534
  53.2 2.7 %collective-permute-start.4 = (bf16[2048,128]{1,0:T(8,128)(2,1)S(1)}, bf16[2048,128]{1,0:T(8,128)(2,1)S(1)}, u32[]{:S(2)}, u32[]{:S(2)}) collective-permute-start(bf16[2048,128]{1,0:T(8,128)(2,1)S(1)} %slice.36), channel_id=1, source_target_pairs={{0,16},{16,0},{1,17},{17,1},{2,18},{18,2},{3,19},{19,3},{4,20},{20... | collective-permute-start | bytes 1572872 | tf_op jit(solution)/shard_map/ppermute | solution.py:515
  55.9 0.8 copy-start.7
  68.5 4.4 %collective-permute-start.9 = (bf16[4096,128]{1,0:T(8,128)(2,1)S(1)}, bf16[4096,128]{1,0:T(8,128)(2,1)S(1)}, u32[]{:S(2)}, u32[]{:S(2)}) collective-permute-start(bf16[4096,128]{1,0:T(8,128)(2,1)S(1)} %bitcast.38), channel_id=1, source_target_pairs={{0,16},{16,0},{1,17},{17,1},{2,18},{18,2},{3,19},{19,3},{4,20},{20... | collective-permute-start | bytes 3145736 | tf_op jit(solution)/shard_map/ppermute | solution.py:538
  113.5 3.2 %collective-permute-start.10 = (bf16[8,128,256]{2,1,0:T(8,128)(2,1)S(1)}, bf16[8,128,256]{2,1,0:T(8,128)(2,1)S(1)}, u32[]{:S(2)}, u32[]{:S(2)}) collective-permute-start(bf16[8,128,256]{2,1,0:T(8,128)(2,1)S(1)} %dynamic-slice_bitcast_fusion), channel_id=1, source_target_pairs={{0,16},{16,0},{1,17},{17,1},{2,18},{18,2},{3,19},{19,3},{4,20},{20... | collective-permute-start | bytes 1572872 | tf_op jit(solution)/shard_map/ppermute | solution.py:545

commit v13 on v8

--- a/solution.py
+++ b/solution.py
@@ -115,10 +115,7 @@
 
 def turn(here, own, mate, cosine, sine):
     tok = own[0].shape[0]
-    whole = [
-        pl.BlockSpec(part.shape, lambda i, here: (0, 0), pipeline_mode=pl.Buffered(1))
-        for part in own + mate
-    ]
+    whole = [pl.BlockSpec(memory_space=pltpu.VMEM)] * 6
     table = pl.BlockSpec(cosine.shape, lambda i, here: (0, 0, 0), pipeline_mode=pl.Buffered(1))
     return pl.pallas_call(
         turn_kernel,
@@ -131,7 +128,7 @@
         ),
         compiler_params=pltpu.CompilerParams(vmem_limit_bytes=32 * 1024 * 1024),
         name="turn",
-    )(here, *own, *mate, cosine, sine)
+    )(here, *[inside(part) for part in own + mate], cosine, sine)
 
 
 def held_at(x, core, group):
@@ -185,6 +182,10 @@
             ).wait()
 
 
+def inside(part):
+    return pltpu.with_memory_space_constraint(part, pltpu.VMEM)
+
+
 def moved(kernel, shape, sems, scalars, arrays):
     return pl.pallas_call(
         kernel,
@@ -192,12 +193,13 @@
         grid_spec=pltpu.PrefetchScalarGridSpec(
             num_scalar_prefetch=len(scalars),
             grid=(1,),
-            in_specs=[pl.BlockSpec(memory_space=pl.ANY)] * len(arrays),
-            out_specs=pl.BlockSpec(shape, lambda *_: (0,) * len(shape)),
+            in_specs=[pl.BlockSpec(memory_space=pltpu.VMEM)] * len(arrays),
+            out_specs=pl.BlockSpec(memory_space=pl.ANY),
             scratch_shapes=[pltpu.SemaphoreType.DMA(sems)],
         ),
+        compiler_params=pltpu.CompilerParams(vmem_limit_bytes=16 * 1024 * 1024),
         name=kernel.__name__,
-    )(*scalars, *arrays)
+    )(*scalars, *[inside(part) for part in arrays])
 
 
 def flipped_dot(left, right):
@@ -398,7 +400,6 @@
 def stem_part(core, arrived, mine, other, before):
     pack = arrived.shape[0]
     stem = mine.shape[0]
-    once = dict(pipeline_mode=pl.Buffered(1))
     return pl.pallas_call(
         stem_kernel,
         out_shape=jax.ShapeDtypeStruct((pack, 2 * HD), jnp.bfloat16),
@@ -407,8 +408,8 @@
             grid=(pack // BQ,),
             in_specs=[
                 pl.BlockSpec((BQ, 2 * HD), lambda i, *_: (i, 0)),
-                pl.BlockSpec((stem, HD), lambda i, *_: (0, 0), **once),
-                pl.BlockSpec((stem, HD), lambda i, *_: (0, 0), **once),
+                pl.BlockSpec(memory_space=pltpu.VMEM),
+                pl.BlockSpec(memory_space=pltpu.VMEM),
                 pl.BlockSpec((1, HD + 16, 2 * BQ), lambda i, *_: (i, 0, 0)),
             ],
             out_specs=pl.BlockSpec((BQ, 2 * HD), lambda i, *_: (i, 0)),
@@ -420,41 +421,39 @@
                 pltpu.VMEM((HD + 8, 2 * BQ), jnp.float32),
             ],
         ),
-        compiler_params=pltpu.CompilerParams(vmem_limit_bytes=ROOM),
+        compiler_params=pltpu.CompilerParams(vmem_limit_bytes=48 * 1024 * 1024),
         cost_estimate=pl.CostEstimate(
             flops=8 * pack * stem * HD, bytes_accessed=8 << 20, transcendentals=2 * pack * stem
         ),
         name="stem_part",
-    )(core, arrived, mine, other, before)
+    )(core, arrived, inside(mine), inside(other), before)
 
 
 def gather_kernel(core, mine_ref, other_ref, o_ref):
+    step = pl.program_id(0)
+    heads = KVH // 2
     first = core[0] == 0
-    for e in range(mine_ref.shape[1]):
-        mine = mine_ref[0, e]
-        other = other_ref[e]
+    for e in range(heads):
+        own, got = mine_ref[core[0], step * heads + e], other_ref[step * heads + e]
         at = 4 * HD * e
-        o_ref[:, at : at + 2 * HD] = jnp.where(first, mine, other)
-        o_ref[:, at + 2 * HD : at + 4 * HD] = jnp.where(first, other, mine)
+        o_ref[:, at : at + 2 * HD] = jnp.where(first, own, got)
+        o_ref[:, at + 2 * HD : at + 4 * HD] = jnp.where(first, got, own)
 
 
 def gather(core, mine, other):
     tok = mine.shape[2]
-    heads = KVH // 2
+    whole = pl.BlockSpec(memory_space=pltpu.VMEM)
     return pl.pallas_call(
         gather_kernel,
         out_shape=jax.ShapeDtypeStruct((tok, H * HD), jnp.bfloat16),
         grid_spec=pltpu.PrefetchScalarGridSpec(
             num_scalar_prefetch=1,
             grid=(2,),
-            in_specs=[
-                pl.BlockSpec((1, heads, tok, 2 * HD), lambda i, core: (core[0], i, 0, 0)),
-                pl.BlockSpec((heads, tok, 2 * HD), lambda i, core: (i, 0, 0)),
-            ],
+            in_specs=[whole, whole],
             out_specs=pl.BlockSpec((tok, H * HD // 2), lambda i, core: (0, i)),
         ),
         name="gather",
-    )(core, mine, other)
+    )(core, inside(mine), inside(other))
 
 
 def shards(queries, keys, values, stem_kv, seg_ids, seg_parent, stem_owner):

time: 121 us -> 118 us (0.975)
  local copies, waits for them, and re-layouts: 5.84 us -> 3.76 us
  Pallas kernels: 42.6 us -> 41.1 us
    unnamed x26 -> x18, local copies, waits for them, and re-layouts: 2.8 us -> 0.03 us
    pallas_call x1, Pallas kernels: 20.2 us -> 18.8 us  [stem_part(): pl.pallas_call(stem_kernel, out_shape=jax.ShapeDtypeStruct((pack, 2 * HD)...]
    pallas_call x1, Pallas kernels: 2.42 us -> 3.67 us  [turn(): pl.pallas_call(turn_kernel, out_shape=jax.ShapeDtypeStruct((2, KVH, tok,...]
    all_to_all x1, waiting for transfers between devices: 5.65 us -> 6.86 us  [shards(): lax.all_to_all(sent.reshape(16, tok, 3 * HD), SEQ, split_axis=0, concat_a...]
  transfers between devices with their start and end apart: 13 -> 13, of which waited for: 7 -> 7; matrix products, arithmetic and copies ran while one was open for 6% -> 7% of each run, Pallas kernels for 17% -> 18%
where the time goes in v13:
time: 118 us
  Pallas kernels  41.1 us (35%)
  waiting for transfers between devices  23.3 us (20%)
  starting transfers between devices  22.1 us (19%)
  blocking collectives  20.6 us (17%)
  local copies, waits for them, and re-layouts  3.76 us (3%)
  other arithmetic  3.58 us (3%)
  matrix products  2.98 us (3%)
    all_to_all x1, blocking collectives, shards(): lax.all_to_all(mixed.reshape(16, tok, 2 * HD), SEQ, split_axis=0, concat_...  20.6 us
    pallas_call x1, Pallas kernels, stem_part(): pl.pallas_call(stem_kernel, out_shape=jax.ShapeDtypeStruct((pack, 2 * HD)...  18.8 us
    pallas_call x1, Pallas kernels, pack_part(): pl.pallas_call(pack_kernel, out_shape=jax.ShapeDtypeStruct((pack // BQ, H...  12.1 us
    ppermute x1, waiting for transfers between devices, shards(): two = lax.ppermute(wanted, ('x', 'core'), joint(1, 0))  10.7 us
    all_to_all x1, starting transfers between devices, shards(): lax.all_to_all(sent.reshape(16, tok, 3 * HD), SEQ, split_axis=0, concat_a...  7.9 us
    all_to_all x1, waiting for transfers between devices, shards(): lax.all_to_all(sent.reshape(16, tok, 3 * HD), SEQ, split_axis=0, concat_a...  6.86 us
    pallas_call x2, Pallas kernels, moved(): pl.pallas_call(kernel, out_shape=jax.ShapeDtypeStruct(shape, jnp.bfloat16...  5.58 us
    pallas_call x1, Pallas kernels, turn(): pl.pallas_call(turn_kernel, out_shape=jax.ShapeDtypeStruct((2, KVH, tok,...  3.67 us
  transfers between devices with their start and end apart: 13, of which 7 were waited for; matrix products, arithmetic and copies ran while one was open for 7% of the time, Pallas kernels for 18%

profile of v13, /device:TPU:1, one launch (start us, length us, event | category | flops | bytes accessed | tf_op | source)
XLA Modules:
  0.0 117.7 jit_solution(724958844358086081)
XLA Ops:
  0.0 2.2 %dynamic-slice_bitcast_fusion.1 = (bf16[256,1024]{1,0:T(8,128)(2,1)}, bf16[256,1024]{1,0:T(8,128)(2,1)S(1)}) fusion(bf16[1,2,256,1024]{3,2,1,0:T(8,128)(2,1)} %param.11, s32[]{:T(128)S(6)} %select_n.53, s32[]{:T(128)S(6)} %select_n.52), kind=kLoop, calls=%fused_computation.27 | loop fusion | bytes 2097160 | tf_op jit(solution)/shard_map/jit(dynamic_index_in_dim)/squeeze | solution.py:475
  2.2 2.6 %collective-permute-start.6 = (bf16[256,1024]{1,0:T(8,128)(2,1)}, bf16[256,1024]{1,0:T(8,128)(2,1)S(1)}, u32[]{:S(2)}, u32[]{:S(2)}) collective-permute-start(bf16[256,1024]{1,0:T(8,128)(2,1)} %get-tuple-element.27), channel_id=1, source_target_pairs={{16,32},{48,0},{80,96},{112,64},{0,112},{96,16},{32,80},{64,48},{1... | collective-permute-start | bytes 1572872 | tf_op jit(solution)/shard_map/ppermute | solution.py:477
  4.8 1.1 collective-permute-start.7
  6.0 0.5 collective-permute-start
  6.8 0.7 collective-permute-done.3
  9.2 0.4 collective-permute-done.1.k_mate
  9.6 0.9 collective-permute-start.5
  10.5 0.5 fusion.23
  11.2 3.7 %turn.1 = bf16[2,8,128,384]{3,2,1,0:T(8,128)(2,1)} custom-call(s32[2]{0:T(128)S(1)} %pad_add_fusion.2.spot, bf16[128,4096]{1,0:T(8,128)(2,1)S(1)} %bitcast.41, bf16[128,1024]{1,0:T(8,128)(2,1)S(1)} %bitcast.46, bf16[128,1024]{1,0:T(8,128)(2,1)S(1)} %bitcast.48, bf16[128,4096]{1,0:T(8,128)(2,1)} %collective-permute-done.q_mate, ...), custom_call_target="tpu_custom_call" | custom-call | tf_op jit(solution)/shard_map/turn/pallas_call | solution.py:120
  14.8 7.9 %all-to-all-start = ((bf16[16,128,384]{2,1,0:T(8,128)(2,1)}), bf16[16,128,384]{2,1,0:T(8,128)(2,1)S(1)}, u32[]{:S(2)}, u32[]{:S(2)}) async-start(bf16[16,128,384]{2,1,0:T(8,128)(2,1)} %bitcast.7), calls=%async_computation | async-start | bytes 3145728 | tf_op jit(solution)/shard_map/all_to_all | solution.py:493
  22.8 2.6 %relay_kernel.1 = bf16[2,256,1024]{2,1,0:T(8,128)(2,1)} custom-call(s32[2]{0:T(128)S(1)} %pad_add_fusion.2.spot, s32[8]{0:T(128)S(1)} %copy-done.5, bf16[256,1024]{1,0:T(8,128)(2,1)S(1)} %get-tuple-element.28.own, bf16[256,1024]{1,0:T(8,128)(2,1)} %collective-permute-done.5.same, bf16[256,1024]{1,0:T(8,128)(2,1)S(1)} %collective-permute-done.7.flip, ...), custom_call_target="tpu_custom_call" | custom-call | tf_op jit(solution)/shard_map/relay_kernel/pallas_call | solution.py:190
  25.4 0.4 collective-permute-start.8
  25.8 0.6 broadcast.78
  26.4 0.7 fusion.42
  27.5 1.5 %convolution_convert_fusion.qb_ref = bf16[2048,128]{1,0:T(8,128)(2,1)} fusion(s32[2048]{0:T(1024)S(1)} %bitcast.49, f32[16,16]{0,1:T(8,128)S(1)} %fusion.33), kind=kOutput, calls=%fused_computation | convolution fusion | flops 403177472 | bytes 533504 | tf_op jit(solution)/shard_map/dot_general | solution.py:509
  29.0 10.7 %collective-permute-done.8.two = bf16[2,256,1024]{2,1,0:T(8,128)(2,1)} collective-permute-done((bf16[2,256,1024]{2,1,0:T(8,128)(2,1)}, bf16[2,256,1024]{2,1,0:T(8,128)(2,1)}, u32[]{:S(2)}, u32[]{:S(2)}) %collective-permute-start.8) | collective-permute-done | bytes 1048608 | tf_op jit(solution)/shard_map/ppermute | solution.py:500
  39.7 3.0 %settle_kernel.1 = bf16[2,8,256,128]{3,2,1,0:T(8,128)(2,1)} custom-call(s32[2]{0:T(128)S(1)} %pad_add_fusion.2.spot, s32[8]{0:T(128)S(1)} %copy-done.5, bf16[256,1024]{1,0:T(8,128)(2,1)S(1)} %get-tuple-element.28.own, bf16[256,1024]{1,0:T(8,128)(2,1)} %collective-permute-done.5.same, bf16[256,1024]{1,0:T(8,128)(2,1)S(1)} %collective-permute-done.7.flip, ...), custom_call_target="tpu_custom_call" | custom-call | tf_op jit(solution)/shard_map/settle_kernel/pallas_call | solution.py:190
  42.8 6.9 %all-to-all-done = bf16[16,128,384]{2,1,0:T(8,128)(2,1)S(1)} async-done(((bf16[16,128,384]{2,1,0:T(8,128)(2,1)}), bf16[16,128,384]{2,1,0:T(8,128)(2,1)S(1)}, u32[]{:S(2)}, u32[]{:S(2)}) %all-to-all-start) | async-done | bytes 1572896 | tf_op jit(solution)/shard_map/all_to_all | solution.py:493
  49.6 3.7 %all-to-all-start.1 = ((bf16[16,256,128]{2,1,0:T(8,128)(2,1)}), bf16[16,256,128]{2,1,0:T(8,128)(2,1)S(1)}, u32[]{:S(2)}, u32[]{:S(2)}) async-start(bf16[16,256,128]{2,1,0:T(8,128)(2,1)} %bitcast.11), calls=%async_computation.1 | async-start | bytes 2097152 | tf_op jit(solution)/shard_map/all_to_all | solution.py:521
  53.3 0.8 slice.36
  54.1 0.7 collective-permute-start.4
  54.8 0.8 fusion.18.seen
  55.6 1.1 select_convert_fusion.kb_ref
  56.7 12.1 %pack_part.1.part_ref = f32[4,144,1024]{2,1,0:T(8,128)} custom-call(s32[1]{0:T(128)} %bitcast.core, s32[4,4]{1,0:T(4,128)} %fusion.18.seen, bf16[2048,384]{1,0:T(8,128)(2,1)} %bitcast.37, bf16[2048,384]{1,0:T(8,128)(2,1)} %bitcast.38, bf16[2048,128]{1,0:T(8,128)(2,1)} %collective-permute-done.4.other_ref, bf16[2048,128]{1,0:T(8,128)(2,1)} %convolution_convert_fusion.qb_ref, ...), custom_call_target="tpu_custom_call" | custom-call | flops 4294967296 | bytes 8388608 | tf_op jit(solution)/shard_map/pack_part/pallas_call | solution.py:310
  68.8 0.8 all-to-all-done.1
  69.6 2.1 %collective-permute-start.9 = (bf16[4096,128]{1,0:T(8,128)(2,1)S(1)}, bf16[4096,128]{1,0:T(8,128)(2,1)S(1)}, u32[]{:S(2)}, u32[]{:S(2)}) collective-permute-start(bf16[4096,128]{1,0:T(8,128)(2,1)S(1)} %bitcast.42), channel_id=1, source_target_pairs={{0,16},{16,0},{1,17},{17,1},{2,18},{18,2},{3,19},{19,3},{4,20},{20... | collective-permute-start | bytes 3145736 | tf_op jit(solution)/shard_map/ppermute | solution.py:525
  71.7 2.3 %collective-permute-done.9.other_ref = bf16[4096,128]{1,0:T(8,128)(2,1)S(1)} collective-permute-done((bf16[4096,128]{1,0:T(8,128)(2,1)S(1)}, bf16[4096,128]{1,0:T(8,128)(2,1)S(1)}, u32[]{:S(2)}, u32[]{:S(2)}) %collective-permute-start.9) | collective-permute-done | bytes 1048608 | tf_op jit(solution)/shard_map/ppermute | solution.py:525
  74.0 18.8 %stem_part.1 = bf16[2048,256]{1,0:T(8,128)(2,1)S(1)} custom-call(s32[1]{0:T(128)} %bitcast.core, bf16[2048,384]{1,0:T(8,128)(2,1)S(1)} %bitcast.39, bf16[4096,128]{1,0:T(8,128)(2,1)S(1)} %bitcast.43, bf16[4096,128]{1,0:T(8,128)(2,1)S(1)} %collective-permute-done.9.other_ref, f32[4,144,1024]{2,1,0:T(8,128)} %pack_part.1.part_ref), custom_call_target="tpu_custom_call" | custom-call | flops 8589934592 | bytes 8388608 | tf_op jit(solution)/shard_map/stem_part/pallas_call | solution.py:403
  92.8 20.6 %all_to_all.15 = bf16[16,128,256]{2,1,0:T(8,128)(2,1)S(1)} all-to-all(bf16[16,128,256]{2,1,0:T(8,128)(2,1)S(1)} %bitcast.44), channel_id=1, replica_groups=mesh['x'=4,'core'=2,'z'=4,'y'=4] {'z','y'}, dimensions={0} | all-to-all | bytes 2097152 | tf_op jit(solution)/shard_map/all_to_all | solution.py:528
  113.4 1.8 %collective-permute-start.10 = (bf16[8,128,256]{2,1,0:T(8,128)(2,1)S(1)}, bf16[8,128,256]{2,1,0:T(8,128)(2,1)S(1)}, u32[]{:S(2)}, u32[]{:S(2)}) collective-permute-start(bf16[8,128,256]{2,1,0:T(8,128)(2,1)S(1)} %dynamic-slice_bitcast_fusion), channel_id=1, source_target_pairs={{0,16},{16,0},{1,17},{17,1},{2,18},{18,2},{3,19},{19,3},{4,20},{20... | collective-permute-start | bytes 1572872 | tf_op jit(solution)/shard_map/ppermute | solution.py:532
  115.2 1.5 %collective-permute-done.10.other_ref = bf16[8,128,256]{2,1,0:T(8,128)(2,1)S(1)} collective-permute-done((bf16[8,128,256]{2,1,0:T(8,128)(2,1)S(1)}, bf16[8,128,256]{2,1,0:T(8,128)(2,1)S(1)}, u32[]{:S(2)}, u32[]{:S(2)}) %collective-permute-start.10) | collective-permute-done | bytes 524320 | tf_op jit(solution)/shard_map/ppermute | solution.py:532
  116.7 1.0 gather.1
  (56 shorter events, 2.6 us)
Async XLA Ops:
  0.0 10.5 %copy-start.7 = (f32[64]{0:T(128)S(1)}, f32[64]{0:T(128)}, u32[]{:S(2)}) copy-start(f32[64]{0:T(128)} %constant.81.clone) | copy-start | bytes 772
  0.0 5.9 %copy-start.6 = (s32[1,2048]{1,0:T(1,128)S(1)}, s32[1,2048]{1,0:T(1,128)}, u32[]{:S(2)}) copy-start(s32[1,2048]{1,0:T(1,128)} %param.12) | copy-start | bytes 24580
  0.0 5.9 %copy-start.8 = (s32[1,16]{1,0:T(1,128)S(1)}, s32[1,16]{1,0:T(1,128)}, u32[]{:S(2)}) copy-start(s32[1,16]{1,0:T(1,128)} %param.13) | copy-start | bytes 196
  0.0 6.0 %copy-start.2 = (bf16[1,128,4096]{2,1,0:T(8,128)(2,1)S(1)}, bf16[1,128,4096]{2,1,0:T(8,128)(2,1)}, u32[]{:S(2)}) copy-start(bf16[1,128,4096]{2,1,0:T(8,128)(2,1)} %param.8) | copy-start | bytes 3145732
  0.0 6.5 %copy-start.3 = (bf16[1,128,1024]{2,1,0:T(8,128)(2,1)S(1)}, bf16[1,128,1024]{2,1,0:T(8,128)(2,1)}, u32[]{:S(2)}) copy-start(bf16[1,128,1024]{2,1,0:T(8,128)(2,1)} %param.9) | copy-start | bytes 786436
  0.0 7.5 %copy-start.4 = (bf16[1,128,1024]{2,1,0:T(8,128)(2,1)S(1)}, bf16[1,128,1024]{2,1,0:T(8,128)(2,1)}, u32[]{:S(2)}) copy-start(bf16[1,128,1024]{2,1,0:T(8,128)(2,1)} %param.10) | copy-start | bytes 786436
  2.2 20.6 %collective-permute-start.6 = (bf16[256,1024]{1,0:T(8,128)(2,1)}, bf16[256,1024]{1,0:T(8,128)(2,1)S(1)}, u32[]{:S(2)}, u32[]{:S(2)}) collective-permute-start(bf16[256,1024]{1,0:T(8,128)(2,1)} %get-tuple-element.27), channel_id=1, source_target_pairs={{16,32},{48,0},{80,96},{112,64},{0,112},{96,16},{32,80},{64,48},{1... | collective-permute-start | bytes 1572872 | tf_op jit(solution)/shard_map/ppermute | solution.py:477
  4.8 18.0 %collective-permute-start.7 = (bf16[256,1024]{1,0:T(8,128)(2,1)}, bf16[256,1024]{1,0:T(8,128)(2,1)S(1)}, u32[]{:S(2)}, u32[]{:S(2)}) collective-permute-start(bf16[256,1024]{1,0:T(8,128)(2,1)} %get-tuple-element.27), channel_id=1, source_target_pairs={{0,16},{16,0},{1,17},{17,1},{2,18},{18,2},{3,19},{19,3},{4,20},{20... | collective-permute-start | bytes 1572872 | tf_op jit(solution)/shard_map/ppermute | solution.py:478
  5.9 1.6 %collective-permute-start.3 = (s32[2064]{0:T(1024)S(1)}, s32[2064]{0:T(1024)S(1)}, u32[]{:S(2)}, u32[]{:S(2)}) collective-permute-start(s32[2064]{0:T(1024)S(1)} %pad_add_fusion.1), channel_id=1, source_target_pairs={{0,16},{16,0},{1,17},{17,1},{2,18},{18,2},{3,19},{19,3},{4,20},{20... | collective-permute-start | bytes 24776 | tf_op jit(solution)/shard_map/ppermute | solution.py:470
  6.0 5.1 %collective-permute-start = (bf16[128,4096]{1,0:T(8,128)(2,1)S(1)}, bf16[128,4096]{1,0:T(8,128)(2,1)}, u32[]{:S(2)}, u32[]{:S(2)}) collective-permute-start(bf16[128,4096]{1,0:T(8,128)(2,1)S(1)} %bitcast.40), channel_id=1, source_target_pairs={{0,16},{16,0},{1,17},{17,1},{2,18},{18,2},{3,19},{19,3},{4,20},{20... | collective-permute-start | bytes 3145736 | tf_op jit(solution)/shard_map/ppermute | solution.py:471
  6.5 3.1 %collective-permute-start.1 = (bf16[128,1024]{1,0:T(8,128)(2,1)S(1)}, bf16[128,1024]{1,0:T(8,128)(2,1)S(1)}, u32[]{:S(2)}, u32[]{:S(2)}) collective-permute-start(bf16[128,1024]{1,0:T(8,128)(2,1)S(1)} %bitcast.45), channel_id=1, source_target_pairs={{0,16},{16,0},{1,17},{17,1},{2,18},{18,2},{3,19},{19,3},{4,20},{20... | collective-permute-start | bytes 786440 | tf_op jit(solution)/shard_map/ppermute | solution.py:471
  7.5 3.6 %collective-permute-start.2 = (bf16[128,1024]{1,0:T(8,128)(2,1)S(1)}, bf16[128,1024]{1,0:T(8,128)(2,1)}, u32[]{:S(2)}, u32[]{:S(2)}) collective-permute-start(bf16[128,1024]{1,0:T(8,128)(2,1)S(1)} %bitcast.47), channel_id=1, source_target_pairs={{0,16},{16,0},{1,17},{17,1},{2,18},{18,2},{3,19},{19,3},{4,20},{20... | collective-permute-start | bytes 786440 | tf_op jit(solution)/shard_map/ppermute | solution.py:471
  9.6 13.2 %collective-permute-start.5 = (bf16[256,1024]{1,0:T(8,128)(2,1)S(1)}, bf16[256,1024]{1,0:T(8,128)(2,1)}, u32[]{:S(2)}, u32[]{:S(2)}) collective-permute-start(bf16[256,1024]{1,0:T(8,128)(2,1)S(1)} %get-tuple-element.28.own), channel_id=1, source_target_pairs={{0,32},{32,0},{64,96},{96,64},{16,112},{112,16},{48,80},{80,48},{1... | collective-permute-start | bytes 1572872 | tf_op jit(solution)/shard_map/ppermute | solution.py:476
  14.8 8.0 %copy-start.5 = (s32[8]{0:T(128)S(1)}, s32[8]{0:T(128)}, u32[]{:S(2)}) copy-start(s32[8]{0:T(128)} %owner.3) | copy-start | bytes 100
  14.8 34.8 %all-to-all-start = ((bf16[16,128,384]{2,1,0:T(8,128)(2,1)}), bf16[16,128,384]{2,1,0:T(8,128)(2,1)S(1)}, u32[]{:S(2)}, u32[]{:S(2)}) async-start(bf16[16,128,384]{2,1,0:T(8,128)(2,1)} %bitcast.7), calls=%async_computation | async-start | bytes 3145728 | tf_op jit(solution)/shard_map/all_to_all | solution.py:493
  25.4 14.3 %collective-permute-start.8 = (bf16[2,256,1024]{2,1,0:T(8,128)(2,1)}, bf16[2,256,1024]{2,1,0:T(8,128)(2,1)}, u32[]{:S(2)}, u32[]{:S(2)}) collective-permute-start(bf16[2,256,1024]{2,1,0:T(8,128)(2,1)} %relay_kernel.1), channel_id=1, source_target_pairs={{0,96},{96,0},{32,64},{64,32},{16,48},{48,16},{80,112},{112,80},{1... | collective-permute-start | bytes 3145736 | tf_op jit(solution)/shard_map/ppermute | solution.py:500
  49.6 4.5 %copy-start = (bf16[16,128,384]{2,1,0:T(8,128)(2,1)}, bf16[16,128,384]{2,1,0:T(8,128)(2,1)S(1)}, u32[]{:S(2)}) copy-start(bf16[16,128,384]{2,1,0:T(8,128)(2,1)S(1)} %all-to-all-done) | copy-start | bytes 4718596
  49.6 19.9 %all-to-all-start.1 = ((bf16[16,256,128]{2,1,0:T(8,128)(2,1)}), bf16[16,256,128]{2,1,0:T(8,128)(2,1)S(1)}, u32[]{:S(2)}, u32[]{:S(2)}) async-start(bf16[16,256,128]{2,1,0:T(8,128)(2,1)} %bitcast.11), calls=%async_computation.1 | async-start | bytes 2097152 | tf_op jit(solution)/shard_map/all_to_all | solution.py:521
  54.1 2.6 %collective-permute-start.4 = (bf16[2048,128]{1,0:T(8,128)(2,1)}, bf16[2048,128]{1,0:T(8,128)(2,1)}, u32[]{:S(2)}, u32[]{:S(2)}) collective-permute-start(bf16[2048,128]{1,0:T(8,128)(2,1)} %slice.36), channel_id=1, source_target_pairs={{0,16},{16,0},{1,17},{17,1},{2,18},{18,2},{3,19},{19,3},{4,20},{20... | collective-permute-start | bytes 1572872 | tf_op jit(solution)/shard_map/ppermute | solution.py:502
  56.7 17.3 %copy-start.1 = (bf16[16,128,384]{2,1,0:T(8,128)(2,1)S(1)}, bf16[16,128,384]{2,1,0:T(8,128)(2,1)}, u32[]{:S(2)}) copy-start(bf16[16,128,384]{2,1,0:T(8,128)(2,1)} %copy-done) | copy-start | bytes 4718596
  69.6 4.4 %collective-permute-start.9 = (bf16[4096,128]{1,0:T(8,128)(2,1)S(1)}, bf16[4096,128]{1,0:T(8,128)(2,1)S(1)}, u32[]{:S(2)}, u32[]{:S(2)}) collective-permute-start(bf16[4096,128]{1,0:T(8,128)(2,1)S(1)} %bitcast.42), channel_id=1, source_target_pairs={{0,16},{16,0},{1,17},{17,1},{2,18},{18,2},{3,19},{19,3},{4,20},{20... | collective-permute-start | bytes 3145736 | tf_op jit(solution)/shard_map/ppermute | solution.py:525
  113.4 3.3 %collective-permute-start.10 = (bf16[8,128,256]{2,1,0:T(8,128)(2,1)S(1)}, bf16[8,128,256]{2,1,0:T(8,128)(2,1)S(1)}, u32[]{:S(2)}, u32[]{:S(2)}) collective-permute-start(bf16[8,128,256]{2,1,0:T(8,128)(2,1)S(1)} %dynamic-slice_bitcast_fusion), channel_id=1, source_target_pairs={{0,16},{16,0},{1,17},{17,1},{2,18},{18,2},{3,19},{19,3},{4,20},{20... | collective-permute-start | bytes 1572872 | tf_op jit(solution)/shard_map/ppermute | solution.py:532

commit v14 on v13

--- a/solution.py
+++ b/solution.py
@@ -115,7 +115,10 @@
 
 def turn(here, own, mate, cosine, sine):
     tok = own[0].shape[0]
-    whole = [pl.BlockSpec(memory_space=pltpu.VMEM)] * 6
+    whole = [
+        pl.BlockSpec(part.shape, lambda i, here: (0, 0), pipeline_mode=pl.Buffered(1))
+        for part in own + mate
+    ]
     table = pl.BlockSpec(cosine.shape, lambda i, here: (0, 0, 0), pipeline_mode=pl.Buffered(1))
     return pl.pallas_call(
         turn_kernel,
@@ -128,7 +131,7 @@
         ),
         compiler_params=pltpu.CompilerParams(vmem_limit_bytes=32 * 1024 * 1024),
         name="turn",
-    )(here, *[inside(part) for part in own + mate], cosine, sine)
+    )(here, *own, *mate, cosine, sine)
 
 
 def held_at(x, core, group):

time: 118 us -> 118 us (level)
  no operation moved by 1% of the time
where the time goes in v14:
time: 118 us
  Pallas kernels  41.1 us (35%)
  waiting for transfers between devices  23.3 us (20%)
  starting transfers between devices  22.1 us (19%)
  blocking collectives  20.6 us (17%)
  local copies, waits for them, and re-layouts  3.76 us (3%)
  other arithmetic  3.58 us (3%)
  matrix products  2.98 us (3%)
    all_to_all x1, blocking collectives, shards(): lax.all_to_all(mixed.reshape(16, tok, 2 * HD), SEQ, split_axis=0, concat_...  20.6 us
    pallas_call x1, Pallas kernels, stem_part(): pl.pallas_call(stem_kernel, out_shape=jax.ShapeDtypeStruct((pack, 2 * HD)...  18.8 us
    pallas_call x1, Pallas kernels, pack_part(): pl.pallas_call(pack_kernel, out_shape=jax.ShapeDtypeStruct((pack // BQ, H...  12.1 us
    ppermute x1, waiting for transfers between devices, shards(): two = lax.ppermute(wanted, ('x', 'core'), joint(1, 0))  10.7 us
    all_to_all x1, starting transfers between devices, shards(): lax.all_to_all(sent.reshape(16, tok, 3 * HD), SEQ, split_axis=0, concat_a...  7.9 us
    all_to_all x1, waiting for transfers between devices, shards(): lax.all_to_all(sent.reshape(16, tok, 3 * HD), SEQ, split_axis=0, concat_a...  6.86 us
    pallas_call x2, Pallas kernels, moved(): pl.pallas_call(kernel, out_shape=jax.ShapeDtypeStruct(shape, jnp.bfloat16...  5.58 us
    pallas_call x1, Pallas kernels, turn(): pl.pallas_call(turn_kernel, out_shape=jax.ShapeDtypeStruct((2, KVH, tok,...  3.67 us
  transfers between devices with their start and end apart: 13, of which 7 were waited for; matrix products, arithmetic and copies ran while one was open for 7% of the time, Pallas kernels for 18%

profile of v14, /device:TPU:1, one launch (start us, length us, event | category | flops | bytes accessed | tf_op | source)
XLA Modules:
  0.0 117.7 jit_solution(724958844358086081)
XLA Ops:
  0.0 2.2 %dynamic-slice_bitcast_fusion.1 = (bf16[256,1024]{1,0:T(8,128)(2,1)}, bf16[256,1024]{1,0:T(8,128)(2,1)S(1)}) fusion(bf16[1,2,256,1024]{3,2,1,0:T(8,128)(2,1)} %param.11, s32[]{:T(128)S(6)} %select_n.53, s32[]{:T(128)S(6)} %select_n.52), kind=kLoop, calls=%fused_computation.27 | loop fusion | bytes 2097160 | tf_op jit(solution)/shard_map/jit(dynamic_index_in_dim)/squeeze | solution.py:478
  2.2 2.6 %collective-permute-start.6 = (bf16[256,1024]{1,0:T(8,128)(2,1)}, bf16[256,1024]{1,0:T(8,128)(2,1)S(1)}, u32[]{:S(2)}, u32[]{:S(2)}) collective-permute-start(bf16[256,1024]{1,0:T(8,128)(2,1)} %get-tuple-element.27), channel_id=1, source_target_pairs={{16,32},{48,0},{80,96},{112,64},{0,112},{96,16},{32,80},{64,48},{1... | collective-permute-start | bytes 1572872 | tf_op jit(solution)/shard_map/ppermute | solution.py:480
  4.8 1.1 collective-permute-start.7
  6.0 0.5 collective-permute-start
  6.8 0.7 collective-permute-done.3
  9.2 0.4 collective-permute-done.1.k_mate
  9.6 0.9 collective-permute-start.5
  10.5 0.5 fusion.23
  11.2 3.7 %turn.1 = bf16[2,8,128,384]{3,2,1,0:T(8,128)(2,1)} custom-call(s32[2]{0:T(128)S(1)} %pad_add_fusion.2.spot, bf16[128,4096]{1,0:T(8,128)(2,1)S(1)} %bitcast.41, bf16[128,1024]{1,0:T(8,128)(2,1)S(1)} %bitcast.46, bf16[128,1024]{1,0:T(8,128)(2,1)S(1)} %bitcast.48, bf16[128,4096]{1,0:T(8,128)(2,1)} %collective-permute-done.q_mate, ...), custom_call_target="tpu_custom_call" | custom-call | tf_op jit(solution)/shard_map/turn/pallas_call | solution.py:123
  14.8 7.9 %all-to-all-start = ((bf16[16,128,384]{2,1,0:T(8,128)(2,1)}), bf16[16,128,384]{2,1,0:T(8,128)(2,1)S(1)}, u32[]{:S(2)}, u32[]{:S(2)}) async-start(bf16[16,128,384]{2,1,0:T(8,128)(2,1)} %bitcast.7), calls=%async_computation | async-start | bytes 3145728 | tf_op jit(solution)/shard_map/all_to_all | solution.py:496
  22.8 2.6 %relay_kernel.1 = bf16[2,256,1024]{2,1,0:T(8,128)(2,1)} custom-call(s32[2]{0:T(128)S(1)} %pad_add_fusion.2.spot, s32[8]{0:T(128)S(1)} %copy-done.5, bf16[256,1024]{1,0:T(8,128)(2,1)S(1)} %get-tuple-element.28.own, bf16[256,1024]{1,0:T(8,128)(2,1)} %collective-permute-done.5.same, bf16[256,1024]{1,0:T(8,128)(2,1)S(1)} %collective-permute-done.7.flip, ...), custom_call_target="tpu_custom_call" | custom-call | tf_op jit(solution)/shard_map/relay_kernel/pallas_call | solution.py:193
  25.4 0.4 collective-permute-start.8
  25.8 0.6 broadcast.78
  26.4 0.7 fusion.42
  27.5 1.5 %convolution_convert_fusion.qb_ref = bf16[2048,128]{1,0:T(8,128)(2,1)} fusion(s32[2048]{0:T(1024)S(1)} %bitcast.49, f32[16,16]{0,1:T(8,128)S(1)} %fusion.33), kind=kOutput, calls=%fused_computation | convolution fusion | flops 403177472 | bytes 533504 | tf_op jit(solution)/shard_map/dot_general | solution.py:512
  29.0 10.7 %collective-permute-done.8.two = bf16[2,256,1024]{2,1,0:T(8,128)(2,1)} collective-permute-done((bf16[2,256,1024]{2,1,0:T(8,128)(2,1)}, bf16[2,256,1024]{2,1,0:T(8,128)(2,1)}, u32[]{:S(2)}, u32[]{:S(2)}) %collective-permute-start.8) | collective-permute-done | bytes 1048608 | tf_op jit(solution)/shard_map/ppermute | solution.py:503
  39.7 3.0 %settle_kernel.1 = bf16[2,8,256,128]{3,2,1,0:T(8,128)(2,1)} custom-call(s32[2]{0:T(128)S(1)} %pad_add_fusion.2.spot, s32[8]{0:T(128)S(1)} %copy-done.5, bf16[256,1024]{1,0:T(8,128)(2,1)S(1)} %get-tuple-element.28.own, bf16[256,1024]{1,0:T(8,128)(2,1)} %collective-permute-done.5.same, bf16[256,1024]{1,0:T(8,128)(2,1)S(1)} %collective-permute-done.7.flip, ...), custom_call_target="tpu_custom_call" | custom-call | tf_op jit(solution)/shard_map/settle_kernel/pallas_call | solution.py:193
  42.8 6.9 %all-to-all-done = bf16[16,128,384]{2,1,0:T(8,128)(2,1)S(1)} async-done(((bf16[16,128,384]{2,1,0:T(8,128)(2,1)}), bf16[16,128,384]{2,1,0:T(8,128)(2,1)S(1)}, u32[]{:S(2)}, u32[]{:S(2)}) %all-to-all-start) | async-done | bytes 1572896 | tf_op jit(solution)/shard_map/all_to_all | solution.py:496
  49.6 3.7 %all-to-all-start.1 = ((bf16[16,256,128]{2,1,0:T(8,128)(2,1)}), bf16[16,256,128]{2,1,0:T(8,128)(2,1)S(1)}, u32[]{:S(2)}, u32[]{:S(2)}) async-start(bf16[16,256,128]{2,1,0:T(8,128)(2,1)} %bitcast.11), calls=%async_computation.1 | async-start | bytes 2097152 | tf_op jit(solution)/shard_map/all_to_all | solution.py:524
  53.3 0.8 slice.36
  54.1 0.7 collective-permute-start.4
  54.8 0.8 fusion.18.seen
  55.6 1.1 select_convert_fusion.kb_ref
  56.7 12.1 %pack_part.1.part_ref = f32[4,144,1024]{2,1,0:T(8,128)} custom-call(s32[1]{0:T(128)} %bitcast.core, s32[4,4]{1,0:T(4,128)} %fusion.18.seen, bf16[2048,384]{1,0:T(8,128)(2,1)} %bitcast.37, bf16[2048,384]{1,0:T(8,128)(2,1)} %bitcast.38, bf16[2048,128]{1,0:T(8,128)(2,1)} %collective-permute-done.4.other_ref, bf16[2048,128]{1,0:T(8,128)(2,1)} %convolution_convert_fusion.qb_ref, ...), custom_call_target="tpu_custom_call" | custom-call | flops 4294967296 | bytes 8388608 | tf_op jit(solution)/shard_map/pack_part/pallas_call | solution.py:313
  68.8 0.8 all-to-all-done.1
  69.6 2.1 %collective-permute-start.9 = (bf16[4096,128]{1,0:T(8,128)(2,1)S(1)}, bf16[4096,128]{1,0:T(8,128)(2,1)S(1)}, u32[]{:S(2)}, u32[]{:S(2)}) collective-permute-start(bf16[4096,128]{1,0:T(8,128)(2,1)S(1)} %bitcast.42), channel_id=1, source_target_pairs={{0,16},{16,0},{1,17},{17,1},{2,18},{18,2},{3,19},{19,3},{4,20},{20... | collective-permute-start | bytes 3145736 | tf_op jit(solution)/shard_map/ppermute | solution.py:528
  71.7 2.3 %collective-permute-done.9.other_ref = bf16[4096,128]{1,0:T(8,128)(2,1)S(1)} collective-permute-done((bf16[4096,128]{1,0:T(8,128)(2,1)S(1)}, bf16[4096,128]{1,0:T(8,128)(2,1)S(1)}, u32[]{:S(2)}, u32[]{:S(2)}) %collective-permute-start.9) | collective-permute-done | bytes 1048608 | tf_op jit(solution)/shard_map/ppermute | solution.py:528
  74.0 18.8 %stem_part.1 = bf16[2048,256]{1,0:T(8,128)(2,1)S(1)} custom-call(s32[1]{0:T(128)} %bitcast.core, bf16[2048,384]{1,0:T(8,128)(2,1)S(1)} %bitcast.39, bf16[4096,128]{1,0:T(8,128)(2,1)S(1)} %bitcast.43, bf16[4096,128]{1,0:T(8,128)(2,1)S(1)} %collective-permute-done.9.other_ref, f32[4,144,1024]{2,1,0:T(8,128)} %pack_part.1.part_ref), custom_call_target="tpu_custom_call" | custom-call | flops 8589934592 | bytes 8388608 | tf_op jit(solution)/shard_map/stem_part/pallas_call | solution.py:406
  92.8 20.6 %all_to_all.15 = bf16[16,128,256]{2,1,0:T(8,128)(2,1)S(1)} all-to-all(bf16[16,128,256]{2,1,0:T(8,128)(2,1)S(1)} %bitcast.44), channel_id=1, replica_groups=mesh['x'=4,'core'=2,'z'=4,'y'=4] {'z','y'}, dimensions={0} | all-to-all | bytes 2097152 | tf_op jit(solution)/shard_map/all_to_all | solution.py:531
  113.4 1.8 %collective-permute-start.10 = (bf16[8,128,256]{2,1,0:T(8,128)(2,1)S(1)}, bf16[8,128,256]{2,1,0:T(8,128)(2,1)S(1)}, u32[]{:S(2)}, u32[]{:S(2)}) collective-permute-start(bf16[8,128,256]{2,1,0:T(8,128)(2,1)S(1)} %dynamic-slice_bitcast_fusion), channel_id=1, source_target_pairs={{0,16},{16,0},{1,17},{17,1},{2,18},{18,2},{3,19},{19,3},{4,20},{20... | collective-permute-start | bytes 1572872 | tf_op jit(solution)/shard_map/ppermute | solution.py:535
  115.2 1.5 %collective-permute-done.10.other_ref = bf16[8,128,256]{2,1,0:T(8,128)(2,1)S(1)} collective-permute-done((bf16[8,128,256]{2,1,0:T(8,128)(2,1)S(1)}, bf16[8,128,256]{2,1,0:T(8,128)(2,1)S(1)}, u32[]{:S(2)}, u32[]{:S(2)}) %collective-permute-start.10) | collective-permute-done | bytes 524320 | tf_op jit(solution)/shard_map/ppermute | solution.py:535
  116.7 1.0 gather.1
  (56 shorter events, 2.6 us)
Async XLA Ops:
  0.0 10.5 %copy-start.7 = (f32[64]{0:T(128)S(1)}, f32[64]{0:T(128)}, u32[]{:S(2)}) copy-start(f32[64]{0:T(128)} %constant.81.clone) | copy-start | bytes 772
  0.0 5.9 %copy-start.6 = (s32[1,2048]{1,0:T(1,128)S(1)}, s32[1,2048]{1,0:T(1,128)}, u32[]{:S(2)}) copy-start(s32[1,2048]{1,0:T(1,128)} %param.12) | copy-start | bytes 24580
  0.0 5.9 %copy-start.8 = (s32[1,16]{1,0:T(1,128)S(1)}, s32[1,16]{1,0:T(1,128)}, u32[]{:S(2)}) copy-start(s32[1,16]{1,0:T(1,128)} %param.13) | copy-start | bytes 196
  0.0 6.0 %copy-start.2 = (bf16[1,128,4096]{2,1,0:T(8,128)(2,1)S(1)}, bf16[1,128,4096]{2,1,0:T(8,128)(2,1)}, u32[]{:S(2)}) copy-start(bf16[1,128,4096]{2,1,0:T(8,128)(2,1)} %param.8) | copy-start | bytes 3145732
  0.0 6.5 %copy-start.3 = (bf16[1,128,1024]{2,1,0:T(8,128)(2,1)S(1)}, bf16[1,128,1024]{2,1,0:T(8,128)(2,1)}, u32[]{:S(2)}) copy-start(bf16[1,128,1024]{2,1,0:T(8,128)(2,1)} %param.9) | copy-start | bytes 786436
  0.0 7.5 %copy-start.4 = (bf16[1,128,1024]{2,1,0:T(8,128)(2,1)S(1)}, bf16[1,128,1024]{2,1,0:T(8,128)(2,1)}, u32[]{:S(2)}) copy-start(bf16[1,128,1024]{2,1,0:T(8,128)(2,1)} %param.10) | copy-start | bytes 786436
  2.2 20.6 %collective-permute-start.6 = (bf16[256,1024]{1,0:T(8,128)(2,1)}, bf16[256,1024]{1,0:T(8,128)(2,1)S(1)}, u32[]{:S(2)}, u32[]{:S(2)}) collective-permute-start(bf16[256,1024]{1,0:T(8,128)(2,1)} %get-tuple-element.27), channel_id=1, source_target_pairs={{16,32},{48,0},{80,96},{112,64},{0,112},{96,16},{32,80},{64,48},{1... | collective-permute-start | bytes 1572872 | tf_op jit(solution)/shard_map/ppermute | solution.py:480
  4.8 18.0 %collective-permute-start.7 = (bf16[256,1024]{1,0:T(8,128)(2,1)}, bf16[256,1024]{1,0:T(8,128)(2,1)S(1)}, u32[]{:S(2)}, u32[]{:S(2)}) collective-permute-start(bf16[256,1024]{1,0:T(8,128)(2,1)} %get-tuple-element.27), channel_id=1, source_target_pairs={{0,16},{16,0},{1,17},{17,1},{2,18},{18,2},{3,19},{19,3},{4,20},{20... | collective-permute-start | bytes 1572872 | tf_op jit(solution)/shard_map/ppermute | solution.py:481
  5.9 1.6 %collective-permute-start.3 = (s32[2064]{0:T(1024)S(1)}, s32[2064]{0:T(1024)S(1)}, u32[]{:S(2)}, u32[]{:S(2)}) collective-permute-start(s32[2064]{0:T(1024)S(1)} %pad_add_fusion.1), channel_id=1, source_target_pairs={{0,16},{16,0},{1,17},{17,1},{2,18},{18,2},{3,19},{19,3},{4,20},{20... | collective-permute-start | bytes 24776 | tf_op jit(solution)/shard_map/ppermute | solution.py:473
  6.0 5.1 %collective-permute-start = (bf16[128,4096]{1,0:T(8,128)(2,1)S(1)}, bf16[128,4096]{1,0:T(8,128)(2,1)}, u32[]{:S(2)}, u32[]{:S(2)}) collective-permute-start(bf16[128,4096]{1,0:T(8,128)(2,1)S(1)} %bitcast.40), channel_id=1, source_target_pairs={{0,16},{16,0},{1,17},{17,1},{2,18},{18,2},{3,19},{19,3},{4,20},{20... | collective-permute-start | bytes 3145736 | tf_op jit(solution)/shard_map/ppermute | solution.py:474
  6.5 3.1 %collective-permute-start.1 = (bf16[128,1024]{1,0:T(8,128)(2,1)S(1)}, bf16[128,1024]{1,0:T(8,128)(2,1)S(1)}, u32[]{:S(2)}, u32[]{:S(2)}) collective-permute-start(bf16[128,1024]{1,0:T(8,128)(2,1)S(1)} %bitcast.45), channel_id=1, source_target_pairs={{0,16},{16,0},{1,17},{17,1},{2,18},{18,2},{3,19},{19,3},{4,20},{20... | collective-permute-start | bytes 786440 | tf_op jit(solution)/shard_map/ppermute | solution.py:474
  7.5 3.6 %collective-permute-start.2 = (bf16[128,1024]{1,0:T(8,128)(2,1)S(1)}, bf16[128,1024]{1,0:T(8,128)(2,1)}, u32[]{:S(2)}, u32[]{:S(2)}) collective-permute-start(bf16[128,1024]{1,0:T(8,128)(2,1)S(1)} %bitcast.47), channel_id=1, source_target_pairs={{0,16},{16,0},{1,17},{17,1},{2,18},{18,2},{3,19},{19,3},{4,20},{20... | collective-permute-start | bytes 786440 | tf_op jit(solution)/shard_map/ppermute | solution.py:474
  9.6 13.2 %collective-permute-start.5 = (bf16[256,1024]{1,0:T(8,128)(2,1)S(1)}, bf16[256,1024]{1,0:T(8,128)(2,1)}, u32[]{:S(2)}, u32[]{:S(2)}) collective-permute-start(bf16[256,1024]{1,0:T(8,128)(2,1)S(1)} %get-tuple-element.28.own), channel_id=1, source_target_pairs={{0,32},{32,0},{64,96},{96,64},{16,112},{112,16},{48,80},{80,48},{1... | collective-permute-start | bytes 1572872 | tf_op jit(solution)/shard_map/ppermute | solution.py:479
  14.8 8.0 %copy-start.5 = (s32[8]{0:T(128)S(1)}, s32[8]{0:T(128)}, u32[]{:S(2)}) copy-start(s32[8]{0:T(128)} %owner.3) | copy-start | bytes 100
  14.8 34.8 %all-to-all-start = ((bf16[16,128,384]{2,1,0:T(8,128)(2,1)}), bf16[16,128,384]{2,1,0:T(8,128)(2,1)S(1)}, u32[]{:S(2)}, u32[]{:S(2)}) async-start(bf16[16,128,384]{2,1,0:T(8,128)(2,1)} %bitcast.7), calls=%async_computation | async-start | bytes 3145728 | tf_op jit(solution)/shard_map/all_to_all | solution.py:496
  25.4 14.3 %collective-permute-start.8 = (bf16[2,256,1024]{2,1,0:T(8,128)(2,1)}, bf16[2,256,1024]{2,1,0:T(8,128)(2,1)}, u32[]{:S(2)}, u32[]{:S(2)}) collective-permute-start(bf16[2,256,1024]{2,1,0:T(8,128)(2,1)} %relay_kernel.1), channel_id=1, source_target_pairs={{0,96},{96,0},{32,64},{64,32},{16,48},{48,16},{80,112},{112,80},{1... | collective-permute-start | bytes 3145736 | tf_op jit(solution)/shard_map/ppermute | solution.py:503
  49.6 4.5 %copy-start = (bf16[16,128,384]{2,1,0:T(8,128)(2,1)}, bf16[16,128,384]{2,1,0:T(8,128)(2,1)S(1)}, u32[]{:S(2)}) copy-start(bf16[16,128,384]{2,1,0:T(8,128)(2,1)S(1)} %all-to-all-done) | copy-start | bytes 4718596
  49.6 19.9 %all-to-all-start.1 = ((bf16[16,256,128]{2,1,0:T(8,128)(2,1)}), bf16[16,256,128]{2,1,0:T(8,128)(2,1)S(1)}, u32[]{:S(2)}, u32[]{:S(2)}) async-start(bf16[16,256,128]{2,1,0:T(8,128)(2,1)} %bitcast.11), calls=%async_computation.1 | async-start | bytes 2097152 | tf_op jit(solution)/shard_map/all_to_all | solution.py:524
  54.1 2.6 %collective-permute-start.4 = (bf16[2048,128]{1,0:T(8,128)(2,1)}, bf16[2048,128]{1,0:T(8,128)(2,1)}, u32[]{:S(2)}, u32[]{:S(2)}) collective-permute-start(bf16[2048,128]{1,0:T(8,128)(2,1)} %slice.36), channel_id=1, source_target_pairs={{0,16},{16,0},{1,17},{17,1},{2,18},{18,2},{3,19},{19,3},{4,20},{20... | collective-permute-start | bytes 1572872 | tf_op jit(solution)/shard_map/ppermute | solution.py:505
  56.7 17.3 %copy-start.1 = (bf16[16,128,384]{2,1,0:T(8,128)(2,1)S(1)}, bf16[16,128,384]{2,1,0:T(8,128)(2,1)}, u32[]{:S(2)}) copy-start(bf16[16,128,384]{2,1,0:T(8,128)(2,1)} %copy-done) | copy-start | bytes 4718596
  69.6 4.4 %collective-permute-start.9 = (bf16[4096,128]{1,0:T(8,128)(2,1)S(1)}, bf16[4096,128]{1,0:T(8,128)(2,1)S(1)}, u32[]{:S(2)}, u32[]{:S(2)}) collective-permute-start(bf16[4096,128]{1,0:T(8,128)(2,1)S(1)} %bitcast.42), channel_id=1, source_target_pairs={{0,16},{16,0},{1,17},{17,1},{2,18},{18,2},{3,19},{19,3},{4,20},{20... | collective-permute-start | bytes 3145736 | tf_op jit(solution)/shard_map/ppermute | solution.py:528
  113.4 3.3 %collective-permute-start.10 = (bf16[8,128,256]{2,1,0:T(8,128)(2,1)S(1)}, bf16[8,128,256]{2,1,0:T(8,128)(2,1)S(1)}, u32[]{:S(2)}, u32[]{:S(2)}) collective-permute-start(bf16[8,128,256]{2,1,0:T(8,128)(2,1)S(1)} %dynamic-slice_bitcast_fusion), channel_id=1, source_target_pairs={{0,16},{16,0},{1,17},{17,1},{2,18},{18,2},{3,19},{19,3},{4,20},{20... | collective-permute-start | bytes 1572872 | tf_op jit(solution)/shard_map/ppermute | solution.py:535
